TPU v7x, 128 devices: a whole 4x4x4 slice. The times are simulated.
128 devices in a mesh: ctx: 32 (over z, x, core), head: 4 (over y).
Axes of the slice: x: 4, y: 4, z: 4, core: 2. Of those that a mesh axis runs over, the one named last changes fastest.
Arguments:
- inputs: bfloat16 [4096, 2048], P('ctx'), may hold values from -6 to 6
- grad_out: bfloat16 [4096, 2048], P('ctx'), may hold values from -6 to 6
- w_query: bfloat16 [2048, 4096], P(None, 'head'), may hold values from -0.125 to 0.125
- w_key: bfloat16 [2048, 4096], P(None, 'head'), may hold values from -0.125 to 0.125
- w_value: bfloat16 [2048, 4096], P(None, 'head'), may hold values from -0.125 to 0.125
- w_beta: bfloat16 [2048, 32], P(None, 'head'), may hold values from -0.125 to 0.125
- w_out: bfloat16 [4096, 2048], P('head'), may hold values from -0.09375 to 0.09375
- log_decay: float32 [4096, 32], P('ctx', 'head'), may hold values from -0.69 to 0
- lengths: int32 [16], replicated, may hold values from 1 to 1024, 4096 in all
Outputs:
- grad_x: bfloat16 [4096, 2048], P('ctx', 'head')
- grad_log_decay: float32 [4096, 32], P('ctx', 'head')
Inputs may be any that keep to these rules, and one draw needn't show every extreme that they name: The lengths sum to 4096, and the longest document has exactly 1024 tokens.
All inputs are finite; a program needn't handle non-finite values.
Results may differ from a plain program's by a relative error of at most 0.005.
Values sent between devices are 32-bit elements; how exact they have to be, the bound alone decides.
No kernel may reach another device: no remote copies, remote signals or barrier semaphores. Data moves between devices by JAX's collectives and lax.ppermute only.
A program may use at most 192 MiB of HBM per device.

v0:
```python
from functools import partial

import jax
import jax.numpy as jnp
from jax import lax
from jax.sharding import PartitionSpec as P

STRETCH = 64


def entering(array, axis, combine, identity, reverse):
    size, position = (lax.axis_size(axis), lax.axis_index(axis))
    everything = jax.tree.map(lambda part: lax.all_gather(part, axis), array)
    start = jax.tree.map(
        lambda part, zero: jnp.broadcast_to(jnp.asarray(zero, part.dtype), part.shape),
        array,
        identity,
    )

    def step(k, before):
        at = size - 1 - k if reverse else k
        reached = at > position if reverse else at < position
        new = combine(before, jax.tree.map(lambda part: part[at], everything))
        return jax.tree.map(lambda a, b: jnp.where(reached, a, b), new, before)

    return lax.fori_loop(0, size, step, start)


def normalize(raw, width):
    rows = raw.shape[0]
    shaped = raw.reshape(rows, -1, width)
    return shaped * lax.rsqrt(jnp.sum(shaped * shaped, axis=-1, keepdims=True) + 1e-06)


def stretch_step(state, pieces):
    query, key_rows, values, beta, decay, flags = pieces
    highest = lax.Precision.HIGHEST
    count = jnp.cumsum(flags)
    same = count[:, None] == count[None, :]
    length = flags.shape[0]
    index = jnp.arange(length)
    lower = index[:, None] >= index[None, :]
    strict = index[:, None] > index[None, :]
    running = jnp.cumsum(decay, axis=1)
    spread = running[:, :, None] - running[:, None, :]
    keep = jnp.logical_and(same, lower)[None]
    weight = jnp.where(keep, jnp.exp(jnp.where(keep, spread, 0.0)), 0.0)
    carried = jnp.exp(running) * (count == 0).astype(running.dtype)[None, :]
    key_key = jnp.einsum("htk,hsk->hts", key_rows, key_rows, precision=highest)
    query_key = jnp.einsum("htk,hsk->hts", query, key_rows, precision=highest)
    mixing = jnp.where(strict[None], weight, 0.0) * key_key * beta[:, :, None]
    identity = jnp.eye(length, dtype=mixing.dtype)
    known = jnp.einsum("htk,hvk->htv", key_rows, state, precision=highest)
    right = beta[:, :, None] * (values - carried[:, :, None] * known)
    fresh = jax.vmap(partial(jax.scipy.linalg.solve_triangular, lower=True, unit_diagonal=True))(
        identity[None] + mixing, right
    )
    seen = jnp.einsum("htk,hvk->htv", query, state, precision=highest)
    output = carried[:, :, None] * seen + jnp.einsum(
        "hts,hsv->htv", weight * query_key, fresh, precision=highest
    )
    closing = weight[:, -1, :]
    state = carried[:, -1][:, None, None] * state + jnp.einsum(
        "hs,hsv,hsk->hvk", closing, fresh, key_rows, precision=highest
    )
    return (state, output)


def layer_core(raw_q, raw_k, raw_v, logits, decay, flags, state):
    heads = logits.shape[1]
    width = state.shape[2]
    vwidth = state.shape[1]
    rows = raw_q.shape[0]
    blocks = rows // STRETCH
    query = normalize(raw_q, width) * width ** (-0.5)
    key_rows = normalize(raw_k, width)
    values = raw_v.reshape(rows, heads, vwidth)
    beta = jax.nn.sigmoid(logits)

    def split(array):
        array = array.reshape((blocks, STRETCH) + array.shape[1:])
        return jnp.moveaxis(array, 1, 2)

    pieces = (
        split(query),
        split(key_rows),
        split(values),
        split(beta),
        split(decay),
        flags.reshape(blocks, STRETCH),
    )
    state, output = lax.scan(stretch_step, state, pieces)
    output = jnp.moveaxis(output, 1, 2).reshape(rows, heads * vwidth)
    return (output, state)


def project_back(grad, weight):
    return lax.dot_general(
        grad.astype(jnp.bfloat16),
        weight,
        (((1,), (1,)), ((), ())),
        preferred_element_type=jnp.float32,
    )


def compose(earlier, later):
    highest = lax.Precision.HIGHEST
    joined = jnp.einsum("hij,hjk->hik", earlier[0], later[0], precision=highest)
    offset = jnp.einsum("hvj,hjk->hvk", earlier[1], later[0], precision=highest) + later[1]
    return (joined, offset)


def per_device(inputs, grad_out, w_query, w_key, w_value, w_beta, w_out, log_decay, lengths):
    rows = inputs.shape[0]
    heads = w_beta.shape[1]
    width = w_query.shape[1] // heads
    vwidth = w_value.shape[1] // heads
    raw_q = jnp.dot(inputs, w_query, preferred_element_type=jnp.float32)
    raw_k = jnp.dot(inputs, w_key, preferred_element_type=jnp.float32)
    raw_v = jnp.dot(inputs, w_value, preferred_element_type=jnp.float32)
    logits = jnp.dot(inputs, w_beta, preferred_element_type=jnp.float32)
    finish = jnp.cumsum(lengths)
    begins = finish - lengths
    places = lax.axis_index("ctx") * rows + jnp.arange(rows, dtype=jnp.int32)
    flags = jnp.sum((places[:, None] == begins[None, :]).astype(jnp.int32), axis=1)
    blank = jnp.zeros((heads, vwidth, width), jnp.float32)
    identity = jnp.broadcast_to(jnp.eye(width, dtype=jnp.float32), (heads, width, width))
    widened = jnp.concatenate(
        [raw_v.reshape(rows, heads, vwidth), jnp.zeros((rows, heads, width), jnp.float32)], axis=2
    )
    widened = widened.reshape(rows, heads * (vwidth + width))
    _, closing = layer_core(
        raw_q, raw_k, widened, logits, log_decay, flags, jnp.concatenate([blank, identity], axis=1)
    )
    offset_part = closing[:, :vwidth]
    transition = closing[:, vwidth:]
    flipped = jnp.swapaxes(transition, 1, 2)
    grad_heads = lax.dot_general(
        grad_out, w_out, (((1,), (1,)), ((), ())), preferred_element_type=jnp.float32
    )

    def outputs_only(state):
        return layer_core(raw_q, raw_k, raw_v, logits, log_decay, flags, state)[0]

    _, pull_state = jax.vjp(outputs_only, blank)
    (own_grad,) = pull_state(grad_heads)
    start_state = entering((transition, offset_part), "ctx", compose, (identity, blank), False)[1]
    end_grad = entering((flipped, own_grad), "ctx", compose, (identity, blank), True)[1]

    def forward(part_q, part_k, part_v, part_b, part_d):
        return layer_core(part_q, part_k, part_v, part_b, part_d, flags, start_state)

    _, pullback = jax.vjp(forward, raw_q, raw_k, raw_v, logits, log_decay)
    grad_q, grad_k, grad_v, grad_b, grad_d = pullback((grad_heads, end_grad))
    total = project_back(grad_q, w_query) + project_back(grad_k, w_key)
    total = total + project_back(grad_v, w_value) + project_back(grad_b, w_beta)
    grad_x = lax.psum_scatter(total, "head", scatter_dimension=1, tiled=True).astype(jnp.bfloat16)
    return (grad_x, grad_d)


def solution(mesh):
    placed = (
        P("ctx", None),
        P("ctx", None),
        P(None, "head"),
        P(None, "head"),
        P(None, "head"),
        P(None, "head"),
        P("head", None),
        P("ctx", "head"),
        P(),
    )
    return jax.shard_map(
        per_device,
        mesh=mesh,
        in_specs=placed,
        out_specs=(P("ctx", "head"), P("ctx", "head")),
        check_vma=False,
    )
```

profile of v0, /device:TPU:1, one launch (start us, length us, event | category | flops | bytes accessed | tf_op | source)
XLA Modules:
  0.0 949.3 jit_solution(12773677626569694916)
XLA Ops:
  13.5 3.9 convolution_bitcast_fusion.3
  24.0 8.5 while.177
  32.5 91.4 %while.180 = (s32[]{:T(128)}, f32[8,128,128]{2,1,0:T(8,128)S(1)}, f32[2,8,1,1]{1,3,2,0:T(1,128)S(1)}, f32[2,8,64,1]{2,1,3,0:T(8,128)S(1)}, f32[2,8,64,128]{3,2,1...) while((s32[]{:T(128)}, f32[8,128,128]{2,1,0:T(8,128)S(1)}, ...), condition=%wide.region_13.15_spmd.clone.clone, body=%wide.region_12.14_spmd.clone.sunk.clone | while | flops 403779648 | bytes 6229723 | solution.py:92
  36.3 39.3 %custom-call.55 = f32[8,1,64,64]{2,3,1,0:T(8,128)S(1)} custom-call(f32[8,1,64,64]{3,2,1,0:T(8,128)S(1)} %fusion.532), custom_call_target="InvertDiagBlocksLowerTriangular" | custom-call | tf_op jit(solution)/shard_map/transpose(jvp())/while/body/eval_jaxpr/vmap(jit(_solve_triangular))/triangular_solve/custom-call.0 | solution.py:55
  82.1 39.3 %custom-call.55 = f32[8,1,64,64]{2,3,1,0:T(8,128)S(1)} custom-call(f32[8,1,64,64]{3,2,1,0:T(8,128)S(1)} %fusion.532), custom_call_target="InvertDiagBlocksLowerTriangular" | custom-call | tf_op jit(solution)/shard_map/transpose(jvp())/while/body/eval_jaxpr/vmap(jit(_solve_triangular))/triangular_solve/custom-call.0 | solution.py:55
  129.6 96.8 %while.176 = (s32[]{:T(128)}, f32[8,256,128]{2,1,0:T(8,128)S(1)}, f32[2,8,64]{2,1,0:T(8,128)S(1)}, s32[2,64]{1,0:T(2,128)}, f32[2,8,64,128]{3,2,1,0:T(8,128)S(1)...) while((s32[]{:T(128)}, f32[8,256,128]{2,1,0:T(8,128)S(1)}, f32[2,8,64]{2,1,0:T(8,128)S(1)}, ...), condition=%wide.region_6.7_spmd.clone, body=%wide.region_3.6_spmd.sunk.clone | while | flops 555098240 | bytes 8186033 | solution.py:92
  134.7 40.0 %custom-call.51 = f32[8,1,64,64]{2,3,1,0:T(8,128)S(1)} custom-call(f32[8,1,64,64]{3,2,1,0:T(8,128)} %fusion.461), custom_call_target="InvertDiagBlocksLowerTriangular" | custom-call | tf_op jit(solution)/shard_map/while/body/eval_jaxpr/vmap(jit(_solve_triangular))/triangular_solve | solution.py:55
  183.1 40.1 %custom-call.51 = f32[8,1,64,64]{2,3,1,0:T(8,128)S(1)} custom-call(f32[8,1,64,64]{3,2,1,0:T(8,128)} %fusion.461), custom_call_target="InvertDiagBlocksLowerTriangular" | custom-call | tf_op jit(solution)/shard_map/while/body/eval_jaxpr/vmap(jit(_solve_triangular))/triangular_solve | solution.py:55
  234.4 71.7 %all-gather.9.cloned.1.call-done = f32[256,128,128]{2,1,0:T(8,128)} async-done(((f32[8,128,128]{2,1,0:T(8,128)}), f32[256,128,128]{2,1,0:T(8,128)}) %all-gather.9.cloned.1.call-update) | async-done | bytes 16777232 | tf_op jit(solution)/shard_map/all_gather | solution.py:13
  306.1 110.9 %while.181 = (s32[]{:T(128)}, f32[8,128,128]{1,2,0:T(8,128)S(1)}, s32[]{:T(128)}, f32[32,8,128,128]{3,2,1,0:T(8,128)}, f32[32,8,128,128]{3,2,1,0:T(8,128)}) while((s32[]{:T(128)}, f32[8,128,128]{1,2,0:T(8,128)S(1)}, s32[]{:T(128)}, f32[32,8,128,128]{3,2,1,0:T(8,128)}, f32[32,8,128,128]{3,2,1,0:T(8,128)}) %tuple.414), condition=%wide.region_15.17_spmd.clone.clone, body=%wide.region_14.16_spmd.clone.sunk.clone | while | flops 201850880 | bytes 5769345 | solution.py:26
  417.3 37.4 %all-gather.15.cloned.1.call-done = f32[256,128,128]{2,1,0:T(8,128)} async-done(((f32[8,128,128]{2,1,0:T(8,128)}), f32[256,128,128]{2,1,0:T(8,128)}) %all-gather.15.cloned.1.call-update) | async-done | bytes 16777232 | tf_op jit(solution)/shard_map/all_gather | solution.py:13
  454.6 109.4 %while.182 = (s32[]{:T(128)}, f32[8,128,128]{1,2,0:T(8,128)S(1)}, s32[]{:T(128)}, f32[32,8,128,128]{3,2,1,0:T(8,128)}, f32[32,8,128,128]{3,2,1,0:T(8,128)}) while((s32[]{:T(128)}, f32[8,128,128]{1,2,0:T(8,128)S(1)}, s32[]{:T(128)}, f32[32,8,128,128]{3,2,1,0:T(8,128)}, f32[32,8,128,128]{3,2,1,0:T(8,128)}) %tuple.415), condition=%wide.region_17.19_spmd.clone.clone, body=%wide.region_16.18_spmd.clone.sunk.clone | while | flops 201850880 | bytes 5769299 | solution.py:26
  574.9 112.8 %while.179 = (s32[]{:T(128)}, f32[8,128,128]{2,1,0:T(8,128)S(1)}, pred[2,8,64,64]{3,2,1,0:T(32,128)(4,1)}, f32[2,8,64,64]{3,2,1,0:T(8,128)}, f32[2,8,64]{2,1,0:T...) while((s32[]{:T(128)}, f32[8,128,128]{2,1,0:T(8,128)S(1)}, ...), condition=%wide.region_21.23_spmd.clone.clone.clone, body=%wide.region_18.22_spmd.clone.clone.sunk.clone | while | flops 454464256 | bytes 36807960 | solution.py:92
  577.7 40.7 %custom-call.54 = f32[8,1,64,64]{2,3,1,0:T(8,128)} custom-call(f32[8,1,64,64]{3,2,1,0:T(8,128)} %get-tuple-element.4018), custom_call_target="InvertDiagBlocksLowerTriangular" | custom-call | tf_op jit(solution)/shard_map/jvp()/while/body/eval_jaxpr/vmap(jit(_solve_triangular))/triangular_solve | solution.py:55
  618.5 3.1 bitcast_dynamic-update-slice_fusion.30
  634.1 40.7 %custom-call.54 = f32[8,1,64,64]{2,3,1,0:T(8,128)} custom-call(f32[8,1,64,64]{3,2,1,0:T(8,128)} %get-tuple-element.4018), custom_call_target="InvertDiagBlocksLowerTriangular" | custom-call | tf_op jit(solution)/shard_map/jvp()/while/body/eval_jaxpr/vmap(jit(_solve_triangular))/triangular_solve | solution.py:55
  674.9 3.1 bitcast_dynamic-update-slice_fusion.30
  689.3 214.7 %while.178 = (s32[]{:T(128)}, f32[8,128,128]{2,1,0:T(8,128)S(1)}, f32[2,8,64,128]{3,1,2,0:T(8,128)}, f32[2,8,64,128]{3,1,2,0:T(8,128)}, bf16[2,8,64,128]{3,2,1,0...) while((s32[]{:T(128)}, f32[8,128,128]{2,1,0:T(8,128)S(1)}, ...), condition=%wide.region_31.33_spmd.clone.clone, body=%wide.region_22.32_spmd.clone.sunk.clone | while | flops 1035022400 | bytes 39467312 | solution.py:92
  695.0 39.3 %custom-call.53 = f32[8,1,64,64]{2,3,1,0:T(8,128)S(1)} custom-call(f32[8,1,64,64]{3,2,1,0:T(8,128)S(1)} %add_bitcast_fusion.4), custom_call_target="InvertDiagBlocksLowerTriangular" | custom-call | tf_op jit(solution)/shard_map/transpose(jvp())/while/body/eval_jaxpr/vmap(jit(_solve_triangular))/triangular_solve | solution.py:55
  737.9 40.0 %custom-call.52 = f32[8,1,64,64]{2,3,1,0:T(8,128)} custom-call(f32[8,1,64,64]{3,2,1,0:T(8,128)S(1)} %fusion.496), custom_call_target="InvertDiagBlocksLowerTriangular" | custom-call | tf_op jit(solution)/shard_map/transpose(jvp())/while/body/eval_jaxpr/vmap(jit(_solve_triangular))/triangular_solve/custom-call.0 | solution.py:55
  802.1 39.3 %custom-call.53 = f32[8,1,64,64]{2,3,1,0:T(8,128)S(1)} custom-call(f32[8,1,64,64]{3,2,1,0:T(8,128)S(1)} %add_bitcast_fusion.4), custom_call_target="InvertDiagBlocksLowerTriangular" | custom-call | tf_op jit(solution)/shard_map/transpose(jvp())/while/body/eval_jaxpr/vmap(jit(_solve_triangular))/triangular_solve | solution.py:55
  845.0 40.0 %custom-call.52 = f32[8,1,64,64]{2,3,1,0:T(8,128)} custom-call(f32[8,1,64,64]{3,2,1,0:T(8,128)S(1)} %fusion.496), custom_call_target="InvertDiagBlocksLowerTriangular" | custom-call | tf_op jit(solution)/shard_map/transpose(jvp())/while/body/eval_jaxpr/vmap(jit(_solve_triangular))/triangular_solve/custom-call.0 | solution.py:55
  910.1 3.9 fusion.233
  920.2 20.6 %reduce-scatter.2.cloned.1.call-done = f32[128,512]{1,0:T(8,128)} async-done(((f32[128,2048]{1,0:T(8,128)}), f32[128,512]{1,0:T(8,128)}) %reduce-scatter.2.cloned.1.call-update) | async-done | bytes 262160 | tf_op jit(solution)/shard_map/reduce_scatter | solution.py:157
  (783 shorter events, 386.5 us)
Async XLA Ops:
  7.2 227.2 %all-gather.11.cloned.1.call-start = ((), (), s32[]{:S(2)}) async-start(), calls=%async_computation.3 | async-start | bytes 17301504 | tf_op jit(solution)/shard_map/all_gather | solution.py:13
  124.8 181.3 %all-gather.9.cloned.1.call-start = ((), (), s32[]{:S(2)}) async-start(), calls=%async_computation.2 | async-start | bytes 17301504 | tf_op jit(solution)/shard_map/all_gather | solution.py:13
  229.7 187.5 %all-gather.13.cloned.1.call-start = ((), (), s32[]{:S(2)}) async-start(), calls=%async_computation.4 | async-start | bytes 17301504 | tf_op jit(solution)/shard_map/all_gather | solution.py:13
  230.8 223.8 %all-gather.15.cloned.1.call-start = ((), (), s32[]{:S(2)}) async-start(), calls=%async_computation.5 | async-start | bytes 17301504 | tf_op jit(solution)/shard_map/all_gather | solution.py:13
  231.7 709.0 %reduce-scatter.2.cloned.1.call-start = ((), (), s32[]{:S(2)}) async-start(), calls=%async_computation.1 | async-start | bytes 1310720 | tf_op jit(solution)/shard_map/reduce_scatter | solution.py:157
  564.0 10.9 %copy-start.3 = (f32[2,8,64,128]{3,2,1,0:T(8,128)S(1)}, f32[2,8,64,128]{3,2,1,0:T(8,128)}, u32[]{:S(2)}) copy-start(f32[2,8,64,128]{3,2,1,0:T(8,128)} %copy-done.2) | copy-start | bytes 1572868
  618.4 9.0 copy-start.10
  618.4 9.0 copy-start.12
  618.4 9.0 copy-start.14
  618.4 9.0 copy-start.21
  618.4 9.0 copy-start.23
  618.4 9.0 copy-start.25
  618.4 9.0 copy-start.27
  618.5 9.0 copy-start.29
  674.8 9.0 copy-start.21
  689.3 217.2 %copy-start.55 = (f32[128,8]{0,1:T(8,128)S(1)}, f32[128,8]{0,1:T(8,128)}, u32[]{:S(2)}) copy-start(f32[128,8]{0,1:T(8,128)} %copy-done.54) | copy-start | bytes 12292
  689.3 218.9 %copy-start.53 = (f32[128,8]{0,1:T(8,128)S(1)}, f32[128,8]{0,1:T(8,128)}, u32[]{:S(2)}) copy-start(f32[128,8]{0,1:T(8,128)} %copy-done.52) | copy-start | bytes 12292
  693.9 89.4 %copy-start.49 = (f32[2,8,64]{2,1,0:T(8,128)S(1)}, f32[2,8,64]{2,1,0:T(8,128)}, u32[]{:S(2)}) copy-start(f32[2,8,64]{2,1,0:T(8,128)} %get-tuple-element.4431) | copy-start | bytes 12292 | tf_op jit(solution)/shard_map/transpose(jvp())/while
  783.7 10.1 %copy-start.33 = (f32[2,8,64,128]{3,1,2,0:T(8,128)S(1)}, f32[2,8,64,128]{3,1,2,0:T(8,128)}, u32[]{:S(2)}) copy-start(f32[2,8,64,128]{3,1,2,0:T(8,128)} %get-tuple-element.4374) | copy-start | bytes 1572868 | tf_op jit(solution)/shard_map/transpose(jvp())/while
  783.8 10.1 %copy-start.38 = (f32[2,8,64,128]{3,1,2,0:T(8,128)S(1)}, f32[2,8,64,128]{3,1,2,0:T(8,128)}, u32[]{:S(2)}) copy-start(f32[2,8,64,128]{3,1,2,0:T(8,128)} %get-tuple-element.4375) | copy-start | bytes 1572868 | tf_op jit(solution)/shard_map/transpose(jvp())/while
  801.0 89.4 %copy-start.49 = (f32[2,8,64]{2,1,0:T(8,128)S(1)}, f32[2,8,64]{2,1,0:T(8,128)}, u32[]{:S(2)}) copy-start(f32[2,8,64]{2,1,0:T(8,128)} %get-tuple-element.4431) | copy-start | bytes 12292 | tf_op jit(solution)/shard_map/transpose(jvp())/while
  890.9 10.1 %copy-start.33 = (f32[2,8,64,128]{3,1,2,0:T(8,128)S(1)}, f32[2,8,64,128]{3,1,2,0:T(8,128)}, u32[]{:S(2)}) copy-start(f32[2,8,64,128]{3,1,2,0:T(8,128)} %get-tuple-element.4374) | copy-start | bytes 1572868 | tf_op jit(solution)/shard_map/transpose(jvp())/while
  890.9 10.1 %copy-start.38 = (f32[2,8,64,128]{3,1,2,0:T(8,128)S(1)}, f32[2,8,64,128]{3,1,2,0:T(8,128)}, u32[]{:S(2)}) copy-start(f32[2,8,64,128]{3,1,2,0:T(8,128)} %get-tuple-element.4375) | copy-start | bytes 1572868 | tf_op jit(solution)/shard_map/transpose(jvp())/while
  916.0 26.3 %copy-start.1 = (bf16[128,2048]{1,0:T(8,128)(2,1)S(1)}, bf16[128,2048]{1,0:T(8,128)(2,1)}, u32[]{:S(2)}) copy-start(bf16[128,2048]{1,0:T(8,128)(2,1)} %param.25) | copy-start | bytes 1572868
  (74 other events, 297.0 us)
Sparse Core Ops, SparseCore 0:
  124.9 77.0 all-gather.10
  229.8 76.2 all-gather.8
  308.4 71.9 all-gather.12
  382.6 71.9 all-gather.14
  919.6 21.0 reduce-scatter.1
where the time goes:
time: 965 us; the launch traced here: 949 us
  other arithmetic  427 us (44%)
  matrix products  239 us (25%)
  local copies, waits for them, and re-layouts  132 us (14%)
  waiting for transfers between devices  130 us (13%)
  between operations  14.8 us (2%)
    another operation x36, other arithmetic, stretch_step(): jax.vmap(partial(jax.scipy.linalg.solve_triangular, lower=True, unit_diag...  405 us
    dot_general x64, matrix products, compose(): jnp.einsum('hvj,hjk->hvk', earlier[1], later[0], precision=highest)  132 us
    all_gather x4, waiting for transfers between devices, entering(): everything = jax.tree.map(lambda part: lax.all_gather(part, axis), array)  109 us
    dynamic_slice x128, local copies, waits for them, and re-layouts, step(): new = combine(before, jax.tree.map(lambda part: part[at], everything))  82.3 us
    reduce_scatter x1, waiting for transfers between devices, per_device(): lax.psum_scatter(total, 'head', scatter_dimension=1, tiled=True)  20.6 us
  transfers between devices with their start and end apart: 5, of which 3 were waited for; matrix products, arithmetic and copies ran while one was open for 23% of the time, Pallas kernels for 0%

commit v1 on v0

v1 whole, which is shorter than its diff:
```python
import jax
import jax.numpy as jnp
from jax import lax
from jax.experimental import pallas as pl
from jax.experimental.pallas import tpu as pltpu
from jax.sharding import PartitionSpec as P

F32 = jnp.float32
BF16 = jnp.bfloat16
W = 128
GROUP = 4
ROW = 8
NN = (((1,), (0,)), ((), ()))
NT = (((1,), (1,)), ((), ()))
TN = (((0,), (0,)), ((), ()))


def dot(a, b, dims=NN):
    return lax.dot_general(a, b, dims, preferred_element_type=F32)


def exact(a, b, dims=NN):
    return lax.dot_general(a, b, dims, precision=lax.Precision.HIGHEST, preferred_element_type=F32)


def halves(a):
    high = a.astype(BF16)
    return high, (a - high.astype(F32)).astype(BF16)


def mm3(a, b, dims=NN):
    ah, al = halves(a)
    bh, bl = halves(b)
    return dot(ah, bh, dims) + (dot(ah, bl, dims) + dot(al, bh, dims))


def iotas(shape):
    return lax.broadcasted_iota(jnp.int32, shape, 0), lax.broadcasted_iota(jnp.int32, shape, 1)


def column(array, index):
    lanes = lax.broadcasted_iota(jnp.int32, array.shape, 1)
    return jnp.sum(jnp.where(lanes == index, array, 0.0), axis=1, keepdims=True)


def inverse_all(mixes):
    ti, si = iotas((W, W))
    eye = jnp.where(ti == si, 1.0, 0.0)
    below = jnp.logical_and((ti >> 1) == (si >> 1), ti > si)
    done = [eye - jnp.where(below, a, 0.0) for a in mixes]
    for shift in range(1, 7):
        below = jnp.logical_and((ti >> (shift + 1)) == (si >> (shift + 1)), (ti >> shift) > (si >> shift))
        parts = [jnp.where(below, a, 0.0) for a in mixes]
        inner = [mm3(p, d) for p, d in zip(parts, done)]
        done = [d - mm3(d, i) for d, i in zip(done, inner)]
    return done


def first_kernel(
    len_ref, base_ref, x_ref, go_ref, wq_ref, wk_ref, wv_ref, wb_ref, wo_ref, dec_ref,
    send_ref, k_ref, q_ref, v_ref, do_ref, p_ref, l_ref, wkk_ref, w_ref, uv_ref, kw_ref, col_ref,
):
    step = pl.program_id(0)
    base = base_ref[0]
    ti, si = iotas((W, W))
    begin = jnp.int32(0)
    seg_t = jnp.zeros((W, W), jnp.int32)
    seg_s = jnp.zeros((W, W), jnp.int32)
    seg_in = jnp.int32(0)
    for j in range(len_ref.shape[0]):
        seg_t = seg_t + (ti + base >= begin).astype(jnp.int32)
        seg_s = seg_s + (si + base >= begin).astype(jnp.int32)
        seg_in = seg_in + (base - 1 >= begin).astype(jnp.int32)
        begin = begin + len_ref[j]
    keep = jnp.logical_and(seg_t == seg_s, ti >= si)
    strict = ti > si
    first = (seg_t == seg_in)[:, :1]
    x = x_ref[...]
    raw_q = dot(x, wq_ref[...])
    raw_k = dot(x, wk_ref[...])
    raw_v = dot(x, wv_ref[...])
    grad_o = dot(go_ref[...], wo_ref[...], NT)
    beta_all = 1.0 / (1.0 + jnp.exp(-dot(x, wb_ref[...])))
    tril = jnp.where(ti >= si, 1.0, 0.0)
    run_all = exact(tril, dec_ref[...])
    heads = range(GROUP)
    cut = lambda a, i: a[:, i * W:(i + 1) * W]
    ks, qs, betas, carries, weights, wkks, mixes, pmats = [], [], [], [], [], [], [], []
    for i in heads:
        head = step * GROUP + i
        rk = cut(raw_k, i)
        rq = cut(raw_q, i)
        inv_k = lax.rsqrt(jnp.sum(rk * rk, axis=1, keepdims=True) + 1e-06)
        inv_q = lax.rsqrt(jnp.sum(rq * rq, axis=1, keepdims=True) + 1e-06)
        k = rk * inv_k
        q = rq * inv_q * (W ** -0.5)
        beta = column(beta_all, head)
        run = column(run_all, head)
        run_b = jnp.broadcast_to(run, (W, W))
        spread = run_b - run_b.T
        weight = jnp.where(keep, jnp.exp(jnp.where(keep, spread, 0.0)), 0.0)
        carried = jnp.where(first, jnp.exp(run), 0.0)
        both = mm3(jnp.concatenate([k, q], axis=0), k, NT)
        wkk = jnp.where(strict, weight, 0.0) * both[:W]
        pmat = weight * both[W:]
        ks.append(k)
        qs.append(q)
        betas.append(beta)
        carries.append(carried)
        weights.append(weight)
        wkks.append(wkk)
        mixes.append(wkk * beta)
        pmats.append(pmat)
        lanes = si
        closing = jnp.sum(jnp.where(ti == si, jnp.broadcast_to(weight[W - 1:W, :], (W, W)), 0.0), axis=1, keepdims=True)
        col = jnp.where(lanes == 0, beta, jnp.where(lanes == 1, carried, jnp.where(lanes == 2, closing, jnp.where(lanes == 3, inv_k, inv_q))))
        col_ref[i] = col
        k_ref[i] = k
        q_ref[i] = q
        v_ref[i] = cut(raw_v, i)
        do_ref[i] = cut(grad_o, i)
        p_ref[i] = pmat
        wkk_ref[i] = wkk
        w_ref[i] = weight
    solved = inverse_all(mixes)
    for i in heads:
        k, q, beta, carried = ks[i], qs[i], betas[i], carries[i]
        l_ref[i] = solved[i]
        right = jnp.concatenate([beta * cut(raw_v, i), (beta * carried) * k], axis=1)
        both = mm3(solved[i], right)
        uv = both[:, :W]
        kw = both[:, W:]
        uv_ref[i] = uv
        kw_ref[i] = kw
        eff = carried * q - mm3(pmats[i], kw)
        closing = col_ref[i][:, 2:3]
        ends = mm3(jnp.concatenate([kw, uv], axis=1), closing * k, TN)
        last = carried[W - 1:W, :]
        send_ref[i, 0] = jnp.where(ti == si, last, 0.0) - ends[:W]
        send_ref[i, 1] = ends[W:]
        send_ref[i, 2] = mm3(cut(grad_o, i), eff, TN)


def row_kernel(r_ref, out_ref):
    state = r_ref[0, 1]
    grad = r_ref[ROW - 1, 2]
    for j in range(1, ROW):
        state = mm3(state, r_ref[j, 0]) + r_ref[j, 1]
        b = ROW - 1 - j
        grad = mm3(grad, r_ref[b, 0], NT) + r_ref[b, 2]
    out_ref[0] = state
    out_ref[1] = grad


def spread_kernel(r_ref, s_ref, g_ref, out_ref):
    state = s_ref[...]
    grad = g_ref[...]
    out_ref[0, 0] = state
    out_ref[ROW - 1, 1] = grad
    for j in range(1, ROW):
        state = mm3(state, r_ref[j - 1, 0]) + r_ref[j - 1, 1]
        out_ref[j, 0] = state
        b = ROW - j
        grad = mm3(grad, r_ref[b, 0], NT) + r_ref[b, 2]
        out_ref[b - 1, 1] = grad


def second_kernel(
    back_ref, k_ref, q_ref, v_ref, do_ref, p_ref, l_ref, wkk_ref, w_ref, uv_ref, kw_ref, col_ref,
    wq_ref, wk_ref, wv_ref, wb_ref, total_ref, gd_ref, cterm_ref, fterm_ref, eterm_ref, db_ref,
):
    step = pl.program_id(0)
    ti, si = iotas((W, W))
    strict = ti > si
    upper = jnp.where(si >= ti, 1.0, 0.0)
    t8, h8 = iotas((W, ROW))

    @pl.when(step == 0)
    def _():
        cterm_ref[...] = jnp.zeros((W, ROW), F32)
        fterm_ref[...] = jnp.zeros((W, ROW), F32)
        eterm_ref[...] = jnp.zeros((W, ROW), F32)
        db_ref[...] = jnp.zeros((W, ROW), F32)

    cterm, fterm, eterm, dball = cterm_ref[...], fterm_ref[...], eterm_ref[...], db_ref[...]
    gqs, gks, gvs = [], [], []
    for i in range(GROUP):
        head = step * GROUP + i
        s0, g1 = back_ref[i, 0], back_ref[i, 1]
        k, q, v, do = k_ref[i], q_ref[i], v_ref[i], do_ref[i]
        pmat, wkk, weight = p_ref[i], wkk_ref[i], w_ref[i]
        col = col_ref[i]
        beta, carried, closing, inv_k, inv_q = (col[:, j:j + 1] for j in range(5))
        u = uv_ref[i] - mm3(kw_ref[i], s0, NT)
        du = mm3(pmat, do, TN) + mm3(closing * k, g1, NT)
        dr = mm3(l_ref[i], du, TN)
        dpa = mm3(jnp.concatenate([do, dr], axis=0), u, NT)
        dp = dpa[:W]
        da = -dpa[W:]
        ds = mm3(jnp.concatenate([carried * do, dr], axis=0), s0)
        dq_state = ds[:W]
        dr_s = carried * ds[W:]
        ug = closing * mm3(u, g1)
        dqk = weight * dp
        dkk = jnp.where(strict, weight, 0.0) * da * beta
        front = mm3(jnp.concatenate([dqk, dkk], axis=0), k)
        dq = front[:W] + dq_state
        dk = front[W:] + mm3(jnp.concatenate([dkk, dqk], axis=0), jnp.concatenate([k, q], axis=0), TN)
        dk = dk - beta * dr_s + ug
        known = jnp.sum(dr_s * k, axis=1, keepdims=True)
        dbeta = jnp.sum(dr * v, axis=1, keepdims=True) - known + jnp.sum(da * wkk, axis=1, keepdims=True)
        dlogit = dbeta * beta * (1.0 - beta)
        pairs = dp * pmat + da * wkk * beta
        ph, plow = halves(pairs)
        ub = upper.astype(BF16)
        across = dot(ub, ph) + dot(ub, plow)
        evec = jnp.sum(jnp.where(strict, across, 0.0), axis=1, keepdims=True)
        fvec = jnp.sum(ug * k, axis=1, keepdims=True)
        cvec = jnp.sum(dq_state * q, axis=1, keepdims=True) - beta * known
        ends = carried[W - 1:W, :] * jnp.sum(jnp.sum(g1 * s0, axis=1, keepdims=True), axis=0, keepdims=True)
        cvec = cvec + jnp.where(t8[:, :1] == W - 1, ends, 0.0)
        here = h8 == head
        cterm = jnp.where(here, cvec, cterm)
        fterm = jnp.where(here, fvec, fterm)
        eterm = jnp.where(here, evec, eterm)
        dball = jnp.where(here, dlogit, dball)
        gk = inv_k * (dk - k * jnp.sum(k * dk, axis=1, keepdims=True))
        gq = (inv_q * (W ** -0.5)) * (dq - (q * float(W)) * jnp.sum(q * dq, axis=1, keepdims=True))
        gqs.append(gq.astype(BF16))
        gks.append(gk.astype(BF16))
        gvs.append((beta * dr).astype(BF16))
    cterm_ref[...], fterm_ref[...], eterm_ref[...], db_ref[...] = cterm, fterm, eterm, dball
    part = dot(jnp.concatenate(gqs, axis=1), wq_ref[...], NT)
    part = part + dot(jnp.concatenate(gks, axis=1), wk_ref[...], NT)
    part = part + dot(jnp.concatenate(gvs, axis=1), wv_ref[...], NT)

    @pl.when(step == 0)
    def _():
        total_ref[...] = part

    @pl.when(step > 0)
    def _():
        total_ref[...] += part

    @pl.when(step == pl.num_programs(0) - 1)
    def _():
        total_ref[...] += dot(dball.astype(BF16), wb_ref[...], NT)
        lower = jnp.where(strict, 1.0, 0.0)
        gd_ref[...] = exact(upper, cterm) + exact(lower, fterm) + eterm


def per_device(inputs, grad_out, w_query, w_key, w_value, w_beta, w_out, log_decay, lengths):
    rows, width = inputs.shape
    heads = w_beta.shape[1]
    steps = heads // GROUP
    span = GROUP * W
    base = (lax.axis_index("ctx") * rows).astype(jnp.int32).reshape(1)
    smem = pl.BlockSpec(memory_space=pltpu.SMEM)
    whole = lambda *shape: pl.BlockSpec(shape, lambda g: (0,) * len(shape))
    mats = pl.BlockSpec((GROUP, W, W), lambda g: (g, 0, 0))
    cols = pl.BlockSpec((width, span), lambda g: (0, g))
    mat_shape = jax.ShapeDtypeStruct((heads, W, W), F32)
    params = pltpu.CompilerParams(dimension_semantics=("arbitrary",), vmem_limit_bytes=56 << 20)
    send, *kept = pl.pallas_call(
        first_kernel,
        grid=(steps,),
        in_specs=[
            smem, smem, whole(rows, width), whole(rows, width), cols, cols, cols, whole(width, heads),
            pl.BlockSpec((span, width), lambda g: (g, 0)), whole(rows, heads),
        ],
        out_specs=[pl.BlockSpec((GROUP, 3, W, W), lambda g: (g, 0, 0, 0))] + [mats] * 11,
        out_shape=[jax.ShapeDtypeStruct((heads, 3, W, W), F32)] + [mat_shape] * 11,
        compiler_params=params,
        name="block_forward",
    )(lengths, base, inputs, grad_out, w_query, w_key, w_value, w_beta, w_out, log_decay)
    size = lax.axis_size("ctx")
    groups = [[z * ROW + j for j in range(ROW)] for z in range(size // ROW)]
    mine = lax.all_to_all(send, "ctx", 0, 0, axis_index_groups=groups, tiled=True)
    small = pltpu.CompilerParams(vmem_limit_bytes=32 << 20)
    ends = pl.pallas_call(
        row_kernel, out_shape=jax.ShapeDtypeStruct((2, W, W), F32), compiler_params=small, name="row_ends"
    )(mine)
    state = lax.ppermute(ends[0], "ctx", [(j, j + ROW) for j in range(size - ROW)])
    grad = lax.ppermute(ends[1], "ctx", [(j + ROW, j) for j in range(size - ROW)])
    spread = pl.pallas_call(
        spread_kernel, out_shape=jax.ShapeDtypeStruct((ROW, 2, W, W), F32), compiler_params=small, name="row_states"
    )(mine, state, grad)
    back = lax.all_to_all(spread, "ctx", 0, 0, axis_index_groups=groups, tiled=True)
    total, grad_d = pl.pallas_call(
        second_kernel,
        grid=(steps,),
        in_specs=[pl.BlockSpec((GROUP, 2, W, W), lambda g: (g, 0, 0, 0))] + [mats] * 11 + [cols, cols, cols, whole(width, heads)],
        out_specs=[whole(rows, width), whole(rows, heads)],
        out_shape=[jax.ShapeDtypeStruct((rows, width), F32), jax.ShapeDtypeStruct((rows, heads), F32)],
        scratch_shapes=[pltpu.VMEM((rows, heads), F32)] * 4,
        compiler_params=params,
        name="block_backward",
    )(back, *kept, w_query, w_key, w_value, w_beta)
    grad_x = lax.psum_scatter(total, "head", scatter_dimension=1, tiled=True).astype(BF16)
    return (grad_x, grad_d)


def solution(mesh):
    placed = (
        P("ctx", None),
        P("ctx", None),
        P(None, "head"),
        P(None, "head"),
        P(None, "head"),
        P(None, "head"),
        P("head", None),
        P("ctx", "head"),
        P(),
    )
    return jax.shard_map(
        per_device,
        mesh=mesh,
        in_specs=placed,
        out_specs=(P("ctx", "head"), P("ctx", "head")),
        check_vma=False,
    )
```

time: 965 us -> 135 us (0.14); the launches traced: 949 us -> 134 us
  other arithmetic: 427 us -> 1.62 us
  matrix products: 239 us -> 0 us
  local copies, waits for them, and re-layouts: 132 us -> 4.69 us
  waiting for transfers between devices: 130 us -> 23.8 us
  blocking collectives: 0 us -> 46.7 us
  Pallas kernels: 0 us -> 38 us
    another operation x58 -> x0, other arithmetic: 408 us -> none  [the longest x36 405 us: stretch_step(): jax.vmap(partial(jax.scipy.linalg.solve_triangular, lower=True, unit_diag...]
    dot_general x127 -> x0, matrix products: 227 us -> none  [the longest x64 132 us: compose(): jnp.einsum('hvj,hjk->hvk', earlier[1], later[0], precision=highest)]
    all_gather x4 -> x0, waiting for transfers between devices: 109 us -> none  [entering(): everything = jax.tree.map(lambda part: lax.all_gather(part, axis), array)]
    dynamic_slice x130 -> x0, local copies, waits for them, and re-layouts: 84.5 us -> none  [the longest x128 82.3 us: step(): new = combine(before, jax.tree.map(lambda part: part[at], everything))]
    all_to_all x0 -> x2, blocking collectives: none -> 46.7 us  [the longest x1 26.6 us: per_device(): lax.all_to_all(send, 'ctx', 0, 0, axis_index_groups=groups, tiled=True)]
    pallas_call x0 -> x4, Pallas kernels: none -> 38 us  [the longest x1 18.4 us: per_device(): pl.pallas_call(first_kernel, grid=(steps,), in_specs=[smem, smem, whole(r...]
    another operation x40 -> x0, local copies, waits for them, and re-layouts: 19.2 us -> none
    another operation x10 -> x0, matrix products: 12.4 us -> none  [stretch_step(): jax.vmap(partial(jax.scipy.linalg.solve_triangular, lower=True, unit_diag...]
  transfers between devices with their start and end apart: 5 -> 3, of which waited for: 3 -> 2; matrix products, arithmetic and copies ran while one was open for 23% -> 1% of each run, Pallas kernels for 0% -> 0%
where the time goes in v1:
time: 135 us; the launch traced here: 134 us
  blocking collectives  46.7 us (35%)
  Pallas kernels  38 us (28%)
  waiting for transfers between devices  23.8 us (18%)
  between operations  14.1 us (10%)
  starting transfers between devices  5.5 us (4%)
  local copies, waits for them, and re-layouts  4.69 us (3%)
  other arithmetic  1.62 us (1%)
    all_to_all x1, blocking collectives, per_device(): lax.all_to_all(send, 'ctx', 0, 0, axis_index_groups=groups, tiled=True)  26.6 us
    reduce_scatter x1, waiting for transfers between devices, per_device(): lax.psum_scatter(total, 'head', scatter_dimension=1, tiled=True)  22.5 us
    all_to_all x1, blocking collectives, per_device(): lax.all_to_all(spread, 'ctx', 0, 0, axis_index_groups=groups, tiled=True)  20.2 us
    pallas_call x1, Pallas kernels, per_device(): pl.pallas_call(first_kernel, grid=(steps,), in_specs=[smem, smem, whole(r...  18.4 us
    pallas_call x1, Pallas kernels, per_device(): pl.pallas_call(second_kernel, grid=(steps,), in_specs=[pl.BlockSpec((GROU...  16.7 us
    unnamed x3, local copies, waits for them, and re-layouts  4.68 us
    ppermute x1, starting transfers between devices, per_device(): lax.ppermute(ends[0], 'ctx', [(j, j + ROW) for j in range(size - ROW)])  4.17 us
  transfers between devices with their start and end apart: 3, of which 2 were waited for; matrix products, arithmetic and copies ran while one was open for 1% of the time, Pallas kernels for 0%

profile of v1, /device:TPU:1, one launch (start us, length us, event | category | flops | bytes accessed | tf_op | source)
XLA Modules:
  0.0 134.4 jit_solution(3502301085610926036)
XLA Ops:
  7.2 0.0 reduce-scatter.2.cloned.1.call-start
  7.2 1.4 %copy.12.dec_ref = f32[128,8]{1,0:T(8,128)} copy(f32[128,8]{0,1:T(8,128)} %param.16) | data formatting | bytes 8192 | tf_op args[7]
  8.6 1.8 %copy.11.wb_ref = bf16[2048,8]{1,0:T(8,128)(2,1)} copy(bf16[2048,8]{0,1:T(8,128)(2,1)} %param.14) | data formatting | bytes 65536 | tf_op args[5]
  10.4 18.4 %block_forward.1 = (f32[8,3,128,128]{3,2,1,0:T(8,128)}, f32[8,128,128]{2,1,0:T(8,128)}, f32[8,128,128]{2,1,0:T(8,128)}, f32[8,128,128]{2,1,0:T(8,128)}, f32[8,12...) custom-call(s32[16]{0:T(128)} %len_ref.1, ...), custom_call_target="tpu_custom_call" | custom-call | tf_op jit(solution)/shard_map/block_forward/pallas_call | solution.py:264
  28.8 26.6 %all_to_all.10.r_ref = f32[8,3,128,128]{3,2,1,0:T(8,128)S(1)} all-to-all(f32[8,3,128,128]{3,2,1,0:T(8,128)} %get-tuple-element.16), channel_id=1, replica_groups={{0,4,8,12,16,20,24,28},{32,36,40,44,48,52,56,60},{64,68,72,76,80,84,88,..., dimensions={0} | all-to-all | bytes 3145728 | tf_op jit(solution)/shard_map/all_to_all | solution.py:278
  55.3 1.4 %row_ends.1 = f32[2,128,128]{2,1,0:T(8,128)S(1)} custom-call(f32[8,3,128,128]{3,2,1,0:T(8,128)S(1)} %all_to_all.10.r_ref), custom_call_target="tpu_custom_call" | custom-call | tf_op jit(solution)/shard_map/row_ends/pallas_call | solution.py:280
  56.8 1.3 collective-permute-start.1
  58.1 4.2 %collective-permute-start = (f32[128,128]{1,0:T(8,128)S(1)}, f32[128,128]{1,0:T(8,128)S(1)}, u32[]{:S(2)}, u32[]{:S(2)}) collective-permute-start(f32[128,128]{1,0:T(8,128)S(1)} %get-tuple-element.33), channel_id=1, source_target_pairs={{0,32},{4,36},{8,40},{12,44},{16,48},{20,52},{24,56},{28,60},{32,6... | collective-permute-start | bytes 196616 | tf_op jit(solution)/shard_map/ppermute | solution.py:283
  62.3 0.0 collective-permute-done.1.g_ref
  62.3 1.3 collective-permute-done.s_ref
  63.6 1.4 %row_states.1 = f32[8,2,128,128]{3,2,1,0:T(8,128)S(1)} custom-call(f32[8,3,128,128]{3,2,1,0:T(8,128)S(1)} %all_to_all.10.r_ref, f32[128,128]{1,0:T(8,128)S(1)} %collective-permute-done.s_ref, f32[128,128]{1,0:T(8,128)S(1)} %collective-permute-done.1.g_ref), custom_call_target="tpu_custom_call" | custom-call | tf_op jit(solution)/shard_map/row_states/pallas_call | solution.py:285
  65.0 20.2 %all_to_all.11.back_ref = f32[8,2,128,128]{3,2,1,0:T(8,128)} all-to-all(f32[8,2,128,128]{3,2,1,0:T(8,128)S(1)} %row_states.1), channel_id=1, replica_groups={{0,4,8,12,16,20,24,28},{32,36,40,44,48,52,56,60},{64,68,72,76,80,84,88,..., dimensions={0} | all-to-all | bytes 2097152 | tf_op jit(solution)/shard_map/all_to_all | solution.py:288
  85.2 16.7 %block_backward.1 = (f32[128,2048]{1,0:T(8,128)}, f32[128,8]{1,0:T(8,128)}) custom-call(f32[8,2,128,128]{3,2,1,0:T(8,128)} %all_to_all.11.back_ref, f32[8,128,128]{2,1,0:T(8,128)} %get-tuple-element.17.k_ref, f32[8,128,128]{2,1,0:T(8,128)} %get-tuple-element.18.q_ref, f32[8,128,128]{2,1,0:T(8,128)} %get-tuple-element.19.v_ref, ...), custom_call_target="tpu_custom_call" | custom-call | tf_op jit(solution)/shard_map/block_backward/pallas_call | solution.py:289
  101.9 0.0 reduce-scatter.2.cloned.1.call-update
  101.9 1.5 %copy.14 = f32[128,8]{0,1:T(8,128)} copy(f32[128,8]{1,0:T(8,128)} %get-tuple-element.31) | data formatting | bytes 8192
  103.4 22.5 %reduce-scatter.2.cloned.1.call-done = f32[128,512]{1,0:T(8,128)} async-done(((f32[128,2048]{1,0:T(8,128)}), f32[128,512]{1,0:T(8,128)}) %reduce-scatter.2.cloned.1.call-update) | async-done | bytes 262160 | tf_op jit(solution)/shard_map/reduce_scatter | solution.py:299
  125.9 1.6 %convert_element_type.3 = bf16[128,512]{1,0:T(8,128)(2,1)} convert(f32[128,512]{1,0:T(8,128)} %reduce-scatter.2.cloned.1.call-done) | non-fusion elementwise | flops 65536 | bytes 393216 | tf_op jit(solution)/shard_map/convert_element_type | solution.py:299
  (1 shorter events, 0.0 us)
Async XLA Ops:
  7.2 118.7 %reduce-scatter.2.cloned.1.call-start = ((), (), s32[]{:S(2)}) async-start(), calls=%async_computation.3 | async-start | bytes 1310720 | tf_op jit(solution)/shard_map/reduce_scatter | solution.py:299
  56.8 5.5 %collective-permute-start.1 = (f32[128,128]{1,0:T(8,128)S(1)}, f32[128,128]{1,0:T(8,128)S(1)}, u32[]{:S(2)}, u32[]{:S(2)}) collective-permute-start(f32[128,128]{1,0:T(8,128)S(1)} %get-tuple-element.32), channel_id=1, source_target_pairs={{32,0},{36,4},{40,8},{44,12},{48,16},{52,20},{56,24},{60,28},{64,3... | collective-permute-start | bytes 196616 | tf_op jit(solution)/shard_map/ppermute | solution.py:284
  58.1 5.5 %collective-permute-start = (f32[128,128]{1,0:T(8,128)S(1)}, f32[128,128]{1,0:T(8,128)S(1)}, u32[]{:S(2)}, u32[]{:S(2)}) collective-permute-start(f32[128,128]{1,0:T(8,128)S(1)} %get-tuple-element.33), channel_id=1, source_target_pairs={{0,32},{4,36},{8,40},{12,44},{16,48},{20,52},{24,56},{28,60},{32,6... | collective-permute-start | bytes 196616 | tf_op jit(solution)/shard_map/ppermute | solution.py:283
Sparse Core Ops, SparseCore 0:
  102.0 23.7 reduce-scatter.1

commit v2 on v1

--- a/solution.py
+++ b/solution.py
@@ -80,9 +80,10 @@
     raw_k = dot(x, wk_ref[...])
     raw_v = dot(x, wv_ref[...])
     grad_o = dot(go_ref[...], wo_ref[...], NT)
-    beta_all = 1.0 / (1.0 + jnp.exp(-dot(x, wb_ref[...])))
+    beta_all = 1.0 / (1.0 + jnp.exp(-dot(x, wb_ref[...], NT)))
     tril = jnp.where(ti >= si, 1.0, 0.0)
-    run_all = exact(tril, dec_ref[...])
+    run_all = exact(tril, dec_ref[...], NT)
+    run_rows = exact(dec_ref[...], tril, NT)
     heads = range(GROUP)
     cut = lambda a, i: a[:, i * W:(i + 1) * W]
     ks, qs, betas, carries, weights, wkks, mixes, pmats = [], [], [], [], [], [], [], []
@@ -96,8 +97,8 @@
         q = rq * inv_q * (W ** -0.5)
         beta = column(beta_all, head)
         run = column(run_all, head)
-        run_b = jnp.broadcast_to(run, (W, W))
-        spread = run_b - run_b.T
+        heads_at = lax.broadcasted_iota(jnp.int32, run_rows.shape, 0)
+        spread = run - jnp.sum(jnp.where(heads_at == head, run_rows, 0.0), axis=0, keepdims=True)
         weight = jnp.where(keep, jnp.exp(jnp.where(keep, spread, 0.0)), 0.0)
         carried = jnp.where(first, jnp.exp(run), 0.0)
         both = mm3(jnp.concatenate([k, q], axis=0), k, NT)
@@ -234,19 +235,22 @@
     part = part + dot(jnp.concatenate(gks, axis=1), wk_ref[...], NT)
     part = part + dot(jnp.concatenate(gvs, axis=1), wv_ref[...], NT)
 
+    chunks, _, wide = total_ref.shape
+
     @pl.when(step == 0)
     def _():
-        total_ref[...] = part
+        for c in range(chunks):
+            total_ref[c] = part[:, c * wide:(c + 1) * wide]
 
     @pl.when(step > 0)
     def _():
-        total_ref[...] += part
-
-    @pl.when(step == pl.num_programs(0) - 1)
-    def _():
-        total_ref[...] += dot(dball.astype(BF16), wb_ref[...], NT)
+        full = part + dot(dball.astype(BF16), wb_ref[...])
+        for c in range(chunks):
+            total_ref[c] += full[:, c * wide:(c + 1) * wide]
         lower = jnp.where(strict, 1.0, 0.0)
-        gd_ref[...] = exact(upper, cterm) + exact(lower, fterm) + eterm
+        eye = jnp.where(ti == si, 1.0, 0.0)
+        turn = (((0,), (1,)), ((), ()))
+        gd_ref[...] = exact(cterm, upper, turn) + exact(fterm, lower, turn) + exact(eterm, eye, turn)
 
 
 def per_device(inputs, grad_out, w_query, w_key, w_value, w_beta, w_out, log_decay, lengths):
@@ -265,14 +269,14 @@
         first_kernel,
         grid=(steps,),
         in_specs=[
-            smem, smem, whole(rows, width), whole(rows, width), cols, cols, cols, whole(width, heads),
-            pl.BlockSpec((span, width), lambda g: (g, 0)), whole(rows, heads),
+            smem, smem, whole(rows, width), whole(rows, width), cols, cols, cols, whole(heads, width),
+            pl.BlockSpec((span, width), lambda g: (g, 0)), whole(heads, rows),
         ],
         out_specs=[pl.BlockSpec((GROUP, 3, W, W), lambda g: (g, 0, 0, 0))] + [mats] * 11,
         out_shape=[jax.ShapeDtypeStruct((heads, 3, W, W), F32)] + [mat_shape] * 11,
         compiler_params=params,
         name="block_forward",
-    )(lengths, base, inputs, grad_out, w_query, w_key, w_value, w_beta, w_out, log_decay)
+    )(lengths, base, inputs, grad_out, w_query, w_key, w_value, w_beta.T, w_out, log_decay.T)
     size = lax.axis_size("ctx")
     groups = [[z * ROW + j for j in range(ROW)] for z in range(size // ROW)]
     mine = lax.all_to_all(send, "ctx", 0, 0, axis_index_groups=groups, tiled=True)
@@ -286,18 +290,19 @@
         spread_kernel, out_shape=jax.ShapeDtypeStruct((ROW, 2, W, W), F32), compiler_params=small, name="row_states"
     )(mine, state, grad)
     back = lax.all_to_all(spread, "ctx", 0, 0, axis_index_groups=groups, tiled=True)
+    sides = lax.axis_size("head")
     total, grad_d = pl.pallas_call(
         second_kernel,
         grid=(steps,),
-        in_specs=[pl.BlockSpec((GROUP, 2, W, W), lambda g: (g, 0, 0, 0))] + [mats] * 11 + [cols, cols, cols, whole(width, heads)],
-        out_specs=[whole(rows, width), whole(rows, heads)],
-        out_shape=[jax.ShapeDtypeStruct((rows, width), F32), jax.ShapeDtypeStruct((rows, heads), F32)],
+        in_specs=[pl.BlockSpec((GROUP, 2, W, W), lambda g: (g, 0, 0, 0))] + [mats] * 11 + [cols, cols, cols, whole(heads, width)],
+        out_specs=[whole(sides, rows, width // sides), whole(heads, rows)],
+        out_shape=[jax.ShapeDtypeStruct((sides, rows, width // sides), F32), jax.ShapeDtypeStruct((heads, rows), F32)],
         scratch_shapes=[pltpu.VMEM((rows, heads), F32)] * 4,
         compiler_params=params,
         name="block_backward",
-    )(back, *kept, w_query, w_key, w_value, w_beta)
-    grad_x = lax.psum_scatter(total, "head", scatter_dimension=1, tiled=True).astype(BF16)
-    return (grad_x, grad_d)
+    )(back, *kept, w_query, w_key, w_value, w_beta.T)
+    grad_x = jnp.sum(lax.all_to_all(total, "head", 0, 0, tiled=True), axis=0).astype(BF16)
+    return (grad_x, grad_d.T)
 
 
 def solution(mesh):

time: 135 us -> 113 us (0.84); the launches traced: 134 us -> 111 us
  waiting for transfers between devices: 23.8 us -> 1.3 us
  blocking collectives: 46.7 us -> 64.5 us
  between operations: 14.1 us -> 0.7 us
  local copies, waits for them, and re-layouts: 4.69 us -> 0.01 us
    reduce_scatter x1 -> x0, waiting for transfers between devices: 22.5 us -> none  [per_device(): lax.psum_scatter(total, 'head', scatter_dimension=1, tiled=True)]
    all_to_all x0 -> x1, blocking collectives: none -> 17.7 us  [per_device(): lax.all_to_all(total, 'head', 0, 0, tiled=True)]
    unnamed x3 -> x0, local copies, waits for them, and re-layouts: 4.68 us -> none
    convert_element_type x1 -> x0, other arithmetic: 1.62 us -> none  [per_device(): lax.psum_scatter(total, 'head', scatter_dimension=1, tiled=True)]
  transfers between devices with their start and end apart: 3 -> 2, of which waited for: 2 -> 1; matrix products, arithmetic and copies ran while one was open for 1% -> 0% of each run, Pallas kernels for 0% -> 0%
where the time goes in v2:
time: 113 us; the launch traced here: 111 us
  blocking collectives  64.5 us (57%)
  Pallas kernels  38 us (34%)
  starting transfers between devices  5.46 us (5%)
  waiting for transfers between devices  1.3 us (1%)
    all_to_all x1, blocking collectives, per_device(): lax.all_to_all(send, 'ctx', 0, 0, axis_index_groups=groups, tiled=True)  26.6 us
    all_to_all x1, blocking collectives, per_device(): lax.all_to_all(spread, 'ctx', 0, 0, axis_index_groups=groups, tiled=True)  20.2 us
    pallas_call x1, Pallas kernels, per_device(): pl.pallas_call(first_kernel, grid=(steps,), in_specs=[smem, smem, whole(r...  18.3 us
    all_to_all x1, blocking collectives, per_device(): lax.all_to_all(total, 'head', 0, 0, tiled=True)  17.7 us
    pallas_call x1, Pallas kernels, per_device(): pl.pallas_call(second_kernel, grid=(steps,), in_specs=[pl.BlockSpec((GROU...  16.8 us
    ppermute x1, starting transfers between devices, per_device(): lax.ppermute(ends[0], 'ctx', [(j, j + ROW) for j in range(size - ROW)])  4.17 us
  transfers between devices with their start and end apart: 2, of which 1 were waited for; matrix products, arithmetic and copies ran while one was open for 0% of the time, Pallas kernels for 0%

profile of v2, /device:TPU:1, one launch (start us, length us, event | category | flops | bytes accessed | tf_op | source)
XLA Modules:
  0.0 110.6 jit_solution(10903032510985872447)
XLA Ops:
  0.6 18.3 %block_forward.1 = (f32[8,3,128,128]{3,2,1,0:T(8,128)}, f32[8,128,128]{2,1,0:T(8,128)}, f32[8,128,128]{2,1,0:T(8,128)}, f32[8,128,128]{2,1,0:T(8,128)}, f32[8,12...) custom-call(s32[16]{0:T(128)} %len_ref.1, ...), custom_call_target="tpu_custom_call" | custom-call | tf_op jit(solution)/shard_map/block_forward/pallas_call | solution.py:268
  18.9 26.6 %all_to_all.15.r_ref = f32[8,3,128,128]{3,2,1,0:T(8,128)S(1)} all-to-all(f32[8,3,128,128]{3,2,1,0:T(8,128)} %get-tuple-element.16), channel_id=1, replica_groups={{0,4,8,12,16,20,24,28},{32,36,40,44,48,52,56,60},{64,68,72,76,80,84,88,..., dimensions={0} | all-to-all | bytes 3145728 | tf_op jit(solution)/shard_map/all_to_all | solution.py:282
  45.5 1.4 %row_ends.1 = f32[2,128,128]{2,1,0:T(8,128)S(1)} custom-call(f32[8,3,128,128]{3,2,1,0:T(8,128)S(1)} %all_to_all.15.r_ref), custom_call_target="tpu_custom_call" | custom-call | tf_op jit(solution)/shard_map/row_ends/pallas_call | solution.py:284
  46.9 1.3 %collective-permute-start.1 = (f32[128,128]{1,0:T(8,128)S(1)}, f32[128,128]{1,0:T(8,128)S(1)}, u32[]{:S(2)}, u32[]{:S(2)}) collective-permute-start(f32[128,128]{1,0:T(8,128)S(1)} %get-tuple-element.30), channel_id=1, source_target_pairs={{32,0},{36,4},{40,8},{44,12},{48,16},{52,20},{56,24},{60,28},{64,3... | collective-permute-start | bytes 196616 | tf_op jit(solution)/shard_map/ppermute | solution.py:288
  48.2 4.2 %collective-permute-start = (f32[128,128]{1,0:T(8,128)S(1)}, f32[128,128]{1,0:T(8,128)S(1)}, u32[]{:S(2)}, u32[]{:S(2)}) collective-permute-start(f32[128,128]{1,0:T(8,128)S(1)} %get-tuple-element.31), channel_id=1, source_target_pairs={{0,32},{4,36},{8,40},{12,44},{16,48},{20,52},{24,56},{28,60},{32,6... | collective-permute-start | bytes 196616 | tf_op jit(solution)/shard_map/ppermute | solution.py:287
  52.4 0.0 collective-permute-done.1.g_ref
  52.4 1.3 %collective-permute-done.s_ref = f32[128,128]{1,0:T(8,128)S(1)} collective-permute-done((f32[128,128]{1,0:T(8,128)S(1)}, f32[128,128]{1,0:T(8,128)S(1)}, u32[]{:S(2)}, u32[]{:S(2)}) %collective-permute-start) | collective-permute-done | bytes 65568 | tf_op jit(solution)/shard_map/ppermute | solution.py:287
  53.7 1.4 %row_states.1 = f32[8,2,128,128]{3,2,1,0:T(8,128)S(1)} custom-call(f32[8,3,128,128]{3,2,1,0:T(8,128)S(1)} %all_to_all.15.r_ref, f32[128,128]{1,0:T(8,128)S(1)} %collective-permute-done.s_ref, f32[128,128]{1,0:T(8,128)S(1)} %collective-permute-done.1.g_ref), custom_call_target="tpu_custom_call" | custom-call | tf_op jit(solution)/shard_map/row_states/pallas_call | solution.py:289
  55.2 20.2 %all_to_all.16.back_ref = f32[8,2,128,128]{3,2,1,0:T(8,128)} all-to-all(f32[8,2,128,128]{3,2,1,0:T(8,128)S(1)} %row_states.1), channel_id=1, replica_groups={{0,4,8,12,16,20,24,28},{32,36,40,44,48,52,56,60},{64,68,72,76,80,84,88,..., dimensions={0} | all-to-all | bytes 2097152 | tf_op jit(solution)/shard_map/all_to_all | solution.py:292
  75.3 16.8 %block_backward.1 = (f32[4,128,512]{2,1,0:T(8,128)}, f32[8,128]{1,0:T(8,128)}) custom-call(f32[8,2,128,128]{3,2,1,0:T(8,128)} %all_to_all.16.back_ref, f32[8,128,128]{2,1,0:T(8,128)} %get-tuple-element.17.k_ref, f32[8,128,128]{2,1,0:T(8,128)} %get-tuple-element.18.q_ref, f32[8,128,128]{2,1,0:T(8,128)} %get-tuple-element.19.v_ref, ...), custom_call_target="tpu_custom_call" | custom-call | tf_op jit(solution)/shard_map/block_backward/pallas_call | solution.py:294
  92.2 17.7 %all_to_all.17 = f32[4,128,512]{2,1,0:T(8,128)S(1)} all-to-all(f32[4,128,512]{2,1,0:T(8,128)} %get-tuple-element.28), channel_id=1, replica_groups=mesh['ctx'=32,'head'=4] {'head'}, dimensions={0} | all-to-all | bytes 2097152 | tf_op jit(solution)/shard_map/all_to_all | solution.py:304
  109.9 0.8 reduce_sum.9
  (1 shorter events, 0.0 us)
Async XLA Ops:
  46.9 5.5 %collective-permute-start.1 = (f32[128,128]{1,0:T(8,128)S(1)}, f32[128,128]{1,0:T(8,128)S(1)}, u32[]{:S(2)}, u32[]{:S(2)}) collective-permute-start(f32[128,128]{1,0:T(8,128)S(1)} %get-tuple-element.30), channel_id=1, source_target_pairs={{32,0},{36,4},{40,8},{44,12},{48,16},{52,20},{56,24},{60,28},{64,3... | collective-permute-start | bytes 196616 | tf_op jit(solution)/shard_map/ppermute | solution.py:288
  48.2 5.5 %collective-permute-start = (f32[128,128]{1,0:T(8,128)S(1)}, f32[128,128]{1,0:T(8,128)S(1)}, u32[]{:S(2)}, u32[]{:S(2)}) collective-permute-start(f32[128,128]{1,0:T(8,128)S(1)} %get-tuple-element.31), channel_id=1, source_target_pairs={{0,32},{4,36},{8,40},{12,44},{16,48},{20,52},{24,56},{28,60},{32,6... | collective-permute-start | bytes 196616 | tf_op jit(solution)/shard_map/ppermute | solution.py:287

commit v3 on v2

--- a/solution.py
+++ b/solution.py
@@ -1,3 +1,5 @@
+from functools import partial
+
 import jax
 import jax.numpy as jnp
 from jax import lax
@@ -9,7 +11,6 @@
 BF16 = jnp.bfloat16
 W = 128
 GROUP = 4
-ROW = 8
 NN = (((1,), (0,)), ((), ()))
 NT = (((1,), (1,)), ((), ()))
 TN = (((0,), (0,)), ((), ()))
@@ -57,38 +58,46 @@
 
 
 def first_kernel(
-    len_ref, base_ref, x_ref, go_ref, wq_ref, wk_ref, wv_ref, wb_ref, wo_ref, dec_ref,
+    meta_ref, x_ref, go_ref, wb_ref, dec_ref, wk_hbm, wq_hbm, wo_hbm, wv_hbm,
     send_ref, k_ref, q_ref, v_ref, do_ref, p_ref, l_ref, wkk_ref, w_ref, uv_ref, kw_ref, col_ref,
+    wk_ref, wq_ref, wo_ref, wv_ref, sems,
 ):
-    step = pl.program_id(0)
-    base = base_ref[0]
+    head0 = meta_ref[0]
+    base = meta_ref[1]
+    at = pl.ds(pl.multiple_of(head0 * W, GROUP * W), GROUP * W)
+    get_k = pltpu.make_async_copy(wk_hbm.at[:, at], wk_ref, sems.at[0])
+    get_q = pltpu.make_async_copy(wq_hbm.at[:, at], wq_ref, sems.at[1])
+    get_o = pltpu.make_async_copy(wo_hbm.at[at, :], wo_ref, sems.at[2])
+    get_v = pltpu.make_async_copy(wv_hbm.at[:, at], wv_ref, sems.at[3])
+    for get in (get_k, get_q, get_v, get_o):
+        get.start()
     ti, si = iotas((W, W))
     begin = jnp.int32(0)
     seg_t = jnp.zeros((W, W), jnp.int32)
     seg_s = jnp.zeros((W, W), jnp.int32)
     seg_in = jnp.int32(0)
-    for j in range(len_ref.shape[0]):
+    for j in range(2, meta_ref.shape[0]):
         seg_t = seg_t + (ti + base >= begin).astype(jnp.int32)
         seg_s = seg_s + (si + base >= begin).astype(jnp.int32)
         seg_in = seg_in + (base - 1 >= begin).astype(jnp.int32)
-        begin = begin + len_ref[j]
+        begin = begin + meta_ref[j]
     keep = jnp.logical_and(seg_t == seg_s, ti >= si)
     strict = ti > si
     first = (seg_t == seg_in)[:, :1]
     x = x_ref[...]
-    raw_q = dot(x, wq_ref[...])
-    raw_k = dot(x, wk_ref[...])
-    raw_v = dot(x, wv_ref[...])
-    grad_o = dot(go_ref[...], wo_ref[...], NT)
     beta_all = 1.0 / (1.0 + jnp.exp(-dot(x, wb_ref[...], NT)))
     tril = jnp.where(ti >= si, 1.0, 0.0)
     run_all = exact(tril, dec_ref[...], NT)
     run_rows = exact(dec_ref[...], tril, NT)
     heads = range(GROUP)
     cut = lambda a, i: a[:, i * W:(i + 1) * W]
-    ks, qs, betas, carries, weights, wkks, mixes, pmats = [], [], [], [], [], [], [], []
+    get_k.wait()
+    raw_k = dot(x, wk_ref[...])
+    get_q.wait()
+    raw_q = dot(x, wq_ref[...])
+    ks, qs, betas, carries, wkks, mixes, pmats = [], [], [], [], [], [], []
     for i in heads:
-        head = step * GROUP + i
+        head = head0 + i
         rk = cut(raw_k, i)
         rq = cut(raw_q, i)
         inv_k = lax.rsqrt(jnp.sum(rk * rk, axis=1, keepdims=True) + 1e-06)
@@ -108,7 +117,6 @@
         qs.append(q)
         betas.append(beta)
         carries.append(carried)
-        weights.append(weight)
         wkks.append(wkk)
         mixes.append(wkk * beta)
         pmats.append(pmat)
@@ -118,15 +126,19 @@
         col_ref[i] = col
         k_ref[i] = k
         q_ref[i] = q
-        v_ref[i] = cut(raw_v, i)
-        do_ref[i] = cut(grad_o, i)
         p_ref[i] = pmat
         wkk_ref[i] = wkk
         w_ref[i] = weight
+    get_v.wait()
+    raw_v = dot(x, wv_ref[...])
+    get_o.wait()
+    grad_o = dot(go_ref[...], wo_ref[...], NT)
     solved = inverse_all(mixes)
     for i in heads:
         k, q, beta, carried = ks[i], qs[i], betas[i], carries[i]
         l_ref[i] = solved[i]
+        v_ref[i] = cut(raw_v, i)
+        do_ref[i] = cut(grad_o, i)
         right = jnp.concatenate([beta * cut(raw_v, i), (beta * carried) * k], axis=1)
         both = mm3(solved[i], right)
         uv = both[:, :W]
@@ -142,51 +154,88 @@
         send_ref[i, 2] = mm3(cut(grad_o, i), eff, TN)
 
 
-def row_kernel(r_ref, out_ref):
+def join_kernel(core_ref, own_ref, other_ref, out_ref):
+    second = core_ref[0] == 1
+    for i in range(GROUP):
+        ta = jnp.where(second, other_ref[i, 0], own_ref[i, 0])
+        tb = jnp.where(second, own_ref[i, 0], other_ref[i, 0])
+        oa = jnp.where(second, other_ref[i, 1], own_ref[i, 1])
+        ob = jnp.where(second, own_ref[i, 1], other_ref[i, 1])
+        ga = jnp.where(second, other_ref[i, 2], own_ref[i, 2])
+        gb = jnp.where(second, own_ref[i, 2], other_ref[i, 2])
+        front = mm3(jnp.concatenate([ta, oa], axis=0), tb)
+        out_ref[i, 0] = front[:W]
+        out_ref[i, 1] = front[W:] + ob
+        out_ref[i, 2] = mm3(gb, ta, NT) + ga
+
+
+def row_kernel(r_ref, state_ref, grad_ref):
+    size = r_ref.shape[0]
     state = r_ref[0, 1]
-    grad = r_ref[ROW - 1, 2]
-    for j in range(1, ROW):
+    grad = r_ref[size - 1, 2]
+    for j in range(1, size):
         state = mm3(state, r_ref[j, 0]) + r_ref[j, 1]
-        b = ROW - 1 - j
+        b = size - 1 - j
         grad = mm3(grad, r_ref[b, 0], NT) + r_ref[b, 2]
-    out_ref[0] = state
-    out_ref[1] = grad
+    state_ref[...] = state
+    grad_ref[...] = grad
 
 
 def spread_kernel(r_ref, s_ref, g_ref, out_ref):
+    size = r_ref.shape[0]
     state = s_ref[...]
     grad = g_ref[...]
     out_ref[0, 0] = state
-    out_ref[ROW - 1, 1] = grad
-    for j in range(1, ROW):
+    out_ref[size - 1, 1] = grad
+    for j in range(1, size):
         state = mm3(state, r_ref[j - 1, 0]) + r_ref[j - 1, 1]
         out_ref[j, 0] = state
-        b = ROW - j
+        b = size - j
         grad = mm3(grad, r_ref[b, 0], NT) + r_ref[b, 2]
         out_ref[b - 1, 1] = grad
 
 
-def second_kernel(
-    back_ref, k_ref, q_ref, v_ref, do_ref, p_ref, l_ref, wkk_ref, w_ref, uv_ref, kw_ref, col_ref,
-    wq_ref, wk_ref, wv_ref, wb_ref, total_ref, gd_ref, cterm_ref, fterm_ref, eterm_ref, db_ref,
-):
-    step = pl.program_id(0)
+def part_kernel(core_ref, own_ref, other_ref, chip_ref, mine_ref, give_ref):
+    second = core_ref[0] == 1
+    for i in range(GROUP):
+        ta = jnp.where(second, other_ref[i, 0], own_ref[i, 0])
+        tb = jnp.where(second, own_ref[i, 0], other_ref[i, 0])
+        oa = jnp.where(second, other_ref[i, 1], own_ref[i, 1])
+        gb = jnp.where(second, own_ref[i, 2], other_ref[i, 2])
+        s_in, g_end = chip_ref[i, 0], chip_ref[i, 1]
+        s_mid = mm3(s_in, ta) + oa
+        g_mid = mm3(g_end, tb, NT) + gb
+        mine_ref[i, 0] = jnp.where(second, s_mid, s_in)
+        mine_ref[i, 1] = jnp.where(second, g_end, g_mid)
+        give_ref[i, 0] = jnp.where(second, s_in, s_mid)
+        give_ref[i, 1] = jnp.where(second, g_mid, g_end)
+
+
+def second_kernel(chained, *refs):
+    (meta_ref, back_ref, k_ref, q_ref, v_ref, do_ref, p_ref, l_ref, wkk_ref, w_ref, uv_ref, kw_ref, col_ref,
+     wb_ref, wq_hbm, wk_hbm, wv_hbm) = refs[:17]
+    refs = refs[17:]
+    if chained:
+        before_ref, gd_before_ref = refs[:2]
+        refs = refs[2:]
+    total_ref, gd_ref, wq_ref, wk_ref, wv_ref, sems = refs
+    head0 = meta_ref[0]
+    at = pl.ds(pl.multiple_of(head0 * W, GROUP * W), GROUP * W)
+    gets = [
+        pltpu.make_async_copy(hbm.at[:, at], ref, sems.at[j])
+        for j, (hbm, ref) in enumerate(((wq_hbm, wq_ref), (wk_hbm, wk_ref), (wv_hbm, wv_ref)))
+    ]
+    for get in gets:
+        get.start()
     ti, si = iotas((W, W))
     strict = ti > si
     upper = jnp.where(si >= ti, 1.0, 0.0)
-    t8, h8 = iotas((W, ROW))
-
-    @pl.when(step == 0)
-    def _():
-        cterm_ref[...] = jnp.zeros((W, ROW), F32)
-        fterm_ref[...] = jnp.zeros((W, ROW), F32)
-        eterm_ref[...] = jnp.zeros((W, ROW), F32)
-        db_ref[...] = jnp.zeros((W, ROW), F32)
-
-    cterm, fterm, eterm, dball = cterm_ref[...], fterm_ref[...], eterm_ref[...], db_ref[...]
+    t8, h8 = iotas((W, 8))
+    none = jnp.zeros((W, 8), F32)
+    cterm, fterm, eterm, dball = none, none, none, none
     gqs, gks, gvs = [], [], []
     for i in range(GROUP):
-        head = step * GROUP + i
+        head = head0 + i
         s0, g1 = back_ref[i, 0], back_ref[i, 1]
         k, q, v, do = k_ref[i], q_ref[i], v_ref[i], do_ref[i]
         pmat, wkk, weight = p_ref[i], wkk_ref[i], w_ref[i]
@@ -230,77 +279,91 @@
         gqs.append(gq.astype(BF16))
         gks.append(gk.astype(BF16))
         gvs.append((beta * dr).astype(BF16))
-    cterm_ref[...], fterm_ref[...], eterm_ref[...], db_ref[...] = cterm, fterm, eterm, dball
+    for get in gets:
+        get.wait()
     part = dot(jnp.concatenate(gqs, axis=1), wq_ref[...], NT)
     part = part + dot(jnp.concatenate(gks, axis=1), wk_ref[...], NT)
     part = part + dot(jnp.concatenate(gvs, axis=1), wv_ref[...], NT)
-
+    part = part + dot(dball.astype(BF16), wb_ref[...])
     chunks, _, wide = total_ref.shape
-
-    @pl.when(step == 0)
-    def _():
-        for c in range(chunks):
-            total_ref[c] = part[:, c * wide:(c + 1) * wide]
-
-    @pl.when(step > 0)
-    def _():
-        full = part + dot(dball.astype(BF16), wb_ref[...])
-        for c in range(chunks):
-            total_ref[c] += full[:, c * wide:(c + 1) * wide]
-        lower = jnp.where(strict, 1.0, 0.0)
-        eye = jnp.where(ti == si, 1.0, 0.0)
-        turn = (((0,), (1,)), ((), ()))
-        gd_ref[...] = exact(cterm, upper, turn) + exact(fterm, lower, turn) + exact(eterm, eye, turn)
+    for c in range(chunks):
+        piece = part[:, c * wide:(c + 1) * wide]
+        total_ref[c] = before_ref[c] + piece if chained else piece
+    lower = jnp.where(strict, 1.0, 0.0)
+    eye = jnp.where(ti == si, 1.0, 0.0)
+    turn = (((0,), (1,)), ((), ()))
+    decays = exact(cterm, upper, turn) + exact(fterm, lower, turn) + exact(eterm, eye, turn)
+    gd_ref[...] = gd_before_ref[...] + decays if chained else decays
 
 
 def per_device(inputs, grad_out, w_query, w_key, w_value, w_beta, w_out, log_decay, lengths):
     rows, width = inputs.shape
     heads = w_beta.shape[1]
-    steps = heads // GROUP
     span = GROUP * W
-    base = (lax.axis_index("ctx") * rows).astype(jnp.int32).reshape(1)
+    size = lax.axis_size("ctx")
+    sides = lax.axis_size("head")
+    place = lax.axis_index("ctx").astype(jnp.int32)
+    core = (place & 1).reshape(1)
+    keep0 = core * GROUP
+    give0 = GROUP - keep0
+    base = (place * rows).reshape(1)
+    beta_t, decay_t = w_beta.T, log_decay.T
     smem = pl.BlockSpec(memory_space=pltpu.SMEM)
-    whole = lambda *shape: pl.BlockSpec(shape, lambda g: (0,) * len(shape))
-    mats = pl.BlockSpec((GROUP, W, W), lambda g: (g, 0, 0))
-    cols = pl.BlockSpec((width, span), lambda g: (0, g))
-    mat_shape = jax.ShapeDtypeStruct((heads, W, W), F32)
-    params = pltpu.CompilerParams(dimension_semantics=("arbitrary",), vmem_limit_bytes=56 << 20)
-    send, *kept = pl.pallas_call(
-        first_kernel,
-        grid=(steps,),
-        in_specs=[
-            smem, smem, whole(rows, width), whole(rows, width), cols, cols, cols, whole(heads, width),
-            pl.BlockSpec((span, width), lambda g: (g, 0)), whole(heads, rows),
-        ],
-        out_specs=[pl.BlockSpec((GROUP, 3, W, W), lambda g: (g, 0, 0, 0))] + [mats] * 11,
-        out_shape=[jax.ShapeDtypeStruct((heads, 3, W, W), F32)] + [mat_shape] * 11,
-        compiler_params=params,
-        name="block_forward",
-    )(lengths, base, inputs, grad_out, w_query, w_key, w_value, w_beta.T, w_out, log_decay.T)
-    size = lax.axis_size("ctx")
-    groups = [[z * ROW + j for j in range(ROW)] for z in range(size // ROW)]
-    mine = lax.all_to_all(send, "ctx", 0, 0, axis_index_groups=groups, tiled=True)
+    vmem = pl.BlockSpec(memory_space=pltpu.VMEM)
+    hbm = pl.BlockSpec(memory_space=pl.ANY)
+    shape = lambda *dims: jax.ShapeDtypeStruct(dims, F32)
+    params = pltpu.CompilerParams(vmem_limit_bytes=56 << 20)
     small = pltpu.CompilerParams(vmem_limit_bytes=32 << 20)
+    tall, flat = pltpu.VMEM((width, span), BF16), pltpu.VMEM((span, width), BF16)
+
+    def forward(head0):
+        send, *kept = pl.pallas_call(
+            first_kernel,
+            in_specs=[smem] + [vmem] * 4 + [hbm] * 4,
+            out_specs=[vmem] * 12,
+            out_shape=[shape(GROUP, 3, W, W)] + [shape(GROUP, W, W)] * 11,
+            scratch_shapes=[tall, tall, flat, tall, pltpu.SemaphoreType.DMA((4,))],
+            compiler_params=params,
+            name="block_forward",
+        )(jnp.concatenate([head0, base, lengths]), inputs, grad_out, beta_t, decay_t, w_key, w_query, w_out, w_value)
+        return send, kept
+
+    def backward(head0, back, kept, before):
+        return pl.pallas_call(
+            partial(second_kernel, bool(before)),
+            in_specs=[smem] + [vmem] * 13 + [hbm] * 3 + [vmem] * len(before),
+            out_specs=[vmem] * 2,
+            out_shape=[shape(sides, rows, width // sides), shape(heads, rows)],
+            scratch_shapes=[tall, tall, tall, pltpu.SemaphoreType.DMA((3,))],
+            compiler_params=params,
+            name="block_backward",
+        )(head0, back, *kept, beta_t, w_query, w_key, w_value, *before)
+
+    pair = [(j, j ^ 1) for j in range(size)]
+    groups = [[z + j * 2 + c for j in range(GROUP)] for z in range(0, size, 2 * GROUP) for c in range(2)]
+    give, give_kept = forward(give0)
+    other = lax.ppermute(give, "ctx", pair)
+    own, own_kept = forward(keep0)
+    whole = pl.pallas_call(
+        join_kernel, in_specs=[smem, vmem, vmem], out_shape=shape(GROUP, 3, W, W), compiler_params=small, name="chip_join"
+    )(core, own, other)
+    mine = lax.all_to_all(whole, "ctx", 0, 0, axis_index_groups=groups, tiled=True)
     ends = pl.pallas_call(
-        row_kernel, out_shape=jax.ShapeDtypeStruct((2, W, W), F32), compiler_params=small, name="row_ends"
+        row_kernel, out_shape=[shape(W, W)] * 2, compiler_params=small, name="row_ends"
     )(mine)
-    state = lax.ppermute(ends[0], "ctx", [(j, j + ROW) for j in range(size - ROW)])
-    grad = lax.ppermute(ends[1], "ctx", [(j + ROW, j) for j in range(size - ROW)])
+    step = 2 * GROUP
+    state = lax.ppermute(ends[0], "ctx", [(j, j + step) for j in range(size - step)])
+    grad = lax.ppermute(ends[1], "ctx", [(j + step, j) for j in range(size - step)])
     spread = pl.pallas_call(
-        spread_kernel, out_shape=jax.ShapeDtypeStruct((ROW, 2, W, W), F32), compiler_params=small, name="row_states"
+        spread_kernel, out_shape=shape(GROUP, 2, W, W), compiler_params=small, name="row_states"
     )(mine, state, grad)
-    back = lax.all_to_all(spread, "ctx", 0, 0, axis_index_groups=groups, tiled=True)
-    sides = lax.axis_size("head")
-    total, grad_d = pl.pallas_call(
-        second_kernel,
-        grid=(steps,),
-        in_specs=[pl.BlockSpec((GROUP, 2, W, W), lambda g: (g, 0, 0, 0))] + [mats] * 11 + [cols, cols, cols, whole(heads, width)],
-        out_specs=[whole(sides, rows, width // sides), whole(heads, rows)],
-        out_shape=[jax.ShapeDtypeStruct((sides, rows, width // sides), F32), jax.ShapeDtypeStruct((heads, rows), F32)],
-        scratch_shapes=[pltpu.VMEM((rows, heads), F32)] * 4,
-        compiler_params=params,
-        name="block_backward",
-    )(back, *kept, w_query, w_key, w_value, w_beta.T)
+    chips = lax.all_to_all(spread, "ctx", 0, 0, axis_index_groups=groups, tiled=True)
+    own_back, give_back = pl.pallas_call(
+        part_kernel, in_specs=[smem, vmem, vmem, vmem], out_shape=[shape(GROUP, 2, W, W)] * 2, compiler_params=small, name="chip_part"
+    )(core, own, other, chips)
+    other_back = lax.ppermute(give_back, "ctx", pair)
+    before = backward(keep0, own_back, own_kept, ())
+    total, grad_d = backward(give0, other_back, give_kept, before)
     grad_x = jnp.sum(lax.all_to_all(total, "head", 0, 0, tiled=True), axis=0).astype(BF16)
     return (grad_x, grad_d.T)
 

time: 113 us -> 110 us (0.973); the launches traced: 111 us -> 109 us
  blocking collectives: 64.5 us -> 44.4 us
  Pallas kernels: 38 us -> 45.4 us
  starting transfers between devices: 5.46 us -> 9.87 us
  local copies, waits for them, and re-layouts: 0.01 us -> 2.72 us
  waiting for transfers between devices: 1.3 us -> 3.89 us
  other arithmetic: 0.76 us -> 2.07 us
    all_to_all x1, blocking collectives: 20.2 us -> 9.35 us  [per_device(): lax.all_to_all(spread, 'ctx', 0, 0, axis_index_groups=groups, tiled=True)]
    all_to_all x1, blocking collectives: 26.6 us -> 16 us  [per_device(): lax.all_to_all(whole, 'ctx', 0, 0, axis_index_groups=groups, tiled=True)]
    pallas_call x4 -> x8, Pallas kernels: 38 us -> 45.4 us  [the longest x2 21.9 us: forward(): pl.pallas_call(first_kernel, in_specs=[smem] + [vmem] * 4 + [hbm] * 4, ou...]
    ppermute x2 -> x4, starting transfers between devices: 5.46 us -> 9.87 us  [the longest x1 3.57 us: per_device(): lax.ppermute(ends[0], 'ctx', [(j, j + step) for j in range(size - step)])]
    unnamed x0 -> x6, local copies, waits for them, and re-layouts: none -> 2.72 us
    ppermute x2 -> x4, waiting for transfers between devices: 1.3 us -> 3.89 us  [the longest x1 3.88 us: per_device(): lax.ppermute(ends[1], 'ctx', [(j + step, j) for j in range(size - step)])]
    all_to_all x1, blocking collectives: 17.7 us -> 19.1 us  [per_device(): lax.all_to_all(total, 'head', 0, 0, tiled=True)]
    concatenate x0 -> x1, other arithmetic: none -> 1.31 us  [forward(): jnp.concatenate([head0, base, lengths])]
  transfers between devices with their start and end apart: 2 -> 4, of which waited for: 1 -> 1; matrix products, arithmetic and copies ran while one was open for 0% -> 0% of each run, Pallas kernels for 0% -> 19%
where the time goes in v3:
time: 110 us; the launch traced here: 109 us
  Pallas kernels  45.4 us (41%)
  blocking collectives  44.4 us (40%)
  starting transfers between devices  9.87 us (9%)
  waiting for transfers between devices  3.89 us (4%)
  local copies, waits for them, and re-layouts  2.72 us (2%)
  other arithmetic  2.07 us (2%)
    pallas_call x2, Pallas kernels, forward(): pl.pallas_call(first_kernel, in_specs=[smem] + [vmem] * 4 + [hbm] * 4, ou...  21.9 us
    pallas_call x2, Pallas kernels, backward(): pl.pallas_call(partial(second_kernel, bool(before)), in_specs=[smem] + [v...  21.1 us
    all_to_all x1, blocking collectives, per_device(): lax.all_to_all(total, 'head', 0, 0, tiled=True)  19.1 us
    all_to_all x1, blocking collectives, per_device(): lax.all_to_all(whole, 'ctx', 0, 0, axis_index_groups=groups, tiled=True)  16 us
    all_to_all x1, blocking collectives, per_device(): lax.all_to_all(spread, 'ctx', 0, 0, axis_index_groups=groups, tiled=True)  9.35 us
    ppermute x1, waiting for transfers between devices, per_device(): lax.ppermute(ends[1], 'ctx', [(j + step, j) for j in range(size - step)])  3.88 us
    ppermute x1, starting transfers between devices, per_device(): lax.ppermute(ends[0], 'ctx', [(j, j + step) for j in range(size - step)])  3.57 us
    ppermute x1, starting transfers between devices, per_device(): other_back = lax.ppermute(give_back, 'ctx', pair)  3.55 us
  transfers between devices with their start and end apart: 4, of which 1 were waited for; matrix products, arithmetic and copies ran while one was open for 0% of the time, Pallas kernels for 19%

profile of v3, /device:TPU:1, one launch (start us, length us, event | category | flops | bytes accessed | tf_op | source)
XLA Modules:
  0.0 109.1 jit_solution(9698788861127754937)
XLA Ops:
  0.6 1.3 %add_add_fusion.1 = (s32[18]{0:T(128)}, s32[18]{0:T(128)}) fusion(s32[1]{0:T(128)S(6)} %sub.3.refs_0_, s32[16]{0:T(128)} %param.17, s32[1]{0:T(128)} %bitcast.1, s32[1]{0:T(128)S(6)} %mul.6.refs_0_), kind=kLoop, calls=%fused_computation.1 | loop fusion | flops 72 | bytes 220 | tf_op jit(solution)/shard_map/concatenate | solution.py:328
  1.9 10.9 %block_forward.3 = (f32[4,3,128,128]{3,2,1,0:T(8,128)}, f32[4,128,128]{2,1,0:T(8,128)}, f32[4,128,128]{2,1,0:T(8,128)}, f32[4,128,128]{2,1,0:T(8,128)}, f32[4,12...) custom-call(s32[18]{0:T(128)} %get-tuple-element.66.meta_ref, ...), custom_call_target="tpu_custom_call" | custom-call | tf_op jit(solution)/shard_map/block_forward/pallas_call | solution.py:320
  12.9 1.5 %collective-permute-start = (f32[4,3,128,128]{3,2,1,0:T(8,128)}, f32[4,3,128,128]{3,2,1,0:T(8,128)S(1)}, u32[]{:S(2)}, u32[]{:S(2)}) collective-permute-start(f32[4,3,128,128]{3,2,1,0:T(8,128)} %get-tuple-element.35), channel_id=1, source_target_pairs={{0,4},{4,0},{8,12},{12,8},{16,20},{20,16},{24,28},{28,24},{32,36},... | collective-permute-start | bytes 2359304 | tf_op jit(solution)/shard_map/ppermute | solution.py:345
  14.4 10.9 %block_forward.2 = (f32[4,3,128,128]{3,2,1,0:T(8,128)}, f32[4,128,128]{2,1,0:T(8,128)}, f32[4,128,128]{2,1,0:T(8,128)}, f32[4,128,128]{2,1,0:T(8,128)}, f32[4,12...) custom-call(s32[18]{0:T(128)} %get-tuple-element.67.meta_ref, ...), custom_call_target="tpu_custom_call" | custom-call | tf_op jit(solution)/shard_map/block_forward/pallas_call | solution.py:320
  25.3 0.0 collective-permute-done.other_ref
  25.3 1.1 %copy-done = f32[4,3,128,128]{3,2,1,0:T(8,128)S(1)} copy-done((f32[4,3,128,128]{3,2,1,0:T(8,128)S(1)}, f32[4,3,128,128]{3,2,1,0:T(8,128)}, u32[]{:S(2)}) %copy-start) | copy-done | bytes 786456
  26.5 0.6 chip_join.1
  27.1 16.0 %all_to_all.15.r_ref = f32[4,3,128,128]{3,2,1,0:T(8,128)S(1)} all-to-all(f32[4,3,128,128]{3,2,1,0:T(8,128)S(1)} %chip_join.1), channel_id=1, replica_groups={{0,8,16,24},{4,12,20,28},{32,40,48,56},{36,44,52,60},{64,72,80,88},{68,..., dimensions={0} | all-to-all | bytes 1572864 | tf_op jit(solution)/shard_map/all_to_all | solution.py:350
  43.0 0.6 row_ends.1
  43.7 3.6 %collective-permute-start.1 = (f32[128,128]{1,0:T(8,128)S(1)}, f32[128,128]{1,0:T(8,128)S(1)}, u32[]{:S(2)}, u32[]{:S(2)}) collective-permute-start(f32[128,128]{1,0:T(8,128)S(1)} %get-tuple-element.36), channel_id=1, source_target_pairs={{0,32},{4,36},{8,40},{12,44},{16,48},{20,52},{24,56},{28,60},{32,6... | collective-permute-start | bytes 196616 | tf_op jit(solution)/shard_map/ppermute | solution.py:355
  47.3 1.3 %collective-permute-start.2 = (f32[128,128]{1,0:T(8,128)S(1)}, f32[128,128]{1,0:T(8,128)S(1)}, u32[]{:S(2)}, u32[]{:S(2)}) collective-permute-start(f32[128,128]{1,0:T(8,128)S(1)} %get-tuple-element.37), channel_id=1, source_target_pairs={{32,0},{36,4},{40,8},{44,12},{48,16},{52,20},{56,24},{60,28},{64,3... | collective-permute-start | bytes 196616 | tf_op jit(solution)/shard_map/ppermute | solution.py:356
  48.6 0.0 collective-permute-done.1.s_ref
  48.6 3.9 %collective-permute-done.2.g_ref = f32[128,128]{1,0:T(8,128)S(1)} collective-permute-done((f32[128,128]{1,0:T(8,128)S(1)}, f32[128,128]{1,0:T(8,128)S(1)}, u32[]{:S(2)}, u32[]{:S(2)}) %collective-permute-start.2) | collective-permute-done | bytes 65568 | tf_op jit(solution)/shard_map/ppermute | solution.py:356
  52.4 0.6 row_states.1
  53.1 9.4 %all_to_all.16.chip_ref = f32[4,2,128,128]{3,2,1,0:T(8,128)S(1)} all-to-all(f32[4,2,128,128]{3,2,1,0:T(8,128)S(1)} %row_states.1), channel_id=1, replica_groups={{0,8,16,24},{4,12,20,28},{32,40,48,56},{36,44,52,60},{64,72,80,88},{68,..., dimensions={0} | all-to-all | bytes 1048576 | tf_op jit(solution)/shard_map/all_to_all | solution.py:360
  62.4 0.5 chip_part.1
  63.0 0.8 copy-done.1
  63.8 3.5 %collective-permute-start.3 = (f32[4,2,128,128]{3,2,1,0:T(8,128)S(1)}, f32[4,2,128,128]{3,2,1,0:T(8,128)S(1)}, u32[]{:S(2)}, u32[]{:S(2)}) collective-permute-start(f32[4,2,128,128]{3,2,1,0:T(8,128)S(1)} %get-tuple-element.38), channel_id=1, source_target_pairs={{0,4},{4,0},{8,12},{12,8},{16,20},{20,16},{24,28},{28,24},{32,36},... | collective-permute-start | bytes 1572872 | tf_op jit(solution)/shard_map/ppermute | solution.py:364
  67.4 9.9 %block_backward.2 = (f32[4,128,512]{2,1,0:T(8,128)}, f32[8,128]{1,0:T(8,128)}) custom-call(s32[1]{0:T(128)S(6)} %mul.6.refs_0_, f32[4,2,128,128]{3,2,1,0:T(8,128)} %copy-done.1, f32[4,128,128]{2,1,0:T(8,128)} %get-tuple-element.51.refs_2_, f32[4,128,128]{2,1,0:T(8,128)} %get-tuple-element.52.refs_3_, f32[4,128,128]{2,1,0:T(8,128)} %get-tuple-element.53.refs_4_, ...), custom_call_target="tpu_custom_call" | custom-call | tf_op jit(solution)/shard_map/block_backward/pallas_call | solution.py:332
  77.3 0.0 collective-permute-done.3.refs_1_
  77.3 0.8 copy-done.2
  78.1 11.2 %block_backward.3 = (f32[4,128,512]{2,1,0:T(8,128)}, f32[8,128]{1,0:T(8,128)}) custom-call(s32[1]{0:T(128)S(6)} %sub.3.refs_0_, f32[4,2,128,128]{3,2,1,0:T(8,128)} %copy-done.2, f32[4,128,128]{2,1,0:T(8,128)} %get-tuple-element.39.refs_2_, f32[4,128,128]{2,1,0:T(8,128)} %get-tuple-element.40.refs_3_, f32[4,128,128]{2,1,0:T(8,128)} %get-tuple-element.41.refs_4_, ...), custom_call_target="tpu_custom_call" | custom-call | tf_op jit(solution)/shard_map/block_backward/pallas_call | solution.py:332
  89.3 19.1 %all_to_all.17 = f32[4,128,512]{2,1,0:T(8,128)S(1)} all-to-all(f32[4,128,512]{2,1,0:T(8,128)} %get-tuple-element.64), channel_id=1, replica_groups=mesh['ctx'=32,'head'=4] {'head'}, dimensions={0} | all-to-all | bytes 2097152 | tf_op jit(solution)/shard_map/all_to_all | solution.py:367
  108.4 0.8 reduce_sum.9
  (3 shorter events, 0.0 us)
Async XLA Ops:
  12.9 12.4 %collective-permute-start = (f32[4,3,128,128]{3,2,1,0:T(8,128)}, f32[4,3,128,128]{3,2,1,0:T(8,128)S(1)}, u32[]{:S(2)}, u32[]{:S(2)}) collective-permute-start(f32[4,3,128,128]{3,2,1,0:T(8,128)} %get-tuple-element.35), channel_id=1, source_target_pairs={{0,4},{4,0},{8,12},{12,8},{16,20},{20,16},{24,28},{28,24},{32,36},... | collective-permute-start | bytes 2359304 | tf_op jit(solution)/shard_map/ppermute | solution.py:345
  25.3 1.1 %copy-start = (f32[4,3,128,128]{3,2,1,0:T(8,128)S(1)}, f32[4,3,128,128]{3,2,1,0:T(8,128)}, u32[]{:S(2)}) copy-start(f32[4,3,128,128]{3,2,1,0:T(8,128)} %get-tuple-element.34.own_ref) | copy-start | bytes 2359300
  43.7 4.9 %collective-permute-start.1 = (f32[128,128]{1,0:T(8,128)S(1)}, f32[128,128]{1,0:T(8,128)S(1)}, u32[]{:S(2)}, u32[]{:S(2)}) collective-permute-start(f32[128,128]{1,0:T(8,128)S(1)} %get-tuple-element.36), channel_id=1, source_target_pairs={{0,32},{4,36},{8,40},{12,44},{16,48},{20,52},{24,56},{28,60},{32,6... | collective-permute-start | bytes 196616 | tf_op jit(solution)/shard_map/ppermute | solution.py:355
  47.3 5.2 %collective-permute-start.2 = (f32[128,128]{1,0:T(8,128)S(1)}, f32[128,128]{1,0:T(8,128)S(1)}, u32[]{:S(2)}, u32[]{:S(2)}) collective-permute-start(f32[128,128]{1,0:T(8,128)S(1)} %get-tuple-element.37), channel_id=1, source_target_pairs={{32,0},{36,4},{40,8},{44,12},{48,16},{52,20},{56,24},{60,28},{64,3... | collective-permute-start | bytes 196616 | tf_op jit(solution)/shard_map/ppermute | solution.py:356
  63.0 0.8 copy-start.1
  63.8 13.5 %collective-permute-start.3 = (f32[4,2,128,128]{3,2,1,0:T(8,128)S(1)}, f32[4,2,128,128]{3,2,1,0:T(8,128)S(1)}, u32[]{:S(2)}, u32[]{:S(2)}) collective-permute-start(f32[4,2,128,128]{3,2,1,0:T(8,128)S(1)} %get-tuple-element.38), channel_id=1, source_target_pairs={{0,4},{4,0},{8,12},{12,8},{16,20},{20,16},{24,28},{28,24},{32,36},... | collective-permute-start | bytes 1572872 | tf_op jit(solution)/shard_map/ppermute | solution.py:364
  77.3 0.8 copy-start.2

commit v4 on v3

--- a/solution.py
+++ b/solution.py
@@ -32,7 +32,8 @@
 def mm3(a, b, dims=NN):
     ah, al = halves(a)
     bh, bl = halves(b)
-    return dot(ah, bh, dims) + (dot(ah, bl, dims) + dot(al, bh, dims))
+    (ca,), (cb,) = dims[0]
+    return dot(jnp.concatenate([ah, al], axis=ca), jnp.concatenate([bh, bh], axis=cb), dims) + dot(ah, bl, dims)
 
 
 def iotas(shape):
@@ -57,43 +58,94 @@
     return done
 
 
-def first_kernel(
-    meta_ref, x_ref, go_ref, wb_ref, dec_ref, wk_hbm, wq_hbm, wo_hbm, wv_hbm,
-    send_ref, k_ref, q_ref, v_ref, do_ref, p_ref, l_ref, wkk_ref, w_ref, uv_ref, kw_ref, col_ref,
-    wk_ref, wq_ref, wo_ref, wv_ref, sems,
+def head_columns(head0):
+    return pl.ds(pl.multiple_of(head0 * W, GROUP * W), GROUP * W)
+
+
+def give_kernel(
+    head_ref, keep_head_ref, base_ref, len_hbm, x_hbm, go_hbm, wb_hbm, dec_hbm, wk_hbm, wq_hbm, wo_hbm, wv_hbm, *refs
 ):
-    head0 = meta_ref[0]
-    base = meta_ref[1]
-    at = pl.ds(pl.multiple_of(head0 * W, GROUP * W), GROUP * W)
-    get_k = pltpu.make_async_copy(wk_hbm.at[:, at], wk_ref, sems.at[0])
-    get_q = pltpu.make_async_copy(wq_hbm.at[:, at], wq_ref, sems.at[1])
-    get_o = pltpu.make_async_copy(wo_hbm.at[at, :], wo_ref, sems.at[2])
-    get_v = pltpu.make_async_copy(wv_hbm.at[:, at], wv_ref, sems.at[3])
-    for get in (get_k, get_q, get_v, get_o):
+    outs, refs = refs[:12], refs[12:]
+    x_ref, go_ref, beta_ref, run_ref, rows_ref, keep_ref, first_ref, wk_ref, wq_ref, wv_ref, wk2_ref, wq2_ref = refs[:12]
+    len_ref, wb_ref, dec_ref, wo_ref, sems = refs[12:]
+    head0 = head_ref[0]
+    base = base_ref[0]
+    at = head_columns(head0)
+    at2 = head_columns(keep_head_ref[0])
+    pairs = (
+        (wk_hbm.at[:, at], wk_ref), (x_hbm, x_ref), (len_hbm, len_ref), (dec_hbm, dec_ref), (wb_hbm, wb_ref),
+        (wq_hbm.at[:, at], wq_ref), (wv_hbm.at[:, at], wv_ref), (go_hbm, go_ref), (wo_hbm.at[at, :], wo_ref),
+        (wk_hbm.at[:, at2], wk2_ref), (wq_hbm.at[:, at2], wq2_ref),
+    )
+    gets = [pltpu.make_async_copy(src, dst, sems.at[j]) for j, (src, dst) in enumerate(pairs)]
+    for get in gets:
         get.start()
+    gets[2].wait()
     ti, si = iotas((W, W))
     begin = jnp.int32(0)
-    seg_t = jnp.zeros((W, W), jnp.int32)
-    seg_s = jnp.zeros((W, W), jnp.int32)
+    seg_t = jnp.zeros((W, 1), jnp.int32)
+    seg_s = jnp.zeros((1, W), jnp.int32)
     seg_in = jnp.int32(0)
-    for j in range(2, meta_ref.shape[0]):
-        seg_t = seg_t + (ti + base >= begin).astype(jnp.int32)
-        seg_s = seg_s + (si + base >= begin).astype(jnp.int32)
+    for j in range(len_ref.shape[0]):
+        seg_t = seg_t + (ti[:, :1] + base >= begin).astype(jnp.int32)
+        seg_s = seg_s + (si[:1, :] + base >= begin).astype(jnp.int32)
         seg_in = seg_in + (base - 1 >= begin).astype(jnp.int32)
-        begin = begin + meta_ref[j]
-    keep = jnp.logical_and(seg_t == seg_s, ti >= si)
+        begin = begin + len_ref[j]
+    keep_ref[...] = jnp.where(jnp.logical_and(seg_t == seg_s, ti >= si), 1.0, 0.0)
+    first_ref[...] = jnp.broadcast_to(jnp.where(seg_t == seg_in, 1.0, 0.0), first_ref.shape)
+    gets[3].wait()
+    tril = jnp.where(ti >= si, 1.0, 0.0)
+    run_ref[...] = exact(tril, dec_ref[...], NT)
+    rows_ref[...] = exact(dec_ref[...], tril, NT)
+    gets[4].wait()
+    gets[1].wait()
+    beta_ref[...] = 1.0 / (1.0 + jnp.exp(-dot(x_ref[...], wb_ref[...], NT)))
+    block_body(
+        head0, x_ref, go_ref, beta_ref, run_ref, rows_ref, keep_ref, first_ref, wk_ref, wq_ref, wv_ref, wo_ref,
+        (gets[0], gets[5], gets[6], gets[7], gets[8]), outs,
+    )
+    gets[9].wait()
+    gets[10].wait()
+
+
+def keep_kernel(
+    head_ref, x_ref, go_ref, beta_ref, run_ref, rows_ref, keep_ref, first_ref, wk_ref, wq_ref, wo_hbm, wv_hbm, *refs
+):
+    outs = refs[:12]
+    wv_ref, wo_ref, sems = refs[12:]
+    head0 = head_ref[0]
+    at = head_columns(head0)
+    get_v = pltpu.make_async_copy(wv_hbm.at[:, at], wv_ref, sems.at[0])
+    get_o = pltpu.make_async_copy(wo_hbm.at[at, :], wo_ref, sems.at[1])
+    get_v.start()
+    get_o.start()
+    block_body(
+        head0, x_ref, go_ref, beta_ref, run_ref, rows_ref, keep_ref, first_ref, wk_ref, wq_ref, wv_ref, wo_ref,
+        (None, None, get_v, None, get_o), outs,
+    )
+
+
+def block_body(
+    head0, x_ref, go_ref, beta_ref, run_ref, rows_ref, keep_ref, first_ref, wk_ref, wq_ref, wv_ref, wo_ref, gets, outs
+):
+    send_ref, k_ref, q_ref, v_ref, do_ref, p_ref, l_ref, wkk_ref, w_ref, uv_ref, kw_ref, col_ref = outs
+
+    def ready(*which):
+        for j in which:
+            if gets[j] is not None:
+                gets[j].wait()
+
+    ti, si = iotas((W, W))
     strict = ti > si
-    first = (seg_t == seg_in)[:, :1]
-    x = x_ref[...]
-    beta_all = 1.0 / (1.0 + jnp.exp(-dot(x, wb_ref[...], NT)))
-    tril = jnp.where(ti >= si, 1.0, 0.0)
-    run_all = exact(tril, dec_ref[...], NT)
-    run_rows = exact(dec_ref[...], tril, NT)
+    keep = keep_ref[...] > 0.0
+    first = first_ref[...][:, :1] > 0.0
+    beta_all, run_all, run_rows = beta_ref[...], run_ref[...], rows_ref[...]
     heads = range(GROUP)
     cut = lambda a, i: a[:, i * W:(i + 1) * W]
-    get_k.wait()
+    ready(0)
+    x = x_ref[...]
     raw_k = dot(x, wk_ref[...])
-    get_q.wait()
+    ready(1)
     raw_q = dot(x, wq_ref[...])
     ks, qs, betas, carries, wkks, mixes, pmats = [], [], [], [], [], [], []
     for i in heads:
@@ -129,9 +181,9 @@
         p_ref[i] = pmat
         wkk_ref[i] = wkk
         w_ref[i] = weight
-    get_v.wait()
+    ready(2)
     raw_v = dot(x, wv_ref[...])
-    get_o.wait()
+    ready(3, 4)
     grad_o = dot(go_ref[...], wo_ref[...], NT)
     solved = inverse_all(mixes)
     for i in heads:
@@ -213,20 +265,13 @@
 
 def second_kernel(chained, *refs):
     (meta_ref, back_ref, k_ref, q_ref, v_ref, do_ref, p_ref, l_ref, wkk_ref, w_ref, uv_ref, kw_ref, col_ref,
-     wb_ref, wq_hbm, wk_hbm, wv_hbm) = refs[:17]
+     wb_ref, wq_ref, wk_ref, wv_ref) = refs[:17]
     refs = refs[17:]
     if chained:
         before_ref, gd_before_ref = refs[:2]
         refs = refs[2:]
-    total_ref, gd_ref, wq_ref, wk_ref, wv_ref, sems = refs
+    total_ref, gd_ref = refs
     head0 = meta_ref[0]
-    at = pl.ds(pl.multiple_of(head0 * W, GROUP * W), GROUP * W)
-    gets = [
-        pltpu.make_async_copy(hbm.at[:, at], ref, sems.at[j])
-        for j, (hbm, ref) in enumerate(((wq_hbm, wq_ref), (wk_hbm, wk_ref), (wv_hbm, wv_ref)))
-    ]
-    for get in gets:
-        get.start()
     ti, si = iotas((W, W))
     strict = ti > si
     upper = jnp.where(si >= ti, 1.0, 0.0)
@@ -279,8 +324,6 @@
         gqs.append(gq.astype(BF16))
         gks.append(gk.astype(BF16))
         gvs.append((beta * dr).astype(BF16))
-    for get in gets:
-        get.wait()
     part = dot(jnp.concatenate(gqs, axis=1), wq_ref[...], NT)
     part = part + dot(jnp.concatenate(gks, axis=1), wk_ref[...], NT)
     part = part + dot(jnp.concatenate(gvs, axis=1), wv_ref[...], NT)
@@ -296,10 +339,72 @@
     gd_ref[...] = gd_before_ref[...] + decays if chained else decays
 
 
+SMEM = pl.BlockSpec(memory_space=pltpu.SMEM)
+VMEM = pl.BlockSpec(memory_space=pltpu.VMEM)
+HBM = pl.BlockSpec(memory_space=pltpu.HBM)
+
+
+def shape(*dims):
+    return jax.ShapeDtypeStruct(dims, F32)
+
+
+def in_hbm(*arrays):
+    return [pltpu.with_memory_space_constraint(a, pltpu.HBM) for a in arrays]
+
+
+def block_shapes():
+    return [shape(GROUP, 3, W, W)] + [shape(GROUP, W, W)] * 11
+
+
+def run_give(give0, keep0, base, lengths, inputs, grad_out, beta_t, decay_t, w_key, w_query, w_out, w_value):
+    rows, width = inputs.shape
+    heads, span = beta_t.shape[0], GROUP * W
+    wide = jax.ShapeDtypeStruct((rows, width), BF16)
+    tall = jax.ShapeDtypeStruct((width, span), BF16)
+    out = pl.pallas_call(
+        give_kernel,
+        in_specs=[SMEM] * 3 + [HBM] * 9,
+        out_specs=[VMEM] * 24,
+        out_shape=block_shapes() + [wide, wide, shape(rows, heads), shape(rows, heads), shape(heads, rows), shape(W, W), shape(W, heads)] + [tall] * 5,
+        scratch_shapes=[
+            pltpu.SMEM(lengths.shape, jnp.int32), pltpu.VMEM(beta_t.shape, BF16), pltpu.VMEM(decay_t.shape, F32),
+            pltpu.VMEM((span, width), BF16), pltpu.SemaphoreType.DMA((11,)),
+        ],
+        compiler_params=pltpu.CompilerParams(vmem_limit_bytes=28 << 20),
+        name="block_forward_give",
+    )(give0, keep0, base, *in_hbm(lengths, inputs, grad_out, beta_t, decay_t, w_key, w_query, w_out, w_value))
+    return out[0], out[1:12], out[12:19], out[19:22], out[22:]
+
+
+def run_keep(keep0, shared, w_key2, w_query2, w_out, w_value):
+    width, span = w_key2.shape
+    out = pl.pallas_call(
+        keep_kernel,
+        in_specs=[SMEM] + [VMEM] * 9 + [HBM] * 2,
+        out_specs=[VMEM] * 13,
+        out_shape=block_shapes() + [jax.ShapeDtypeStruct((width, span), BF16)],
+        scratch_shapes=[pltpu.VMEM((span, width), BF16), pltpu.SemaphoreType.DMA((2,))],
+        compiler_params=pltpu.CompilerParams(vmem_limit_bytes=24 << 20),
+        name="block_forward_keep",
+    )(keep0, *shared, w_key2, w_query2, *in_hbm(w_out, w_value))
+    return out[0], out[1:12], out[12]
+
+
+def run_backward(sides, head0, back, kept, beta_t, w_key, w_query, w_value, before):
+    heads, width = beta_t.shape
+    return pl.pallas_call(
+        partial(second_kernel, bool(before)),
+        in_specs=[SMEM] + [VMEM] * 16 + [VMEM] * len(before),
+        out_specs=[VMEM] * 2,
+        out_shape=[shape(sides, W, width // sides), shape(heads, W)],
+        compiler_params=pltpu.CompilerParams(vmem_limit_bytes=24 << 20),
+        name="block_backward",
+    )(head0, back, *kept, beta_t, w_query, w_key, w_value, *before)
+
+
 def per_device(inputs, grad_out, w_query, w_key, w_value, w_beta, w_out, log_decay, lengths):
     rows, width = inputs.shape
     heads = w_beta.shape[1]
-    span = GROUP * W
     size = lax.axis_size("ctx")
     sides = lax.axis_size("head")
     place = lax.axis_index("ctx").astype(jnp.int32)
@@ -308,44 +413,17 @@
     give0 = GROUP - keep0
     base = (place * rows).reshape(1)
     beta_t, decay_t = w_beta.T, log_decay.T
-    smem = pl.BlockSpec(memory_space=pltpu.SMEM)
-    vmem = pl.BlockSpec(memory_space=pltpu.VMEM)
-    hbm = pl.BlockSpec(memory_space=pl.ANY)
-    shape = lambda *dims: jax.ShapeDtypeStruct(dims, F32)
-    params = pltpu.CompilerParams(vmem_limit_bytes=56 << 20)
-    small = pltpu.CompilerParams(vmem_limit_bytes=32 << 20)
-    tall, flat = pltpu.VMEM((width, span), BF16), pltpu.VMEM((span, width), BF16)
-
-    def forward(head0):
-        send, *kept = pl.pallas_call(
-            first_kernel,
-            in_specs=[smem] + [vmem] * 4 + [hbm] * 4,
-            out_specs=[vmem] * 12,
-            out_shape=[shape(GROUP, 3, W, W)] + [shape(GROUP, W, W)] * 11,
-            scratch_shapes=[tall, tall, flat, tall, pltpu.SemaphoreType.DMA((4,))],
-            compiler_params=params,
-            name="block_forward",
-        )(jnp.concatenate([head0, base, lengths]), inputs, grad_out, beta_t, decay_t, w_key, w_query, w_out, w_value)
-        return send, kept
-
-    def backward(head0, back, kept, before):
-        return pl.pallas_call(
-            partial(second_kernel, bool(before)),
-            in_specs=[smem] + [vmem] * 13 + [hbm] * 3 + [vmem] * len(before),
-            out_specs=[vmem] * 2,
-            out_shape=[shape(sides, rows, width // sides), shape(heads, rows)],
-            scratch_shapes=[tall, tall, tall, pltpu.SemaphoreType.DMA((3,))],
-            compiler_params=params,
-            name="block_backward",
-        )(head0, back, *kept, beta_t, w_query, w_key, w_value, *before)
+    small = pltpu.CompilerParams(vmem_limit_bytes=8 << 20)
 
     pair = [(j, j ^ 1) for j in range(size)]
     groups = [[z + j * 2 + c for j in range(GROUP)] for z in range(0, size, 2 * GROUP) for c in range(2)]
-    give, give_kept = forward(give0)
+    give, give_kept, shared, give_w, keep_w = run_give(
+        give0, keep0, base, lengths, inputs, grad_out, beta_t, decay_t, w_key, w_query, w_out, w_value
+    )
     other = lax.ppermute(give, "ctx", pair)
-    own, own_kept = forward(keep0)
+    own, own_kept, keep_v = run_keep(keep0, shared, *keep_w, w_out, w_value)
     whole = pl.pallas_call(
-        join_kernel, in_specs=[smem, vmem, vmem], out_shape=shape(GROUP, 3, W, W), compiler_params=small, name="chip_join"
+        join_kernel, in_specs=[SMEM] + [VMEM] * 2, out_shape=shape(GROUP, 3, W, W), compiler_params=small, name="chip_join"
     )(core, own, other)
     mine = lax.all_to_all(whole, "ctx", 0, 0, axis_index_groups=groups, tiled=True)
     ends = pl.pallas_call(
@@ -359,11 +437,11 @@
     )(mine, state, grad)
     chips = lax.all_to_all(spread, "ctx", 0, 0, axis_index_groups=groups, tiled=True)
     own_back, give_back = pl.pallas_call(
-        part_kernel, in_specs=[smem, vmem, vmem, vmem], out_shape=[shape(GROUP, 2, W, W)] * 2, compiler_params=small, name="chip_part"
+        part_kernel, in_specs=[SMEM] + [VMEM] * 3, out_shape=[shape(GROUP, 2, W, W)] * 2, compiler_params=small, name="chip_part"
     )(core, own, other, chips)
     other_back = lax.ppermute(give_back, "ctx", pair)
-    before = backward(keep0, own_back, own_kept, ())
-    total, grad_d = backward(give0, other_back, give_kept, before)
+    before = run_backward(sides, keep0, own_back, own_kept, beta_t, *keep_w, keep_v, ())
+    total, grad_d = run_backward(sides, give0, other_back, give_kept, beta_t, *give_w, before)
     grad_x = jnp.sum(lax.all_to_all(total, "head", 0, 0, tiled=True), axis=0).astype(BF16)
     return (grad_x, grad_d.T)
 

time: 110 us -> 90.9 us (0.83)
  Pallas kernels: 45.4 us -> 31 us
  local copies, waits for them, and re-layouts: 2.72 us -> 0.01 us
  other arithmetic: 2.07 us -> 0.76 us
    pallas_call x6, Pallas kernels: 44.1 us -> 30 us  [the longest x2 12.2 us: run_backward(): pl.pallas_call(partial(second_kernel, bool(before)), in_specs=[SMEM] + [V...]
    unnamed x6 -> x2, local copies, waits for them, and re-layouts: 2.72 us -> 0.01 us
    concatenate x1 -> x0, other arithmetic: 1.31 us -> none  [forward(): jnp.concatenate([head0, base, lengths])]
  transfers between devices with their start and end apart: 4 -> 4, of which waited for: 1 -> 1; matrix products, arithmetic and copies ran while one was open for 0% -> 0% of each run, Pallas kernels for 19% -> 15%
where the time goes in v4:
time: 90.9 us; the launch traced here: 90.6 us
  blocking collectives  44.2 us (49%)
  Pallas kernels  31 us (34%)
  starting transfers between devices  9.92 us (11%)
  waiting for transfers between devices  3.92 us (4%)
    all_to_all x1, blocking collectives, per_device(): lax.all_to_all(total, 'head', 0, 0, tiled=True)  18.9 us
    all_to_all x1, blocking collectives, per_device(): lax.all_to_all(whole, 'ctx', 0, 0, axis_index_groups=groups, tiled=True)  16 us
    pallas_call x2, Pallas kernels, run_backward(): pl.pallas_call(partial(second_kernel, bool(before)), in_specs=[SMEM] + [V...  12.2 us
    all_to_all x1, blocking collectives, per_device(): lax.all_to_all(spread, 'ctx', 0, 0, axis_index_groups=groups, tiled=True)  9.36 us
    pallas_call x1, Pallas kernels, run_give(): pl.pallas_call(give_kernel, in_specs=[SMEM] * 3 + [HBM] * 9, out_specs=[V...  8.92 us
    pallas_call x1, Pallas kernels, run_keep(): pl.pallas_call(keep_kernel, in_specs=[SMEM] + [VMEM] * 9 + [HBM] * 2, out...  7.88 us
    ppermute x1, waiting for transfers between devices, per_device(): lax.ppermute(ends[1], 'ctx', [(j + step, j) for j in range(size - step)])  3.92 us
    ppermute x1, starting transfers between devices, per_device(): other_back = lax.ppermute(give_back, 'ctx', pair)  3.55 us
  transfers between devices with their start and end apart: 4, of which 1 were waited for; matrix products, arithmetic and copies ran while one was open for 0% of the time, Pallas kernels for 15%

profile of v4, /device:TPU:1, one launch (start us, length us, event | category | flops | bytes accessed | tf_op | source)
XLA Modules:
  0.0 90.6 jit_solution(18128221560401647604)
XLA Ops:
  0.6 8.9 %block_forward_give.1 = (f32[4,3,128,128]{3,2,1,0:T(8,128)S(1)}, f32[4,128,128]{2,1,0:T(8,128)S(1)}, f32[4,128,128]{2,1,0:T(8,128)S(1)}, f32[4,128,128]{2,1,0:T(...) custom-call(s32[1]{0:T(128)S(6)} %sub.3.head_ref.refs_0_, ...), custom_call_target="tpu_custom_call" | custom-call | tf_op jit(solution)/shard_map/block_forward_give/pallas_call | solution.py:364
  9.6 1.5 %collective-permute-start = (f32[4,3,128,128]{3,2,1,0:T(8,128)S(1)}, f32[4,3,128,128]{3,2,1,0:T(8,128)S(1)}, u32[]{:S(2)}, u32[]{:S(2)}) collective-permute-start(f32[4,3,128,128]{3,2,1,0:T(8,128)S(1)} %get-tuple-element.57), channel_id=1, source_target_pairs={{0,4},{4,0},{8,12},{12,8},{16,20},{20,16},{24,28},{28,24},{32,36},... | collective-permute-start | bytes 2359304 | tf_op jit(solution)/shard_map/ppermute | solution.py:423
  11.1 7.9 %block_forward_keep.1 = (f32[4,3,128,128]{3,2,1,0:T(8,128)S(1)}, f32[4,128,128]{2,1,0:T(8,128)S(1)}, f32[4,128,128]{2,1,0:T(8,128)S(1)}, f32[4,128,128]{2,1,0:T(...) custom-call(s32[1]{0:T(128)S(6)} %mul.6.keep_head_ref.head_ref.refs_, ...), custom_call_target="tpu_custom_call" | custom-call | tf_op jit(solution)/shard_map/block_forward_keep/pallas_call | solution.py:381
  19.0 0.0 collective-permute-done.other_ref
  19.0 0.5 chip_join.1
  19.6 16.0 %all_to_all.15.r_ref = f32[4,3,128,128]{3,2,1,0:T(8,128)S(1)} all-to-all(f32[4,3,128,128]{3,2,1,0:T(8,128)S(1)} %chip_join.1), channel_id=1, replica_groups={{0,8,16,24},{4,12,20,28},{32,40,48,56},{36,44,52,60},{64,72,80,88},{68,..., dimensions={0} | all-to-all | bytes 1572864 | tf_op jit(solution)/shard_map/all_to_all | solution.py:428
  35.5 0.5 row_ends.1
  36.1 3.5 %collective-permute-start.1 = (f32[128,128]{1,0:T(8,128)S(1)}, f32[128,128]{1,0:T(8,128)S(1)}, u32[]{:S(2)}, u32[]{:S(2)}) collective-permute-start(f32[128,128]{1,0:T(8,128)S(1)} %get-tuple-element.58), channel_id=1, source_target_pairs={{0,32},{4,36},{8,40},{12,44},{16,48},{20,52},{24,56},{28,60},{32,6... | collective-permute-start | bytes 196616 | tf_op jit(solution)/shard_map/ppermute | solution.py:433
  39.6 0.0 copy-start
  39.6 1.3 %collective-permute-start.2 = (f32[128,128]{1,0:T(8,128)S(1)}, f32[128,128]{1,0:T(8,128)S(1)}, u32[]{:S(2)}, u32[]{:S(2)}) collective-permute-start(f32[128,128]{1,0:T(8,128)S(1)} %get-tuple-element.59), channel_id=1, source_target_pairs={{32,0},{36,4},{40,8},{44,12},{48,16},{52,20},{56,24},{60,28},{64,3... | collective-permute-start | bytes 196616 | tf_op jit(solution)/shard_map/ppermute | solution.py:434
  40.9 0.0 collective-permute-done.1.s_ref
  40.9 3.9 %collective-permute-done.2.g_ref = f32[128,128]{1,0:T(8,128)S(1)} collective-permute-done((f32[128,128]{1,0:T(8,128)S(1)}, f32[128,128]{1,0:T(8,128)S(1)}, u32[]{:S(2)}, u32[]{:S(2)}) %collective-permute-start.2) | collective-permute-done | bytes 65568 | tf_op jit(solution)/shard_map/ppermute | solution.py:434
  44.9 0.5 row_states.1
  45.4 9.4 %all_to_all.16.chip_ref = f32[4,2,128,128]{3,2,1,0:T(8,128)S(1)} all-to-all(f32[4,2,128,128]{3,2,1,0:T(8,128)S(1)} %row_states.1), channel_id=1, replica_groups={{0,8,16,24},{4,12,20,28},{32,40,48,56},{36,44,52,60},{64,72,80,88},{68,..., dimensions={0} | all-to-all | bytes 1048576 | tf_op jit(solution)/shard_map/all_to_all | solution.py:438
  54.8 0.4 chip_part.1
  55.2 3.5 %collective-permute-start.3 = (f32[4,2,128,128]{3,2,1,0:T(8,128)S(1)}, f32[4,2,128,128]{3,2,1,0:T(8,128)S(1)}, u32[]{:S(2)}, u32[]{:S(2)}) collective-permute-start(f32[4,2,128,128]{3,2,1,0:T(8,128)S(1)} %get-tuple-element.60), channel_id=1, source_target_pairs={{0,4},{4,0},{8,12},{12,8},{16,20},{20,16},{24,28},{28,24},{32,36},... | collective-permute-start | bytes 1572872 | tf_op jit(solution)/shard_map/ppermute | solution.py:442
  58.7 0.0 copy-done
  58.7 6.0 %block_backward.2 = (f32[4,128,512]{2,1,0:T(8,128)S(1)}, f32[8,128]{1,0:T(8,128)S(1)}) custom-call(s32[1]{0:T(128)S(6)} %mul.6.keep_head_ref.head_ref.refs_0_, f32[4,2,128,128]{3,2,1,0:T(8,128)S(1)} %get-tuple-element.75.refs_1_, f32[4,128,128]{2,1,0:T(8,128)S(1)} %get-tuple-element.76.refs_2_, f32[4,128,128]{2,1,0:T(8,128)S(1)} %get-tuple-element.77.refs_3_, ...), custom_call_target="tpu_custom_call" | custom-call | tf_op jit(solution)/shard_map/block_backward/pallas_call | solution.py:395
  64.7 0.0 collective-permute-done.3.refs_1_
  64.8 6.2 %block_backward.3 = (f32[4,128,512]{2,1,0:T(8,128)S(1)}, f32[8,128]{1,0:T(8,128)}) custom-call(s32[1]{0:T(128)S(6)} %sub.3.head_ref.refs_0_, f32[4,2,128,128]{3,2,1,0:T(8,128)S(1)} %collective-permute-done.3.refs_1_, f32[4,128,128]{2,1,0:T(8,128)S(1)} %get-tuple-element.61.refs_2_, f32[4,128,128]{2,1,0:T(8,128)S(1)} %get-tuple-element.62.refs_3_, ...), custom_call_target="tpu_custom_call" | custom-call | tf_op jit(solution)/shard_map/block_backward/pallas_call | solution.py:395
  70.9 18.9 %all_to_all.17 = f32[4,128,512]{2,1,0:T(8,128)S(1)} all-to-all(f32[4,128,512]{2,1,0:T(8,128)S(1)} %get-tuple-element.90), channel_id=1, replica_groups=mesh['ctx'=32,'head'=4] {'head'}, dimensions={0} | all-to-all | bytes 2097152 | tf_op jit(solution)/shard_map/all_to_all | solution.py:445
  89.8 0.8 reduce_sum.9
Async XLA Ops:
  9.6 9.4 %collective-permute-start = (f32[4,3,128,128]{3,2,1,0:T(8,128)S(1)}, f32[4,3,128,128]{3,2,1,0:T(8,128)S(1)}, u32[]{:S(2)}, u32[]{:S(2)}) collective-permute-start(f32[4,3,128,128]{3,2,1,0:T(8,128)S(1)} %get-tuple-element.57), channel_id=1, source_target_pairs={{0,4},{4,0},{8,12},{12,8},{16,20},{20,16},{24,28},{28,24},{32,36},... | collective-permute-start | bytes 2359304 | tf_op jit(solution)/shard_map/ppermute | solution.py:423
  36.1 4.9 %collective-permute-start.1 = (f32[128,128]{1,0:T(8,128)S(1)}, f32[128,128]{1,0:T(8,128)S(1)}, u32[]{:S(2)}, u32[]{:S(2)}) collective-permute-start(f32[128,128]{1,0:T(8,128)S(1)} %get-tuple-element.58), channel_id=1, source_target_pairs={{0,32},{4,36},{8,40},{12,44},{16,48},{20,52},{24,56},{28,60},{32,6... | collective-permute-start | bytes 196616 | tf_op jit(solution)/shard_map/ppermute | solution.py:433
  39.6 19.1 %copy-start = (bf16[2048,8]{0,1:T(8,128)(2,1)S(1)}, bf16[2048,8]{0,1:T(8,128)(2,1)}, u32[]{:S(2)}) copy-start(bf16[2048,8]{0,1:T(8,128)(2,1)} %param.14) | copy-start | bytes 98308
  39.6 5.2 %collective-permute-start.2 = (f32[128,128]{1,0:T(8,128)S(1)}, f32[128,128]{1,0:T(8,128)S(1)}, u32[]{:S(2)}, u32[]{:S(2)}) collective-permute-start(f32[128,128]{1,0:T(8,128)S(1)} %get-tuple-element.59), channel_id=1, source_target_pairs={{32,0},{36,4},{40,8},{44,12},{48,16},{52,20},{56,24},{60,28},{64,3... | collective-permute-start | bytes 196616 | tf_op jit(solution)/shard_map/ppermute | solution.py:434
  55.2 9.6 %collective-permute-start.3 = (f32[4,2,128,128]{3,2,1,0:T(8,128)S(1)}, f32[4,2,128,128]{3,2,1,0:T(8,128)S(1)}, u32[]{:S(2)}, u32[]{:S(2)}) collective-permute-start(f32[4,2,128,128]{3,2,1,0:T(8,128)S(1)} %get-tuple-element.60), channel_id=1, source_target_pairs={{0,4},{4,0},{8,12},{12,8},{16,20},{20,16},{24,28},{28,24},{32,36},... | collective-permute-start | bytes 1572872 | tf_op jit(solution)/shard_map/ppermute | solution.py:442

commit v5 on v4

v5 whole, which is shorter than its diff:
```python
from functools import partial

import jax
import jax.numpy as jnp
from jax import lax
from jax.experimental import pallas as pl
from jax.experimental.pallas import tpu as pltpu
from jax.sharding import PartitionSpec as P

F32 = jnp.float32
BF16 = jnp.bfloat16
W = 128
GROUP = 4
SIDES = 4
NN = (((1,), (0,)), ((), ()))
NT = (((1,), (1,)), ((), ()))
TN = (((0,), (0,)), ((), ()))


def dot(a, b, dims=NN):
    return lax.dot_general(a, b, dims, preferred_element_type=F32)


def exact(a, b, dims=NN):
    return lax.dot_general(a, b, dims, precision=lax.Precision.HIGHEST, preferred_element_type=F32)


def halves(a):
    high = a.astype(BF16)
    return high, (a - high.astype(F32)).astype(BF16)


def mm3(a, b, dims=NN):
    ah, al = halves(a)
    bh, bl = halves(b)
    (ca,), (cb,) = dims[0]
    return dot(jnp.concatenate([ah, al], axis=ca), jnp.concatenate([bh, bh], axis=cb), dims) + dot(ah, bl, dims)


def iotas(shape):
    return lax.broadcasted_iota(jnp.int32, shape, 0), lax.broadcasted_iota(jnp.int32, shape, 1)


def column(array, index):
    lanes = lax.broadcasted_iota(jnp.int32, array.shape, 1)
    return jnp.sum(jnp.where(lanes == index, array, 0.0), axis=1, keepdims=True)


def inverse_all(mixes):
    ti, si = iotas((W, W))
    eye = jnp.where(ti == si, 1.0, 0.0)
    below = jnp.logical_and((ti >> 1) == (si >> 1), ti > si)
    done = [eye - jnp.where(below, a, 0.0) for a in mixes]
    for shift in range(1, 7):
        below = jnp.logical_and((ti >> (shift + 1)) == (si >> (shift + 1)), (ti >> shift) > (si >> shift))
        parts = [jnp.where(below, a, 0.0) for a in mixes]
        inner = [mm3(p, d) for p, d in zip(parts, done)]
        done = [d - mm3(d, i) for d, i in zip(done, inner)]
    return done


def head_columns(head0):
    return pl.ds(pl.multiple_of(head0 * W, GROUP * W), GROUP * W)


def give_kernel(
    place_ref, side_ref, len_hbm, x_hbm, go_hbm, wb_hbm, dec_hbm, wk_hbm, wq_hbm, wo_hbm, wv_hbm, *refs
):
    ids_ref, outs, refs = refs[0], refs[1:3], refs[3:]
    x_ref, go_ref, beta_ref, run_ref, rows_ref, keep_ref, first_ref, wkq_ref, wv_ref, wkq2_ref = refs[:10]
    len_ref, wb_ref, dec_ref, wo_ref, sems = refs[10:]
    keep0 = (place_ref[0] & 1) * GROUP
    head0 = GROUP - keep0
    ids_ref[0] = place_ref[0]
    ids_ref[1] = side_ref[0]
    base = place_ref[0] * W
    at = head_columns(head0)
    at2 = head_columns(keep0)
    pairs = (
        (wk_hbm.at[:, at], wkq_ref.at[0]), (x_hbm, x_ref), (len_hbm, len_ref), (dec_hbm, dec_ref), (wb_hbm, wb_ref),
        (wq_hbm.at[:, at], wkq_ref.at[1]), (wv_hbm.at[:, at], wv_ref), (go_hbm, go_ref), (wo_hbm.at[at, :], wo_ref),
        (wk_hbm.at[:, at2], wkq2_ref.at[0]), (wq_hbm.at[:, at2], wkq2_ref.at[1]),
    )
    gets = [pltpu.make_async_copy(src, dst, sems.at[j]) for j, (src, dst) in enumerate(pairs)]
    for get in gets:
        get.start()
    gets[2].wait()
    ti, si = iotas((W, W))
    begin = jnp.int32(0)
    seg_t = jnp.zeros((W, 1), jnp.int32)
    seg_s = jnp.zeros((1, W), jnp.int32)
    seg_in = jnp.int32(0)
    for j in range(len_ref.shape[0]):
        seg_t = seg_t + (ti[:, :1] + base >= begin).astype(jnp.int32)
        seg_s = seg_s + (si[:1, :] + base >= begin).astype(jnp.int32)
        seg_in = seg_in + (base - 1 >= begin).astype(jnp.int32)
        begin = begin + len_ref[j]
    keep_ref[...] = jnp.where(jnp.logical_and(seg_t == seg_s, ti >= si), 1.0, 0.0)
    first_ref[...] = jnp.broadcast_to(jnp.where(seg_t == seg_in, 1.0, 0.0), first_ref.shape)
    gets[3].wait()
    tril = jnp.where(ti >= si, 1.0, 0.0)
    run_ref[...] = exact(tril, dec_ref[...], NT)
    rows_ref[...] = exact(dec_ref[...], tril, NT)
    gets[4].wait()
    gets[1].wait()
    beta_ref[...] = 1.0 / (1.0 + jnp.exp(-dot(x_ref[...], wb_ref[...], NT)))
    block_body(
        head0, x_ref, go_ref, beta_ref, run_ref, rows_ref, keep_ref, first_ref, wkq_ref, wv_ref, wo_ref,
        (gets[0], gets[5], gets[6], gets[7], gets[8]), outs,
    )
    gets[9].wait()
    gets[10].wait()


def keep_kernel(
    ids_ref, x_ref, go_ref, beta_ref, run_ref, rows_ref, keep_ref, first_ref, wkq_ref, wo_hbm, wv_hbm, *refs
):
    outs = refs[:2]
    wv_ref, wo_ref, sems = refs[2:]
    head0 = (ids_ref[0] & 1) * GROUP
    at = head_columns(head0)
    get_v = pltpu.make_async_copy(wv_hbm.at[:, at], wv_ref, sems.at[0])
    get_o = pltpu.make_async_copy(wo_hbm.at[at, :], wo_ref, sems.at[1])
    get_v.start()
    get_o.start()
    block_body(
        head0, x_ref, go_ref, beta_ref, run_ref, rows_ref, keep_ref, first_ref, wkq_ref, wv_ref, wo_ref,
        (None, None, get_v, None, get_o), outs,
    )


def block_body(
    head0, x_ref, go_ref, beta_ref, run_ref, rows_ref, keep_ref, first_ref, wkq_ref, wv_ref, wo_ref, gets, outs
):
    send_ref, kept_ref = outs

    def ready(*which):
        for j in which:
            if gets[j] is not None:
                gets[j].wait()

    ti, si = iotas((W, W))
    strict = ti > si
    keep = keep_ref[...] > 0.0
    first = first_ref[...][:, :1] > 0.0
    beta_all, run_all, run_rows = beta_ref[...], run_ref[...], rows_ref[...]
    heads = range(GROUP)
    cut = lambda a, i: a[:, i * W:(i + 1) * W]
    ready(0)
    x = x_ref[...]
    raw_k = dot(x, wkq_ref[0])
    ready(1)
    raw_q = dot(x, wkq_ref[1])
    ks, qs, betas, carries, wkks, mixes, pmats = [], [], [], [], [], [], []
    for i in heads:
        head = head0 + i
        rk = cut(raw_k, i)
        rq = cut(raw_q, i)
        inv_k = lax.rsqrt(jnp.sum(rk * rk, axis=1, keepdims=True) + 1e-06)
        inv_q = lax.rsqrt(jnp.sum(rq * rq, axis=1, keepdims=True) + 1e-06)
        k = rk * inv_k
        q = rq * inv_q * (W ** -0.5)
        beta = column(beta_all, head)
        run = column(run_all, head)
        heads_at = lax.broadcasted_iota(jnp.int32, run_rows.shape, 0)
        spread = run - jnp.sum(jnp.where(heads_at == head, run_rows, 0.0), axis=0, keepdims=True)
        weight = jnp.where(keep, jnp.exp(jnp.where(keep, spread, 0.0)), 0.0)
        carried = jnp.where(first, jnp.exp(run), 0.0)
        both = mm3(jnp.concatenate([k, q], axis=0), k, NT)
        wkk = jnp.where(strict, weight, 0.0) * both[:W]
        pmat = weight * both[W:]
        ks.append(k)
        qs.append(q)
        betas.append(beta)
        carries.append(carried)
        wkks.append(wkk)
        mixes.append(wkk * beta)
        pmats.append(pmat)
        lanes = si
        closing = jnp.sum(jnp.where(ti == si, jnp.broadcast_to(weight[W - 1:W, :], (W, W)), 0.0), axis=1, keepdims=True)
        col = jnp.where(lanes == 0, beta, jnp.where(lanes == 1, carried, jnp.where(lanes == 2, closing, jnp.where(lanes == 3, inv_k, inv_q))))
        kept_ref[i, 10] = col
        kept_ref[i, 0] = k
        kept_ref[i, 1] = q
        kept_ref[i, 4] = pmat
        kept_ref[i, 6] = wkk
        kept_ref[i, 7] = weight
    ready(2)
    raw_v = dot(x, wv_ref[...])
    ready(3, 4)
    grad_o = dot(go_ref[...], wo_ref[...], NT)
    solved = inverse_all(mixes)
    for i in heads:
        k, q, beta, carried = ks[i], qs[i], betas[i], carries[i]
        kept_ref[i, 5] = solved[i]
        kept_ref[i, 2] = cut(raw_v, i)
        kept_ref[i, 3] = cut(grad_o, i)
        right = jnp.concatenate([beta * cut(raw_v, i), (beta * carried) * k], axis=1)
        both = mm3(solved[i], right)
        uv = both[:, :W]
        kw = both[:, W:]
        kept_ref[i, 8] = uv
        kept_ref[i, 9] = kw
        eff = carried * q - mm3(pmats[i], kw)
        closing = kept_ref[i, 10][:, 2:3]
        ends = mm3(jnp.concatenate([kw, uv], axis=1), closing * k, TN)
        last = carried[W - 1:W, :]
        send_ref[i, 0] = jnp.where(ti == si, last, 0.0) - ends[:W]
        send_ref[i, 1] = ends[W:]
        send_ref[i, 2] = mm3(cut(grad_o, i), eff, TN)


def join_kernel(place_ref, own_ref, other_ref, *out_refs):
    second = (place_ref[0] & 1) == 1
    x = place_ref[0] >> 1
    for d in range(GROUP):
        i = (x + d) & (GROUP - 1)
        out_ref = out_refs[d]
        ta = jnp.where(second, other_ref[i, 0], own_ref[i, 0])
        tb = jnp.where(second, own_ref[i, 0], other_ref[i, 0])
        oa = jnp.where(second, other_ref[i, 1], own_ref[i, 1])
        ob = jnp.where(second, own_ref[i, 1], other_ref[i, 1])
        ga = jnp.where(second, other_ref[i, 2], own_ref[i, 2])
        gb = jnp.where(second, own_ref[i, 2], other_ref[i, 2])
        front = mm3(jnp.concatenate([ta, oa], axis=0), tb)
        out_ref[0] = front[:W]
        out_ref[1] = front[W:] + ob
        out_ref[2] = mm3(gb, ta, NT) + ga


def row_kernel(place_ref, *refs):
    x = place_ref[0] >> 1
    parts, (r_ref, state_ref, grad_ref) = refs[:GROUP], refs[GROUP:]
    for d, part in enumerate(parts):
        r_ref[(x - d) & (GROUP - 1)] = part[...]
    state = r_ref[0, 1]
    grad = r_ref[GROUP - 1, 2]
    for j in range(1, GROUP):
        state = mm3(state, r_ref[j, 0]) + r_ref[j, 1]
        b = GROUP - 1 - j
        grad = mm3(grad, r_ref[b, 0], NT) + r_ref[b, 2]
    state_ref[...] = state
    grad_ref[...] = grad


def spread_kernel(place_ref, r_ref, s_ref, g_ref, *refs):
    x = place_ref[0] >> 1
    outs, all_ref = refs[:GROUP], refs[GROUP]
    state = s_ref[...]
    grad = g_ref[...]
    all_ref[0, 0] = state
    all_ref[GROUP - 1, 1] = grad
    for j in range(1, GROUP):
        state = mm3(state, r_ref[j - 1, 0]) + r_ref[j - 1, 1]
        all_ref[j, 0] = state
        b = GROUP - j
        grad = mm3(grad, r_ref[b, 0], NT) + r_ref[b, 2]
        all_ref[b - 1, 1] = grad
    for d, out in enumerate(outs):
        out[...] = all_ref[(x + d) & (GROUP - 1)]


def part_kernel(place_ref, own_ref, other_ref, *refs):
    chips, (mine_ref, give_ref) = refs[:GROUP], refs[GROUP:]
    second = (place_ref[0] & 1) == 1
    x = place_ref[0] >> 1
    for d, chip_ref in enumerate(chips):
        i = (x - d) & (GROUP - 1)
        ta = jnp.where(second, other_ref[i, 0], own_ref[i, 0])
        tb = jnp.where(second, own_ref[i, 0], other_ref[i, 0])
        oa = jnp.where(second, other_ref[i, 1], own_ref[i, 1])
        gb = jnp.where(second, own_ref[i, 2], other_ref[i, 2])
        s_in, g_end = chip_ref[0], chip_ref[1]
        s_mid = mm3(s_in, ta) + oa
        g_mid = mm3(g_end, tb, NT) + gb
        mine_ref[i, 0] = jnp.where(second, s_mid, s_in)
        mine_ref[i, 1] = jnp.where(second, g_end, g_mid)
        give_ref[i, 0] = jnp.where(second, s_in, s_mid)
        give_ref[i, 1] = jnp.where(second, g_mid, g_end)


def back_project(side, grads, db, wkq_ref, wv_ref, wb_ref, wide):
    at = pl.ds(pl.multiple_of(side * wide, wide), wide)
    n = grads.shape[1] // 3
    piece = dot(grads[:, :n], wkq_ref[1, at, :], NT) + dot(grads[:, n:2 * n], wkq_ref[0, at, :], NT)
    return piece + dot(grads[:, 2 * n:], wv_ref[at, :], NT) + dot(db, wb_ref[:, at])


def chunk_kernel(distance, ids_ref, grads_ref, db_ref, before_ref, wb_ref, wkq_ref, wv_ref, out_ref):
    side = (ids_ref[1] + distance) & (SIDES - 1)
    piece = back_project(side, grads_ref[...], db_ref[...], wkq_ref, wv_ref, wb_ref, out_ref.shape[1])
    out_ref[...] = before_ref[distance] + piece


def second_kernel(chained, *refs):
    ids_ref, back_ref, kept_ref, wb_ref, wkq_ref, wv_ref = refs[:6]
    refs = refs[6:]
    if chained:
        before_ref, gd_before_ref, total_ref, gd_ref, grads_ref, db_ref = refs
    else:
        total_ref, gd_ref = refs
    keep0 = (ids_ref[0] & 1) * GROUP
    head0 = GROUP - keep0 if chained else keep0
    side = ids_ref[1]
    ti, si = iotas((W, W))
    strict = ti > si
    upper = jnp.where(si >= ti, 1.0, 0.0)
    t8, h8 = iotas((W, 8))
    none = jnp.zeros((W, 8), F32)
    cterm, fterm, eterm, dball = none, none, none, none
    gqs, gks, gvs = [], [], []
    for i in range(GROUP):
        head = head0 + i
        s0, g1 = back_ref[i, 0], back_ref[i, 1]
        k, q, v, do = kept_ref[i, 0], kept_ref[i, 1], kept_ref[i, 2], kept_ref[i, 3]
        pmat, wkk, weight = kept_ref[i, 4], kept_ref[i, 6], kept_ref[i, 7]
        col = kept_ref[i, 10]
        beta, carried, closing, inv_k, inv_q = (col[:, j:j + 1] for j in range(5))
        u = kept_ref[i, 8] - mm3(kept_ref[i, 9], s0, NT)
        du = mm3(pmat, do, TN) + mm3(closing * k, g1, NT)
        dr = mm3(kept_ref[i, 5], du, TN)
        dpa = mm3(jnp.concatenate([do, dr], axis=0), u, NT)
        dp = dpa[:W]
        da = -dpa[W:]
        ds = mm3(jnp.concatenate([carried * do, dr], axis=0), s0)
        dq_state = ds[:W]
        dr_s = carried * ds[W:]
        ug = closing * mm3(u, g1)
        dqk = weight * dp
        dkk = jnp.where(strict, weight, 0.0) * da * beta
        front = mm3(jnp.concatenate([dqk, dkk], axis=0), k)
        dq = front[:W] + dq_state
        dk = front[W:] + mm3(jnp.concatenate([dkk, dqk], axis=0), jnp.concatenate([k, q], axis=0), TN)
        dk = dk - beta * dr_s + ug
        known = jnp.sum(dr_s * k, axis=1, keepdims=True)
        dbeta = jnp.sum(dr * v, axis=1, keepdims=True) - known + jnp.sum(da * wkk, axis=1, keepdims=True)
        dlogit = dbeta * beta * (1.0 - beta)
        pairs = dp * pmat + da * wkk * beta
        ph, plow = halves(pairs)
        ub = upper.astype(BF16)
        across = dot(ub, ph) + dot(ub, plow)
        evec = jnp.sum(jnp.where(strict, across, 0.0), axis=1, keepdims=True)
        fvec = jnp.sum(ug * k, axis=1, keepdims=True)
        cvec = jnp.sum(dq_state * q, axis=1, keepdims=True) - beta * known
        ends = carried[W - 1:W, :] * jnp.sum(jnp.sum(g1 * s0, axis=1, keepdims=True), axis=0, keepdims=True)
        cvec = cvec + jnp.where(t8[:, :1] == W - 1, ends, 0.0)
        here = h8 == head
        cterm = jnp.where(here, cvec, cterm)
        fterm = jnp.where(here, fvec, fterm)
        eterm = jnp.where(here, evec, eterm)
        dball = jnp.where(here, dlogit, dball)
        gk = inv_k * (dk - k * jnp.sum(k * dk, axis=1, keepdims=True))
        gq = (inv_q * (W ** -0.5)) * (dq - (q * float(W)) * jnp.sum(q * dq, axis=1, keepdims=True))
        gqs.append(gq.astype(BF16))
        gks.append(gk.astype(BF16))
        gvs.append((beta * dr).astype(BF16))
    grads = jnp.concatenate(gqs + gks + gvs, axis=1)
    db = dball.astype(BF16)
    wide = total_ref.shape[-1]
    project = lambda d: back_project((side + d) & (SIDES - 1), grads, db, wkq_ref, wv_ref, wb_ref, wide)
    if chained:
        total_ref[...] = before_ref[2] + project(2)
        grads_ref[...] = grads
        db_ref[...] = db
    else:
        for d in range(SIDES):
            total_ref[d] = project(d)
    lower = jnp.where(strict, 1.0, 0.0)
    eye = jnp.where(ti == si, 1.0, 0.0)
    turn = (((0,), (1,)), ((), ()))
    decays = exact(cterm, upper, turn) + exact(fterm, lower, turn) + exact(eterm, eye, turn)
    gd_ref[...] = gd_before_ref[...] + decays if chained else decays


SMEM = pl.BlockSpec(memory_space=pltpu.SMEM)
VMEM = pl.BlockSpec(memory_space=pltpu.VMEM)
HBM = pl.BlockSpec(memory_space=pltpu.HBM)


def shape(*dims):
    return jax.ShapeDtypeStruct(dims, F32)


def in_hbm(*arrays):
    return [pltpu.with_memory_space_constraint(a, pltpu.HBM) for a in arrays]


def block_shapes():
    return [shape(GROUP, 3, W, W), shape(GROUP, 11, W, W)]


def run_give(place, side, lengths, inputs, grad_out, beta_t, decay_t, w_key, w_query, w_out, w_value):
    rows, width = inputs.shape
    heads, span = beta_t.shape[0], GROUP * W
    wide = jax.ShapeDtypeStruct((rows, width), BF16)
    tall = jax.ShapeDtypeStruct((width, span), BF16)
    two = jax.ShapeDtypeStruct((2, width, span), BF16)
    out = pl.pallas_call(
        give_kernel,
        in_specs=[SMEM] * 2 + [HBM] * 9,
        out_specs=[SMEM] + [VMEM] * 12,
        out_shape=[jax.ShapeDtypeStruct((2,), jnp.int32)] + block_shapes() + [wide, wide, shape(rows, heads), shape(rows, heads), shape(heads, rows), shape(W, W), shape(W, heads)] + [two, tall, two],
        scratch_shapes=[
            pltpu.SMEM(lengths.shape, jnp.int32), pltpu.VMEM(beta_t.shape, BF16), pltpu.VMEM(decay_t.shape, F32),
            pltpu.VMEM((span, width), BF16), pltpu.SemaphoreType.DMA((11,)),
        ],
        compiler_params=pltpu.CompilerParams(vmem_limit_bytes=28 << 20),
        name="block_forward_give",
    )(place, side, *in_hbm(lengths, inputs, grad_out, beta_t, decay_t, w_key, w_query, w_out, w_value))
    return out[0], out[1], out[2], out[3:10], out[10:12], out[12]


def run_keep(ids, shared, w_keep, w_out, w_value):
    _, width, span = w_keep.shape
    out = pl.pallas_call(
        keep_kernel,
        in_specs=[SMEM] + [VMEM] * 8 + [HBM] * 2,
        out_specs=[VMEM] * 3,
        out_shape=block_shapes() + [jax.ShapeDtypeStruct((width, span), BF16)],
        scratch_shapes=[pltpu.VMEM((span, width), BF16), pltpu.SemaphoreType.DMA((2,))],
        compiler_params=pltpu.CompilerParams(vmem_limit_bytes=24 << 20),
        name="block_forward_keep",
    )(ids, *shared, w_keep, *in_hbm(w_out, w_value))
    return out


def run_backward(ids, back, kept, beta_t, w_both, w_value, before):
    heads, width = beta_t.shape
    wide = width // SIDES
    if before:
        out_shape = [shape(W, wide), shape(heads, W), jax.ShapeDtypeStruct((W, 3 * GROUP * W), BF16), jax.ShapeDtypeStruct((W, heads), BF16)]
    else:
        out_shape = [shape(SIDES, W, wide), shape(heads, W)]
    return pl.pallas_call(
        partial(second_kernel, bool(before)),
        in_specs=[SMEM] + [VMEM] * 5 + [VMEM] * len(before),
        out_specs=[VMEM] * len(out_shape),
        out_shape=out_shape,
        compiler_params=pltpu.CompilerParams(vmem_limit_bytes=24 << 20),
        name="block_backward",
    )(ids, back, kept, beta_t, w_both, w_value, *before)


def run_chunk(distance, ids, grads, db, before, beta_t, w_both, w_value):
    return pl.pallas_call(
        partial(chunk_kernel, distance),
        in_specs=[SMEM] + [VMEM] * 6,
        out_specs=VMEM,
        out_shape=shape(*before.shape[1:]),
        compiler_params=pltpu.CompilerParams(vmem_limit_bytes=16 << 20),
        name="chunk",
    )(ids, grads, db, before, beta_t, w_both, w_value)


def per_device(inputs, grad_out, w_query, w_key, w_value, w_beta, w_out, log_decay, lengths):
    size = lax.axis_size("ctx")
    place = lax.axis_index("ctx").astype(jnp.int32).reshape(1)
    side = lax.axis_index("head").astype(jnp.int32).reshape(1)
    beta_t, decay_t = w_beta.T, log_decay.T
    small = pltpu.CompilerParams(vmem_limit_bytes=8 << 20)

    pair = [(j, j ^ 1) for j in range(size)]
    ids, give, give_kept, shared, give_w, keep_w = run_give(
        place, side, lengths, inputs, grad_out, beta_t, decay_t, w_key, w_query, w_out, w_value
    )
    other = lax.ppermute(give, "ctx", pair)
    own, own_kept, keep_v = run_keep(ids, shared, keep_w, w_out, w_value)
    row = 2 * GROUP

    def call(kernel, name, scalars, arrays, out_shape, scratch=()):
        return pl.pallas_call(
            kernel,
            in_specs=[SMEM] * len(scalars) + [VMEM] * len(arrays),
            out_specs=[VMEM] * len(out_shape),
            out_shape=out_shape,
            scratch_shapes=list(scratch),
            compiler_params=small,
            name=name,
        )(*scalars, *arrays)

    def along_x(parts):
        got = {0: parts[0]}
        for d in (2, 1, 3):
            moves = [(j, j - j % row + (j + 2 * d) % row) for j in range(size)]
            got[d] = lax.ppermute(parts[d], "ctx", moves)
        return [got[d] for d in range(GROUP)]

    whole = call(join_kernel, "chip_join", (ids,), (own, other), [shape(3, W, W)] * GROUP)
    mine, state, grad = call(
        row_kernel, "row_ends", (ids,), along_x(whole), [shape(GROUP, 3, W, W), shape(W, W), shape(W, W)]
    )
    state = lax.ppermute(state, "ctx", [(j, j + row) for j in range(size - row)])
    grad = lax.ppermute(grad, "ctx", [(j + row, j) for j in range(size - row)])
    spread = call(
        spread_kernel, "row_states", (ids,), (mine, state, grad), [shape(2, W, W)] * GROUP, [pltpu.VMEM((GROUP, 2, W, W), F32)]
    )
    own_back, give_back = call(
        part_kernel, "chip_part", (ids,), (own, other, *along_x(spread)), [shape(GROUP, 2, W, W)] * 2
    )
    other_back = lax.ppermute(give_back, "ctx", pair)
    before = run_backward(ids, own_back, own_kept, beta_t, keep_w, keep_v, ())
    far, grad_d, grads, db = run_backward(ids, other_back, give_kept, beta_t, *give_w, before)
    total = 0.0
    for d in (2, 1, 3, 0):
        chunk = far if d == 2 else run_chunk(d, ids, grads, db, before[0], beta_t, *give_w)
        if d:
            chunk = lax.ppermute(chunk, "head", [(j, (j + d) % SIDES) for j in range(SIDES)])
        total = total + chunk
    return (total.astype(BF16), grad_d.T)


def solution(mesh):
    placed = (
        P("ctx", None),
        P("ctx", None),
        P(None, "head"),
        P(None, "head"),
        P(None, "head"),
        P(None, "head"),
        P("head", None),
        P("ctx", "head"),
        P(),
    )
    return jax.shard_map(
        per_device,
        mesh=mesh,
        in_specs=placed,
        out_specs=(P("ctx", "head"), P("ctx", "head")),
        check_vma=False,
    )
```

time: 90.9 us -> 88.6 us (0.975)
  blocking collectives: 44.2 us -> 0 us
  waiting for transfers between devices: 3.92 us -> 26.1 us
  starting transfers between devices: 9.92 us -> 23.2 us
  Pallas kernels: 31 us -> 37.7 us
    all_to_all x3 -> x0, blocking collectives: 44.2 us -> none  [the longest x1 18.9 us: per_device(): lax.all_to_all(total, 'head', 0, 0, tiled=True)]
    ppermute x2 -> x11, waiting for transfers between devices: 3.92 us -> 26.1 us  [the longest x6 11.8 us: along_x(): got[d] = lax.ppermute(parts[d], 'ctx', moves)]
    ppermute x2 -> x11, starting transfers between devices: 4.83 us -> 18.6 us  [the longest x6 9.35 us: along_x(): got[d] = lax.ppermute(parts[d], 'ctx', moves)]
    pallas_call x6 -> x9, Pallas kernels: 18.8 us -> 25.8 us  [the longest x1 9.48 us: run_give(): pl.pallas_call(give_kernel, in_specs=[SMEM] * 2 + [HBM] * 9, out_specs=[S...]
  transfers between devices with their start and end apart: 4 -> 13, of which waited for: 1 -> 8; matrix products, arithmetic and copies ran while one was open for 0% -> 0% of each run, Pallas kernels for 15% -> 18%
where the time goes in v5:
time: 88.6 us; the launch traced here: 88.5 us
  Pallas kernels  37.7 us (43%)
  waiting for transfers between devices  26.1 us (29%)
  starting transfers between devices  23.2 us (26%)
    pallas_call x2, Pallas kernels, run_backward(): pl.pallas_call(partial(second_kernel, bool(before)), in_specs=[SMEM] + [V...  11.9 us
    ppermute x6, waiting for transfers between devices, along_x(): got[d] = lax.ppermute(parts[d], 'ctx', moves)  11.8 us
    ppermute x3, waiting for transfers between devices, per_device(): lax.ppermute(chunk, 'head', [(j, (j + d) % SIDES) for j in range(SIDES)])  10.4 us
    pallas_call x1, Pallas kernels, run_give(): pl.pallas_call(give_kernel, in_specs=[SMEM] * 2 + [HBM] * 9, out_specs=[S...  9.48 us
    ppermute x6, starting transfers between devices, along_x(): got[d] = lax.ppermute(parts[d], 'ctx', moves)  9.35 us
    pallas_call x1, Pallas kernels, run_keep(): pl.pallas_call(keep_kernel, in_specs=[SMEM] + [VMEM] * 8 + [HBM] * 2, out...  8.39 us
    ppermute x3, starting transfers between devices, per_device(): lax.ppermute(chunk, 'head', [(j, (j + d) % SIDES) for j in range(SIDES)])  4.46 us
    pallas_call x4, Pallas kernels, call(): pl.pallas_call(kernel, in_specs=[SMEM] * len(scalars) + [VMEM] * len(arra...  4.28 us
  transfers between devices with their start and end apart: 13, of which 8 were waited for; matrix products, arithmetic and copies ran while one was open for 0% of the time, Pallas kernels for 18%

profile of v5, /device:TPU:1, one launch (start us, length us, event | category | flops | bytes accessed | tf_op | source)
XLA Modules:
  0.0 88.5 jit_solution(16572778912657882675)
XLA Ops:
  0.6 9.5 %block_forward_give.1 = (s32[2]{0:T(128)S(1)}, f32[4,3,128,128]{3,2,1,0:T(8,128)S(1)}, f32[4,11,128,128]{3,2,1,0:T(8,128)S(1)}, bf16[128,2048]{1,0:T(8,128)(2,1)...) custom-call(s32[1]{0:T(128)} %bitcast.place_ref, ...), custom_call_target="tpu_custom_call" | custom-call | tf_op jit(solution)/shard_map/block_forward_give/pallas_call | solution.py:398
  10.1 1.5 %collective-permute-start = (f32[4,3,128,128]{3,2,1,0:T(8,128)S(1)}, f32[4,3,128,128]{3,2,1,0:T(8,128)S(1)}, u32[]{:S(2)}, u32[]{:S(2)}) collective-permute-start(f32[4,3,128,128]{3,2,1,0:T(8,128)S(1)} %get-tuple-element.47), channel_id=1, source_target_pairs={{0,4},{4,0},{8,12},{12,8},{16,20},{20,16},{24,28},{28,24},{32,36},... | collective-permute-start | bytes 2359304 | tf_op jit(solution)/shard_map/ppermute | solution.py:466
  11.7 8.4 %block_forward_keep.1 = (f32[4,3,128,128]{3,2,1,0:T(8,128)S(1)}, f32[4,11,128,128]{3,2,1,0:T(8,128)S(1)}, bf16[2048,512]{1,0:T(8,128)(2,1)S(1)}) custom-call(s32[2]{0:T(128)S(1)} %get-tuple-element.37.ids_ref.place_ref.refs_0_, bf16[128,2048]{1,0:T(8,128)(2,1)S(1)} %get-tuple-element.38.x_ref, bf16[128,2048]{1,0:T(8,128)(2,1)S(1)} %get-tuple-element.39.go_ref, ...), custom_call_target="tpu_custom_call" | custom-call | tf_op jit(solution)/shard_map/block_forward_keep/pallas_call | solution.py:415
  21.2 1.5 %collective-permute-start.1 = (f32[3,128,128]{2,1,0:T(8,128)S(1)}, f32[3,128,128]{2,1,0:T(8,128)S(1)}, u32[]{:S(2)}, u32[]{:S(2)}) collective-permute-start(f32[3,128,128]{2,1,0:T(8,128)S(1)} %get-tuple-element.49), channel_id=1, source_target_pairs={{0,8},{4,12},{8,16},{12,20},{16,24},{20,28},{24,0},{28,4},{32,40},... | collective-permute-start | bytes 589832 | tf_op jit(solution)/shard_map/ppermute | solution.py:485
  22.7 2.5 %collective-permute-start.2 = (f32[3,128,128]{2,1,0:T(8,128)S(1)}, f32[3,128,128]{2,1,0:T(8,128)S(1)}, u32[]{:S(2)}, u32[]{:S(2)}) collective-permute-start(f32[3,128,128]{2,1,0:T(8,128)S(1)} %get-tuple-element.50), channel_id=1, source_target_pairs={{0,16},{4,20},{8,24},{12,28},{16,0},{20,4},{24,8},{28,12},{32,48},... | collective-permute-start | bytes 589832 | tf_op jit(solution)/shard_map/ppermute | solution.py:485
  25.2 1.2 %collective-permute-start.3 = (f32[3,128,128]{2,1,0:T(8,128)S(1)}, f32[3,128,128]{2,1,0:T(8,128)S(1)}, u32[]{:S(2)}, u32[]{:S(2)}) collective-permute-start(f32[3,128,128]{2,1,0:T(8,128)S(1)} %get-tuple-element.51), channel_id=1, source_target_pairs={{0,24},{4,28},{8,0},{12,4},{16,8},{20,12},{24,16},{28,20},{32,56},... | collective-permute-start | bytes 589832 | tf_op jit(solution)/shard_map/ppermute | solution.py:485
  26.3 2.8 %collective-permute-done.1.refs_1_ = f32[3,128,128]{2,1,0:T(8,128)S(1)} collective-permute-done((f32[3,128,128]{2,1,0:T(8,128)S(1)}, f32[3,128,128]{2,1,0:T(8,128)S(1)}, u32[]{:S(2)}, u32[]{:S(2)}) %collective-permute-start.1) | collective-permute-done | bytes 196640 | tf_op jit(solution)/shard_map/ppermute | solution.py:485
  29.1 5.3 %collective-permute-done.2.refs_2_ = f32[3,128,128]{2,1,0:T(8,128)S(1)} collective-permute-done((f32[3,128,128]{2,1,0:T(8,128)S(1)}, f32[3,128,128]{2,1,0:T(8,128)S(1)}, u32[]{:S(2)}, u32[]{:S(2)}) %collective-permute-start.2) | collective-permute-done | bytes 196640 | tf_op jit(solution)/shard_map/ppermute | solution.py:485
  35.5 3.5 %collective-permute-start.4 = (f32[128,128]{1,0:T(8,128)S(1)}, f32[128,128]{1,0:T(8,128)S(1)}, u32[]{:S(2)}, u32[]{:S(2)}) collective-permute-start(f32[128,128]{1,0:T(8,128)S(1)} %get-tuple-element.53), channel_id=1, source_target_pairs={{0,32},{4,36},{8,40},{12,44},{16,48},{20,52},{24,56},{28,60},{32,6... | collective-permute-start | bytes 196616 | tf_op jit(solution)/shard_map/ppermute | solution.py:492
  39.1 1.3 %collective-permute-start.5 = (f32[128,128]{1,0:T(8,128)S(1)}, f32[128,128]{1,0:T(8,128)S(1)}, u32[]{:S(2)}, u32[]{:S(2)}) collective-permute-start(f32[128,128]{1,0:T(8,128)S(1)} %get-tuple-element.54), channel_id=1, source_target_pairs={{32,0},{36,4},{40,8},{44,12},{48,16},{52,20},{56,24},{60,28},{64,3... | collective-permute-start | bytes 196616 | tf_op jit(solution)/shard_map/ppermute | solution.py:493
  40.4 3.9 %collective-permute-done.5.g_ref = f32[128,128]{1,0:T(8,128)S(1)} collective-permute-done((f32[128,128]{1,0:T(8,128)S(1)}, f32[128,128]{1,0:T(8,128)S(1)}, u32[]{:S(2)}, u32[]{:S(2)}) %collective-permute-start.5) | collective-permute-done | bytes 65568 | tf_op jit(solution)/shard_map/ppermute | solution.py:493
  46.2 2.8 %collective-permute-start.7 = (f32[2,128,128]{2,1,0:T(8,128)S(1)}, f32[2,128,128]{2,1,0:T(8,128)S(1)}, u32[]{:S(2)}, u32[]{:S(2)}) collective-permute-start(f32[2,128,128]{2,1,0:T(8,128)S(1)} %get-tuple-element.57), channel_id=1, source_target_pairs={{0,16},{4,20},{8,24},{12,28},{16,0},{20,4},{24,8},{28,12},{32,48},... | collective-permute-start | bytes 393224 | tf_op jit(solution)/shard_map/ppermute | solution.py:485
  50.5 2.7 %collective-permute-done.7.refs_2_ = f32[2,128,128]{2,1,0:T(8,128)S(1)} collective-permute-done((f32[2,128,128]{2,1,0:T(8,128)S(1)}, f32[2,128,128]{2,1,0:T(8,128)S(1)}, u32[]{:S(2)}, u32[]{:S(2)}) %collective-permute-start.7) | collective-permute-done | bytes 131104 | tf_op jit(solution)/shard_map/ppermute | solution.py:485
  54.3 3.0 %collective-permute-start.9 = (f32[4,2,128,128]{3,2,1,0:T(8,128)S(1)}, f32[4,2,128,128]{3,2,1,0:T(8,128)S(1)}, u32[]{:S(2)}, u32[]{:S(2)}) collective-permute-start(f32[4,2,128,128]{3,2,1,0:T(8,128)S(1)} %get-tuple-element.59), channel_id=1, source_target_pairs={{0,4},{4,0},{8,12},{12,8},{16,20},{20,16},{24,28},{28,24},{32,36},... | collective-permute-start | bytes 1572872 | tf_op jit(solution)/shard_map/ppermute | solution.py:500
  57.3 6.6 %block_backward.2 = (f32[4,128,512]{2,1,0:T(8,128)S(1)}, f32[8,128]{1,0:T(8,128)S(1)}) custom-call(s32[2]{0:T(128)S(1)} %get-tuple-element.37.ids_ref.place_ref.refs_0_, f32[4,2,128,128]{3,2,1,0:T(8,128)S(1)} %get-tuple-element.63.refs_1_, f32[4,11,128,128]{3,2,1,0:T(8,128)S(1)} %get-tuple-element.64.refs_2_, bf16[8,2048]{1,0:T(8,128)(2,1)S(1)} %bitcast.6, ...), custom_call_target="tpu_custom_call" | custom-call | tf_op jit(solution)/shard_map/block_backward/pallas_call | solution.py:434
  63.9 5.3 %block_backward.3 = (f32[128,512]{1,0:T(8,128)S(1)}, f32[8,128]{1,0:T(8,128)}, bf16[128,1536]{1,0:T(8,128)(2,1)S(1)}, bf16[128,8]{1,0:T(8,128)(2,1)S(1)}) custom-call(s32[2]{0:T(128)S(1)} %get-tuple-element.37.ids_ref.place_ref.refs_0_, f32[4,2,128,128]{3,2,1,0:T(8,128)S(1)} %collective-permute-done.9.refs_1_, ...), custom_call_target="tpu_custom_call" | custom-call | tf_op jit(solution)/shard_map/block_backward/pallas_call | solution.py:434
  69.2 1.2 %chunk.4 = f32[128,512]{1,0:T(8,128)S(1)} custom-call(s32[2]{0:T(128)S(1)} %get-tuple-element.37.ids_ref.place_ref.refs_0_, bf16[128,1536]{1,0:T(8,128)(2,1)S(1)} %get-tuple-element.69.grads_ref, bf16[128,8]{1,0:T(8,128)(2,1)S(1)} %get-tuple-element.70.db_ref, f32[4,128,512]{2,1,0:T(8,128)S(1)} %get-tuple-element.66.refs_6_.before_ref, ...), custom_call_target="tpu_custom_call" | custom-call | tf_op jit(solution)/shard_map/chunk/pallas_call | solution.py:445
  70.4 1.2 %chunk.3 = f32[128,512]{1,0:T(8,128)S(1)} custom-call(s32[2]{0:T(128)S(1)} %get-tuple-element.37.ids_ref.place_ref.refs_0_, bf16[128,1536]{1,0:T(8,128)(2,1)S(1)} %get-tuple-element.69.grads_ref, bf16[128,8]{1,0:T(8,128)(2,1)S(1)} %get-tuple-element.70.db_ref, f32[4,128,512]{2,1,0:T(8,128)S(1)} %get-tuple-element.66.refs_6_.before_ref, ...), custom_call_target="tpu_custom_call" | custom-call | tf_op jit(solution)/shard_map/chunk/pallas_call | solution.py:445
  71.7 1.4 %collective-permute-start.11 = (f32[128,512]{1,0:T(8,128)S(1)}, f32[128,512]{1,0:T(8,128)S(1)}, u32[]{:S(2)}, u32[]{:S(2)}) collective-permute-start(f32[128,512]{1,0:T(8,128)S(1)} %chunk.3), channel_id=1, source_target_pairs={{0,1},{1,2},{2,3},{3,0},{4,5},{5,6},{6,7},{7,4},{8,9},{9,10},{10,1... | collective-permute-start | bytes 786440 | tf_op jit(solution)/shard_map/ppermute | solution.py:507
  73.0 1.5 %collective-permute-start.12 = (f32[128,512]{1,0:T(8,128)S(1)}, f32[128,512]{1,0:T(8,128)S(1)}, u32[]{:S(2)}, u32[]{:S(2)}) collective-permute-start(f32[128,512]{1,0:T(8,128)S(1)} %chunk.4), channel_id=1, source_target_pairs={{0,3},{1,0},{2,1},{3,2},{4,7},{5,4},{6,5},{7,6},{8,11},{9,8},{10,9... | collective-permute-start | bytes 786440 | tf_op jit(solution)/shard_map/ppermute | solution.py:507
  74.6 1.6 %collective-permute-start.10 = (f32[128,512]{1,0:T(8,128)S(1)}, f32[128,512]{1,0:T(8,128)S(1)}, u32[]{:S(2)}, u32[]{:S(2)}) collective-permute-start(f32[128,512]{1,0:T(8,128)S(1)} %get-tuple-element.68), channel_id=1, source_target_pairs={{0,2},{1,3},{2,0},{3,1},{4,6},{5,7},{6,4},{7,5},{8,10},{9,11},{10,... | collective-permute-start | bytes 786440 | tf_op jit(solution)/shard_map/ppermute | solution.py:507
  76.1 1.2 %chunk.5 = f32[128,512]{1,0:T(8,128)S(1)} custom-call(s32[2]{0:T(128)S(1)} %get-tuple-element.37.ids_ref.place_ref.refs_0_, bf16[128,1536]{1,0:T(8,128)(2,1)S(1)} %get-tuple-element.69.grads_ref, bf16[128,8]{1,0:T(8,128)(2,1)S(1)} %get-tuple-element.70.db_ref, f32[4,128,512]{2,1,0:T(8,128)S(1)} %get-tuple-element.66.refs_6_.before_ref, ...), custom_call_target="tpu_custom_call" | custom-call | tf_op jit(solution)/shard_map/chunk/pallas_call | solution.py:445
  77.4 3.7 %collective-permute-done.11 = f32[128,512]{1,0:T(8,128)S(1)} collective-permute-done((f32[128,512]{1,0:T(8,128)S(1)}, f32[128,512]{1,0:T(8,128)S(1)}, u32[]{:S(2)}, u32[]{:S(2)}) %collective-permute-start.11) | collective-permute-done | bytes 262176 | tf_op jit(solution)/shard_map/ppermute | solution.py:507
  81.0 6.7 %collective-permute-done.10 = f32[128,512]{1,0:T(8,128)S(1)} collective-permute-done((f32[128,512]{1,0:T(8,128)S(1)}, f32[128,512]{1,0:T(8,128)S(1)}, u32[]{:S(2)}, u32[]{:S(2)}) %collective-permute-start.10) | collective-permute-done | bytes 262176 | tf_op jit(solution)/shard_map/ppermute | solution.py:507
  (16 shorter events, 7.4 us)
Async XLA Ops:
  10.1 9.9 %collective-permute-start = (f32[4,3,128,128]{3,2,1,0:T(8,128)S(1)}, f32[4,3,128,128]{3,2,1,0:T(8,128)S(1)}, u32[]{:S(2)}, u32[]{:S(2)}) collective-permute-start(f32[4,3,128,128]{3,2,1,0:T(8,128)S(1)} %get-tuple-element.47), channel_id=1, source_target_pairs={{0,4},{4,0},{8,12},{12,8},{16,20},{20,16},{24,28},{28,24},{32,36},... | collective-permute-start | bytes 2359304 | tf_op jit(solution)/shard_map/ppermute | solution.py:466
  20.0 37.3 %copy-start = (bf16[2048,8]{0,1:T(8,128)(2,1)S(1)}, bf16[2048,8]{0,1:T(8,128)(2,1)}, u32[]{:S(2)}) copy-start(bf16[2048,8]{0,1:T(8,128)(2,1)} %param.14) | copy-start | bytes 98308
  21.2 8.0 %collective-permute-start.1 = (f32[3,128,128]{2,1,0:T(8,128)S(1)}, f32[3,128,128]{2,1,0:T(8,128)S(1)}, u32[]{:S(2)}, u32[]{:S(2)}) collective-permute-start(f32[3,128,128]{2,1,0:T(8,128)S(1)} %get-tuple-element.49), channel_id=1, source_target_pairs={{0,8},{4,12},{8,16},{12,20},{16,24},{20,28},{24,0},{28,4},{32,40},... | collective-permute-start | bytes 589832 | tf_op jit(solution)/shard_map/ppermute | solution.py:485
  22.7 11.7 %collective-permute-start.2 = (f32[3,128,128]{2,1,0:T(8,128)S(1)}, f32[3,128,128]{2,1,0:T(8,128)S(1)}, u32[]{:S(2)}, u32[]{:S(2)}) collective-permute-start(f32[3,128,128]{2,1,0:T(8,128)S(1)} %get-tuple-element.50), channel_id=1, source_target_pairs={{0,16},{4,20},{8,24},{12,28},{16,0},{20,4},{24,8},{28,12},{32,48},... | collective-permute-start | bytes 589832 | tf_op jit(solution)/shard_map/ppermute | solution.py:485
  25.2 9.3 %collective-permute-start.3 = (f32[3,128,128]{2,1,0:T(8,128)S(1)}, f32[3,128,128]{2,1,0:T(8,128)S(1)}, u32[]{:S(2)}, u32[]{:S(2)}) collective-permute-start(f32[3,128,128]{2,1,0:T(8,128)S(1)} %get-tuple-element.51), channel_id=1, source_target_pairs={{0,24},{4,28},{8,0},{12,4},{16,8},{20,12},{24,16},{28,20},{32,56},... | collective-permute-start | bytes 589832 | tf_op jit(solution)/shard_map/ppermute | solution.py:485
  35.5 4.9 %collective-permute-start.4 = (f32[128,128]{1,0:T(8,128)S(1)}, f32[128,128]{1,0:T(8,128)S(1)}, u32[]{:S(2)}, u32[]{:S(2)}) collective-permute-start(f32[128,128]{1,0:T(8,128)S(1)} %get-tuple-element.53), channel_id=1, source_target_pairs={{0,32},{4,36},{8,40},{12,44},{16,48},{20,52},{24,56},{28,60},{32,6... | collective-permute-start | bytes 196616 | tf_op jit(solution)/shard_map/ppermute | solution.py:492
  39.1 5.2 %collective-permute-start.5 = (f32[128,128]{1,0:T(8,128)S(1)}, f32[128,128]{1,0:T(8,128)S(1)}, u32[]{:S(2)}, u32[]{:S(2)}) collective-permute-start(f32[128,128]{1,0:T(8,128)S(1)} %get-tuple-element.54), channel_id=1, source_target_pairs={{32,0},{36,4},{40,8},{44,12},{48,16},{52,20},{56,24},{60,28},{64,3... | collective-permute-start | bytes 196616 | tf_op jit(solution)/shard_map/ppermute | solution.py:493
  45.4 5.1 %collective-permute-start.6 = (f32[2,128,128]{2,1,0:T(8,128)S(1)}, f32[2,128,128]{2,1,0:T(8,128)S(1)}, u32[]{:S(2)}, u32[]{:S(2)}) collective-permute-start(f32[2,128,128]{2,1,0:T(8,128)S(1)} %get-tuple-element.56), channel_id=1, source_target_pairs={{0,8},{4,12},{8,16},{12,20},{16,24},{20,28},{24,0},{28,4},{32,40},... | collective-permute-start | bytes 393224 | tf_op jit(solution)/shard_map/ppermute | solution.py:485
  46.2 7.1 %collective-permute-start.7 = (f32[2,128,128]{2,1,0:T(8,128)S(1)}, f32[2,128,128]{2,1,0:T(8,128)S(1)}, u32[]{:S(2)}, u32[]{:S(2)}) collective-permute-start(f32[2,128,128]{2,1,0:T(8,128)S(1)} %get-tuple-element.57), channel_id=1, source_target_pairs={{0,16},{4,20},{8,24},{12,28},{16,0},{20,4},{24,8},{28,12},{32,48},... | collective-permute-start | bytes 393224 | tf_op jit(solution)/shard_map/ppermute | solution.py:485
  49.0 4.4 %collective-permute-start.8 = (f32[2,128,128]{2,1,0:T(8,128)S(1)}, f32[2,128,128]{2,1,0:T(8,128)S(1)}, u32[]{:S(2)}, u32[]{:S(2)}) collective-permute-start(f32[2,128,128]{2,1,0:T(8,128)S(1)} %get-tuple-element.58), channel_id=1, source_target_pairs={{0,24},{4,28},{8,0},{12,4},{16,8},{20,12},{24,16},{28,20},{32,56},... | collective-permute-start | bytes 393224 | tf_op jit(solution)/shard_map/ppermute | solution.py:485
  54.3 9.6 %collective-permute-start.9 = (f32[4,2,128,128]{3,2,1,0:T(8,128)S(1)}, f32[4,2,128,128]{3,2,1,0:T(8,128)S(1)}, u32[]{:S(2)}, u32[]{:S(2)}) collective-permute-start(f32[4,2,128,128]{3,2,1,0:T(8,128)S(1)} %get-tuple-element.59), channel_id=1, source_target_pairs={{0,4},{4,0},{8,12},{12,8},{16,20},{20,16},{24,28},{28,24},{32,36},... | collective-permute-start | bytes 1572872 | tf_op jit(solution)/shard_map/ppermute | solution.py:500
  71.7 9.4 %collective-permute-start.11 = (f32[128,512]{1,0:T(8,128)S(1)}, f32[128,512]{1,0:T(8,128)S(1)}, u32[]{:S(2)}, u32[]{:S(2)}) collective-permute-start(f32[128,512]{1,0:T(8,128)S(1)} %chunk.3), channel_id=1, source_target_pairs={{0,1},{1,2},{2,3},{3,0},{4,5},{5,6},{6,7},{7,4},{8,9},{9,10},{10,1... | collective-permute-start | bytes 786440 | tf_op jit(solution)/shard_map/ppermute | solution.py:507
  73.0 8.0 %collective-permute-start.12 = (f32[128,512]{1,0:T(8,128)S(1)}, f32[128,512]{1,0:T(8,128)S(1)}, u32[]{:S(2)}, u32[]{:S(2)}) collective-permute-start(f32[128,512]{1,0:T(8,128)S(1)} %chunk.4), channel_id=1, source_target_pairs={{0,3},{1,0},{2,1},{3,2},{4,7},{5,4},{6,5},{7,6},{8,11},{9,8},{10,9... | collective-permute-start | bytes 786440 | tf_op jit(solution)/shard_map/ppermute | solution.py:507
  74.6 13.2 %collective-permute-start.10 = (f32[128,512]{1,0:T(8,128)S(1)}, f32[128,512]{1,0:T(8,128)S(1)}, u32[]{:S(2)}, u32[]{:S(2)}) collective-permute-start(f32[128,512]{1,0:T(8,128)S(1)} %get-tuple-element.68), channel_id=1, source_target_pairs={{0,2},{1,3},{2,0},{3,1},{4,6},{5,7},{6,4},{7,5},{8,10},{9,11},{10,... | collective-permute-start | bytes 786440 | tf_op jit(solution)/shard_map/ppermute | solution.py:507

commit v6 on v5

--- a/solution.py
+++ b/solution.py
@@ -12,6 +12,7 @@
 W = 128
 GROUP = 4
 SIDES = 4
+ORDER = (2, 1, 3)
 NN = (((1,), (0,)), ((), ()))
 NT = (((1,), (1,)), ((), ()))
 TN = (((0,), (0,)), ((), ()))
@@ -66,13 +67,11 @@
 def give_kernel(
     place_ref, side_ref, len_hbm, x_hbm, go_hbm, wb_hbm, dec_hbm, wk_hbm, wq_hbm, wo_hbm, wv_hbm, *refs
 ):
-    ids_ref, outs, refs = refs[0], refs[1:3], refs[3:]
+    outs, refs = refs[:2], refs[2:]
     x_ref, go_ref, beta_ref, run_ref, rows_ref, keep_ref, first_ref, wkq_ref, wv_ref, wkq2_ref = refs[:10]
     len_ref, wb_ref, dec_ref, wo_ref, sems = refs[10:]
     keep0 = (place_ref[0] & 1) * GROUP
     head0 = GROUP - keep0
-    ids_ref[0] = place_ref[0]
-    ids_ref[1] = side_ref[0]
     base = place_ref[0] * W
     at = head_columns(head0)
     at2 = head_columns(keep0)
@@ -113,11 +112,11 @@
 
 
 def keep_kernel(
-    ids_ref, x_ref, go_ref, beta_ref, run_ref, rows_ref, keep_ref, first_ref, wkq_ref, wo_hbm, wv_hbm, *refs
+    place_ref, x_ref, go_ref, beta_ref, run_ref, rows_ref, keep_ref, first_ref, wkq_ref, wo_hbm, wv_hbm, *refs
 ):
     outs = refs[:2]
     wv_ref, wo_ref, sems = refs[2:]
-    head0 = (ids_ref[0] & 1) * GROUP
+    head0 = (place_ref[0] & 1) * GROUP
     at = head_columns(head0)
     get_v = pltpu.make_async_copy(wv_hbm.at[:, at], wv_ref, sems.at[0])
     get_o = pltpu.make_async_copy(wo_hbm.at[at, :], wo_ref, sems.at[1])
@@ -243,11 +242,11 @@
     grad_ref[...] = grad
 
 
-def spread_kernel(place_ref, r_ref, s_ref, g_ref, *refs):
+def spread_kernel(size, place_ref, r_ref, s_ref, g_ref, *refs):
     x = place_ref[0] >> 1
     outs, all_ref = refs[:GROUP], refs[GROUP]
-    state = s_ref[...]
-    grad = g_ref[...]
+    state = jnp.where(place_ref[0] < 2 * GROUP, 0.0, s_ref[...])
+    grad = jnp.where(place_ref[0] >= size - 2 * GROUP, 0.0, g_ref[...])
     all_ref[0, 0] = state
     all_ref[GROUP - 1, 1] = grad
     for j in range(1, GROUP):
@@ -286,22 +285,23 @@
     return piece + dot(grads[:, 2 * n:], wv_ref[at, :], NT) + dot(db, wb_ref[:, at])
 
 
-def chunk_kernel(distance, ids_ref, grads_ref, db_ref, before_ref, wb_ref, wkq_ref, wv_ref, out_ref):
-    side = (ids_ref[1] + distance) & (SIDES - 1)
-    piece = back_project(side, grads_ref[...], db_ref[...], wkq_ref, wv_ref, wb_ref, out_ref.shape[1])
-    out_ref[...] = before_ref[distance] + piece
+def chunk_kernel(side_ref, grads_ref, db_ref, before_ref, wb_ref, wkq_ref, wv_ref, out_ref):
+    piece = back_project(side_ref[0], grads_ref[...], db_ref[...], wkq_ref, wv_ref, wb_ref, out_ref.shape[1])
+    out_ref[...] = before_ref[0] + piece
 
 
 def second_kernel(chained, *refs):
-    ids_ref, back_ref, kept_ref, wb_ref, wkq_ref, wv_ref = refs[:6]
-    refs = refs[6:]
+    place_ref, side_ref, back_ref, kept_ref, wb_ref, wkq_ref, wv_ref = refs[:7]
+    refs = refs[7:]
     if chained:
-        before_ref, gd_before_ref, total_ref, gd_ref, grads_ref, db_ref = refs
+        before_ref, gd_before_ref, *total_refs, gd_ref, grads_ref, db_ref = refs
+        wide = total_refs[0].shape[-1]
     else:
         total_ref, gd_ref = refs
-    keep0 = (ids_ref[0] & 1) * GROUP
+        wide = total_ref.shape[-1]
+    keep0 = (place_ref[0] & 1) * GROUP
     head0 = GROUP - keep0 if chained else keep0
-    side = ids_ref[1]
+    side = side_ref[0]
     ti, si = iotas((W, W))
     strict = ti > si
     upper = jnp.where(si >= ti, 1.0, 0.0)
@@ -356,10 +356,10 @@
         gvs.append((beta * dr).astype(BF16))
     grads = jnp.concatenate(gqs + gks + gvs, axis=1)
     db = dball.astype(BF16)
-    wide = total_ref.shape[-1]
     project = lambda d: back_project((side + d) & (SIDES - 1), grads, db, wkq_ref, wv_ref, wb_ref, wide)
     if chained:
-        total_ref[...] = before_ref[2] + project(2)
+        for d, total_ref in zip(ORDER, total_refs):
+            total_ref[...] = before_ref[d] + project(d)
         grads_ref[...] = grads
         db_ref[...] = db
     else:
@@ -398,8 +398,8 @@
     out = pl.pallas_call(
         give_kernel,
         in_specs=[SMEM] * 2 + [HBM] * 9,
-        out_specs=[SMEM] + [VMEM] * 12,
-        out_shape=[jax.ShapeDtypeStruct((2,), jnp.int32)] + block_shapes() + [wide, wide, shape(rows, heads), shape(rows, heads), shape(heads, rows), shape(W, W), shape(W, heads)] + [two, tall, two],
+        out_specs=[VMEM] * 12,
+        out_shape=block_shapes() + [wide, wide, shape(rows, heads), shape(rows, heads), shape(heads, rows), shape(W, W), shape(W, heads)] + [two, tall, two],
         scratch_shapes=[
             pltpu.SMEM(lengths.shape, jnp.int32), pltpu.VMEM(beta_t.shape, BF16), pltpu.VMEM(decay_t.shape, F32),
             pltpu.VMEM((span, width), BF16), pltpu.SemaphoreType.DMA((11,)),
@@ -407,10 +407,10 @@
         compiler_params=pltpu.CompilerParams(vmem_limit_bytes=28 << 20),
         name="block_forward_give",
     )(place, side, *in_hbm(lengths, inputs, grad_out, beta_t, decay_t, w_key, w_query, w_out, w_value))
-    return out[0], out[1], out[2], out[3:10], out[10:12], out[12]
-
-
-def run_keep(ids, shared, w_keep, w_out, w_value):
+    return out[0], out[1], out[2:9], out[9:11], out[11]
+
+
+def run_keep(place, shared, w_keep, w_out, w_value):
     _, width, span = w_keep.shape
     out = pl.pallas_call(
         keep_kernel,
@@ -420,36 +420,36 @@
         scratch_shapes=[pltpu.VMEM((span, width), BF16), pltpu.SemaphoreType.DMA((2,))],
         compiler_params=pltpu.CompilerParams(vmem_limit_bytes=24 << 20),
         name="block_forward_keep",
-    )(ids, *shared, w_keep, *in_hbm(w_out, w_value))
+    )(place, *shared, w_keep, *in_hbm(w_out, w_value))
     return out
 
 
-def run_backward(ids, back, kept, beta_t, w_both, w_value, before):
+def run_backward(place, side, back, kept, beta_t, w_both, w_value, before):
     heads, width = beta_t.shape
     wide = width // SIDES
     if before:
-        out_shape = [shape(W, wide), shape(heads, W), jax.ShapeDtypeStruct((W, 3 * GROUP * W), BF16), jax.ShapeDtypeStruct((W, heads), BF16)]
+        out_shape = [shape(W, wide)] * 3 + [shape(heads, W), jax.ShapeDtypeStruct((W, 3 * GROUP * W), BF16), jax.ShapeDtypeStruct((W, heads), BF16)]
     else:
         out_shape = [shape(SIDES, W, wide), shape(heads, W)]
     return pl.pallas_call(
         partial(second_kernel, bool(before)),
-        in_specs=[SMEM] + [VMEM] * 5 + [VMEM] * len(before),
+        in_specs=[SMEM] * 2 + [VMEM] * 5 + [VMEM] * len(before),
         out_specs=[VMEM] * len(out_shape),
         out_shape=out_shape,
         compiler_params=pltpu.CompilerParams(vmem_limit_bytes=24 << 20),
         name="block_backward",
-    )(ids, back, kept, beta_t, w_both, w_value, *before)
-
-
-def run_chunk(distance, ids, grads, db, before, beta_t, w_both, w_value):
+    )(place, side, back, kept, beta_t, w_both, w_value, *before)
+
+
+def run_chunk(side, grads, db, before, beta_t, w_both, w_value):
     return pl.pallas_call(
-        partial(chunk_kernel, distance),
+        chunk_kernel,
         in_specs=[SMEM] + [VMEM] * 6,
         out_specs=VMEM,
         out_shape=shape(*before.shape[1:]),
         compiler_params=pltpu.CompilerParams(vmem_limit_bytes=16 << 20),
-        name="chunk",
-    )(ids, grads, db, before, beta_t, w_both, w_value)
+        name="own_chunk",
+    )(side, grads, db, before, beta_t, w_both, w_value)
 
 
 def per_device(inputs, grad_out, w_query, w_key, w_value, w_beta, w_out, log_decay, lengths):
@@ -460,11 +460,11 @@
     small = pltpu.CompilerParams(vmem_limit_bytes=8 << 20)
 
     pair = [(j, j ^ 1) for j in range(size)]
-    ids, give, give_kept, shared, give_w, keep_w = run_give(
+    give, give_kept, shared, give_w, keep_w = run_give(
         place, side, lengths, inputs, grad_out, beta_t, decay_t, w_key, w_query, w_out, w_value
     )
     other = lax.ppermute(give, "ctx", pair)
-    own, own_kept, keep_v = run_keep(ids, shared, keep_w, w_out, w_value)
+    own, own_kept, keep_v = run_keep(place, shared, keep_w, w_out, w_value)
     row = 2 * GROUP
 
     def call(kernel, name, scalars, arrays, out_shape, scratch=()):
@@ -485,27 +485,24 @@
             got[d] = lax.ppermute(parts[d], "ctx", moves)
         return [got[d] for d in range(GROUP)]
 
-    whole = call(join_kernel, "chip_join", (ids,), (own, other), [shape(3, W, W)] * GROUP)
+    whole = call(join_kernel, "chip_join", (place,), (own, other), [shape(3, W, W)] * GROUP)
     mine, state, grad = call(
-        row_kernel, "row_ends", (ids,), along_x(whole), [shape(GROUP, 3, W, W), shape(W, W), shape(W, W)]
-    )
-    state = lax.ppermute(state, "ctx", [(j, j + row) for j in range(size - row)])
-    grad = lax.ppermute(grad, "ctx", [(j + row, j) for j in range(size - row)])
+        row_kernel, "row_ends", (place,), along_x(whole), [shape(GROUP, 3, W, W), shape(W, W), shape(W, W)]
+    )
+    state = lax.ppermute(state, "ctx", [(j, (j + row) % size) for j in range(size)])
+    grad = lax.ppermute(grad, "ctx", [((j + row) % size, j) for j in range(size)])
     spread = call(
-        spread_kernel, "row_states", (ids,), (mine, state, grad), [shape(2, W, W)] * GROUP, [pltpu.VMEM((GROUP, 2, W, W), F32)]
+        partial(spread_kernel, size), "row_states", (place,), (mine, state, grad), [shape(2, W, W)] * GROUP, [pltpu.VMEM((GROUP, 2, W, W), F32)]
     )
     own_back, give_back = call(
-        part_kernel, "chip_part", (ids,), (own, other, *along_x(spread)), [shape(GROUP, 2, W, W)] * 2
+        part_kernel, "chip_part", (place,), (own, other, *along_x(spread)), [shape(GROUP, 2, W, W)] * 2
     )
     other_back = lax.ppermute(give_back, "ctx", pair)
-    before = run_backward(ids, own_back, own_kept, beta_t, keep_w, keep_v, ())
-    far, grad_d, grads, db = run_backward(ids, other_back, give_kept, beta_t, *give_w, before)
-    total = 0.0
-    for d in (2, 1, 3, 0):
-        chunk = far if d == 2 else run_chunk(d, ids, grads, db, before[0], beta_t, *give_w)
-        if d:
-            chunk = lax.ppermute(chunk, "head", [(j, (j + d) % SIDES) for j in range(SIDES)])
-        total = total + chunk
+    before = run_backward(place, side, own_back, own_kept, beta_t, keep_w, keep_v, ())
+    *chunks, grad_d, grads, db = run_backward(place, side, other_back, give_kept, beta_t, *give_w, before)
+    total = run_chunk(side, grads, db, before[0], beta_t, *give_w)
+    for d, chunk in zip(ORDER, chunks):
+        total = total + lax.ppermute(chunk, "head", [(j, (j + d) % SIDES) for j in range(SIDES)])
     return (total.astype(BF16), grad_d.T)
 
 

time: 88.6 us -> 79.4 us (0.90)
  Pallas kernels: 37.7 us -> 31.6 us
  waiting for transfers between devices: 26.1 us -> 23.6 us
    pallas_call x6 -> x4, Pallas kernels: 25 us -> 21.6 us  [the longest x2 12 us: run_backward(): pl.pallas_call(partial(second_kernel, bool(before)), in_specs=[SMEM] * 2...]
    ppermute x2, waiting for transfers between devices: 3.9 us -> 1.58 us  [the longest x1 1.57 us: per_device(): lax.ppermute(state, 'ctx', [(j, (j + row) % size) for j in range(size)])]
    pallas_call x4, Pallas kernels: 4.28 us -> 2.14 us  [call(): pl.pallas_call(kernel, in_specs=[SMEM] * len(scalars) + [VMEM] * len(arra...]
    ppermute x3, waiting for transfers between devices: 10.4 us -> 9.14 us  [per_device(): lax.ppermute(chunk, 'head', [(j, (j + d) % SIDES) for j in range(SIDES)])]
    ppermute x3, starting transfers between devices: 4.46 us -> 5.59 us  [per_device(): lax.ppermute(chunk, 'head', [(j, (j + d) % SIDES) for j in range(SIDES)])]
    ppermute x6, waiting for transfers between devices: 11.8 us -> 12.8 us  [along_x(): got[d] = lax.ppermute(parts[d], 'ctx', moves)]
    ppermute x2, starting transfers between devices: 4.83 us -> 3.9 us  [the longest x1 2.2 us: per_device(): lax.ppermute(grad, 'ctx', [((j + row) % size, j) for j in range(size)])]
  transfers between devices with their start and end apart: 13 -> 13, of which waited for: 8 -> 7; matrix products, arithmetic and copies ran while one was open for 0% -> 0% of each run, Pallas kernels for 18% -> 18%
where the time goes in v6:
time: 79.4 us; the launch traced here: 79.3 us
  Pallas kernels  31.6 us (40%)
  waiting for transfers between devices  23.6 us (30%)
  starting transfers between devices  22.7 us (29%)
    ppermute x6, waiting for transfers between devices, along_x(): got[d] = lax.ppermute(parts[d], 'ctx', moves)  12.8 us
    pallas_call x2, Pallas kernels, run_backward(): pl.pallas_call(partial(second_kernel, bool(before)), in_specs=[SMEM] * 2...  12 us
    ppermute x6, starting transfers between devices, along_x(): got[d] = lax.ppermute(parts[d], 'ctx', moves)  9.36 us
    ppermute x3, waiting for transfers between devices, per_device(): lax.ppermute(chunk, 'head', [(j, (j + d) % SIDES) for j in range(SIDES)])  9.14 us
    pallas_call x1, Pallas kernels, run_give(): pl.pallas_call(give_kernel, in_specs=[SMEM] * 2 + [HBM] * 9, out_specs=[V...  8.91 us
    pallas_call x1, Pallas kernels, run_keep(): pl.pallas_call(keep_kernel, in_specs=[SMEM] + [VMEM] * 8 + [HBM] * 2, out...  7.83 us
    ppermute x3, starting transfers between devices, per_device(): lax.ppermute(chunk, 'head', [(j, (j + d) % SIDES) for j in range(SIDES)])  5.59 us
    ppermute x1, starting transfers between devices, per_device(): other_back = lax.ppermute(give_back, 'ctx', pair)  2.38 us
  transfers between devices with their start and end apart: 13, of which 7 were waited for; matrix products, arithmetic and copies ran while one was open for 0% of the time, Pallas kernels for 18%

profile of v6, /device:TPU:1, one launch (start us, length us, event | category | flops | bytes accessed | tf_op | source)
XLA Modules:
  0.0 79.3 jit_solution(17126977007790592386)
XLA Ops:
  0.6 8.9 %block_forward_give.1 = (f32[4,3,128,128]{3,2,1,0:T(8,128)S(1)}, f32[4,11,128,128]{3,2,1,0:T(8,128)S(1)}, bf16[128,2048]{1,0:T(8,128)(2,1)S(1)}, bf16[128,2048]{...) custom-call(s32[1]{0:T(128)} %bitcast.1.place_ref.refs_0_, ...), custom_call_target="tpu_custom_call" | custom-call | tf_op jit(solution)/shard_map/block_forward_give/pallas_call | solution.py:398
  9.6 1.5 %collective-permute-start = (f32[4,3,128,128]{3,2,1,0:T(8,128)S(1)}, f32[4,3,128,128]{3,2,1,0:T(8,128)S(1)}, u32[]{:S(2)}, u32[]{:S(2)}) collective-permute-start(f32[4,3,128,128]{3,2,1,0:T(8,128)S(1)} %get-tuple-element.47), channel_id=1, source_target_pairs={{0,4},{4,0},{8,12},{12,8},{16,20},{20,16},{24,28},{28,24},{32,36},... | collective-permute-start | bytes 2359304 | tf_op jit(solution)/shard_map/ppermute | solution.py:466
  11.1 7.8 %block_forward_keep.1 = (f32[4,3,128,128]{3,2,1,0:T(8,128)S(1)}, f32[4,11,128,128]{3,2,1,0:T(8,128)S(1)}, bf16[2048,512]{1,0:T(8,128)(2,1)S(1)}) custom-call(s32[1]{0:T(128)} %bitcast.1.place_ref.refs_0_, bf16[128,2048]{1,0:T(8,128)(2,1)S(1)} %get-tuple-element.38.x_ref, bf16[128,2048]{1,0:T(8,128)(2,1)S(1)} %get-tuple-element.39.go_ref, ...), custom_call_target="tpu_custom_call" | custom-call | tf_op jit(solution)/shard_map/block_forward_keep/pallas_call | solution.py:415
  19.5 1.5 %collective-permute-start.1 = (f32[3,128,128]{2,1,0:T(8,128)S(1)}, f32[3,128,128]{2,1,0:T(8,128)S(1)}, u32[]{:S(2)}, u32[]{:S(2)}) collective-permute-start(f32[3,128,128]{2,1,0:T(8,128)S(1)} %get-tuple-element.49), channel_id=1, source_target_pairs={{0,8},{4,12},{8,16},{12,20},{16,24},{20,28},{24,0},{28,4},{32,40},... | collective-permute-start | bytes 589832 | tf_op jit(solution)/shard_map/ppermute | solution.py:485
  21.0 2.5 %collective-permute-start.2 = (f32[3,128,128]{2,1,0:T(8,128)S(1)}, f32[3,128,128]{2,1,0:T(8,128)S(1)}, u32[]{:S(2)}, u32[]{:S(2)}) collective-permute-start(f32[3,128,128]{2,1,0:T(8,128)S(1)} %get-tuple-element.50), channel_id=1, source_target_pairs={{0,16},{4,20},{8,24},{12,28},{16,0},{20,4},{24,8},{28,12},{32,48},... | collective-permute-start | bytes 589832 | tf_op jit(solution)/shard_map/ppermute | solution.py:485
  23.5 1.1 %collective-permute-start.3 = (f32[3,128,128]{2,1,0:T(8,128)S(1)}, f32[3,128,128]{2,1,0:T(8,128)S(1)}, u32[]{:S(2)}, u32[]{:S(2)}) collective-permute-start(f32[3,128,128]{2,1,0:T(8,128)S(1)} %get-tuple-element.51), channel_id=1, source_target_pairs={{0,24},{4,28},{8,0},{12,4},{16,8},{20,12},{24,16},{28,20},{32,56},... | collective-permute-start | bytes 589832 | tf_op jit(solution)/shard_map/ppermute | solution.py:485
  24.6 2.8 %collective-permute-done.1.refs_1_ = f32[3,128,128]{2,1,0:T(8,128)S(1)} collective-permute-done((f32[3,128,128]{2,1,0:T(8,128)S(1)}, f32[3,128,128]{2,1,0:T(8,128)S(1)}, u32[]{:S(2)}, u32[]{:S(2)}) %collective-permute-start.1) | collective-permute-done | bytes 196640 | tf_op jit(solution)/shard_map/ppermute | solution.py:485
  27.5 5.3 %collective-permute-done.2.refs_2_ = f32[3,128,128]{2,1,0:T(8,128)S(1)} collective-permute-done((f32[3,128,128]{2,1,0:T(8,128)S(1)}, f32[3,128,128]{2,1,0:T(8,128)S(1)}, u32[]{:S(2)}, u32[]{:S(2)}) %collective-permute-start.2) | collective-permute-done | bytes 196640 | tf_op jit(solution)/shard_map/ppermute | solution.py:485
  33.4 1.7 %collective-permute-start.4 = (f32[128,128]{1,0:T(8,128)S(1)}, f32[128,128]{1,0:T(8,128)S(1)}, u32[]{:S(2)}, u32[]{:S(2)}) collective-permute-start(f32[128,128]{1,0:T(8,128)S(1)} %get-tuple-element.53), channel_id=1, source_target_pairs={{0,32},{4,36},{8,40},{12,44},{16,48},{20,52},{24,56},{28,60},{32,6... | collective-permute-start | bytes 196616 | tf_op jit(solution)/shard_map/ppermute | solution.py:492
  35.1 2.2 %collective-permute-start.5 = (f32[128,128]{1,0:T(8,128)S(1)}, f32[128,128]{1,0:T(8,128)S(1)}, u32[]{:S(2)}, u32[]{:S(2)}) collective-permute-start(f32[128,128]{1,0:T(8,128)S(1)} %get-tuple-element.54), channel_id=1, source_target_pairs={{32,0},{36,4},{40,8},{44,12},{48,16},{52,20},{56,24},{60,28},{64,3... | collective-permute-start | bytes 196616 | tf_op jit(solution)/shard_map/ppermute | solution.py:493
  37.3 1.6 %collective-permute-done.4.s_ref = f32[128,128]{1,0:T(8,128)S(1)} collective-permute-done((f32[128,128]{1,0:T(8,128)S(1)}, f32[128,128]{1,0:T(8,128)S(1)}, u32[]{:S(2)}, u32[]{:S(2)}) %collective-permute-start.4) | collective-permute-done | bytes 65568 | tf_op jit(solution)/shard_map/ppermute | solution.py:492
  39.4 0.7 collective-permute-start.6
  40.2 3.2 %collective-permute-start.7 = (f32[2,128,128]{2,1,0:T(8,128)S(1)}, f32[2,128,128]{2,1,0:T(8,128)S(1)}, u32[]{:S(2)}, u32[]{:S(2)}) collective-permute-start(f32[2,128,128]{2,1,0:T(8,128)S(1)} %get-tuple-element.57), channel_id=1, source_target_pairs={{0,16},{4,20},{8,24},{12,28},{16,0},{20,4},{24,8},{28,12},{32,48},... | collective-permute-start | bytes 393224 | tf_op jit(solution)/shard_map/ppermute | solution.py:485
  43.6 0.9 %collective-permute-done.6.refs_1_ = f32[2,128,128]{2,1,0:T(8,128)S(1)} collective-permute-done((f32[2,128,128]{2,1,0:T(8,128)S(1)}, f32[2,128,128]{2,1,0:T(8,128)S(1)}, u32[]{:S(2)}, u32[]{:S(2)}) %collective-permute-start.6) | collective-permute-done | bytes 131104 | tf_op jit(solution)/shard_map/ppermute | solution.py:485
  44.5 3.8 %collective-permute-done.7.refs_2_ = f32[2,128,128]{2,1,0:T(8,128)S(1)} collective-permute-done((f32[2,128,128]{2,1,0:T(8,128)S(1)}, f32[2,128,128]{2,1,0:T(8,128)S(1)}, u32[]{:S(2)}, u32[]{:S(2)}) %collective-permute-start.7) | collective-permute-done | bytes 131104 | tf_op jit(solution)/shard_map/ppermute | solution.py:485
  48.8 2.4 %collective-permute-start.9 = (f32[4,2,128,128]{3,2,1,0:T(8,128)S(1)}, f32[4,2,128,128]{3,2,1,0:T(8,128)S(1)}, u32[]{:S(2)}, u32[]{:S(2)}) collective-permute-start(f32[4,2,128,128]{3,2,1,0:T(8,128)S(1)} %get-tuple-element.59), channel_id=1, source_target_pairs={{0,4},{4,0},{8,12},{12,8},{16,20},{20,16},{24,28},{28,24},{32,36},... | collective-permute-start | bytes 1572872 | tf_op jit(solution)/shard_map/ppermute | solution.py:500
  51.2 6.1 %block_backward.2 = (f32[4,128,512]{2,1,0:T(8,128)S(1)}, f32[8,128]{1,0:T(8,128)S(1)}) custom-call(s32[1]{0:T(128)} %bitcast.1.place_ref.refs_0_, s32[1]{0:T(128)} %bitcast.side_ref.refs_1_, f32[4,2,128,128]{3,2,1,0:T(8,128)S(1)} %get-tuple-element.63.refs_2_, f32[4,11,128,128]{3,2,1,0:T(8,128)S(1)} %get-tuple-element.64.refs_3_, ...), custom_call_target="tpu_custom_call" | custom-call | tf_op jit(solution)/shard_map/block_backward/pallas_call | solution.py:434
  57.3 5.9 %block_backward.3 = (f32[128,512]{1,0:T(8,128)S(1)}, f32[128,512]{1,0:T(8,128)S(1)}, f32[128,512]{1,0:T(8,128)S(1)}, f32[8,128]{1,0:T(8,128)}, bf16[128,1536]{1,...) custom-call(s32[1]{0:T(128)} %bitcast.1.place_ref.refs_0_, s32[1]{0:T(128)} %bitcast.side_ref.refs_1_, ...), custom_call_target="tpu_custom_call" | custom-call | tf_op jit(solution)/shard_map/block_backward/pallas_call | solution.py:434
  63.2 2.9 %collective-permute-start.10 = (f32[128,512]{1,0:T(8,128)S(1)}, f32[128,512]{1,0:T(8,128)S(1)}, u32[]{:S(2)}, u32[]{:S(2)}) collective-permute-start(f32[128,512]{1,0:T(8,128)S(1)} %get-tuple-element.70), channel_id=1, source_target_pairs={{0,2},{1,3},{2,0},{3,1},{4,6},{5,7},{6,4},{7,5},{8,10},{9,11},{10,... | collective-permute-start | bytes 786440 | tf_op jit(solution)/shard_map/ppermute | solution.py:505
  66.5 2.3 %collective-permute-start.12 = (f32[128,512]{1,0:T(8,128)S(1)}, f32[128,512]{1,0:T(8,128)S(1)}, u32[]{:S(2)}, u32[]{:S(2)}) collective-permute-start(f32[128,512]{1,0:T(8,128)S(1)} %get-tuple-element.72), channel_id=1, source_target_pairs={{0,3},{1,0},{2,1},{3,2},{4,7},{5,4},{6,5},{7,6},{8,11},{9,8},{10,9... | collective-permute-start | bytes 786440 | tf_op jit(solution)/shard_map/ppermute | solution.py:505
  68.8 0.7 own_chunk.1
  69.5 3.2 %collective-permute-done.10 = f32[128,512]{1,0:T(8,128)S(1)} collective-permute-done((f32[128,512]{1,0:T(8,128)S(1)}, f32[128,512]{1,0:T(8,128)S(1)}, u32[]{:S(2)}, u32[]{:S(2)}) %collective-permute-start.10) | collective-permute-done | bytes 262176 | tf_op jit(solution)/shard_map/ppermute | solution.py:505
  72.6 5.9 %collective-permute-done.11 = f32[128,512]{1,0:T(8,128)S(1)} collective-permute-done((f32[128,512]{1,0:T(8,128)S(1)}, f32[128,512]{1,0:T(8,128)S(1)}, u32[]{:S(2)}, u32[]{:S(2)}) %collective-permute-start.11) | collective-permute-done | bytes 262176 | tf_op jit(solution)/shard_map/ppermute | solution.py:505
  78.6 0.7 add_convert_fusion
  (14 shorter events, 2.9 us)
Async XLA Ops:
  9.6 9.4 %collective-permute-start = (f32[4,3,128,128]{3,2,1,0:T(8,128)S(1)}, f32[4,3,128,128]{3,2,1,0:T(8,128)S(1)}, u32[]{:S(2)}, u32[]{:S(2)}) collective-permute-start(f32[4,3,128,128]{3,2,1,0:T(8,128)S(1)} %get-tuple-element.47), channel_id=1, source_target_pairs={{0,4},{4,0},{8,12},{12,8},{16,20},{20,16},{24,28},{28,24},{32,36},... | collective-permute-start | bytes 2359304 | tf_op jit(solution)/shard_map/ppermute | solution.py:466
  18.9 32.2 %copy-start = (bf16[2048,8]{0,1:T(8,128)(2,1)S(1)}, bf16[2048,8]{0,1:T(8,128)(2,1)}, u32[]{:S(2)}) copy-start(bf16[2048,8]{0,1:T(8,128)(2,1)} %param.14) | copy-start | bytes 98308
  19.5 8.0 %collective-permute-start.1 = (f32[3,128,128]{2,1,0:T(8,128)S(1)}, f32[3,128,128]{2,1,0:T(8,128)S(1)}, u32[]{:S(2)}, u32[]{:S(2)}) collective-permute-start(f32[3,128,128]{2,1,0:T(8,128)S(1)} %get-tuple-element.49), channel_id=1, source_target_pairs={{0,8},{4,12},{8,16},{12,20},{16,24},{20,28},{24,0},{28,4},{32,40},... | collective-permute-start | bytes 589832 | tf_op jit(solution)/shard_map/ppermute | solution.py:485
  21.0 11.7 %collective-permute-start.2 = (f32[3,128,128]{2,1,0:T(8,128)S(1)}, f32[3,128,128]{2,1,0:T(8,128)S(1)}, u32[]{:S(2)}, u32[]{:S(2)}) collective-permute-start(f32[3,128,128]{2,1,0:T(8,128)S(1)} %get-tuple-element.50), channel_id=1, source_target_pairs={{0,16},{4,20},{8,24},{12,28},{16,0},{20,4},{24,8},{28,12},{32,48},... | collective-permute-start | bytes 589832 | tf_op jit(solution)/shard_map/ppermute | solution.py:485
  23.5 9.3 %collective-permute-start.3 = (f32[3,128,128]{2,1,0:T(8,128)S(1)}, f32[3,128,128]{2,1,0:T(8,128)S(1)}, u32[]{:S(2)}, u32[]{:S(2)}) collective-permute-start(f32[3,128,128]{2,1,0:T(8,128)S(1)} %get-tuple-element.51), channel_id=1, source_target_pairs={{0,24},{4,28},{8,0},{12,4},{16,8},{20,12},{24,16},{28,20},{32,56},... | collective-permute-start | bytes 589832 | tf_op jit(solution)/shard_map/ppermute | solution.py:485
  33.4 5.5 %collective-permute-start.4 = (f32[128,128]{1,0:T(8,128)S(1)}, f32[128,128]{1,0:T(8,128)S(1)}, u32[]{:S(2)}, u32[]{:S(2)}) collective-permute-start(f32[128,128]{1,0:T(8,128)S(1)} %get-tuple-element.53), channel_id=1, source_target_pairs={{0,32},{4,36},{8,40},{12,44},{16,48},{20,52},{24,56},{28,60},{32,6... | collective-permute-start | bytes 196616 | tf_op jit(solution)/shard_map/ppermute | solution.py:492
  35.1 3.8 %collective-permute-start.5 = (f32[128,128]{1,0:T(8,128)S(1)}, f32[128,128]{1,0:T(8,128)S(1)}, u32[]{:S(2)}, u32[]{:S(2)}) collective-permute-start(f32[128,128]{1,0:T(8,128)S(1)} %get-tuple-element.54), channel_id=1, source_target_pairs={{32,0},{36,4},{40,8},{44,12},{48,16},{52,20},{56,24},{60,28},{64,3... | collective-permute-start | bytes 196616 | tf_op jit(solution)/shard_map/ppermute | solution.py:493
  39.4 5.1 %collective-permute-start.6 = (f32[2,128,128]{2,1,0:T(8,128)S(1)}, f32[2,128,128]{2,1,0:T(8,128)S(1)}, u32[]{:S(2)}, u32[]{:S(2)}) collective-permute-start(f32[2,128,128]{2,1,0:T(8,128)S(1)} %get-tuple-element.56), channel_id=1, source_target_pairs={{0,8},{4,12},{8,16},{12,20},{16,24},{20,28},{24,0},{28,4},{32,40},... | collective-permute-start | bytes 393224 | tf_op jit(solution)/shard_map/ppermute | solution.py:485
  40.2 8.2 %collective-permute-start.7 = (f32[2,128,128]{2,1,0:T(8,128)S(1)}, f32[2,128,128]{2,1,0:T(8,128)S(1)}, u32[]{:S(2)}, u32[]{:S(2)}) collective-permute-start(f32[2,128,128]{2,1,0:T(8,128)S(1)} %get-tuple-element.57), channel_id=1, source_target_pairs={{0,16},{4,20},{8,24},{12,28},{16,0},{20,4},{24,8},{28,12},{32,48},... | collective-permute-start | bytes 393224 | tf_op jit(solution)/shard_map/ppermute | solution.py:485
  43.3 5.0 %collective-permute-start.8 = (f32[2,128,128]{2,1,0:T(8,128)S(1)}, f32[2,128,128]{2,1,0:T(8,128)S(1)}, u32[]{:S(2)}, u32[]{:S(2)}) collective-permute-start(f32[2,128,128]{2,1,0:T(8,128)S(1)} %get-tuple-element.58), channel_id=1, source_target_pairs={{0,24},{4,28},{8,0},{12,4},{16,8},{20,12},{24,16},{28,20},{32,56},... | collective-permute-start | bytes 393224 | tf_op jit(solution)/shard_map/ppermute | solution.py:485
  48.8 8.5 %collective-permute-start.9 = (f32[4,2,128,128]{3,2,1,0:T(8,128)S(1)}, f32[4,2,128,128]{3,2,1,0:T(8,128)S(1)}, u32[]{:S(2)}, u32[]{:S(2)}) collective-permute-start(f32[4,2,128,128]{3,2,1,0:T(8,128)S(1)} %get-tuple-element.59), channel_id=1, source_target_pairs={{0,4},{4,0},{8,12},{12,8},{16,20},{20,16},{24,28},{28,24},{32,36},... | collective-permute-start | bytes 1572872 | tf_op jit(solution)/shard_map/ppermute | solution.py:500
  63.2 9.5 %collective-permute-start.10 = (f32[128,512]{1,0:T(8,128)S(1)}, f32[128,512]{1,0:T(8,128)S(1)}, u32[]{:S(2)}, u32[]{:S(2)}) collective-permute-start(f32[128,512]{1,0:T(8,128)S(1)} %get-tuple-element.70), channel_id=1, source_target_pairs={{0,2},{1,3},{2,0},{3,1},{4,6},{5,7},{6,4},{7,5},{8,10},{9,11},{10,... | collective-permute-start | bytes 786440 | tf_op jit(solution)/shard_map/ppermute | solution.py:505
  66.1 12.5 %collective-permute-start.11 = (f32[128,512]{1,0:T(8,128)S(1)}, f32[128,512]{1,0:T(8,128)S(1)}, u32[]{:S(2)}, u32[]{:S(2)}) collective-permute-start(f32[128,512]{1,0:T(8,128)S(1)} %get-tuple-element.71), channel_id=1, source_target_pairs={{0,1},{1,2},{2,3},{3,0},{4,5},{5,6},{6,7},{7,4},{8,9},{9,10},{10,1... | collective-permute-start | bytes 786440 | tf_op jit(solution)/shard_map/ppermute | solution.py:505
  66.5 12.1 %collective-permute-start.12 = (f32[128,512]{1,0:T(8,128)S(1)}, f32[128,512]{1,0:T(8,128)S(1)}, u32[]{:S(2)}, u32[]{:S(2)}) collective-permute-start(f32[128,512]{1,0:T(8,128)S(1)} %get-tuple-element.72), channel_id=1, source_target_pairs={{0,3},{1,0},{2,1},{3,2},{4,7},{5,4},{6,5},{7,6},{8,11},{9,8},{10,9... | collective-permute-start | bytes 786440 | tf_op jit(solution)/shard_map/ppermute | solution.py:505

commit v7 on v6

--- a/solution.py
+++ b/solution.py
@@ -81,7 +81,7 @@
         (wk_hbm.at[:, at2], wkq2_ref.at[0]), (wq_hbm.at[:, at2], wkq2_ref.at[1]),
     )
     gets = [pltpu.make_async_copy(src, dst, sems.at[j]) for j, (src, dst) in enumerate(pairs)]
-    for get in gets:
+    for get in (gets[2], gets[3], gets[4], gets[1], gets[0], gets[5], gets[6], gets[7], gets[8], gets[9], gets[10]):
         get.start()
     gets[2].wait()
     ti, si = iotas((W, W))
@@ -95,7 +95,9 @@
         seg_in = seg_in + (base - 1 >= begin).astype(jnp.int32)
         begin = begin + len_ref[j]
     keep_ref[...] = jnp.where(jnp.logical_and(seg_t == seg_s, ti >= si), 1.0, 0.0)
-    first_ref[...] = jnp.broadcast_to(jnp.where(seg_t == seg_in, 1.0, 0.0), first_ref.shape)
+    lane = iotas(first_ref.shape)[1]
+    marked = jnp.where(lane == 0, seg_in, seg_t[W - 1:W, :])
+    first_ref[...] = jnp.where(seg_t == marked, 1.0, 0.0)
     gets[3].wait()
     tril = jnp.where(ti >= si, 1.0, 0.0)
     run_ref[...] = exact(tril, dec_ref[...], NT)
@@ -142,6 +144,7 @@
     strict = ti > si
     keep = keep_ref[...] > 0.0
     first = first_ref[...][:, :1] > 0.0
+    final = first_ref[...][:, 1:2] > 0.0
     beta_all, run_all, run_rows = beta_ref[...], run_ref[...], rows_ref[...]
     heads = range(GROUP)
     cut = lambda a, i: a[:, i * W:(i + 1) * W]
@@ -176,7 +179,7 @@
         mixes.append(wkk * beta)
         pmats.append(pmat)
         lanes = si
-        closing = jnp.sum(jnp.where(ti == si, jnp.broadcast_to(weight[W - 1:W, :], (W, W)), 0.0), axis=1, keepdims=True)
+        closing = jnp.where(final, jnp.exp(jnp.where(final, run[W - 1:W, :] - run, 0.0)), 0.0)
         col = jnp.where(lanes == 0, beta, jnp.where(lanes == 1, carried, jnp.where(lanes == 2, closing, jnp.where(lanes == 3, inv_k, inv_q))))
         kept_ref[i, 10] = col
         kept_ref[i, 0] = k
@@ -184,11 +187,11 @@
         kept_ref[i, 4] = pmat
         kept_ref[i, 6] = wkk
         kept_ref[i, 7] = weight
+    solved = inverse_all(mixes)
     ready(2)
     raw_v = dot(x, wv_ref[...])
     ready(3, 4)
     grad_o = dot(go_ref[...], wo_ref[...], NT)
-    solved = inverse_all(mixes)
     for i in heads:
         k, q, beta, carried = ks[i], qs[i], betas[i], carries[i]
         kept_ref[i, 5] = solved[i]
@@ -365,10 +368,12 @@
     else:
         for d in range(SIDES):
             total_ref[d] = project(d)
-    lower = jnp.where(strict, 1.0, 0.0)
     eye = jnp.where(ti == si, 1.0, 0.0)
-    turn = (((0,), (1,)), ((), ()))
-    decays = exact(cterm, upper, turn) + exact(fterm, lower, turn) + exact(eterm, eye, turn)
+    terms = jnp.concatenate([cterm, fterm, eterm], axis=0)
+    top = terms.astype(BF16)
+    middle, bottom = halves(terms - top.astype(F32))
+    sums = dot(jnp.concatenate([top, middle, bottom], axis=1), jnp.concatenate([jnp.where(ti >= si, 1.0, 0.0), jnp.where(si > ti, 1.0, 0.0), eye], axis=0).astype(BF16), TN)
+    decays = sums[:8] + sums[8:16] + sums[16:]
     gd_ref[...] = gd_before_ref[...] + decays if chained else decays
 
 

time: 79.4 us -> 76.6 us (0.965)
  Pallas kernels: 31.6 us -> 28.7 us
    pallas_call x1, Pallas kernels: 7.83 us -> 6.21 us  [run_keep(): pl.pallas_call(keep_kernel, in_specs=[SMEM] + [VMEM] * 8 + [HBM] * 2, out...]
    pallas_call x2, Pallas kernels: 12 us -> 11 us  [run_backward(): pl.pallas_call(partial(second_kernel, bool(before)), in_specs=[SMEM] * 2...]
  transfers between devices with their start and end apart: 13 -> 13, of which waited for: 7 -> 7; matrix products, arithmetic and copies ran while one was open for 0% -> 0% of each run, Pallas kernels for 18% -> 16%
where the time goes in v7:
time: 76.6 us; the launch traced here: 76.4 us
  Pallas kernels  28.7 us (37%)
  waiting for transfers between devices  23.6 us (31%)
  starting transfers between devices  22.7 us (30%)
    ppermute x6, waiting for transfers between devices, along_x(): got[d] = lax.ppermute(parts[d], 'ctx', moves)  12.8 us
    pallas_call x2, Pallas kernels, run_backward(): pl.pallas_call(partial(second_kernel, bool(before)), in_specs=[SMEM] * 2...  11 us
    ppermute x6, starting transfers between devices, along_x(): got[d] = lax.ppermute(parts[d], 'ctx', moves)  9.33 us
    ppermute x3, waiting for transfers between devices, per_device(): lax.ppermute(chunk, 'head', [(j, (j + d) % SIDES) for j in range(SIDES)])  9.15 us
    pallas_call x1, Pallas kernels, run_give(): pl.pallas_call(give_kernel, in_specs=[SMEM] * 2 + [HBM] * 9, out_specs=[V...  8.69 us
    pallas_call x1, Pallas kernels, run_keep(): pl.pallas_call(keep_kernel, in_specs=[SMEM] + [VMEM] * 8 + [HBM] * 2, out...  6.21 us
    ppermute x3, starting transfers between devices, per_device(): lax.ppermute(chunk, 'head', [(j, (j + d) % SIDES) for j in range(SIDES)])  5.59 us
    ppermute x1, starting transfers between devices, per_device(): other_back = lax.ppermute(give_back, 'ctx', pair)  2.37 us
  transfers between devices with their start and end apart: 13, of which 7 were waited for; matrix products, arithmetic and copies ran while one was open for 0% of the time, Pallas kernels for 16%

profile of v7, /device:TPU:1, one launch (start us, length us, event | category | flops | bytes accessed | tf_op | source)
XLA Modules:
  0.0 76.4 jit_solution(11650161694394678693)
XLA Ops:
  0.6 8.7 %block_forward_give.1 = (f32[4,3,128,128]{3,2,1,0:T(8,128)S(1)}, f32[4,11,128,128]{3,2,1,0:T(8,128)S(1)}, bf16[128,2048]{1,0:T(8,128)(2,1)S(1)}, bf16[128,2048]{...) custom-call(s32[1]{0:T(128)} %bitcast.1.place_ref.refs_0_, ...), custom_call_target="tpu_custom_call" | custom-call | tf_op jit(solution)/shard_map/block_forward_give/pallas_call | solution.py:403
  9.3 1.5 %collective-permute-start = (f32[4,3,128,128]{3,2,1,0:T(8,128)S(1)}, f32[4,3,128,128]{3,2,1,0:T(8,128)S(1)}, u32[]{:S(2)}, u32[]{:S(2)}) collective-permute-start(f32[4,3,128,128]{3,2,1,0:T(8,128)S(1)} %get-tuple-element.47), channel_id=1, source_target_pairs={{0,4},{4,0},{8,12},{12,8},{16,20},{20,16},{24,28},{28,24},{32,36},... | collective-permute-start | bytes 2359304 | tf_op jit(solution)/shard_map/ppermute | solution.py:471
  10.8 6.2 %block_forward_keep.1 = (f32[4,3,128,128]{3,2,1,0:T(8,128)S(1)}, f32[4,11,128,128]{3,2,1,0:T(8,128)S(1)}, bf16[2048,512]{1,0:T(8,128)(2,1)S(1)}) custom-call(s32[1]{0:T(128)} %bitcast.1.place_ref.refs_0_, bf16[128,2048]{1,0:T(8,128)(2,1)S(1)} %get-tuple-element.38.x_ref, bf16[128,2048]{1,0:T(8,128)(2,1)S(1)} %get-tuple-element.39.go_ref, ...), custom_call_target="tpu_custom_call" | custom-call | tf_op jit(solution)/shard_map/block_forward_keep/pallas_call | solution.py:420
  17.6 1.5 %collective-permute-start.1 = (f32[3,128,128]{2,1,0:T(8,128)S(1)}, f32[3,128,128]{2,1,0:T(8,128)S(1)}, u32[]{:S(2)}, u32[]{:S(2)}) collective-permute-start(f32[3,128,128]{2,1,0:T(8,128)S(1)} %get-tuple-element.49), channel_id=1, source_target_pairs={{0,8},{4,12},{8,16},{12,20},{16,24},{20,28},{24,0},{28,4},{32,40},... | collective-permute-start | bytes 589832 | tf_op jit(solution)/shard_map/ppermute | solution.py:490
  19.2 2.4 %collective-permute-start.2 = (f32[3,128,128]{2,1,0:T(8,128)S(1)}, f32[3,128,128]{2,1,0:T(8,128)S(1)}, u32[]{:S(2)}, u32[]{:S(2)}) collective-permute-start(f32[3,128,128]{2,1,0:T(8,128)S(1)} %get-tuple-element.50), channel_id=1, source_target_pairs={{0,16},{4,20},{8,24},{12,28},{16,0},{20,4},{24,8},{28,12},{32,48},... | collective-permute-start | bytes 589832 | tf_op jit(solution)/shard_map/ppermute | solution.py:490
  21.6 1.2 %collective-permute-start.3 = (f32[3,128,128]{2,1,0:T(8,128)S(1)}, f32[3,128,128]{2,1,0:T(8,128)S(1)}, u32[]{:S(2)}, u32[]{:S(2)}) collective-permute-start(f32[3,128,128]{2,1,0:T(8,128)S(1)} %get-tuple-element.51), channel_id=1, source_target_pairs={{0,24},{4,28},{8,0},{12,4},{16,8},{20,12},{24,16},{28,20},{32,56},... | collective-permute-start | bytes 589832 | tf_op jit(solution)/shard_map/ppermute | solution.py:490
  22.8 2.8 %collective-permute-done.1.refs_1_ = f32[3,128,128]{2,1,0:T(8,128)S(1)} collective-permute-done((f32[3,128,128]{2,1,0:T(8,128)S(1)}, f32[3,128,128]{2,1,0:T(8,128)S(1)}, u32[]{:S(2)}, u32[]{:S(2)}) %collective-permute-start.1) | collective-permute-done | bytes 196640 | tf_op jit(solution)/shard_map/ppermute | solution.py:490
  25.6 5.3 %collective-permute-done.2.refs_2_ = f32[3,128,128]{2,1,0:T(8,128)S(1)} collective-permute-done((f32[3,128,128]{2,1,0:T(8,128)S(1)}, f32[3,128,128]{2,1,0:T(8,128)S(1)}, u32[]{:S(2)}, u32[]{:S(2)}) %collective-permute-start.2) | collective-permute-done | bytes 196640 | tf_op jit(solution)/shard_map/ppermute | solution.py:490
  31.5 1.7 %collective-permute-start.4 = (f32[128,128]{1,0:T(8,128)S(1)}, f32[128,128]{1,0:T(8,128)S(1)}, u32[]{:S(2)}, u32[]{:S(2)}) collective-permute-start(f32[128,128]{1,0:T(8,128)S(1)} %get-tuple-element.53), channel_id=1, source_target_pairs={{0,32},{4,36},{8,40},{12,44},{16,48},{20,52},{24,56},{28,60},{32,6... | collective-permute-start | bytes 196616 | tf_op jit(solution)/shard_map/ppermute | solution.py:497
  33.2 2.2 %collective-permute-start.5 = (f32[128,128]{1,0:T(8,128)S(1)}, f32[128,128]{1,0:T(8,128)S(1)}, u32[]{:S(2)}, u32[]{:S(2)}) collective-permute-start(f32[128,128]{1,0:T(8,128)S(1)} %get-tuple-element.54), channel_id=1, source_target_pairs={{32,0},{36,4},{40,8},{44,12},{48,16},{52,20},{56,24},{60,28},{64,3... | collective-permute-start | bytes 196616 | tf_op jit(solution)/shard_map/ppermute | solution.py:498
  35.4 1.6 %collective-permute-done.4.s_ref = f32[128,128]{1,0:T(8,128)S(1)} collective-permute-done((f32[128,128]{1,0:T(8,128)S(1)}, f32[128,128]{1,0:T(8,128)S(1)}, u32[]{:S(2)}, u32[]{:S(2)}) %collective-permute-start.4) | collective-permute-done | bytes 65568 | tf_op jit(solution)/shard_map/ppermute | solution.py:497
  37.6 0.7 collective-permute-start.6
  38.3 3.2 %collective-permute-start.7 = (f32[2,128,128]{2,1,0:T(8,128)S(1)}, f32[2,128,128]{2,1,0:T(8,128)S(1)}, u32[]{:S(2)}, u32[]{:S(2)}) collective-permute-start(f32[2,128,128]{2,1,0:T(8,128)S(1)} %get-tuple-element.57), channel_id=1, source_target_pairs={{0,16},{4,20},{8,24},{12,28},{16,0},{20,4},{24,8},{28,12},{32,48},... | collective-permute-start | bytes 393224 | tf_op jit(solution)/shard_map/ppermute | solution.py:490
  41.8 0.9 %collective-permute-done.6.refs_1_ = f32[2,128,128]{2,1,0:T(8,128)S(1)} collective-permute-done((f32[2,128,128]{2,1,0:T(8,128)S(1)}, f32[2,128,128]{2,1,0:T(8,128)S(1)}, u32[]{:S(2)}, u32[]{:S(2)}) %collective-permute-start.6) | collective-permute-done | bytes 131104 | tf_op jit(solution)/shard_map/ppermute | solution.py:490
  42.7 3.8 %collective-permute-done.7.refs_2_ = f32[2,128,128]{2,1,0:T(8,128)S(1)} collective-permute-done((f32[2,128,128]{2,1,0:T(8,128)S(1)}, f32[2,128,128]{2,1,0:T(8,128)S(1)}, u32[]{:S(2)}, u32[]{:S(2)}) %collective-permute-start.7) | collective-permute-done | bytes 131104 | tf_op jit(solution)/shard_map/ppermute | solution.py:490
  46.9 2.4 %collective-permute-start.9 = (f32[4,2,128,128]{3,2,1,0:T(8,128)S(1)}, f32[4,2,128,128]{3,2,1,0:T(8,128)S(1)}, u32[]{:S(2)}, u32[]{:S(2)}) collective-permute-start(f32[4,2,128,128]{3,2,1,0:T(8,128)S(1)} %get-tuple-element.59), channel_id=1, source_target_pairs={{0,4},{4,0},{8,12},{12,8},{16,20},{20,16},{24,28},{28,24},{32,36},... | collective-permute-start | bytes 1572872 | tf_op jit(solution)/shard_map/ppermute | solution.py:505
  49.3 5.5 %block_backward.2 = (f32[4,128,512]{2,1,0:T(8,128)S(1)}, f32[8,128]{1,0:T(8,128)S(1)}) custom-call(s32[1]{0:T(128)} %bitcast.1.place_ref.refs_0_, s32[1]{0:T(128)} %bitcast.side_ref.refs_1_, f32[4,2,128,128]{3,2,1,0:T(8,128)S(1)} %get-tuple-element.63.refs_2_, f32[4,11,128,128]{3,2,1,0:T(8,128)S(1)} %get-tuple-element.64.refs_3_, ...), custom_call_target="tpu_custom_call" | custom-call | tf_op jit(solution)/shard_map/block_backward/pallas_call | solution.py:439
  54.8 5.5 %block_backward.3 = (f32[128,512]{1,0:T(8,128)S(1)}, f32[128,512]{1,0:T(8,128)S(1)}, f32[128,512]{1,0:T(8,128)S(1)}, f32[8,128]{1,0:T(8,128)}, bf16[128,1536]{1,...) custom-call(s32[1]{0:T(128)} %bitcast.1.place_ref.refs_0_, s32[1]{0:T(128)} %bitcast.side_ref.refs_1_, ...), custom_call_target="tpu_custom_call" | custom-call | tf_op jit(solution)/shard_map/block_backward/pallas_call | solution.py:439
  60.3 2.9 %collective-permute-start.10 = (f32[128,512]{1,0:T(8,128)S(1)}, f32[128,512]{1,0:T(8,128)S(1)}, u32[]{:S(2)}, u32[]{:S(2)}) collective-permute-start(f32[128,512]{1,0:T(8,128)S(1)} %get-tuple-element.70), channel_id=1, source_target_pairs={{0,2},{1,3},{2,0},{3,1},{4,6},{5,7},{6,4},{7,5},{8,10},{9,11},{10,... | collective-permute-start | bytes 786440 | tf_op jit(solution)/shard_map/ppermute | solution.py:510
  63.6 2.3 %collective-permute-start.12 = (f32[128,512]{1,0:T(8,128)S(1)}, f32[128,512]{1,0:T(8,128)S(1)}, u32[]{:S(2)}, u32[]{:S(2)}) collective-permute-start(f32[128,512]{1,0:T(8,128)S(1)} %get-tuple-element.72), channel_id=1, source_target_pairs={{0,3},{1,0},{2,1},{3,2},{4,7},{5,4},{6,5},{7,6},{8,11},{9,8},{10,9... | collective-permute-start | bytes 786440 | tf_op jit(solution)/shard_map/ppermute | solution.py:510
  65.9 0.7 own_chunk.1
  66.6 3.2 %collective-permute-done.10 = f32[128,512]{1,0:T(8,128)S(1)} collective-permute-done((f32[128,512]{1,0:T(8,128)S(1)}, f32[128,512]{1,0:T(8,128)S(1)}, u32[]{:S(2)}, u32[]{:S(2)}) %collective-permute-start.10) | collective-permute-done | bytes 262176 | tf_op jit(solution)/shard_map/ppermute | solution.py:510
  69.8 5.9 %collective-permute-done.11 = f32[128,512]{1,0:T(8,128)S(1)} collective-permute-done((f32[128,512]{1,0:T(8,128)S(1)}, f32[128,512]{1,0:T(8,128)S(1)}, u32[]{:S(2)}, u32[]{:S(2)}) %collective-permute-start.11) | collective-permute-done | bytes 262176 | tf_op jit(solution)/shard_map/ppermute | solution.py:510
  75.7 0.7 add_convert_fusion
  (14 shorter events, 2.9 us)
Async XLA Ops:
  9.3 7.7 %collective-permute-start = (f32[4,3,128,128]{3,2,1,0:T(8,128)S(1)}, f32[4,3,128,128]{3,2,1,0:T(8,128)S(1)}, u32[]{:S(2)}, u32[]{:S(2)}) collective-permute-start(f32[4,3,128,128]{3,2,1,0:T(8,128)S(1)} %get-tuple-element.47), channel_id=1, source_target_pairs={{0,4},{4,0},{8,12},{12,8},{16,20},{20,16},{24,28},{28,24},{32,36},... | collective-permute-start | bytes 2359304 | tf_op jit(solution)/shard_map/ppermute | solution.py:471
  17.1 32.2 %copy-start = (bf16[2048,8]{0,1:T(8,128)(2,1)S(1)}, bf16[2048,8]{0,1:T(8,128)(2,1)}, u32[]{:S(2)}) copy-start(bf16[2048,8]{0,1:T(8,128)(2,1)} %param.14) | copy-start | bytes 98308
  17.6 8.0 %collective-permute-start.1 = (f32[3,128,128]{2,1,0:T(8,128)S(1)}, f32[3,128,128]{2,1,0:T(8,128)S(1)}, u32[]{:S(2)}, u32[]{:S(2)}) collective-permute-start(f32[3,128,128]{2,1,0:T(8,128)S(1)} %get-tuple-element.49), channel_id=1, source_target_pairs={{0,8},{4,12},{8,16},{12,20},{16,24},{20,28},{24,0},{28,4},{32,40},... | collective-permute-start | bytes 589832 | tf_op jit(solution)/shard_map/ppermute | solution.py:490
  19.2 11.7 %collective-permute-start.2 = (f32[3,128,128]{2,1,0:T(8,128)S(1)}, f32[3,128,128]{2,1,0:T(8,128)S(1)}, u32[]{:S(2)}, u32[]{:S(2)}) collective-permute-start(f32[3,128,128]{2,1,0:T(8,128)S(1)} %get-tuple-element.50), channel_id=1, source_target_pairs={{0,16},{4,20},{8,24},{12,28},{16,0},{20,4},{24,8},{28,12},{32,48},... | collective-permute-start | bytes 589832 | tf_op jit(solution)/shard_map/ppermute | solution.py:490
  21.6 9.3 %collective-permute-start.3 = (f32[3,128,128]{2,1,0:T(8,128)S(1)}, f32[3,128,128]{2,1,0:T(8,128)S(1)}, u32[]{:S(2)}, u32[]{:S(2)}) collective-permute-start(f32[3,128,128]{2,1,0:T(8,128)S(1)} %get-tuple-element.51), channel_id=1, source_target_pairs={{0,24},{4,28},{8,0},{12,4},{16,8},{20,12},{24,16},{28,20},{32,56},... | collective-permute-start | bytes 589832 | tf_op jit(solution)/shard_map/ppermute | solution.py:490
  31.5 5.5 %collective-permute-start.4 = (f32[128,128]{1,0:T(8,128)S(1)}, f32[128,128]{1,0:T(8,128)S(1)}, u32[]{:S(2)}, u32[]{:S(2)}) collective-permute-start(f32[128,128]{1,0:T(8,128)S(1)} %get-tuple-element.53), channel_id=1, source_target_pairs={{0,32},{4,36},{8,40},{12,44},{16,48},{20,52},{24,56},{28,60},{32,6... | collective-permute-start | bytes 196616 | tf_op jit(solution)/shard_map/ppermute | solution.py:497
  33.2 3.8 %collective-permute-start.5 = (f32[128,128]{1,0:T(8,128)S(1)}, f32[128,128]{1,0:T(8,128)S(1)}, u32[]{:S(2)}, u32[]{:S(2)}) collective-permute-start(f32[128,128]{1,0:T(8,128)S(1)} %get-tuple-element.54), channel_id=1, source_target_pairs={{32,0},{36,4},{40,8},{44,12},{48,16},{52,20},{56,24},{60,28},{64,3... | collective-permute-start | bytes 196616 | tf_op jit(solution)/shard_map/ppermute | solution.py:498
  37.6 5.1 %collective-permute-start.6 = (f32[2,128,128]{2,1,0:T(8,128)S(1)}, f32[2,128,128]{2,1,0:T(8,128)S(1)}, u32[]{:S(2)}, u32[]{:S(2)}) collective-permute-start(f32[2,128,128]{2,1,0:T(8,128)S(1)} %get-tuple-element.56), channel_id=1, source_target_pairs={{0,8},{4,12},{8,16},{12,20},{16,24},{20,28},{24,0},{28,4},{32,40},... | collective-permute-start | bytes 393224 | tf_op jit(solution)/shard_map/ppermute | solution.py:490
  38.3 8.2 %collective-permute-start.7 = (f32[2,128,128]{2,1,0:T(8,128)S(1)}, f32[2,128,128]{2,1,0:T(8,128)S(1)}, u32[]{:S(2)}, u32[]{:S(2)}) collective-permute-start(f32[2,128,128]{2,1,0:T(8,128)S(1)} %get-tuple-element.57), channel_id=1, source_target_pairs={{0,16},{4,20},{8,24},{12,28},{16,0},{20,4},{24,8},{28,12},{32,48},... | collective-permute-start | bytes 393224 | tf_op jit(solution)/shard_map/ppermute | solution.py:490
  41.5 5.0 %collective-permute-start.8 = (f32[2,128,128]{2,1,0:T(8,128)S(1)}, f32[2,128,128]{2,1,0:T(8,128)S(1)}, u32[]{:S(2)}, u32[]{:S(2)}) collective-permute-start(f32[2,128,128]{2,1,0:T(8,128)S(1)} %get-tuple-element.58), channel_id=1, source_target_pairs={{0,24},{4,28},{8,0},{12,4},{16,8},{20,12},{24,16},{28,20},{32,56},... | collective-permute-start | bytes 393224 | tf_op jit(solution)/shard_map/ppermute | solution.py:490
  46.9 7.8 %collective-permute-start.9 = (f32[4,2,128,128]{3,2,1,0:T(8,128)S(1)}, f32[4,2,128,128]{3,2,1,0:T(8,128)S(1)}, u32[]{:S(2)}, u32[]{:S(2)}) collective-permute-start(f32[4,2,128,128]{3,2,1,0:T(8,128)S(1)} %get-tuple-element.59), channel_id=1, source_target_pairs={{0,4},{4,0},{8,12},{12,8},{16,20},{20,16},{24,28},{28,24},{32,36},... | collective-permute-start | bytes 1572872 | tf_op jit(solution)/shard_map/ppermute | solution.py:505
  60.3 9.5 %collective-permute-start.10 = (f32[128,512]{1,0:T(8,128)S(1)}, f32[128,512]{1,0:T(8,128)S(1)}, u32[]{:S(2)}, u32[]{:S(2)}) collective-permute-start(f32[128,512]{1,0:T(8,128)S(1)} %get-tuple-element.70), channel_id=1, source_target_pairs={{0,2},{1,3},{2,0},{3,1},{4,6},{5,7},{6,4},{7,5},{8,10},{9,11},{10,... | collective-permute-start | bytes 786440 | tf_op jit(solution)/shard_map/ppermute | solution.py:510
  63.2 12.5 %collective-permute-start.11 = (f32[128,512]{1,0:T(8,128)S(1)}, f32[128,512]{1,0:T(8,128)S(1)}, u32[]{:S(2)}, u32[]{:S(2)}) collective-permute-start(f32[128,512]{1,0:T(8,128)S(1)} %get-tuple-element.71), channel_id=1, source_target_pairs={{0,1},{1,2},{2,3},{3,0},{4,5},{5,6},{6,7},{7,4},{8,9},{9,10},{10,1... | collective-permute-start | bytes 786440 | tf_op jit(solution)/shard_map/ppermute | solution.py:510
  63.6 12.1 %collective-permute-start.12 = (f32[128,512]{1,0:T(8,128)S(1)}, f32[128,512]{1,0:T(8,128)S(1)}, u32[]{:S(2)}, u32[]{:S(2)}) collective-permute-start(f32[128,512]{1,0:T(8,128)S(1)} %get-tuple-element.72), channel_id=1, source_target_pairs={{0,3},{1,0},{2,1},{3,2},{4,7},{5,4},{6,5},{7,6},{8,11},{9,8},{10,9... | collective-permute-start | bytes 786440 | tf_op jit(solution)/shard_map/ppermute | solution.py:510

commit v8 on v7

--- a/solution.py
+++ b/solution.py
@@ -293,9 +293,21 @@
     out_ref[...] = before_ref[0] + piece
 
 
+def early_kernel(kept_ref, out_ref):
+    heads = range(GROUP)
+    k, do, uv = ([kept_ref[i, j] for i in heads] for j in (0, 3, 8))
+    ends = [kept_ref[i, 10][:, 2:3] * k[i] for i in heads]
+    inner = [mm3(kept_ref[i, 4], do[i], TN) for i in heads]
+    both = [mm3(kept_ref[i, 5], jnp.concatenate([inner[i], ends[i]], axis=1), TN) for i in heads]
+    for i in heads:
+        out_ref[i, 0] = both[i][:, :W]
+        out_ref[i, 1] = both[i][:, W:]
+        out_ref[i, 2] = mm3(do[i], uv[i], NT)
+
+
 def second_kernel(chained, *refs):
-    place_ref, side_ref, back_ref, kept_ref, wb_ref, wkq_ref, wv_ref = refs[:7]
-    refs = refs[7:]
+    place_ref, side_ref, back_ref, kept_ref, early_ref, wb_ref, wkq_ref, wv_ref = refs[:8]
+    refs = refs[8:]
     if chained:
         before_ref, gd_before_ref, *total_refs, gd_ref, grads_ref, db_ref = refs
         wide = total_refs[0].shape[-1]
@@ -319,15 +331,14 @@
         pmat, wkk, weight = kept_ref[i, 4], kept_ref[i, 6], kept_ref[i, 7]
         col = kept_ref[i, 10]
         beta, carried, closing, inv_k, inv_q = (col[:, j:j + 1] for j in range(5))
-        u = kept_ref[i, 8] - mm3(kept_ref[i, 9], s0, NT)
-        du = mm3(pmat, do, TN) + mm3(closing * k, g1, NT)
-        dr = mm3(kept_ref[i, 5], du, TN)
-        dpa = mm3(jnp.concatenate([do, dr], axis=0), u, NT)
-        dp = dpa[:W]
-        da = -dpa[W:]
-        ds = mm3(jnp.concatenate([carried * do, dr], axis=0), s0)
-        dq_state = ds[:W]
+        kw = kept_ref[i, 9]
+        u = kept_ref[i, 8] - mm3(kw, s0, NT)
+        dr = early_ref[i, 0] + mm3(early_ref[i, 1], g1, NT)
+        ds = mm3(jnp.concatenate([do, dr], axis=0), s0)
+        dq_state = carried * ds[:W]
         dr_s = carried * ds[W:]
+        dp = early_ref[i, 2] - mm3(ds[:W], kw, NT)
+        da = -mm3(dr, u, NT)
         ug = closing * mm3(u, g1)
         dqk = weight * dp
         dkk = jnp.where(strict, weight, 0.0) * da * beta
@@ -429,7 +440,7 @@
     return out
 
 
-def run_backward(place, side, back, kept, beta_t, w_both, w_value, before):
+def run_backward(place, side, back, kept, early, beta_t, w_both, w_value, before):
     heads, width = beta_t.shape
     wide = width // SIDES
     if before:
@@ -438,12 +449,12 @@
         out_shape = [shape(SIDES, W, wide), shape(heads, W)]
     return pl.pallas_call(
         partial(second_kernel, bool(before)),
-        in_specs=[SMEM] * 2 + [VMEM] * 5 + [VMEM] * len(before),
+        in_specs=[SMEM] * 2 + [VMEM] * 6 + [VMEM] * len(before),
         out_specs=[VMEM] * len(out_shape),
         out_shape=out_shape,
         compiler_params=pltpu.CompilerParams(vmem_limit_bytes=24 << 20),
         name="block_backward",
-    )(place, side, back, kept, beta_t, w_both, w_value, *before)
+    )(place, side, back, kept, early, beta_t, w_both, w_value, *before)
 
 
 def run_chunk(side, grads, db, before, beta_t, w_both, w_value):
@@ -490,9 +501,18 @@
             got[d] = lax.ppermute(parts[d], "ctx", moves)
         return [got[d] for d in range(GROUP)]
 
+    def early(kept):
+        return pl.pallas_call(
+            early_kernel, in_specs=[VMEM], out_specs=VMEM, out_shape=shape(GROUP, 3, W, W), name="early",
+            compiler_params=pltpu.CompilerParams(vmem_limit_bytes=12 << 20),
+            cost_estimate=pl.CostEstimate(flops=1 << 30, bytes_accessed=4 << 20, transcendentals=0),
+        )(kept)
+
     whole = call(join_kernel, "chip_join", (place,), (own, other), [shape(3, W, W)] * GROUP)
+    *whole, give_kept, own_kept = lax.optimization_barrier((*whole, give_kept, own_kept))
+    *arrived, own_early, give_early = lax.optimization_barrier((*along_x(whole), early(own_kept), early(give_kept)))
     mine, state, grad = call(
-        row_kernel, "row_ends", (place,), along_x(whole), [shape(GROUP, 3, W, W), shape(W, W), shape(W, W)]
+        row_kernel, "row_ends", (place,), arrived, [shape(GROUP, 3, W, W), shape(W, W), shape(W, W)]
     )
     state = lax.ppermute(state, "ctx", [(j, (j + row) % size) for j in range(size)])
     grad = lax.ppermute(grad, "ctx", [((j + row) % size, j) for j in range(size)])
@@ -503,8 +523,8 @@
         part_kernel, "chip_part", (place,), (own, other, *along_x(spread)), [shape(GROUP, 2, W, W)] * 2
     )
     other_back = lax.ppermute(give_back, "ctx", pair)
-    before = run_backward(place, side, own_back, own_kept, beta_t, keep_w, keep_v, ())
-    *chunks, grad_d, grads, db = run_backward(place, side, other_back, give_kept, beta_t, *give_w, before)
+    before = run_backward(place, side, own_back, own_kept, own_early, beta_t, keep_w, keep_v, ())
+    *chunks, grad_d, grads, db = run_backward(place, side, other_back, give_kept, give_early, beta_t, *give_w, before)
     total = run_chunk(side, grads, db, before[0], beta_t, *give_w)
     for d, chunk in zip(ORDER, chunks):
         total = total + lax.ppermute(chunk, "head", [(j, (j + d) % SIDES) for j in range(SIDES)])

time: 76.6 us -> 76.6 us (level)
  waiting for transfers between devices: 23.6 us -> 22.2 us
  Pallas kernels: 28.7 us -> 29.9 us
    ppermute x6, waiting for transfers between devices: 12.8 us -> 11.4 us  [along_x(): got[d] = lax.ppermute(parts[d], 'ctx', moves)]
    pallas_call x0 -> x2, Pallas kernels: none -> 1.37 us  [early(): pl.pallas_call(early_kernel, in_specs=[VMEM], out_specs=VMEM, out_shape=s...]
  transfers between devices with their start and end apart: 13 -> 13, of which waited for: 7 -> 7; matrix products, arithmetic and copies ran while one was open for 0% -> 0% of each run, Pallas kernels for 16% -> 18%
where the time goes in v8:
time: 76.6 us; the launch traced here: 76.5 us
  Pallas kernels  29.9 us (39%)
  starting transfers between devices  22.9 us (30%)
  waiting for transfers between devices  22.2 us (29%)
    ppermute x6, waiting for transfers between devices, along_x(): got[d] = lax.ppermute(parts[d], 'ctx', moves)  11.4 us
    pallas_call x2, Pallas kernels, run_backward(): pl.pallas_call(partial(second_kernel, bool(before)), in_specs=[SMEM] * 2...  10.9 us
    ppermute x6, starting transfers between devices, along_x(): got[d] = lax.ppermute(parts[d], 'ctx', moves)  9.34 us
    ppermute x3, waiting for transfers between devices, per_device(): lax.ppermute(chunk, 'head', [(j, (j + d) % SIDES) for j in range(SIDES)])  9.14 us
    pallas_call x1, Pallas kernels, run_give(): pl.pallas_call(give_kernel, in_specs=[SMEM] * 2 + [HBM] * 9, out_specs=[V...  8.7 us
    pallas_call x1, Pallas kernels, run_keep(): pl.pallas_call(keep_kernel, in_specs=[SMEM] + [VMEM] * 8 + [HBM] * 2, out...  6.22 us
    ppermute x3, starting transfers between devices, per_device(): lax.ppermute(chunk, 'head', [(j, (j + d) % SIDES) for j in range(SIDES)])  5.58 us
    ppermute x1, starting transfers between devices, per_device(): other_back = lax.ppermute(give_back, 'ctx', pair)  2.59 us
  transfers between devices with their start and end apart: 13, of which 7 were waited for; matrix products, arithmetic and copies ran while one was open for 0% of the time, Pallas kernels for 18%

profile of v8, /device:TPU:1, one launch (start us, length us, event | category | flops | bytes accessed | tf_op | source)
XLA Modules:
  0.0 76.5 jit_solution(12931108551982175024)
XLA Ops:
  0.6 8.7 %block_forward_give.1 = (f32[4,3,128,128]{3,2,1,0:T(8,128)S(1)}, f32[4,11,128,128]{3,2,1,0:T(8,128)S(1)}, bf16[128,2048]{1,0:T(8,128)(2,1)S(1)}, bf16[128,2048]{...) custom-call(s32[1]{0:T(128)} %bitcast.1.place_ref.refs_0_, ...), custom_call_target="tpu_custom_call" | custom-call | tf_op jit(solution)/shard_map/block_forward_give/pallas_call | solution.py:414
  9.3 1.5 %collective-permute-start = (f32[4,3,128,128]{3,2,1,0:T(8,128)S(1)}, f32[4,3,128,128]{3,2,1,0:T(8,128)S(1)}, u32[]{:S(2)}, u32[]{:S(2)}) collective-permute-start(f32[4,3,128,128]{3,2,1,0:T(8,128)S(1)} %get-tuple-element.59), channel_id=1, source_target_pairs={{0,4},{4,0},{8,12},{12,8},{16,20},{20,16},{24,28},{28,24},{32,36},... | collective-permute-start | bytes 2359304 | tf_op jit(solution)/shard_map/ppermute | solution.py:482
  10.9 6.2 %block_forward_keep.1 = (f32[4,3,128,128]{3,2,1,0:T(8,128)S(1)}, f32[4,11,128,128]{3,2,1,0:T(8,128)S(1)}, bf16[2048,512]{1,0:T(8,128)(2,1)S(1)}) custom-call(s32[1]{0:T(128)} %bitcast.1.place_ref.refs_0_, bf16[128,2048]{1,0:T(8,128)(2,1)S(1)} %get-tuple-element.50.x_ref, bf16[128,2048]{1,0:T(8,128)(2,1)S(1)} %get-tuple-element.51.go_ref, ...), custom_call_target="tpu_custom_call" | custom-call | tf_op jit(solution)/shard_map/block_forward_keep/pallas_call | solution.py:431
  17.6 1.5 %collective-permute-start.1 = (f32[3,128,128]{2,1,0:T(8,128)S(1)}, f32[3,128,128]{2,1,0:T(8,128)S(1)}, u32[]{:S(2)}, u32[]{:S(2)}) collective-permute-start(f32[3,128,128]{2,1,0:T(8,128)S(1)} %get-tuple-element.67), channel_id=1, source_target_pairs={{0,8},{4,12},{8,16},{12,20},{16,24},{20,28},{24,0},{28,4},{32,40},... | collective-permute-start | bytes 589832 | tf_op jit(solution)/shard_map/ppermute | solution.py:501
  19.2 2.4 %collective-permute-start.2 = (f32[3,128,128]{2,1,0:T(8,128)S(1)}, f32[3,128,128]{2,1,0:T(8,128)S(1)}, u32[]{:S(2)}, u32[]{:S(2)}) collective-permute-start(f32[3,128,128]{2,1,0:T(8,128)S(1)} %get-tuple-element.68), channel_id=1, source_target_pairs={{0,16},{4,20},{8,24},{12,28},{16,0},{20,4},{24,8},{28,12},{32,48},... | collective-permute-start | bytes 589832 | tf_op jit(solution)/shard_map/ppermute | solution.py:501
  21.6 1.2 %collective-permute-start.3 = (f32[3,128,128]{2,1,0:T(8,128)S(1)}, f32[3,128,128]{2,1,0:T(8,128)S(1)}, u32[]{:S(2)}, u32[]{:S(2)}) collective-permute-start(f32[3,128,128]{2,1,0:T(8,128)S(1)} %get-tuple-element.69), channel_id=1, source_target_pairs={{0,24},{4,28},{8,0},{12,4},{16,8},{20,12},{24,16},{28,20},{32,56},... | collective-permute-start | bytes 589832 | tf_op jit(solution)/shard_map/ppermute | solution.py:501
  23.5 0.7 early.3.refs_4_
  24.2 1.4 %collective-permute-done.1.refs_1_ = f32[3,128,128]{2,1,0:T(8,128)S(1)} collective-permute-done((f32[3,128,128]{2,1,0:T(8,128)S(1)}, f32[3,128,128]{2,1,0:T(8,128)S(1)}, u32[]{:S(2)}, u32[]{:S(2)}) %collective-permute-start.1) | collective-permute-done | bytes 196640 | tf_op jit(solution)/shard_map/ppermute | solution.py:501
  25.6 5.3 %collective-permute-done.2.refs_2_ = f32[3,128,128]{2,1,0:T(8,128)S(1)} collective-permute-done((f32[3,128,128]{2,1,0:T(8,128)S(1)}, f32[3,128,128]{2,1,0:T(8,128)S(1)}, u32[]{:S(2)}, u32[]{:S(2)}) %collective-permute-start.2) | collective-permute-done | bytes 196640 | tf_op jit(solution)/shard_map/ppermute | solution.py:501
  31.5 1.7 %collective-permute-start.4 = (f32[128,128]{1,0:T(8,128)S(1)}, f32[128,128]{1,0:T(8,128)S(1)}, u32[]{:S(2)}, u32[]{:S(2)}) collective-permute-start(f32[128,128]{1,0:T(8,128)S(1)} %get-tuple-element.77), channel_id=1, source_target_pairs={{0,32},{4,36},{8,40},{12,44},{16,48},{20,52},{24,56},{28,60},{32,6... | collective-permute-start | bytes 196616 | tf_op jit(solution)/shard_map/ppermute | solution.py:517
  33.2 2.2 %collective-permute-start.5 = (f32[128,128]{1,0:T(8,128)S(1)}, f32[128,128]{1,0:T(8,128)S(1)}, u32[]{:S(2)}, u32[]{:S(2)}) collective-permute-start(f32[128,128]{1,0:T(8,128)S(1)} %get-tuple-element.78), channel_id=1, source_target_pairs={{32,0},{36,4},{40,8},{44,12},{48,16},{52,20},{56,24},{60,28},{64,3... | collective-permute-start | bytes 196616 | tf_op jit(solution)/shard_map/ppermute | solution.py:518
  35.4 1.6 %collective-permute-done.4.s_ref = f32[128,128]{1,0:T(8,128)S(1)} collective-permute-done((f32[128,128]{1,0:T(8,128)S(1)}, f32[128,128]{1,0:T(8,128)S(1)}, u32[]{:S(2)}, u32[]{:S(2)}) %collective-permute-start.4) | collective-permute-done | bytes 65568 | tf_op jit(solution)/shard_map/ppermute | solution.py:517
  37.6 0.7 collective-permute-start.6
  38.3 3.2 %collective-permute-start.7 = (f32[2,128,128]{2,1,0:T(8,128)S(1)}, f32[2,128,128]{2,1,0:T(8,128)S(1)}, u32[]{:S(2)}, u32[]{:S(2)}) collective-permute-start(f32[2,128,128]{2,1,0:T(8,128)S(1)} %get-tuple-element.81), channel_id=1, source_target_pairs={{0,16},{4,20},{8,24},{12,28},{16,0},{20,4},{24,8},{28,12},{32,48},... | collective-permute-start | bytes 393224 | tf_op jit(solution)/shard_map/ppermute | solution.py:501
  41.8 0.9 %collective-permute-done.6.refs_1_ = f32[2,128,128]{2,1,0:T(8,128)S(1)} collective-permute-done((f32[2,128,128]{2,1,0:T(8,128)S(1)}, f32[2,128,128]{2,1,0:T(8,128)S(1)}, u32[]{:S(2)}, u32[]{:S(2)}) %collective-permute-start.6) | collective-permute-done | bytes 131104 | tf_op jit(solution)/shard_map/ppermute | solution.py:501
  42.7 3.8 %collective-permute-done.7.refs_2_ = f32[2,128,128]{2,1,0:T(8,128)S(1)} collective-permute-done((f32[2,128,128]{2,1,0:T(8,128)S(1)}, f32[2,128,128]{2,1,0:T(8,128)S(1)}, u32[]{:S(2)}, u32[]{:S(2)}) %collective-permute-start.7) | collective-permute-done | bytes 131104 | tf_op jit(solution)/shard_map/ppermute | solution.py:501
  46.9 2.6 %collective-permute-start.9 = (f32[4,2,128,128]{3,2,1,0:T(8,128)S(1)}, f32[4,2,128,128]{3,2,1,0:T(8,128)S(1)}, u32[]{:S(2)}, u32[]{:S(2)}) collective-permute-start(f32[4,2,128,128]{3,2,1,0:T(8,128)S(1)} %get-tuple-element.83), channel_id=1, source_target_pairs={{0,4},{4,0},{8,12},{12,8},{16,20},{20,16},{24,28},{28,24},{32,36},... | collective-permute-start | bytes 1572872 | tf_op jit(solution)/shard_map/ppermute | solution.py:525
  49.5 5.4 %block_backward.2 = (f32[4,128,512]{2,1,0:T(8,128)S(1)}, f32[8,128]{1,0:T(8,128)S(1)}) custom-call(s32[1]{0:T(128)} %bitcast.1.place_ref.refs_0_, s32[1]{0:T(128)} %bitcast.side_ref.refs_1_, f32[4,2,128,128]{3,2,1,0:T(8,128)S(1)} %get-tuple-element.87.refs_2_, f32[4,11,128,128]{3,2,1,0:T(8,128)S(1)} %get-tuple-element.70.kept_ref.refs_3_, ...), custom_call_target="tpu_custom_call" | custom-call | tf_op jit(solution)/shard_map/block_backward/pallas_call | solution.py:450
  54.9 5.5 %block_backward.3 = (f32[128,512]{1,0:T(8,128)S(1)}, f32[128,512]{1,0:T(8,128)S(1)}, f32[128,512]{1,0:T(8,128)S(1)}, f32[8,128]{1,0:T(8,128)}, bf16[128,1536]{1,...) custom-call(s32[1]{0:T(128)} %bitcast.1.place_ref.refs_0_, s32[1]{0:T(128)} %bitcast.side_ref.refs_1_, ...), custom_call_target="tpu_custom_call" | custom-call | tf_op jit(solution)/shard_map/block_backward/pallas_call | solution.py:450
  60.4 2.9 %collective-permute-start.10 = (f32[128,512]{1,0:T(8,128)S(1)}, f32[128,512]{1,0:T(8,128)S(1)}, u32[]{:S(2)}, u32[]{:S(2)}) collective-permute-start(f32[128,512]{1,0:T(8,128)S(1)} %get-tuple-element.94), channel_id=1, source_target_pairs={{0,2},{1,3},{2,0},{3,1},{4,6},{5,7},{6,4},{7,5},{8,10},{9,11},{10,... | collective-permute-start | bytes 786440 | tf_op jit(solution)/shard_map/ppermute | solution.py:530
  63.7 2.3 %collective-permute-start.12 = (f32[128,512]{1,0:T(8,128)S(1)}, f32[128,512]{1,0:T(8,128)S(1)}, u32[]{:S(2)}, u32[]{:S(2)}) collective-permute-start(f32[128,512]{1,0:T(8,128)S(1)} %get-tuple-element.96), channel_id=1, source_target_pairs={{0,3},{1,0},{2,1},{3,2},{4,7},{5,4},{6,5},{7,6},{8,11},{9,8},{10,9... | collective-permute-start | bytes 786440 | tf_op jit(solution)/shard_map/ppermute | solution.py:530
  66.6 3.2 %collective-permute-done.10 = f32[128,512]{1,0:T(8,128)S(1)} collective-permute-done((f32[128,512]{1,0:T(8,128)S(1)}, f32[128,512]{1,0:T(8,128)S(1)}, u32[]{:S(2)}, u32[]{:S(2)}) %collective-permute-start.10) | collective-permute-done | bytes 262176 | tf_op jit(solution)/shard_map/ppermute | solution.py:530
  69.8 5.9 %collective-permute-done.11 = f32[128,512]{1,0:T(8,128)S(1)} collective-permute-done((f32[128,512]{1,0:T(8,128)S(1)}, f32[128,512]{1,0:T(8,128)S(1)}, u32[]{:S(2)}, u32[]{:S(2)}) %collective-permute-start.11) | collective-permute-done | bytes 262176 | tf_op jit(solution)/shard_map/ppermute | solution.py:530
  75.8 0.7 add_convert_fusion
  (16 shorter events, 4.2 us)
Async XLA Ops:
  9.3 7.7 %collective-permute-start = (f32[4,3,128,128]{3,2,1,0:T(8,128)S(1)}, f32[4,3,128,128]{3,2,1,0:T(8,128)S(1)}, u32[]{:S(2)}, u32[]{:S(2)}) collective-permute-start(f32[4,3,128,128]{3,2,1,0:T(8,128)S(1)} %get-tuple-element.59), channel_id=1, source_target_pairs={{0,4},{4,0},{8,12},{12,8},{16,20},{20,16},{24,28},{28,24},{32,36},... | collective-permute-start | bytes 2359304 | tf_op jit(solution)/shard_map/ppermute | solution.py:482
  17.6 8.0 %collective-permute-start.1 = (f32[3,128,128]{2,1,0:T(8,128)S(1)}, f32[3,128,128]{2,1,0:T(8,128)S(1)}, u32[]{:S(2)}, u32[]{:S(2)}) collective-permute-start(f32[3,128,128]{2,1,0:T(8,128)S(1)} %get-tuple-element.67), channel_id=1, source_target_pairs={{0,8},{4,12},{8,16},{12,20},{16,24},{20,28},{24,0},{28,4},{32,40},... | collective-permute-start | bytes 589832 | tf_op jit(solution)/shard_map/ppermute | solution.py:501
  19.2 11.7 %collective-permute-start.2 = (f32[3,128,128]{2,1,0:T(8,128)S(1)}, f32[3,128,128]{2,1,0:T(8,128)S(1)}, u32[]{:S(2)}, u32[]{:S(2)}) collective-permute-start(f32[3,128,128]{2,1,0:T(8,128)S(1)} %get-tuple-element.68), channel_id=1, source_target_pairs={{0,16},{4,20},{8,24},{12,28},{16,0},{20,4},{24,8},{28,12},{32,48},... | collective-permute-start | bytes 589832 | tf_op jit(solution)/shard_map/ppermute | solution.py:501
  21.6 9.3 %collective-permute-start.3 = (f32[3,128,128]{2,1,0:T(8,128)S(1)}, f32[3,128,128]{2,1,0:T(8,128)S(1)}, u32[]{:S(2)}, u32[]{:S(2)}) collective-permute-start(f32[3,128,128]{2,1,0:T(8,128)S(1)} %get-tuple-element.69), channel_id=1, source_target_pairs={{0,24},{4,28},{8,0},{12,4},{16,8},{20,12},{24,16},{28,20},{32,56},... | collective-permute-start | bytes 589832 | tf_op jit(solution)/shard_map/ppermute | solution.py:501
  23.5 26.0 %copy-start = (bf16[2048,8]{0,1:T(8,128)(2,1)S(1)}, bf16[2048,8]{0,1:T(8,128)(2,1)}, u32[]{:S(2)}) copy-start(bf16[2048,8]{0,1:T(8,128)(2,1)} %param.14) | copy-start | bytes 98308
  31.5 5.5 %collective-permute-start.4 = (f32[128,128]{1,0:T(8,128)S(1)}, f32[128,128]{1,0:T(8,128)S(1)}, u32[]{:S(2)}, u32[]{:S(2)}) collective-permute-start(f32[128,128]{1,0:T(8,128)S(1)} %get-tuple-element.77), channel_id=1, source_target_pairs={{0,32},{4,36},{8,40},{12,44},{16,48},{20,52},{24,56},{28,60},{32,6... | collective-permute-start | bytes 196616 | tf_op jit(solution)/shard_map/ppermute | solution.py:517
  33.2 3.8 %collective-permute-start.5 = (f32[128,128]{1,0:T(8,128)S(1)}, f32[128,128]{1,0:T(8,128)S(1)}, u32[]{:S(2)}, u32[]{:S(2)}) collective-permute-start(f32[128,128]{1,0:T(8,128)S(1)} %get-tuple-element.78), channel_id=1, source_target_pairs={{32,0},{36,4},{40,8},{44,12},{48,16},{52,20},{56,24},{60,28},{64,3... | collective-permute-start | bytes 196616 | tf_op jit(solution)/shard_map/ppermute | solution.py:518
  37.6 5.1 %collective-permute-start.6 = (f32[2,128,128]{2,1,0:T(8,128)S(1)}, f32[2,128,128]{2,1,0:T(8,128)S(1)}, u32[]{:S(2)}, u32[]{:S(2)}) collective-permute-start(f32[2,128,128]{2,1,0:T(8,128)S(1)} %get-tuple-element.80), channel_id=1, source_target_pairs={{0,8},{4,12},{8,16},{12,20},{16,24},{20,28},{24,0},{28,4},{32,40},... | collective-permute-start | bytes 393224 | tf_op jit(solution)/shard_map/ppermute | solution.py:501
  38.3 8.2 %collective-permute-start.7 = (f32[2,128,128]{2,1,0:T(8,128)S(1)}, f32[2,128,128]{2,1,0:T(8,128)S(1)}, u32[]{:S(2)}, u32[]{:S(2)}) collective-permute-start(f32[2,128,128]{2,1,0:T(8,128)S(1)} %get-tuple-element.81), channel_id=1, source_target_pairs={{0,16},{4,20},{8,24},{12,28},{16,0},{20,4},{24,8},{28,12},{32,48},... | collective-permute-start | bytes 393224 | tf_op jit(solution)/shard_map/ppermute | solution.py:501
  41.5 5.0 %collective-permute-start.8 = (f32[2,128,128]{2,1,0:T(8,128)S(1)}, f32[2,128,128]{2,1,0:T(8,128)S(1)}, u32[]{:S(2)}, u32[]{:S(2)}) collective-permute-start(f32[2,128,128]{2,1,0:T(8,128)S(1)} %get-tuple-element.82), channel_id=1, source_target_pairs={{0,24},{4,28},{8,0},{12,4},{16,8},{20,12},{24,16},{28,20},{32,56},... | collective-permute-start | bytes 393224 | tf_op jit(solution)/shard_map/ppermute | solution.py:501
  46.9 8.0 %collective-permute-start.9 = (f32[4,2,128,128]{3,2,1,0:T(8,128)S(1)}, f32[4,2,128,128]{3,2,1,0:T(8,128)S(1)}, u32[]{:S(2)}, u32[]{:S(2)}) collective-permute-start(f32[4,2,128,128]{3,2,1,0:T(8,128)S(1)} %get-tuple-element.83), channel_id=1, source_target_pairs={{0,4},{4,0},{8,12},{12,8},{16,20},{20,16},{24,28},{28,24},{32,36},... | collective-permute-start | bytes 1572872 | tf_op jit(solution)/shard_map/ppermute | solution.py:525
  60.4 9.5 %collective-permute-start.10 = (f32[128,512]{1,0:T(8,128)S(1)}, f32[128,512]{1,0:T(8,128)S(1)}, u32[]{:S(2)}, u32[]{:S(2)}) collective-permute-start(f32[128,512]{1,0:T(8,128)S(1)} %get-tuple-element.94), channel_id=1, source_target_pairs={{0,2},{1,3},{2,0},{3,1},{4,6},{5,7},{6,4},{7,5},{8,10},{9,11},{10,... | collective-permute-start | bytes 786440 | tf_op jit(solution)/shard_map/ppermute | solution.py:530
  63.3 12.5 %collective-permute-start.11 = (f32[128,512]{1,0:T(8,128)S(1)}, f32[128,512]{1,0:T(8,128)S(1)}, u32[]{:S(2)}, u32[]{:S(2)}) collective-permute-start(f32[128,512]{1,0:T(8,128)S(1)} %get-tuple-element.95), channel_id=1, source_target_pairs={{0,1},{1,2},{2,3},{3,0},{4,5},{5,6},{6,7},{7,4},{8,9},{9,10},{10,1... | collective-permute-start | bytes 786440 | tf_op jit(solution)/shard_map/ppermute | solution.py:530
  63.7 12.1 %collective-permute-start.12 = (f32[128,512]{1,0:T(8,128)S(1)}, f32[128,512]{1,0:T(8,128)S(1)}, u32[]{:S(2)}, u32[]{:S(2)}) collective-permute-start(f32[128,512]{1,0:T(8,128)S(1)} %get-tuple-element.96), channel_id=1, source_target_pairs={{0,3},{1,0},{2,1},{3,2},{4,7},{5,4},{6,5},{7,6},{8,11},{9,8},{10,9... | collective-permute-start | bytes 786440 | tf_op jit(solution)/shard_map/ppermute | solution.py:530

commit v9 on v8

--- a/solution.py
+++ b/solution.py
@@ -153,7 +153,7 @@
     raw_k = dot(x, wkq_ref[0])
     ready(1)
     raw_q = dot(x, wkq_ref[1])
-    ks, qs, betas, carries, wkks, mixes, pmats = [], [], [], [], [], [], []
+    ks, qs, betas, carries, closings, mixes, pmats = [], [], [], [], [], [], []
     for i in heads:
         head = head0 + i
         rk = cut(raw_k, i)
@@ -175,11 +175,11 @@
         qs.append(q)
         betas.append(beta)
         carries.append(carried)
-        wkks.append(wkk)
         mixes.append(wkk * beta)
         pmats.append(pmat)
         lanes = si
         closing = jnp.where(final, jnp.exp(jnp.where(final, run[W - 1:W, :] - run, 0.0)), 0.0)
+        closings.append(closing)
         col = jnp.where(lanes == 0, beta, jnp.where(lanes == 1, carried, jnp.where(lanes == 2, closing, jnp.where(lanes == 3, inv_k, inv_q))))
         kept_ref[i, 10] = col
         kept_ref[i, 0] = k
@@ -192,24 +192,25 @@
     raw_v = dot(x, wv_ref[...])
     ready(3, 4)
     grad_o = dot(go_ref[...], wo_ref[...], NT)
+    vs = [cut(raw_v, i) for i in heads]
+    dos = [cut(grad_o, i) for i in heads]
+    rights = [jnp.concatenate([betas[i] * vs[i], (betas[i] * carries[i]) * ks[i]], axis=1) for i in heads]
+    boths = [mm3(solved[i], rights[i]) for i in heads]
+    kws = [both[:, W:] for both in boths]
+    inner = [mm3(pmats[i], kws[i]) for i in heads]
+    flipped = [jnp.concatenate([both[:, W:], both[:, :W]], axis=1) for both in boths]
+    ends = [mm3(flipped[i], closings[i] * ks[i], TN) for i in heads]
+    effs = [carries[i] * qs[i] - inner[i] for i in heads]
+    grads = [mm3(dos[i], effs[i], TN) for i in heads]
     for i in heads:
-        k, q, beta, carried = ks[i], qs[i], betas[i], carries[i]
         kept_ref[i, 5] = solved[i]
-        kept_ref[i, 2] = cut(raw_v, i)
-        kept_ref[i, 3] = cut(grad_o, i)
-        right = jnp.concatenate([beta * cut(raw_v, i), (beta * carried) * k], axis=1)
-        both = mm3(solved[i], right)
-        uv = both[:, :W]
-        kw = both[:, W:]
-        kept_ref[i, 8] = uv
-        kept_ref[i, 9] = kw
-        eff = carried * q - mm3(pmats[i], kw)
-        closing = kept_ref[i, 10][:, 2:3]
-        ends = mm3(jnp.concatenate([kw, uv], axis=1), closing * k, TN)
-        last = carried[W - 1:W, :]
-        send_ref[i, 0] = jnp.where(ti == si, last, 0.0) - ends[:W]
-        send_ref[i, 1] = ends[W:]
-        send_ref[i, 2] = mm3(cut(grad_o, i), eff, TN)
+        kept_ref[i, 2] = vs[i]
+        kept_ref[i, 3] = dos[i]
+        kept_ref[i, 8] = boths[i][:, :W]
+        kept_ref[i, 9] = kws[i]
+        send_ref[i, 0] = jnp.where(ti == si, carries[i][W - 1:W, :], 0.0) - ends[i][:W]
+        send_ref[i, 1] = ends[i][W:]
+        send_ref[i, 2] = grads[i]
 
 
 def join_kernel(place_ref, own_ref, other_ref, *out_refs):
@@ -322,52 +323,47 @@
     upper = jnp.where(si >= ti, 1.0, 0.0)
     t8, h8 = iotas((W, 8))
     none = jnp.zeros((W, 8), F32)
+    heads = range(GROUP)
+    s0, g1 = ([back_ref[i, j] for i in heads] for j in range(2))
+    k, q, v, do, pmat, wkk, weight, uv, kw, col = ([kept_ref[i, j] for i in heads] for j in (0, 1, 2, 3, 4, 6, 7, 8, 9, 10))
+    beta, carried, closing, inv_k, inv_q = ([c[:, j:j + 1] for c in col] for j in range(5))
+    dr = [early_ref[i, 0] + mm3(early_ref[i, 1], g1[i], NT) for i in heads]
+    u = [uv[i] - mm3(kw[i], s0[i], NT) for i in heads]
+    ds = [mm3(jnp.concatenate([do[i], dr[i]], axis=0), s0[i]) for i in heads]
+    da = [-mm3(dr[i], u[i], NT) for i in heads]
+    ug = [closing[i] * mm3(u[i], g1[i]) for i in heads]
+    dp = [early_ref[i, 2] - mm3(ds[i][:W], kw[i], NT) for i in heads]
+    dkk = [jnp.where(strict, weight[i], 0.0) * da[i] * beta[i] for i in heads]
+    dqk = [weight[i] * dp[i] for i in heads]
+    pairs = [halves(dp[i] * pmat[i] + da[i] * wkk[i] * beta[i]) for i in heads]
+    ub = upper.astype(BF16)
+    front = [mm3(jnp.concatenate([dqk[i], dkk[i]], axis=0), k[i]) for i in heads]
+    under = [mm3(jnp.concatenate([dkk[i], dqk[i]], axis=0), jnp.concatenate([k[i], q[i]], axis=0), TN) for i in heads]
+    across = [dot(ub, high) + dot(ub, low) for high, low in pairs]
+    dq_state = [carried[i] * ds[i][:W] for i in heads]
+    dr_s = [carried[i] * ds[i][W:] for i in heads]
+    total = lambda a: jnp.sum(a, axis=1, keepdims=True)
+    known = [total(dr_s[i] * k[i]) for i in heads]
+    dbeta = [total(dr[i] * v[i] + da[i] * wkk[i]) - known[i] for i in heads]
+    evec = [total(jnp.where(strict, across[i], 0.0)) for i in heads]
+    fvec = [total(ug[i] * k[i]) for i in heads]
+    cvec = [total(dq_state[i] * q[i]) - beta[i] * known[i] for i in heads]
+    ends = [carried[i][W - 1:W, :] * jnp.sum(total(g1[i] * s0[i]), axis=0, keepdims=True) for i in heads]
+    cvec = [cvec[i] + jnp.where(t8[:, :1] == W - 1, ends[i], 0.0) for i in heads]
+    dq = [front[i][:W] + dq_state[i] for i in heads]
+    dk = [front[i][W:] + under[i] - beta[i] * dr_s[i] + ug[i] for i in heads]
+    along_k = [total(k[i] * dk[i]) for i in heads]
+    along_q = [total(q[i] * dq[i]) for i in heads]
+    gks = [(inv_k[i] * (dk[i] - k[i] * along_k[i])).astype(BF16) for i in heads]
+    gqs = [((inv_q[i] * (W ** -0.5)) * (dq[i] - (q[i] * float(W)) * along_q[i])).astype(BF16) for i in heads]
+    gvs = [(beta[i] * dr[i]).astype(BF16) for i in heads]
     cterm, fterm, eterm, dball = none, none, none, none
-    gqs, gks, gvs = [], [], []
-    for i in range(GROUP):
-        head = head0 + i
-        s0, g1 = back_ref[i, 0], back_ref[i, 1]
-        k, q, v, do = kept_ref[i, 0], kept_ref[i, 1], kept_ref[i, 2], kept_ref[i, 3]
-        pmat, wkk, weight = kept_ref[i, 4], kept_ref[i, 6], kept_ref[i, 7]
-        col = kept_ref[i, 10]
-        beta, carried, closing, inv_k, inv_q = (col[:, j:j + 1] for j in range(5))
-        kw = kept_ref[i, 9]
-        u = kept_ref[i, 8] - mm3(kw, s0, NT)
-        dr = early_ref[i, 0] + mm3(early_ref[i, 1], g1, NT)
-        ds = mm3(jnp.concatenate([do, dr], axis=0), s0)
-        dq_state = carried * ds[:W]
-        dr_s = carried * ds[W:]
-        dp = early_ref[i, 2] - mm3(ds[:W], kw, NT)
-        da = -mm3(dr, u, NT)
-        ug = closing * mm3(u, g1)
-        dqk = weight * dp
-        dkk = jnp.where(strict, weight, 0.0) * da * beta
-        front = mm3(jnp.concatenate([dqk, dkk], axis=0), k)
-        dq = front[:W] + dq_state
-        dk = front[W:] + mm3(jnp.concatenate([dkk, dqk], axis=0), jnp.concatenate([k, q], axis=0), TN)
-        dk = dk - beta * dr_s + ug
-        known = jnp.sum(dr_s * k, axis=1, keepdims=True)
-        dbeta = jnp.sum(dr * v, axis=1, keepdims=True) - known + jnp.sum(da * wkk, axis=1, keepdims=True)
-        dlogit = dbeta * beta * (1.0 - beta)
-        pairs = dp * pmat + da * wkk * beta
-        ph, plow = halves(pairs)
-        ub = upper.astype(BF16)
-        across = dot(ub, ph) + dot(ub, plow)
-        evec = jnp.sum(jnp.where(strict, across, 0.0), axis=1, keepdims=True)
-        fvec = jnp.sum(ug * k, axis=1, keepdims=True)
-        cvec = jnp.sum(dq_state * q, axis=1, keepdims=True) - beta * known
-        ends = carried[W - 1:W, :] * jnp.sum(jnp.sum(g1 * s0, axis=1, keepdims=True), axis=0, keepdims=True)
-        cvec = cvec + jnp.where(t8[:, :1] == W - 1, ends, 0.0)
-        here = h8 == head
-        cterm = jnp.where(here, cvec, cterm)
-        fterm = jnp.where(here, fvec, fterm)
-        eterm = jnp.where(here, evec, eterm)
-        dball = jnp.where(here, dlogit, dball)
-        gk = inv_k * (dk - k * jnp.sum(k * dk, axis=1, keepdims=True))
-        gq = (inv_q * (W ** -0.5)) * (dq - (q * float(W)) * jnp.sum(q * dq, axis=1, keepdims=True))
-        gqs.append(gq.astype(BF16))
-        gks.append(gk.astype(BF16))
-        gvs.append((beta * dr).astype(BF16))
+    for i in heads:
+        here = h8 == head0 + i
+        cterm = jnp.where(here, cvec[i], cterm)
+        fterm = jnp.where(here, fvec[i], fterm)
+        eterm = jnp.where(here, evec[i], eterm)
+        dball = jnp.where(here, dbeta[i] * beta[i] * (1.0 - beta[i]), dball)
     grads = jnp.concatenate(gqs + gks + gvs, axis=1)
     db = dball.astype(BF16)
     project = lambda d: back_project((side + d) & (SIDES - 1), grads, db, wkq_ref, wv_ref, wb_ref, wide)

time: 76.6 us -> 72.2 us (0.943)
  Pallas kernels: 29.9 us -> 25.9 us
    pallas_call x2, Pallas kernels: 10.9 us -> 8.28 us  [run_backward(): pl.pallas_call(partial(second_kernel, bool(before)), in_specs=[SMEM] * 2...]
    pallas_call x1, Pallas kernels: 8.7 us -> 7.92 us  [run_give(): pl.pallas_call(give_kernel, in_specs=[SMEM] * 2 + [HBM] * 9, out_specs=[V...]
  transfers between devices with their start and end apart: 13 -> 13, of which waited for: 7 -> 7; matrix products, arithmetic and copies ran while one was open for 0% -> 0% of each run, Pallas kernels for 18% -> 16%
where the time goes in v9:
time: 72.2 us; the launch traced here: 72.1 us
  Pallas kernels  25.9 us (36%)
  starting transfers between devices  22.5 us (31%)
  waiting for transfers between devices  22.2 us (31%)
  other arithmetic  0.73 us (1%)
    ppermute x6, waiting for transfers between devices, along_x(): got[d] = lax.ppermute(parts[d], 'ctx', moves)  11.4 us
    ppermute x6, starting transfers between devices, along_x(): got[d] = lax.ppermute(parts[d], 'ctx', moves)  9.16 us
    ppermute x3, waiting for transfers between devices, per_device(): lax.ppermute(chunk, 'head', [(j, (j + d) % SIDES) for j in range(SIDES)])  9.15 us
    pallas_call x2, Pallas kernels, run_backward(): pl.pallas_call(partial(second_kernel, bool(before)), in_specs=[SMEM] * 2...  8.28 us
    pallas_call x1, Pallas kernels, run_give(): pl.pallas_call(give_kernel, in_specs=[SMEM] * 2 + [HBM] * 9, out_specs=[V...  7.92 us
    ppermute x3, starting transfers between devices, per_device(): lax.ppermute(chunk, 'head', [(j, (j + d) % SIDES) for j in range(SIDES)])  5.58 us
    pallas_call x1, Pallas kernels, run_keep(): pl.pallas_call(keep_kernel, in_specs=[SMEM] + [VMEM] * 8 + [HBM] * 2, out...  5.57 us
    ppermute x1, starting transfers between devices, per_device(): other_back = lax.ppermute(give_back, 'ctx', pair)  2.38 us
  transfers between devices with their start and end apart: 13, of which 7 were waited for; matrix products, arithmetic and copies ran while one was open for 0% of the time, Pallas kernels for 16%

profile of v9, /device:TPU:1, one launch (start us, length us, event | category | flops | bytes accessed | tf_op | source)
XLA Modules:
  0.0 72.1 jit_solution(14394825372226913917)
XLA Ops:
  0.6 7.9 %block_forward_give.1 = (f32[4,3,128,128]{3,2,1,0:T(8,128)S(1)}, f32[4,11,128,128]{3,2,1,0:T(8,128)S(1)}, bf16[128,2048]{1,0:T(8,128)(2,1)S(1)}, bf16[128,2048]{...) custom-call(s32[1]{0:T(128)} %bitcast.1.place_ref.refs_0_, ...), custom_call_target="tpu_custom_call" | custom-call | tf_op jit(solution)/shard_map/block_forward_give/pallas_call | solution.py:410
  8.6 1.5 %collective-permute-start = (f32[4,3,128,128]{3,2,1,0:T(8,128)S(1)}, f32[4,3,128,128]{3,2,1,0:T(8,128)S(1)}, u32[]{:S(2)}, u32[]{:S(2)}) collective-permute-start(f32[4,3,128,128]{3,2,1,0:T(8,128)S(1)} %get-tuple-element.59), channel_id=1, source_target_pairs={{0,4},{4,0},{8,12},{12,8},{16,20},{20,16},{24,28},{28,24},{32,36},... | collective-permute-start | bytes 2359304 | tf_op jit(solution)/shard_map/ppermute | solution.py:478
  10.1 5.6 %block_forward_keep.1 = (f32[4,3,128,128]{3,2,1,0:T(8,128)S(1)}, f32[4,11,128,128]{3,2,1,0:T(8,128)S(1)}, bf16[2048,512]{1,0:T(8,128)(2,1)S(1)}) custom-call(s32[1]{0:T(128)} %bitcast.1.place_ref.refs_0_, bf16[128,2048]{1,0:T(8,128)(2,1)S(1)} %get-tuple-element.50.x_ref, bf16[128,2048]{1,0:T(8,128)(2,1)S(1)} %get-tuple-element.51.go_ref, ...), custom_call_target="tpu_custom_call" | custom-call | tf_op jit(solution)/shard_map/block_forward_keep/pallas_call | solution.py:427
  16.2 1.4 %collective-permute-start.1 = (f32[3,128,128]{2,1,0:T(8,128)S(1)}, f32[3,128,128]{2,1,0:T(8,128)S(1)}, u32[]{:S(2)}, u32[]{:S(2)}) collective-permute-start(f32[3,128,128]{2,1,0:T(8,128)S(1)} %get-tuple-element.67), channel_id=1, source_target_pairs={{0,8},{4,12},{8,16},{12,20},{16,24},{20,28},{24,0},{28,4},{32,40},... | collective-permute-start | bytes 589832 | tf_op jit(solution)/shard_map/ppermute | solution.py:497
  17.6 2.5 %collective-permute-start.2 = (f32[3,128,128]{2,1,0:T(8,128)S(1)}, f32[3,128,128]{2,1,0:T(8,128)S(1)}, u32[]{:S(2)}, u32[]{:S(2)}) collective-permute-start(f32[3,128,128]{2,1,0:T(8,128)S(1)} %get-tuple-element.68), channel_id=1, source_target_pairs={{0,16},{4,20},{8,24},{12,28},{16,0},{20,4},{24,8},{28,12},{32,48},... | collective-permute-start | bytes 589832 | tf_op jit(solution)/shard_map/ppermute | solution.py:497
  20.0 1.2 %collective-permute-start.3 = (f32[3,128,128]{2,1,0:T(8,128)S(1)}, f32[3,128,128]{2,1,0:T(8,128)S(1)}, u32[]{:S(2)}, u32[]{:S(2)}) collective-permute-start(f32[3,128,128]{2,1,0:T(8,128)S(1)} %get-tuple-element.69), channel_id=1, source_target_pairs={{0,24},{4,28},{8,0},{12,4},{16,8},{20,12},{24,16},{28,20},{32,56},... | collective-permute-start | bytes 589832 | tf_op jit(solution)/shard_map/ppermute | solution.py:497
  21.2 0.7 early.2.refs_4_
  22.6 1.4 %collective-permute-done.1.refs_1_ = f32[3,128,128]{2,1,0:T(8,128)S(1)} collective-permute-done((f32[3,128,128]{2,1,0:T(8,128)S(1)}, f32[3,128,128]{2,1,0:T(8,128)S(1)}, u32[]{:S(2)}, u32[]{:S(2)}) %collective-permute-start.1) | collective-permute-done | bytes 196640 | tf_op jit(solution)/shard_map/ppermute | solution.py:497
  24.0 5.3 %collective-permute-done.2.refs_2_ = f32[3,128,128]{2,1,0:T(8,128)S(1)} collective-permute-done((f32[3,128,128]{2,1,0:T(8,128)S(1)}, f32[3,128,128]{2,1,0:T(8,128)S(1)}, u32[]{:S(2)}, u32[]{:S(2)}) %collective-permute-start.2) | collective-permute-done | bytes 196640 | tf_op jit(solution)/shard_map/ppermute | solution.py:497
  29.9 1.7 %collective-permute-start.4 = (f32[128,128]{1,0:T(8,128)S(1)}, f32[128,128]{1,0:T(8,128)S(1)}, u32[]{:S(2)}, u32[]{:S(2)}) collective-permute-start(f32[128,128]{1,0:T(8,128)S(1)} %get-tuple-element.77), channel_id=1, source_target_pairs={{0,32},{4,36},{8,40},{12,44},{16,48},{20,52},{24,56},{28,60},{32,6... | collective-permute-start | bytes 196616 | tf_op jit(solution)/shard_map/ppermute | solution.py:513
  31.6 2.2 %collective-permute-start.5 = (f32[128,128]{1,0:T(8,128)S(1)}, f32[128,128]{1,0:T(8,128)S(1)}, u32[]{:S(2)}, u32[]{:S(2)}) collective-permute-start(f32[128,128]{1,0:T(8,128)S(1)} %get-tuple-element.78), channel_id=1, source_target_pairs={{32,0},{36,4},{40,8},{44,12},{48,16},{52,20},{56,24},{60,28},{64,3... | collective-permute-start | bytes 196616 | tf_op jit(solution)/shard_map/ppermute | solution.py:514
  33.8 1.6 %collective-permute-done.4.s_ref = f32[128,128]{1,0:T(8,128)S(1)} collective-permute-done((f32[128,128]{1,0:T(8,128)S(1)}, f32[128,128]{1,0:T(8,128)S(1)}, u32[]{:S(2)}, u32[]{:S(2)}) %collective-permute-start.4) | collective-permute-done | bytes 65568 | tf_op jit(solution)/shard_map/ppermute | solution.py:513
  36.0 0.7 %collective-permute-start.6 = (f32[2,128,128]{2,1,0:T(8,128)S(1)}, f32[2,128,128]{2,1,0:T(8,128)S(1)}, u32[]{:S(2)}, u32[]{:S(2)}) collective-permute-start(f32[2,128,128]{2,1,0:T(8,128)S(1)} %get-tuple-element.80), channel_id=1, source_target_pairs={{0,8},{4,12},{8,16},{12,20},{16,24},{20,28},{24,0},{28,4},{32,40},... | collective-permute-start | bytes 393224 | tf_op jit(solution)/shard_map/ppermute | solution.py:497
  36.7 3.2 %collective-permute-start.7 = (f32[2,128,128]{2,1,0:T(8,128)S(1)}, f32[2,128,128]{2,1,0:T(8,128)S(1)}, u32[]{:S(2)}, u32[]{:S(2)}) collective-permute-start(f32[2,128,128]{2,1,0:T(8,128)S(1)} %get-tuple-element.81), channel_id=1, source_target_pairs={{0,16},{4,20},{8,24},{12,28},{16,0},{20,4},{24,8},{28,12},{32,48},... | collective-permute-start | bytes 393224 | tf_op jit(solution)/shard_map/ppermute | solution.py:497
  40.2 0.9 %collective-permute-done.6.refs_1_ = f32[2,128,128]{2,1,0:T(8,128)S(1)} collective-permute-done((f32[2,128,128]{2,1,0:T(8,128)S(1)}, f32[2,128,128]{2,1,0:T(8,128)S(1)}, u32[]{:S(2)}, u32[]{:S(2)}) %collective-permute-start.6) | collective-permute-done | bytes 131104 | tf_op jit(solution)/shard_map/ppermute | solution.py:497
  41.1 3.8 %collective-permute-done.7.refs_2_ = f32[2,128,128]{2,1,0:T(8,128)S(1)} collective-permute-done((f32[2,128,128]{2,1,0:T(8,128)S(1)}, f32[2,128,128]{2,1,0:T(8,128)S(1)}, u32[]{:S(2)}, u32[]{:S(2)}) %collective-permute-start.7) | collective-permute-done | bytes 131104 | tf_op jit(solution)/shard_map/ppermute | solution.py:497
  45.3 2.4 %collective-permute-start.9 = (f32[4,2,128,128]{3,2,1,0:T(8,128)S(1)}, f32[4,2,128,128]{3,2,1,0:T(8,128)S(1)}, u32[]{:S(2)}, u32[]{:S(2)}) collective-permute-start(f32[4,2,128,128]{3,2,1,0:T(8,128)S(1)} %get-tuple-element.83), channel_id=1, source_target_pairs={{0,4},{4,0},{8,12},{12,8},{16,20},{20,16},{24,28},{28,24},{32,36},... | collective-permute-start | bytes 1572872 | tf_op jit(solution)/shard_map/ppermute | solution.py:521
  47.7 4.1 %block_backward.2 = (f32[4,128,512]{2,1,0:T(8,128)S(1)}, f32[8,128]{1,0:T(8,128)S(1)}) custom-call(s32[1]{0:T(128)} %bitcast.1.place_ref.refs_0_, s32[1]{0:T(128)} %bitcast.side_ref.refs_1_, f32[4,2,128,128]{3,2,1,0:T(8,128)S(1)} %get-tuple-element.87.refs_2_, f32[4,11,128,128]{3,2,1,0:T(8,128)S(1)} %get-tuple-element.70.kept_ref.refs_3_, ...), custom_call_target="tpu_custom_call" | custom-call | tf_op jit(solution)/shard_map/block_backward/pallas_call | solution.py:446
  51.7 4.2 %block_backward.3 = (f32[128,512]{1,0:T(8,128)S(1)}, f32[128,512]{1,0:T(8,128)S(1)}, f32[128,512]{1,0:T(8,128)S(1)}, f32[8,128]{1,0:T(8,128)}, bf16[128,1536]{1,...) custom-call(s32[1]{0:T(128)} %bitcast.1.place_ref.refs_0_, s32[1]{0:T(128)} %bitcast.side_ref.refs_1_, ...), custom_call_target="tpu_custom_call" | custom-call | tf_op jit(solution)/shard_map/block_backward/pallas_call | solution.py:446
  55.9 2.9 %collective-permute-start.10 = (f32[128,512]{1,0:T(8,128)S(1)}, f32[128,512]{1,0:T(8,128)S(1)}, u32[]{:S(2)}, u32[]{:S(2)}) collective-permute-start(f32[128,512]{1,0:T(8,128)S(1)} %get-tuple-element.94), channel_id=1, source_target_pairs={{0,2},{1,3},{2,0},{3,1},{4,6},{5,7},{6,4},{7,5},{8,10},{9,11},{10,... | collective-permute-start | bytes 786440 | tf_op jit(solution)/shard_map/ppermute | solution.py:526
  59.3 2.3 %collective-permute-start.12 = (f32[128,512]{1,0:T(8,128)S(1)}, f32[128,512]{1,0:T(8,128)S(1)}, u32[]{:S(2)}, u32[]{:S(2)}) collective-permute-start(f32[128,512]{1,0:T(8,128)S(1)} %get-tuple-element.96), channel_id=1, source_target_pairs={{0,3},{1,0},{2,1},{3,2},{4,7},{5,4},{6,5},{7,6},{8,11},{9,8},{10,9... | collective-permute-start | bytes 786440 | tf_op jit(solution)/shard_map/ppermute | solution.py:526
  62.2 3.2 %collective-permute-done.10 = f32[128,512]{1,0:T(8,128)S(1)} collective-permute-done((f32[128,512]{1,0:T(8,128)S(1)}, f32[128,512]{1,0:T(8,128)S(1)}, u32[]{:S(2)}, u32[]{:S(2)}) %collective-permute-start.10) | collective-permute-done | bytes 262176 | tf_op jit(solution)/shard_map/ppermute | solution.py:526
  65.4 5.9 %collective-permute-done.11 = f32[128,512]{1,0:T(8,128)S(1)} collective-permute-done((f32[128,512]{1,0:T(8,128)S(1)}, f32[128,512]{1,0:T(8,128)S(1)}, u32[]{:S(2)}, u32[]{:S(2)}) %collective-permute-start.11) | collective-permute-done | bytes 262176 | tf_op jit(solution)/shard_map/ppermute | solution.py:526
  71.4 0.7 %add_convert_fusion = bf16[128,512]{1,0:T(8,128)(2,1)} fusion(f32[128,512]{1,0:T(8,128)S(1)} %collective-permute-done.12, f32[128,512]{1,0:T(8,128)S(1)} %collective-permute-done.11, f32[128,512]{1,0:T(8,128)S(1)} %own_chunk.1, f32[128,512]{1,0:T(8,128)S(1)} %collective-permute-done.10), kind=kLoop, calls=%fused_computation | loop fusion | flops 262144 | bytes 1179648 | tf_op jit(solution)/shard_map/convert_element_type | solution.py:527
  (16 shorter events, 4.2 us)
Async XLA Ops:
  8.6 7.1 %collective-permute-start = (f32[4,3,128,128]{3,2,1,0:T(8,128)S(1)}, f32[4,3,128,128]{3,2,1,0:T(8,128)S(1)}, u32[]{:S(2)}, u32[]{:S(2)}) collective-permute-start(f32[4,3,128,128]{3,2,1,0:T(8,128)S(1)} %get-tuple-element.59), channel_id=1, source_target_pairs={{0,4},{4,0},{8,12},{12,8},{16,20},{20,16},{24,28},{28,24},{32,36},... | collective-permute-start | bytes 2359304 | tf_op jit(solution)/shard_map/ppermute | solution.py:478
  16.2 7.8 %collective-permute-start.1 = (f32[3,128,128]{2,1,0:T(8,128)S(1)}, f32[3,128,128]{2,1,0:T(8,128)S(1)}, u32[]{:S(2)}, u32[]{:S(2)}) collective-permute-start(f32[3,128,128]{2,1,0:T(8,128)S(1)} %get-tuple-element.67), channel_id=1, source_target_pairs={{0,8},{4,12},{8,16},{12,20},{16,24},{20,28},{24,0},{28,4},{32,40},... | collective-permute-start | bytes 589832 | tf_op jit(solution)/shard_map/ppermute | solution.py:497
  17.6 11.7 %collective-permute-start.2 = (f32[3,128,128]{2,1,0:T(8,128)S(1)}, f32[3,128,128]{2,1,0:T(8,128)S(1)}, u32[]{:S(2)}, u32[]{:S(2)}) collective-permute-start(f32[3,128,128]{2,1,0:T(8,128)S(1)} %get-tuple-element.68), channel_id=1, source_target_pairs={{0,16},{4,20},{8,24},{12,28},{16,0},{20,4},{24,8},{28,12},{32,48},... | collective-permute-start | bytes 589832 | tf_op jit(solution)/shard_map/ppermute | solution.py:497
  20.0 9.3 %collective-permute-start.3 = (f32[3,128,128]{2,1,0:T(8,128)S(1)}, f32[3,128,128]{2,1,0:T(8,128)S(1)}, u32[]{:S(2)}, u32[]{:S(2)}) collective-permute-start(f32[3,128,128]{2,1,0:T(8,128)S(1)} %get-tuple-element.69), channel_id=1, source_target_pairs={{0,24},{4,28},{8,0},{12,4},{16,8},{20,12},{24,16},{28,20},{32,56},... | collective-permute-start | bytes 589832 | tf_op jit(solution)/shard_map/ppermute | solution.py:497
  21.9 25.8 %copy-start = (bf16[2048,8]{0,1:T(8,128)(2,1)S(1)}, bf16[2048,8]{0,1:T(8,128)(2,1)}, u32[]{:S(2)}) copy-start(bf16[2048,8]{0,1:T(8,128)(2,1)} %param.14) | copy-start | bytes 98308
  29.9 5.5 %collective-permute-start.4 = (f32[128,128]{1,0:T(8,128)S(1)}, f32[128,128]{1,0:T(8,128)S(1)}, u32[]{:S(2)}, u32[]{:S(2)}) collective-permute-start(f32[128,128]{1,0:T(8,128)S(1)} %get-tuple-element.77), channel_id=1, source_target_pairs={{0,32},{4,36},{8,40},{12,44},{16,48},{20,52},{24,56},{28,60},{32,6... | collective-permute-start | bytes 196616 | tf_op jit(solution)/shard_map/ppermute | solution.py:513
  31.6 3.8 %collective-permute-start.5 = (f32[128,128]{1,0:T(8,128)S(1)}, f32[128,128]{1,0:T(8,128)S(1)}, u32[]{:S(2)}, u32[]{:S(2)}) collective-permute-start(f32[128,128]{1,0:T(8,128)S(1)} %get-tuple-element.78), channel_id=1, source_target_pairs={{32,0},{36,4},{40,8},{44,12},{48,16},{52,20},{56,24},{60,28},{64,3... | collective-permute-start | bytes 196616 | tf_op jit(solution)/shard_map/ppermute | solution.py:514
  36.0 5.1 %collective-permute-start.6 = (f32[2,128,128]{2,1,0:T(8,128)S(1)}, f32[2,128,128]{2,1,0:T(8,128)S(1)}, u32[]{:S(2)}, u32[]{:S(2)}) collective-permute-start(f32[2,128,128]{2,1,0:T(8,128)S(1)} %get-tuple-element.80), channel_id=1, source_target_pairs={{0,8},{4,12},{8,16},{12,20},{16,24},{20,28},{24,0},{28,4},{32,40},... | collective-permute-start | bytes 393224 | tf_op jit(solution)/shard_map/ppermute | solution.py:497
  36.7 8.2 %collective-permute-start.7 = (f32[2,128,128]{2,1,0:T(8,128)S(1)}, f32[2,128,128]{2,1,0:T(8,128)S(1)}, u32[]{:S(2)}, u32[]{:S(2)}) collective-permute-start(f32[2,128,128]{2,1,0:T(8,128)S(1)} %get-tuple-element.81), channel_id=1, source_target_pairs={{0,16},{4,20},{8,24},{12,28},{16,0},{20,4},{24,8},{28,12},{32,48},... | collective-permute-start | bytes 393224 | tf_op jit(solution)/shard_map/ppermute | solution.py:497
  39.9 5.0 %collective-permute-start.8 = (f32[2,128,128]{2,1,0:T(8,128)S(1)}, f32[2,128,128]{2,1,0:T(8,128)S(1)}, u32[]{:S(2)}, u32[]{:S(2)}) collective-permute-start(f32[2,128,128]{2,1,0:T(8,128)S(1)} %get-tuple-element.82), channel_id=1, source_target_pairs={{0,24},{4,28},{8,0},{12,4},{16,8},{20,12},{24,16},{28,20},{32,56},... | collective-permute-start | bytes 393224 | tf_op jit(solution)/shard_map/ppermute | solution.py:497
  45.3 6.4 %collective-permute-start.9 = (f32[4,2,128,128]{3,2,1,0:T(8,128)S(1)}, f32[4,2,128,128]{3,2,1,0:T(8,128)S(1)}, u32[]{:S(2)}, u32[]{:S(2)}) collective-permute-start(f32[4,2,128,128]{3,2,1,0:T(8,128)S(1)} %get-tuple-element.83), channel_id=1, source_target_pairs={{0,4},{4,0},{8,12},{12,8},{16,20},{20,16},{24,28},{28,24},{32,36},... | collective-permute-start | bytes 1572872 | tf_op jit(solution)/shard_map/ppermute | solution.py:521
  55.9 9.5 %collective-permute-start.10 = (f32[128,512]{1,0:T(8,128)S(1)}, f32[128,512]{1,0:T(8,128)S(1)}, u32[]{:S(2)}, u32[]{:S(2)}) collective-permute-start(f32[128,512]{1,0:T(8,128)S(1)} %get-tuple-element.94), channel_id=1, source_target_pairs={{0,2},{1,3},{2,0},{3,1},{4,6},{5,7},{6,4},{7,5},{8,10},{9,11},{10,... | collective-permute-start | bytes 786440 | tf_op jit(solution)/shard_map/ppermute | solution.py:526
  58.9 12.5 %collective-permute-start.11 = (f32[128,512]{1,0:T(8,128)S(1)}, f32[128,512]{1,0:T(8,128)S(1)}, u32[]{:S(2)}, u32[]{:S(2)}) collective-permute-start(f32[128,512]{1,0:T(8,128)S(1)} %get-tuple-element.95), channel_id=1, source_target_pairs={{0,1},{1,2},{2,3},{3,0},{4,5},{5,6},{6,7},{7,4},{8,9},{9,10},{10,1... | collective-permute-start | bytes 786440 | tf_op jit(solution)/shard_map/ppermute | solution.py:526
  59.3 12.1 %collective-permute-start.12 = (f32[128,512]{1,0:T(8,128)S(1)}, f32[128,512]{1,0:T(8,128)S(1)}, u32[]{:S(2)}, u32[]{:S(2)}) collective-permute-start(f32[128,512]{1,0:T(8,128)S(1)} %get-tuple-element.96), channel_id=1, source_target_pairs={{0,3},{1,0},{2,1},{3,2},{4,7},{5,4},{6,5},{7,6},{8,11},{9,8},{10,9... | collective-permute-start | bytes 786440 | tf_op jit(solution)/shard_map/ppermute | solution.py:526

commit v10 on v9

--- a/solution.py
+++ b/solution.py
@@ -12,7 +12,7 @@
 W = 128
 GROUP = 4
 SIDES = 4
-ORDER = (2, 1, 3)
+HALF = W // 2
 NN = (((1,), (0,)), ((), ()))
 NT = (((1,), (1,)), ((), ()))
 TN = (((0,), (0,)), ((), ()))
@@ -153,40 +153,34 @@
     raw_k = dot(x, wkq_ref[0])
     ready(1)
     raw_q = dot(x, wkq_ref[1])
-    ks, qs, betas, carries, closings, mixes, pmats = [], [], [], [], [], [], []
+    total = lambda a: jnp.sum(a, axis=1, keepdims=True)
+    heads_at = lax.broadcasted_iota(jnp.int32, run_rows.shape, 0)
+    betas = [column(beta_all, head0 + i) for i in heads]
+    runs = [column(run_all, head0 + i) for i in heads]
+    rows = [jnp.sum(jnp.where(heads_at == head0 + i, run_rows, 0.0), axis=0, keepdims=True) for i in heads]
+    spreads = [runs[i] - rows[i] for i in heads]
+    weights = [jnp.where(keep, jnp.exp(jnp.where(keep, spread, 0.0)), 0.0) for spread in spreads]
+    carries = [jnp.where(first, jnp.exp(run), 0.0) for run in runs]
+    closings = [jnp.where(final, jnp.exp(jnp.where(final, run[W - 1:W, :] - run, 0.0)), 0.0) for run in runs]
+    rks = [cut(raw_k, i) for i in heads]
+    inv_ks = [lax.rsqrt(total(rk * rk) + 1e-06) for rk in rks]
+    ks = [rks[i] * inv_ks[i] for i in heads]
+    key_keys = [mm3(k, k, NT) for k in ks]
+    rqs = [cut(raw_q, i) for i in heads]
+    inv_qs = [lax.rsqrt(total(rq * rq) + 1e-06) for rq in rqs]
+    qs = [rqs[i] * inv_qs[i] * (W ** -0.5) for i in heads]
+    query_keys = [mm3(qs[i], ks[i], NT) for i in heads]
+    wkks = [jnp.where(strict, weights[i], 0.0) * key_keys[i] for i in heads]
+    mixes = [wkks[i] * betas[i] for i in heads]
+    pmats = [weights[i] * query_keys[i] for i in heads]
     for i in heads:
-        head = head0 + i
-        rk = cut(raw_k, i)
-        rq = cut(raw_q, i)
-        inv_k = lax.rsqrt(jnp.sum(rk * rk, axis=1, keepdims=True) + 1e-06)
-        inv_q = lax.rsqrt(jnp.sum(rq * rq, axis=1, keepdims=True) + 1e-06)
-        k = rk * inv_k
-        q = rq * inv_q * (W ** -0.5)
-        beta = column(beta_all, head)
-        run = column(run_all, head)
-        heads_at = lax.broadcasted_iota(jnp.int32, run_rows.shape, 0)
-        spread = run - jnp.sum(jnp.where(heads_at == head, run_rows, 0.0), axis=0, keepdims=True)
-        weight = jnp.where(keep, jnp.exp(jnp.where(keep, spread, 0.0)), 0.0)
-        carried = jnp.where(first, jnp.exp(run), 0.0)
-        both = mm3(jnp.concatenate([k, q], axis=0), k, NT)
-        wkk = jnp.where(strict, weight, 0.0) * both[:W]
-        pmat = weight * both[W:]
-        ks.append(k)
-        qs.append(q)
-        betas.append(beta)
-        carries.append(carried)
-        mixes.append(wkk * beta)
-        pmats.append(pmat)
-        lanes = si
-        closing = jnp.where(final, jnp.exp(jnp.where(final, run[W - 1:W, :] - run, 0.0)), 0.0)
-        closings.append(closing)
-        col = jnp.where(lanes == 0, beta, jnp.where(lanes == 1, carried, jnp.where(lanes == 2, closing, jnp.where(lanes == 3, inv_k, inv_q))))
-        kept_ref[i, 10] = col
-        kept_ref[i, 0] = k
-        kept_ref[i, 1] = q
-        kept_ref[i, 4] = pmat
-        kept_ref[i, 6] = wkk
-        kept_ref[i, 7] = weight
+        last = jnp.where(si == 3, inv_ks[i], inv_qs[i])
+        kept_ref[i, 10] = jnp.where(si == 0, betas[i], jnp.where(si == 1, carries[i], jnp.where(si == 2, closings[i], last)))
+        kept_ref[i, 0] = ks[i]
+        kept_ref[i, 1] = qs[i]
+        kept_ref[i, 4] = pmats[i]
+        kept_ref[i, 6] = wkks[i]
+        kept_ref[i, 7] = weights[i]
     solved = inverse_all(mixes)
     ready(2)
     raw_v = dot(x, wv_ref[...])
@@ -289,9 +283,18 @@
     return piece + dot(grads[:, 2 * n:], wv_ref[at, :], NT) + dot(db, wb_ref[:, at])
 
 
-def chunk_kernel(side_ref, grads_ref, db_ref, before_ref, wb_ref, wkq_ref, wv_ref, out_ref):
-    piece = back_project(side_ref[0], grads_ref[...], db_ref[...], wkq_ref, wv_ref, wb_ref, out_ref.shape[1])
-    out_ref[...] = before_ref[0] + piece
+def chunk_kernel(distances, side_ref, grads_ref, db_ref, before_ref, wb_ref, wkq_ref, wv_ref, *out_refs):
+    for d, out_ref in zip(distances, out_refs):
+        side = (side_ref[0] + d) & (SIDES - 1)
+        piece = back_project(side, grads_ref[...], db_ref[...], wkq_ref, wv_ref, wb_ref, out_ref.shape[1])
+        out_ref[...] = before_ref[d] + piece
+
+
+def relay_kernel(next_ref, last_ref, up_ref, down_ref, next_out, last_out):
+    next_out[:HALF] = next_ref[:HALF] + up_ref[...]
+    next_out[HALF:] = next_ref[HALF:]
+    last_out[:HALF] = last_ref[:HALF]
+    last_out[HALF:] = last_ref[HALF:] + down_ref[...]
 
 
 def early_kernel(kept_ref, out_ref):
@@ -310,8 +313,8 @@
     place_ref, side_ref, back_ref, kept_ref, early_ref, wb_ref, wkq_ref, wv_ref = refs[:8]
     refs = refs[8:]
     if chained:
-        before_ref, gd_before_ref, *total_refs, gd_ref, grads_ref, db_ref = refs
-        wide = total_refs[0].shape[-1]
+        before_ref, gd_before_ref, up_ref, down_ref, gd_ref, grads_ref, db_ref = refs
+        wide = up_ref.shape[-1]
     else:
         total_ref, gd_ref = refs
         wide = total_ref.shape[-1]
@@ -368,8 +371,9 @@
     db = dball.astype(BF16)
     project = lambda d: back_project((side + d) & (SIDES - 1), grads, db, wkq_ref, wv_ref, wb_ref, wide)
     if chained:
-        for d, total_ref in zip(ORDER, total_refs):
-            total_ref[...] = before_ref[d] + project(d)
+        far = before_ref[2] + project(2)
+        up_ref[...] = far[:HALF]
+        down_ref[...] = far[HALF:]
         grads_ref[...] = grads
         db_ref[...] = db
     else:
@@ -440,7 +444,7 @@
     heads, width = beta_t.shape
     wide = width // SIDES
     if before:
-        out_shape = [shape(W, wide)] * 3 + [shape(heads, W), jax.ShapeDtypeStruct((W, 3 * GROUP * W), BF16), jax.ShapeDtypeStruct((W, heads), BF16)]
+        out_shape = [shape(HALF, wide)] * 2 + [shape(heads, W), jax.ShapeDtypeStruct((W, 3 * GROUP * W), BF16), jax.ShapeDtypeStruct((W, heads), BF16)]
     else:
         out_shape = [shape(SIDES, W, wide), shape(heads, W)]
     return pl.pallas_call(
@@ -453,14 +457,14 @@
     )(place, side, back, kept, early, beta_t, w_both, w_value, *before)
 
 
-def run_chunk(side, grads, db, before, beta_t, w_both, w_value):
+def run_chunk(distances, side, grads, db, before, beta_t, w_both, w_value):
     return pl.pallas_call(
-        chunk_kernel,
+        partial(chunk_kernel, distances),
         in_specs=[SMEM] + [VMEM] * 6,
-        out_specs=VMEM,
-        out_shape=shape(*before.shape[1:]),
+        out_specs=[VMEM] * len(distances),
+        out_shape=[shape(*before.shape[1:])] * len(distances),
         compiler_params=pltpu.CompilerParams(vmem_limit_bytes=16 << 20),
-        name="own_chunk",
+        name="near_chunks" if len(distances) > 1 else "own_chunk",
     )(side, grads, db, before, beta_t, w_both, w_value)
 
 
@@ -520,10 +524,15 @@
     )
     other_back = lax.ppermute(give_back, "ctx", pair)
     before = run_backward(place, side, own_back, own_kept, own_early, beta_t, keep_w, keep_v, ())
-    *chunks, grad_d, grads, db = run_backward(place, side, other_back, give_kept, give_early, beta_t, *give_w, before)
-    total = run_chunk(side, grads, db, before[0], beta_t, *give_w)
-    for d, chunk in zip(ORDER, chunks):
-        total = total + lax.ppermute(chunk, "head", [(j, (j + d) % SIDES) for j in range(SIDES)])
+    up, down, grad_d, grads, db = run_backward(place, side, other_back, give_kept, give_early, beta_t, *give_w, before)
+    after = [(j, (j + 1) % SIDES) for j in range(SIDES)]
+    ahead = [((j + 1) % SIDES, j) for j in range(SIDES)]
+    near = run_chunk((1, 3), side, grads, db, before[0], beta_t, *give_w)
+    halfway = (*near, lax.ppermute(up, "head", after), lax.ppermute(down, "head", ahead))
+    near = call(relay_kernel, "relay", (), lax.optimization_barrier(halfway), [shape(*near[0].shape)] * 2)
+    *near, grads = lax.optimization_barrier((*near, grads))
+    (total,) = run_chunk((0,), side, grads, db, before[0], beta_t, *give_w)
+    total = total + lax.ppermute(near[0], "head", after) + lax.ppermute(near[1], "head", ahead)
     return (total.astype(BF16), grad_d.T)
 
 

time: 72.2 us -> 71 us (0.983)
  waiting for transfers between devices: 22.2 us -> 20.5 us
    ppermute x3 -> x4, waiting for transfers between devices: 9.15 us -> 7.43 us  [the longest x1 4.94 us: per_device(): lax.ppermute(near[0], 'head', after)]
    pallas_call x1 -> x2, Pallas kernels: 0.67 us -> 1.9 us  [run_chunk(): pl.pallas_call(partial(chunk_kernel, distances), in_specs=[SMEM] + [VMEM]...]
    pallas_call x2, Pallas kernels: 8.28 us -> 7.53 us  [run_backward(): pl.pallas_call(partial(second_kernel, bool(before)), in_specs=[SMEM] * 2...]
    ppermute x3 -> x4, starting transfers between devices: 5.58 us -> 5.49 us  [the longest x1 1.76 us: per_device(): lax.ppermute(near[1], 'head', ahead)]
    pallas_call x4 -> x5, Pallas kernels: 2.11 us -> 2.2 us  [call(): pl.pallas_call(kernel, in_specs=[SMEM] * len(scalars) + [VMEM] * len(arra...]
  transfers between devices with their start and end apart: 13 -> 14, of which waited for: 7 -> 7; matrix products, arithmetic and copies ran while one was open for 0% -> 0% of each run, Pallas kernels for 16% -> 18%
where the time goes in v10:
time: 71 us; the launch traced here: 70.7 us
  Pallas kernels  26.4 us (37%)
  starting transfers between devices  22.4 us (32%)
  waiting for transfers between devices  20.5 us (29%)
  between operations  0.74 us (1%)
  other arithmetic  0.71 us (1%)
    ppermute x6, waiting for transfers between devices, along_x(): got[d] = lax.ppermute(parts[d], 'ctx', moves)  11.4 us
    ppermute x6, starting transfers between devices, along_x(): got[d] = lax.ppermute(parts[d], 'ctx', moves)  9.17 us
    pallas_call x1, Pallas kernels, run_give(): pl.pallas_call(give_kernel, in_specs=[SMEM] * 2 + [HBM] * 9, out_specs=[V...  7.8 us
    pallas_call x2, Pallas kernels, run_backward(): pl.pallas_call(partial(second_kernel, bool(before)), in_specs=[SMEM] * 2...  7.53 us
    pallas_call x1, Pallas kernels, run_keep(): pl.pallas_call(keep_kernel, in_specs=[SMEM] + [VMEM] * 8 + [HBM] * 2, out...  5.59 us
    ppermute x1, waiting for transfers between devices, per_device(): lax.ppermute(near[0], 'head', after)  4.94 us
    ppermute x1, waiting for transfers between devices, per_device(): lax.ppermute(up, 'head', after)  2.49 us
    ppermute x1, starting transfers between devices, per_device(): other_back = lax.ppermute(give_back, 'ctx', pair)  2.37 us
  transfers between devices with their start and end apart: 14, of which 7 were waited for; matrix products, arithmetic and copies ran while one was open for 0% of the time, Pallas kernels for 18%

profile of v10, /device:TPU:1, one launch (start us, length us, event | category | flops | bytes accessed | tf_op | source)
XLA Modules:
  0.0 70.7 jit_solution(451645265211195773)
XLA Ops:
  0.6 7.8 %block_forward_give.1 = (f32[4,3,128,128]{3,2,1,0:T(8,128)S(1)}, f32[4,11,128,128]{3,2,1,0:T(8,128)S(1)}, bf16[128,2048]{1,0:T(8,128)(2,1)S(1)}, bf16[128,2048]{...) custom-call(s32[1]{0:T(128)} %bitcast.1.place_ref.refs_0_, ...), custom_call_target="tpu_custom_call" | custom-call | tf_op jit(solution)/shard_map/block_forward_give/pallas_call | solution.py:414
  8.4 1.5 %collective-permute-start = (f32[4,3,128,128]{3,2,1,0:T(8,128)S(1)}, f32[4,3,128,128]{3,2,1,0:T(8,128)S(1)}, u32[]{:S(2)}, u32[]{:S(2)}) collective-permute-start(f32[4,3,128,128]{3,2,1,0:T(8,128)S(1)} %get-tuple-element.69), channel_id=1, source_target_pairs={{0,4},{4,0},{8,12},{12,8},{16,20},{20,16},{24,28},{28,24},{32,36},... | collective-permute-start | bytes 2359304 | tf_op jit(solution)/shard_map/ppermute | solution.py:482
  9.9 5.6 %block_forward_keep.1 = (f32[4,3,128,128]{3,2,1,0:T(8,128)S(1)}, f32[4,11,128,128]{3,2,1,0:T(8,128)S(1)}, bf16[2048,512]{1,0:T(8,128)(2,1)S(1)}) custom-call(s32[1]{0:T(128)} %bitcast.1.place_ref.refs_0_, bf16[128,2048]{1,0:T(8,128)(2,1)S(1)} %get-tuple-element.60.x_ref, bf16[128,2048]{1,0:T(8,128)(2,1)S(1)} %get-tuple-element.61.go_ref, ...), custom_call_target="tpu_custom_call" | custom-call | tf_op jit(solution)/shard_map/block_forward_keep/pallas_call | solution.py:431
  16.1 1.4 %collective-permute-start.1 = (f32[3,128,128]{2,1,0:T(8,128)S(1)}, f32[3,128,128]{2,1,0:T(8,128)S(1)}, u32[]{:S(2)}, u32[]{:S(2)}) collective-permute-start(f32[3,128,128]{2,1,0:T(8,128)S(1)} %get-tuple-element.77), channel_id=1, source_target_pairs={{0,8},{4,12},{8,16},{12,20},{16,24},{20,28},{24,0},{28,4},{32,40},... | collective-permute-start | bytes 589832 | tf_op jit(solution)/shard_map/ppermute | solution.py:501
  17.5 2.4 %collective-permute-start.2 = (f32[3,128,128]{2,1,0:T(8,128)S(1)}, f32[3,128,128]{2,1,0:T(8,128)S(1)}, u32[]{:S(2)}, u32[]{:S(2)}) collective-permute-start(f32[3,128,128]{2,1,0:T(8,128)S(1)} %get-tuple-element.78), channel_id=1, source_target_pairs={{0,16},{4,20},{8,24},{12,28},{16,0},{20,4},{24,8},{28,12},{32,48},... | collective-permute-start | bytes 589832 | tf_op jit(solution)/shard_map/ppermute | solution.py:501
  19.9 1.2 %collective-permute-start.3 = (f32[3,128,128]{2,1,0:T(8,128)S(1)}, f32[3,128,128]{2,1,0:T(8,128)S(1)}, u32[]{:S(2)}, u32[]{:S(2)}) collective-permute-start(f32[3,128,128]{2,1,0:T(8,128)S(1)} %get-tuple-element.79), channel_id=1, source_target_pairs={{0,24},{4,28},{8,0},{12,4},{16,8},{20,12},{24,16},{28,20},{32,56},... | collective-permute-start | bytes 589832 | tf_op jit(solution)/shard_map/ppermute | solution.py:501
  22.5 1.4 %collective-permute-done.1.refs_1_ = f32[3,128,128]{2,1,0:T(8,128)S(1)} collective-permute-done((f32[3,128,128]{2,1,0:T(8,128)S(1)}, f32[3,128,128]{2,1,0:T(8,128)S(1)}, u32[]{:S(2)}, u32[]{:S(2)}) %collective-permute-start.1) | collective-permute-done | bytes 196640 | tf_op jit(solution)/shard_map/ppermute | solution.py:501
  23.9 5.3 %collective-permute-done.2.refs_2_ = f32[3,128,128]{2,1,0:T(8,128)S(1)} collective-permute-done((f32[3,128,128]{2,1,0:T(8,128)S(1)}, f32[3,128,128]{2,1,0:T(8,128)S(1)}, u32[]{:S(2)}, u32[]{:S(2)}) %collective-permute-start.2) | collective-permute-done | bytes 196640 | tf_op jit(solution)/shard_map/ppermute | solution.py:501
  29.8 1.7 %collective-permute-start.4 = (f32[128,128]{1,0:T(8,128)S(1)}, f32[128,128]{1,0:T(8,128)S(1)}, u32[]{:S(2)}, u32[]{:S(2)}) collective-permute-start(f32[128,128]{1,0:T(8,128)S(1)} %get-tuple-element.87), channel_id=1, source_target_pairs={{0,32},{4,36},{8,40},{12,44},{16,48},{20,52},{24,56},{28,60},{32,6... | collective-permute-start | bytes 196616 | tf_op jit(solution)/shard_map/ppermute | solution.py:517
  31.5 2.2 %collective-permute-start.5 = (f32[128,128]{1,0:T(8,128)S(1)}, f32[128,128]{1,0:T(8,128)S(1)}, u32[]{:S(2)}, u32[]{:S(2)}) collective-permute-start(f32[128,128]{1,0:T(8,128)S(1)} %get-tuple-element.88), channel_id=1, source_target_pairs={{32,0},{36,4},{40,8},{44,12},{48,16},{52,20},{56,24},{60,28},{64,3... | collective-permute-start | bytes 196616 | tf_op jit(solution)/shard_map/ppermute | solution.py:518
  33.7 1.6 %collective-permute-done.4.s_ref = f32[128,128]{1,0:T(8,128)S(1)} collective-permute-done((f32[128,128]{1,0:T(8,128)S(1)}, f32[128,128]{1,0:T(8,128)S(1)}, u32[]{:S(2)}, u32[]{:S(2)}) %collective-permute-start.4) | collective-permute-done | bytes 65568 | tf_op jit(solution)/shard_map/ppermute | solution.py:517
  36.6 3.2 %collective-permute-start.7 = (f32[2,128,128]{2,1,0:T(8,128)S(1)}, f32[2,128,128]{2,1,0:T(8,128)S(1)}, u32[]{:S(2)}, u32[]{:S(2)}) collective-permute-start(f32[2,128,128]{2,1,0:T(8,128)S(1)} %get-tuple-element.91), channel_id=1, source_target_pairs={{0,16},{4,20},{8,24},{12,28},{16,0},{20,4},{24,8},{28,12},{32,48},... | collective-permute-start | bytes 393224 | tf_op jit(solution)/shard_map/ppermute | solution.py:501
  40.1 0.9 %collective-permute-done.6.refs_1_ = f32[2,128,128]{2,1,0:T(8,128)S(1)} collective-permute-done((f32[2,128,128]{2,1,0:T(8,128)S(1)}, f32[2,128,128]{2,1,0:T(8,128)S(1)}, u32[]{:S(2)}, u32[]{:S(2)}) %collective-permute-start.6) | collective-permute-done | bytes 131104 | tf_op jit(solution)/shard_map/ppermute | solution.py:501
  41.0 3.8 %collective-permute-done.7.refs_2_ = f32[2,128,128]{2,1,0:T(8,128)S(1)} collective-permute-done((f32[2,128,128]{2,1,0:T(8,128)S(1)}, f32[2,128,128]{2,1,0:T(8,128)S(1)}, u32[]{:S(2)}, u32[]{:S(2)}) %collective-permute-start.7) | collective-permute-done | bytes 131104 | tf_op jit(solution)/shard_map/ppermute | solution.py:501
  45.2 2.4 %collective-permute-start.9 = (f32[4,2,128,128]{3,2,1,0:T(8,128)S(1)}, f32[4,2,128,128]{3,2,1,0:T(8,128)S(1)}, u32[]{:S(2)}, u32[]{:S(2)}) collective-permute-start(f32[4,2,128,128]{3,2,1,0:T(8,128)S(1)} %get-tuple-element.93), channel_id=1, source_target_pairs={{0,4},{4,0},{8,12},{12,8},{16,20},{20,16},{24,28},{28,24},{32,36},... | collective-permute-start | bytes 1572872 | tf_op jit(solution)/shard_map/ppermute | solution.py:525
  47.6 4.1 %block_backward.2 = (f32[4,128,512]{2,1,0:T(8,128)S(1)}, f32[8,128]{1,0:T(8,128)S(1)}) custom-call(s32[1]{0:T(128)} %bitcast.1.place_ref.refs_0_, s32[1]{0:T(128)} %bitcast.side_ref.refs_1_, f32[4,2,128,128]{3,2,1,0:T(8,128)S(1)} %get-tuple-element.97.refs_2_, f32[4,11,128,128]{3,2,1,0:T(8,128)S(1)} %get-tuple-element.80.kept_ref.refs_3_, ...), custom_call_target="tpu_custom_call" | custom-call | tf_op jit(solution)/shard_map/block_backward/pallas_call | solution.py:450
  51.6 3.5 %block_backward.3 = (f32[64,512]{1,0:T(8,128)S(1)}, f32[64,512]{1,0:T(8,128)S(1)}, f32[8,128]{1,0:T(8,128)}, bf16[128,1536]{1,0:T(8,128)(2,1)S(1)}, bf16[128,8]{1,0:T(8,128)(2,1)S(1)}) custom-call(s32[1]{0:T(128)} %bitcast.1.place_ref.refs_0_, s32[1]{0:T(128)} %bitcast.side_ref.refs_1_, f32[4,2,128,128]{3,2,1,0:T(8,128)S(1)} %collective-permute-done.9.refs_2_, ...), custom_call_target="tpu_custom_call" | custom-call | tf_op jit(solution)/shard_map/block_backward/pallas_call | solution.py:450
  55.1 1.3 %collective-permute-start.10 = (f32[64,512]{1,0:T(8,128)S(1)}, f32[64,512]{1,0:T(8,128)S(1)}, u32[]{:S(2)}, u32[]{:S(2)}) collective-permute-start(f32[64,512]{1,0:T(8,128)S(1)} %get-tuple-element.106), channel_id=1, source_target_pairs={{0,1},{1,2},{2,3},{3,0},{4,5},{5,6},{6,7},{7,4},{8,9},{9,10},{10,1... | collective-permute-start | bytes 393224 | tf_op jit(solution)/shard_map/ppermute | solution.py:531
  56.4 1.4 %collective-permute-start.11 = (f32[64,512]{1,0:T(8,128)S(1)}, f32[64,512]{1,0:T(8,128)S(1)}, u32[]{:S(2)}, u32[]{:S(2)}) collective-permute-start(f32[64,512]{1,0:T(8,128)S(1)} %get-tuple-element.107), channel_id=1, source_target_pairs={{1,0},{2,1},{3,2},{0,3},{5,4},{6,5},{7,6},{4,7},{9,8},{10,9},{11,1... | collective-permute-start | bytes 393224 | tf_op jit(solution)/shard_map/ppermute | solution.py:531
  57.9 1.2 %near_chunks.1 = (f32[128,512]{1,0:T(8,128)S(1)}, f32[128,512]{1,0:T(8,128)S(1)}) custom-call(s32[1]{0:T(128)} %bitcast.side_ref.refs_1_, bf16[128,1536]{1,0:T(8,128)(2,1)S(1)} %get-tuple-element.114.grads_ref, bf16[128,8]{1,0:T(8,128)(2,1)S(1)} %get-tuple-element.103.db_ref, f32[4,128,512]{2,1,0:T(8,128)S(1)} %get-tuple-element.100.refs_8_.before_ref, ...), custom_call_target="tpu_custom_call" | custom-call | tf_op jit(solution)/shard_map/near_chunks/pallas_call | solution.py:461
  59.1 2.5 %collective-permute-done.10.up_ref = f32[64,512]{1,0:T(8,128)S(1)} collective-permute-done((f32[64,512]{1,0:T(8,128)S(1)}, f32[64,512]{1,0:T(8,128)S(1)}, u32[]{:S(2)}, u32[]{:S(2)}) %collective-permute-start.10) | collective-permute-done | bytes 131104 | tf_op jit(solution)/shard_map/ppermute | solution.py:531
  61.6 1.0 %collective-permute-start.12 = (f32[128,512]{1,0:T(8,128)S(1)}, f32[128,512]{1,0:T(8,128)S(1)}, u32[]{:S(2)}, u32[]{:S(2)}) collective-permute-start(f32[128,512]{1,0:T(8,128)S(1)} %get-tuple-element.115), channel_id=1, source_target_pairs={{0,1},{1,2},{2,3},{3,0},{4,5},{5,6},{6,7},{7,4},{8,9},{9,10},{10,1... | collective-permute-start | bytes 786440 | tf_op jit(solution)/shard_map/ppermute | solution.py:535
  62.6 1.8 %collective-permute-start.13 = (f32[128,512]{1,0:T(8,128)S(1)}, f32[128,512]{1,0:T(8,128)S(1)}, u32[]{:S(2)}, u32[]{:S(2)}) collective-permute-start(f32[128,512]{1,0:T(8,128)S(1)} %get-tuple-element.116), channel_id=1, source_target_pairs={{1,0},{2,1},{3,2},{0,3},{5,4},{6,5},{7,6},{4,7},{9,8},{10,9},{11,1... | collective-permute-start | bytes 786440 | tf_op jit(solution)/shard_map/ppermute | solution.py:535
  65.1 4.9 %collective-permute-done.12 = f32[128,512]{1,0:T(8,128)S(1)} collective-permute-done((f32[128,512]{1,0:T(8,128)S(1)}, f32[128,512]{1,0:T(8,128)S(1)}, u32[]{:S(2)}, u32[]{:S(2)}) %collective-permute-start.12) | collective-permute-done | bytes 262176 | tf_op jit(solution)/shard_map/ppermute | solution.py:535
  (20 shorter events, 6.0 us)
Async XLA Ops:
  8.4 7.1 %collective-permute-start = (f32[4,3,128,128]{3,2,1,0:T(8,128)S(1)}, f32[4,3,128,128]{3,2,1,0:T(8,128)S(1)}, u32[]{:S(2)}, u32[]{:S(2)}) collective-permute-start(f32[4,3,128,128]{3,2,1,0:T(8,128)S(1)} %get-tuple-element.69), channel_id=1, source_target_pairs={{0,4},{4,0},{8,12},{12,8},{16,20},{20,16},{24,28},{28,24},{32,36},... | collective-permute-start | bytes 2359304 | tf_op jit(solution)/shard_map/ppermute | solution.py:482
  16.1 7.8 %collective-permute-start.1 = (f32[3,128,128]{2,1,0:T(8,128)S(1)}, f32[3,128,128]{2,1,0:T(8,128)S(1)}, u32[]{:S(2)}, u32[]{:S(2)}) collective-permute-start(f32[3,128,128]{2,1,0:T(8,128)S(1)} %get-tuple-element.77), channel_id=1, source_target_pairs={{0,8},{4,12},{8,16},{12,20},{16,24},{20,28},{24,0},{28,4},{32,40},... | collective-permute-start | bytes 589832 | tf_op jit(solution)/shard_map/ppermute | solution.py:501
  17.5 11.7 %collective-permute-start.2 = (f32[3,128,128]{2,1,0:T(8,128)S(1)}, f32[3,128,128]{2,1,0:T(8,128)S(1)}, u32[]{:S(2)}, u32[]{:S(2)}) collective-permute-start(f32[3,128,128]{2,1,0:T(8,128)S(1)} %get-tuple-element.78), channel_id=1, source_target_pairs={{0,16},{4,20},{8,24},{12,28},{16,0},{20,4},{24,8},{28,12},{32,48},... | collective-permute-start | bytes 589832 | tf_op jit(solution)/shard_map/ppermute | solution.py:501
  19.9 9.3 %collective-permute-start.3 = (f32[3,128,128]{2,1,0:T(8,128)S(1)}, f32[3,128,128]{2,1,0:T(8,128)S(1)}, u32[]{:S(2)}, u32[]{:S(2)}) collective-permute-start(f32[3,128,128]{2,1,0:T(8,128)S(1)} %get-tuple-element.79), channel_id=1, source_target_pairs={{0,24},{4,28},{8,0},{12,4},{16,8},{20,12},{24,16},{28,20},{32,56},... | collective-permute-start | bytes 589832 | tf_op jit(solution)/shard_map/ppermute | solution.py:501
  21.8 25.8 %copy-start = (bf16[2048,8]{0,1:T(8,128)(2,1)S(1)}, bf16[2048,8]{0,1:T(8,128)(2,1)}, u32[]{:S(2)}) copy-start(bf16[2048,8]{0,1:T(8,128)(2,1)} %param.14) | copy-start | bytes 98308
  29.8 5.5 %collective-permute-start.4 = (f32[128,128]{1,0:T(8,128)S(1)}, f32[128,128]{1,0:T(8,128)S(1)}, u32[]{:S(2)}, u32[]{:S(2)}) collective-permute-start(f32[128,128]{1,0:T(8,128)S(1)} %get-tuple-element.87), channel_id=1, source_target_pairs={{0,32},{4,36},{8,40},{12,44},{16,48},{20,52},{24,56},{28,60},{32,6... | collective-permute-start | bytes 196616 | tf_op jit(solution)/shard_map/ppermute | solution.py:517
  31.5 3.8 %collective-permute-start.5 = (f32[128,128]{1,0:T(8,128)S(1)}, f32[128,128]{1,0:T(8,128)S(1)}, u32[]{:S(2)}, u32[]{:S(2)}) collective-permute-start(f32[128,128]{1,0:T(8,128)S(1)} %get-tuple-element.88), channel_id=1, source_target_pairs={{32,0},{36,4},{40,8},{44,12},{48,16},{52,20},{56,24},{60,28},{64,3... | collective-permute-start | bytes 196616 | tf_op jit(solution)/shard_map/ppermute | solution.py:518
  35.9 5.1 %collective-permute-start.6 = (f32[2,128,128]{2,1,0:T(8,128)S(1)}, f32[2,128,128]{2,1,0:T(8,128)S(1)}, u32[]{:S(2)}, u32[]{:S(2)}) collective-permute-start(f32[2,128,128]{2,1,0:T(8,128)S(1)} %get-tuple-element.90), channel_id=1, source_target_pairs={{0,8},{4,12},{8,16},{12,20},{16,24},{20,28},{24,0},{28,4},{32,40},... | collective-permute-start | bytes 393224 | tf_op jit(solution)/shard_map/ppermute | solution.py:501
  36.6 8.2 %collective-permute-start.7 = (f32[2,128,128]{2,1,0:T(8,128)S(1)}, f32[2,128,128]{2,1,0:T(8,128)S(1)}, u32[]{:S(2)}, u32[]{:S(2)}) collective-permute-start(f32[2,128,128]{2,1,0:T(8,128)S(1)} %get-tuple-element.91), channel_id=1, source_target_pairs={{0,16},{4,20},{8,24},{12,28},{16,0},{20,4},{24,8},{28,12},{32,48},... | collective-permute-start | bytes 393224 | tf_op jit(solution)/shard_map/ppermute | solution.py:501
  39.8 5.0 %collective-permute-start.8 = (f32[2,128,128]{2,1,0:T(8,128)S(1)}, f32[2,128,128]{2,1,0:T(8,128)S(1)}, u32[]{:S(2)}, u32[]{:S(2)}) collective-permute-start(f32[2,128,128]{2,1,0:T(8,128)S(1)} %get-tuple-element.92), channel_id=1, source_target_pairs={{0,24},{4,28},{8,0},{12,4},{16,8},{20,12},{24,16},{28,20},{32,56},... | collective-permute-start | bytes 393224 | tf_op jit(solution)/shard_map/ppermute | solution.py:501
  45.2 6.4 %collective-permute-start.9 = (f32[4,2,128,128]{3,2,1,0:T(8,128)S(1)}, f32[4,2,128,128]{3,2,1,0:T(8,128)S(1)}, u32[]{:S(2)}, u32[]{:S(2)}) collective-permute-start(f32[4,2,128,128]{3,2,1,0:T(8,128)S(1)} %get-tuple-element.93), channel_id=1, source_target_pairs={{0,4},{4,0},{8,12},{12,8},{16,20},{20,16},{24,28},{28,24},{32,36},... | collective-permute-start | bytes 1572872 | tf_op jit(solution)/shard_map/ppermute | solution.py:525
  55.1 6.5 %collective-permute-start.10 = (f32[64,512]{1,0:T(8,128)S(1)}, f32[64,512]{1,0:T(8,128)S(1)}, u32[]{:S(2)}, u32[]{:S(2)}) collective-permute-start(f32[64,512]{1,0:T(8,128)S(1)} %get-tuple-element.106), channel_id=1, source_target_pairs={{0,1},{1,2},{2,3},{3,0},{4,5},{5,6},{6,7},{7,4},{8,9},{9,10},{10,1... | collective-permute-start | bytes 393224 | tf_op jit(solution)/shard_map/ppermute | solution.py:531
  56.4 5.2 %collective-permute-start.11 = (f32[64,512]{1,0:T(8,128)S(1)}, f32[64,512]{1,0:T(8,128)S(1)}, u32[]{:S(2)}, u32[]{:S(2)}) collective-permute-start(f32[64,512]{1,0:T(8,128)S(1)} %get-tuple-element.107), channel_id=1, source_target_pairs={{1,0},{2,1},{3,2},{0,3},{5,4},{6,5},{7,6},{4,7},{9,8},{10,9},{11,1... | collective-permute-start | bytes 393224 | tf_op jit(solution)/shard_map/ppermute | solution.py:531
  61.6 8.4 %collective-permute-start.12 = (f32[128,512]{1,0:T(8,128)S(1)}, f32[128,512]{1,0:T(8,128)S(1)}, u32[]{:S(2)}, u32[]{:S(2)}) collective-permute-start(f32[128,512]{1,0:T(8,128)S(1)} %get-tuple-element.115), channel_id=1, source_target_pairs={{0,1},{1,2},{2,3},{3,0},{4,5},{5,6},{6,7},{7,4},{8,9},{9,10},{10,1... | collective-permute-start | bytes 786440 | tf_op jit(solution)/shard_map/ppermute | solution.py:535
  62.6 7.4 %collective-permute-start.13 = (f32[128,512]{1,0:T(8,128)S(1)}, f32[128,512]{1,0:T(8,128)S(1)}, u32[]{:S(2)}, u32[]{:S(2)}) collective-permute-start(f32[128,512]{1,0:T(8,128)S(1)} %get-tuple-element.116), channel_id=1, source_target_pairs={{1,0},{2,1},{3,2},{0,3},{5,4},{6,5},{7,6},{4,7},{9,8},{10,9},{11,1... | collective-permute-start | bytes 786440 | tf_op jit(solution)/shard_map/ppermute | solution.py:535

commit v11 on v10

--- a/solution.py
+++ b/solution.py
@@ -283,11 +283,15 @@
     return piece + dot(grads[:, 2 * n:], wv_ref[at, :], NT) + dot(db, wb_ref[:, at])
 
 
-def chunk_kernel(distances, side_ref, grads_ref, db_ref, before_ref, wb_ref, wkq_ref, wv_ref, *out_refs):
-    for d, out_ref in zip(distances, out_refs):
+def chunk_kernel(distances, side_ref, wb_ref, *refs):
+    parts = (refs[:4], refs[4:8])
+    for d, out_ref in zip(distances, refs[8:]):
         side = (side_ref[0] + d) & (SIDES - 1)
-        piece = back_project(side, grads_ref[...], db_ref[...], wkq_ref, wv_ref, wb_ref, out_ref.shape[1])
-        out_ref[...] = before_ref[d] + piece
+        pieces = [
+            back_project(side, grads_ref[...], db_ref[...], wkq_ref, wv_ref, wb_ref, out_ref.shape[1])
+            for grads_ref, db_ref, wkq_ref, wv_ref in parts
+        ]
+        out_ref[...] = pieces[0] + pieces[1]
 
 
 def relay_kernel(next_ref, last_ref, up_ref, down_ref, next_out, last_out):
@@ -316,7 +320,7 @@
         before_ref, gd_before_ref, up_ref, down_ref, gd_ref, grads_ref, db_ref = refs
         wide = up_ref.shape[-1]
     else:
-        total_ref, gd_ref = refs
+        total_ref, gd_ref, grads_ref, db_ref = refs
         wide = total_ref.shape[-1]
     keep0 = (place_ref[0] & 1) * GROUP
     head0 = GROUP - keep0 if chained else keep0
@@ -370,15 +374,14 @@
     grads = jnp.concatenate(gqs + gks + gvs, axis=1)
     db = dball.astype(BF16)
     project = lambda d: back_project((side + d) & (SIDES - 1), grads, db, wkq_ref, wv_ref, wb_ref, wide)
+    grads_ref[...] = grads
+    db_ref[...] = db
     if chained:
-        far = before_ref[2] + project(2)
+        far = before_ref[...] + project(2)
         up_ref[...] = far[:HALF]
         down_ref[...] = far[HALF:]
-        grads_ref[...] = grads
-        db_ref[...] = db
     else:
-        for d in range(SIDES):
-            total_ref[d] = project(d)
+        total_ref[...] = project(2)
     eye = jnp.where(ti == si, 1.0, 0.0)
     terms = jnp.concatenate([cterm, fterm, eterm], axis=0)
     top = terms.astype(BF16)
@@ -443,10 +446,8 @@
 def run_backward(place, side, back, kept, early, beta_t, w_both, w_value, before):
     heads, width = beta_t.shape
     wide = width // SIDES
-    if before:
-        out_shape = [shape(HALF, wide)] * 2 + [shape(heads, W), jax.ShapeDtypeStruct((W, 3 * GROUP * W), BF16), jax.ShapeDtypeStruct((W, heads), BF16)]
-    else:
-        out_shape = [shape(SIDES, W, wide), shape(heads, W)]
+    out_shape = [shape(HALF, wide)] * 2 if before else [shape(W, wide)]
+    out_shape += [shape(heads, W), jax.ShapeDtypeStruct((W, 3 * GROUP * W), BF16), jax.ShapeDtypeStruct((W, heads), BF16)]
     return pl.pallas_call(
         partial(second_kernel, bool(before)),
         in_specs=[SMEM] * 2 + [VMEM] * 6 + [VMEM] * len(before),
@@ -457,15 +458,16 @@
     )(place, side, back, kept, early, beta_t, w_both, w_value, *before)
 
 
-def run_chunk(distances, side, grads, db, before, beta_t, w_both, w_value):
+def run_chunk(distances, side, beta_t, first, second):
+    width = beta_t.shape[1]
     return pl.pallas_call(
         partial(chunk_kernel, distances),
-        in_specs=[SMEM] + [VMEM] * 6,
+        in_specs=[SMEM] + [VMEM] * 9,
         out_specs=[VMEM] * len(distances),
-        out_shape=[shape(*before.shape[1:])] * len(distances),
+        out_shape=[shape(W, width // SIDES)] * len(distances),
         compiler_params=pltpu.CompilerParams(vmem_limit_bytes=16 << 20),
         name="near_chunks" if len(distances) > 1 else "own_chunk",
-    )(side, grads, db, before, beta_t, w_both, w_value)
+    )(side, beta_t, *first, *second)
 
 
 def per_device(inputs, grad_out, w_query, w_key, w_value, w_beta, w_out, log_decay, lengths):
@@ -523,15 +525,16 @@
         part_kernel, "chip_part", (place,), (own, other, *along_x(spread)), [shape(GROUP, 2, W, W)] * 2
     )
     other_back = lax.ppermute(give_back, "ctx", pair)
-    before = run_backward(place, side, own_back, own_kept, own_early, beta_t, keep_w, keep_v, ())
+    *before, keep_grads, keep_db = run_backward(place, side, own_back, own_kept, own_early, beta_t, keep_w, keep_v, ())
     up, down, grad_d, grads, db = run_backward(place, side, other_back, give_kept, give_early, beta_t, *give_w, before)
     after = [(j, (j + 1) % SIDES) for j in range(SIDES)]
     ahead = [((j + 1) % SIDES, j) for j in range(SIDES)]
-    near = run_chunk((1, 3), side, grads, db, before[0], beta_t, *give_w)
+    kept_part = (keep_grads, keep_db, keep_w, keep_v)
+    near = run_chunk((1, 3), side, beta_t, kept_part, (grads, db, *give_w))
     halfway = (*near, lax.ppermute(up, "head", after), lax.ppermute(down, "head", ahead))
     near = call(relay_kernel, "relay", (), lax.optimization_barrier(halfway), [shape(*near[0].shape)] * 2)
     *near, grads = lax.optimization_barrier((*near, grads))
-    (total,) = run_chunk((0,), side, grads, db, before[0], beta_t, *give_w)
+    (total,) = run_chunk((0,), side, beta_t, kept_part, (grads, db, *give_w))
     total = total + lax.ppermute(near[0], "head", after) + lax.ppermute(near[1], "head", ahead)
     return (total.astype(BF16), grad_d.T)
 

time: 71 us -> 69.9 us (0.985)
  waiting for transfers between devices: 20.5 us -> 18.9 us
    pallas_call x2, Pallas kernels: 1.9 us -> 3.45 us  [run_chunk(): pl.pallas_call(partial(chunk_kernel, distances), in_specs=[SMEM] + [VMEM]...]
    pallas_call x2, Pallas kernels: 7.53 us -> 6.38 us  [run_backward(): pl.pallas_call(partial(second_kernel, bool(before)), in_specs=[SMEM] * 2...]
    ppermute x1, waiting for transfers between devices: 2.49 us -> 1.44 us  [per_device(): lax.ppermute(up, 'head', after)]
  transfers between devices with their start and end apart: 14 -> 14, of which waited for: 7 -> 7; matrix products, arithmetic and copies ran while one was open for 0% -> 0% of each run, Pallas kernels for 18% -> 19%
where the time goes in v11:
time: 69.9 us; the launch traced here: 69.5 us
  Pallas kernels  26.8 us (38%)
  starting transfers between devices  22.4 us (32%)
  waiting for transfers between devices  18.9 us (27%)
  between operations  0.73 us (1%)
  other arithmetic  0.71 us (1%)
    ppermute x6, waiting for transfers between devices, along_x(): got[d] = lax.ppermute(parts[d], 'ctx', moves)  11.4 us
    ppermute x6, starting transfers between devices, along_x(): got[d] = lax.ppermute(parts[d], 'ctx', moves)  9.17 us
    pallas_call x1, Pallas kernels, run_give(): pl.pallas_call(give_kernel, in_specs=[SMEM] * 2 + [HBM] * 9, out_specs=[V...  7.8 us
    pallas_call x2, Pallas kernels, run_backward(): pl.pallas_call(partial(second_kernel, bool(before)), in_specs=[SMEM] * 2...  6.38 us
    pallas_call x1, Pallas kernels, run_keep(): pl.pallas_call(keep_kernel, in_specs=[SMEM] + [VMEM] * 8 + [HBM] * 2, out...  5.61 us
    ppermute x1, waiting for transfers between devices, per_device(): lax.ppermute(near[0], 'head', after)  4.42 us
    pallas_call x2, Pallas kernels, run_chunk(): pl.pallas_call(partial(chunk_kernel, distances), in_specs=[SMEM] + [VMEM]...  3.45 us
    ppermute x1, starting transfers between devices, per_device(): other_back = lax.ppermute(give_back, 'ctx', pair)  2.37 us
  transfers between devices with their start and end apart: 14, of which 7 were waited for; matrix products, arithmetic and copies ran while one was open for 0% of the time, Pallas kernels for 19%

profile of v11, /device:TPU:1, one launch (start us, length us, event | category | flops | bytes accessed | tf_op | source)
XLA Modules:
  0.0 69.5 jit_solution(12354527327381966260)
XLA Ops:
  0.6 7.8 %block_forward_give.1 = (f32[4,3,128,128]{3,2,1,0:T(8,128)S(1)}, f32[4,11,128,128]{3,2,1,0:T(8,128)S(1)}, bf16[128,2048]{1,0:T(8,128)(2,1)S(1)}, bf16[128,2048]{...) custom-call(s32[1]{0:T(128)} %bitcast.2.place_ref.refs_0_, ...), custom_call_target="tpu_custom_call" | custom-call | tf_op jit(solution)/shard_map/block_forward_give/pallas_call | solution.py:417
  8.4 1.5 %collective-permute-start = (f32[4,3,128,128]{3,2,1,0:T(8,128)S(1)}, f32[4,3,128,128]{3,2,1,0:T(8,128)S(1)}, u32[]{:S(2)}, u32[]{:S(2)}) collective-permute-start(f32[4,3,128,128]{3,2,1,0:T(8,128)S(1)} %get-tuple-element.71), channel_id=1, source_target_pairs={{0,4},{4,0},{8,12},{12,8},{16,20},{20,16},{24,28},{28,24},{32,36},... | collective-permute-start | bytes 2359304 | tf_op jit(solution)/shard_map/ppermute | solution.py:484
  9.9 5.6 %block_forward_keep.1 = (f32[4,3,128,128]{3,2,1,0:T(8,128)S(1)}, f32[4,11,128,128]{3,2,1,0:T(8,128)S(1)}, bf16[2048,512]{1,0:T(8,128)(2,1)S(1)}) custom-call(s32[1]{0:T(128)} %bitcast.2.place_ref.refs_0_, bf16[128,2048]{1,0:T(8,128)(2,1)S(1)} %get-tuple-element.62.x_ref, bf16[128,2048]{1,0:T(8,128)(2,1)S(1)} %get-tuple-element.63.go_ref, ...), custom_call_target="tpu_custom_call" | custom-call | tf_op jit(solution)/shard_map/block_forward_keep/pallas_call | solution.py:434
  16.1 1.4 %collective-permute-start.1 = (f32[3,128,128]{2,1,0:T(8,128)S(1)}, f32[3,128,128]{2,1,0:T(8,128)S(1)}, u32[]{:S(2)}, u32[]{:S(2)}) collective-permute-start(f32[3,128,128]{2,1,0:T(8,128)S(1)} %get-tuple-element.79), channel_id=1, source_target_pairs={{0,8},{4,12},{8,16},{12,20},{16,24},{20,28},{24,0},{28,4},{32,40},... | collective-permute-start | bytes 589832 | tf_op jit(solution)/shard_map/ppermute | solution.py:503
  17.5 2.4 %collective-permute-start.2 = (f32[3,128,128]{2,1,0:T(8,128)S(1)}, f32[3,128,128]{2,1,0:T(8,128)S(1)}, u32[]{:S(2)}, u32[]{:S(2)}) collective-permute-start(f32[3,128,128]{2,1,0:T(8,128)S(1)} %get-tuple-element.80), channel_id=1, source_target_pairs={{0,16},{4,20},{8,24},{12,28},{16,0},{20,4},{24,8},{28,12},{32,48},... | collective-permute-start | bytes 589832 | tf_op jit(solution)/shard_map/ppermute | solution.py:503
  19.9 1.2 %collective-permute-start.3 = (f32[3,128,128]{2,1,0:T(8,128)S(1)}, f32[3,128,128]{2,1,0:T(8,128)S(1)}, u32[]{:S(2)}, u32[]{:S(2)}) collective-permute-start(f32[3,128,128]{2,1,0:T(8,128)S(1)} %get-tuple-element.81), channel_id=1, source_target_pairs={{0,24},{4,28},{8,0},{12,4},{16,8},{20,12},{24,16},{28,20},{32,56},... | collective-permute-start | bytes 589832 | tf_op jit(solution)/shard_map/ppermute | solution.py:503
  22.5 1.4 %collective-permute-done.1.refs_1_ = f32[3,128,128]{2,1,0:T(8,128)S(1)} collective-permute-done((f32[3,128,128]{2,1,0:T(8,128)S(1)}, f32[3,128,128]{2,1,0:T(8,128)S(1)}, u32[]{:S(2)}, u32[]{:S(2)}) %collective-permute-start.1) | collective-permute-done | bytes 196640 | tf_op jit(solution)/shard_map/ppermute | solution.py:503
  23.9 5.3 %collective-permute-done.2.refs_2_ = f32[3,128,128]{2,1,0:T(8,128)S(1)} collective-permute-done((f32[3,128,128]{2,1,0:T(8,128)S(1)}, f32[3,128,128]{2,1,0:T(8,128)S(1)}, u32[]{:S(2)}, u32[]{:S(2)}) %collective-permute-start.2) | collective-permute-done | bytes 196640 | tf_op jit(solution)/shard_map/ppermute | solution.py:503
  29.8 1.7 %collective-permute-start.4 = (f32[128,128]{1,0:T(8,128)S(1)}, f32[128,128]{1,0:T(8,128)S(1)}, u32[]{:S(2)}, u32[]{:S(2)}) collective-permute-start(f32[128,128]{1,0:T(8,128)S(1)} %get-tuple-element.89), channel_id=1, source_target_pairs={{0,32},{4,36},{8,40},{12,44},{16,48},{20,52},{24,56},{28,60},{32,6... | collective-permute-start | bytes 196616 | tf_op jit(solution)/shard_map/ppermute | solution.py:519
  31.5 2.2 %collective-permute-start.5 = (f32[128,128]{1,0:T(8,128)S(1)}, f32[128,128]{1,0:T(8,128)S(1)}, u32[]{:S(2)}, u32[]{:S(2)}) collective-permute-start(f32[128,128]{1,0:T(8,128)S(1)} %get-tuple-element.90), channel_id=1, source_target_pairs={{32,0},{36,4},{40,8},{44,12},{48,16},{52,20},{56,24},{60,28},{64,3... | collective-permute-start | bytes 196616 | tf_op jit(solution)/shard_map/ppermute | solution.py:520
  33.7 1.6 %collective-permute-done.4.s_ref = f32[128,128]{1,0:T(8,128)S(1)} collective-permute-done((f32[128,128]{1,0:T(8,128)S(1)}, f32[128,128]{1,0:T(8,128)S(1)}, u32[]{:S(2)}, u32[]{:S(2)}) %collective-permute-start.4) | collective-permute-done | bytes 65568 | tf_op jit(solution)/shard_map/ppermute | solution.py:519
  36.6 3.2 %collective-permute-start.7 = (f32[2,128,128]{2,1,0:T(8,128)S(1)}, f32[2,128,128]{2,1,0:T(8,128)S(1)}, u32[]{:S(2)}, u32[]{:S(2)}) collective-permute-start(f32[2,128,128]{2,1,0:T(8,128)S(1)} %get-tuple-element.93), channel_id=1, source_target_pairs={{0,16},{4,20},{8,24},{12,28},{16,0},{20,4},{24,8},{28,12},{32,48},... | collective-permute-start | bytes 393224 | tf_op jit(solution)/shard_map/ppermute | solution.py:503
  40.9 3.8 %collective-permute-done.7.refs_2_ = f32[2,128,128]{2,1,0:T(8,128)S(1)} collective-permute-done((f32[2,128,128]{2,1,0:T(8,128)S(1)}, f32[2,128,128]{2,1,0:T(8,128)S(1)}, u32[]{:S(2)}, u32[]{:S(2)}) %collective-permute-start.7) | collective-permute-done | bytes 131104 | tf_op jit(solution)/shard_map/ppermute | solution.py:503
  45.2 2.4 %collective-permute-start.9 = (f32[4,2,128,128]{3,2,1,0:T(8,128)S(1)}, f32[4,2,128,128]{3,2,1,0:T(8,128)S(1)}, u32[]{:S(2)}, u32[]{:S(2)}) collective-permute-start(f32[4,2,128,128]{3,2,1,0:T(8,128)S(1)} %get-tuple-element.100), channel_id=1, source_target_pairs={{0,4},{4,0},{8,12},{12,8},{16,20},{20,16},{24,28},{28,24},{32,36},... | collective-permute-start | bytes 1572872 | tf_op jit(solution)/shard_map/ppermute | solution.py:527
  47.6 2.9 %block_backward.2 = (f32[128,512]{1,0:T(8,128)S(1)}, f32[8,128]{1,0:T(8,128)S(1)}, bf16[128,1536]{1,0:T(8,128)(2,1)S(1)}, bf16[128,8]{1,0:T(8,128)(2,1)S(1)}) custom-call(s32[1]{0:T(128)} %bitcast.2.place_ref.refs_0_, s32[1]{0:T(128)} %bitcast.side_ref.refs_1_, f32[4,2,128,128]{3,2,1,0:T(8,128)S(1)} %get-tuple-element.95.refs_2_, ...), custom_call_target="tpu_custom_call" | custom-call | tf_op jit(solution)/shard_map/block_backward/pallas_call | solution.py:451
  50.5 3.5 %block_backward.3 = (f32[64,512]{1,0:T(8,128)S(1)}, f32[64,512]{1,0:T(8,128)S(1)}, f32[8,128]{1,0:T(8,128)}, bf16[128,1536]{1,0:T(8,128)(2,1)S(1)}, bf16[128,8]{1,0:T(8,128)(2,1)S(1)}) custom-call(s32[1]{0:T(128)} %bitcast.2.place_ref.refs_0_, s32[1]{0:T(128)} %bitcast.side_ref.refs_1_, f32[4,2,128,128]{3,2,1,0:T(8,128)S(1)} %collective-permute-done.9.refs_2_, ...), custom_call_target="tpu_custom_call" | custom-call | tf_op jit(solution)/shard_map/block_backward/pallas_call | solution.py:451
  53.9 1.3 %collective-permute-start.10 = (f32[64,512]{1,0:T(8,128)S(1)}, f32[64,512]{1,0:T(8,128)S(1)}, u32[]{:S(2)}, u32[]{:S(2)}) collective-permute-start(f32[64,512]{1,0:T(8,128)S(1)} %get-tuple-element.110), channel_id=1, source_target_pairs={{0,1},{1,2},{2,3},{3,0},{4,5},{5,6},{6,7},{7,4},{8,9},{9,10},{10,1... | collective-permute-start | bytes 393224 | tf_op jit(solution)/shard_map/ppermute | solution.py:534
  55.2 1.4 %collective-permute-start.11 = (f32[64,512]{1,0:T(8,128)S(1)}, f32[64,512]{1,0:T(8,128)S(1)}, u32[]{:S(2)}, u32[]{:S(2)}) collective-permute-start(f32[64,512]{1,0:T(8,128)S(1)} %get-tuple-element.111), channel_id=1, source_target_pairs={{1,0},{2,1},{3,2},{0,3},{5,4},{6,5},{7,6},{4,7},{9,8},{10,9},{11,1... | collective-permute-start | bytes 393224 | tf_op jit(solution)/shard_map/ppermute | solution.py:534
  56.7 2.3 %near_chunks.1 = (f32[128,512]{1,0:T(8,128)S(1)}, f32[128,512]{1,0:T(8,128)S(1)}) custom-call(s32[1]{0:T(128)} %bitcast.side_ref.refs_1_, bf16[8,2048]{1,0:T(8,128)(2,1)S(1)} %bitcast.8, bf16[128,1536]{1,0:T(8,128)(2,1)S(1)} %get-tuple-element.98.refs_0_, bf16[128,8]{1,0:T(8,128)(2,1)S(1)} %get-tuple-element.99.refs_1_, ...), custom_call_target="tpu_custom_call" | custom-call | tf_op jit(solution)/shard_map/near_chunks/pallas_call | solution.py:463
  59.0 1.4 %collective-permute-done.10.up_ref = f32[64,512]{1,0:T(8,128)S(1)} collective-permute-done((f32[64,512]{1,0:T(8,128)S(1)}, f32[64,512]{1,0:T(8,128)S(1)}, u32[]{:S(2)}, u32[]{:S(2)}) %collective-permute-start.10) | collective-permute-done | bytes 131104 | tf_op jit(solution)/shard_map/ppermute | solution.py:534
  60.5 1.0 %collective-permute-start.12 = (f32[128,512]{1,0:T(8,128)S(1)}, f32[128,512]{1,0:T(8,128)S(1)}, u32[]{:S(2)}, u32[]{:S(2)}) collective-permute-start(f32[128,512]{1,0:T(8,128)S(1)} %get-tuple-element.119), channel_id=1, source_target_pairs={{0,1},{1,2},{2,3},{3,0},{4,5},{5,6},{6,7},{7,4},{8,9},{9,10},{10,1... | collective-permute-start | bytes 786440 | tf_op jit(solution)/shard_map/ppermute | solution.py:538
  61.4 1.8 %collective-permute-start.13 = (f32[128,512]{1,0:T(8,128)S(1)}, f32[128,512]{1,0:T(8,128)S(1)}, u32[]{:S(2)}, u32[]{:S(2)}) collective-permute-start(f32[128,512]{1,0:T(8,128)S(1)} %get-tuple-element.120), channel_id=1, source_target_pairs={{1,0},{2,1},{3,2},{0,3},{5,4},{6,5},{7,6},{4,7},{9,8},{10,9},{11,1... | collective-permute-start | bytes 786440 | tf_op jit(solution)/shard_map/ppermute | solution.py:538
  63.2 1.2 %own_chunk.1 = f32[128,512]{1,0:T(8,128)S(1)} custom-call(s32[1]{0:T(128)} %bitcast.side_ref.refs_1_, bf16[8,2048]{1,0:T(8,128)(2,1)S(1)} %bitcast.9, bf16[128,1536]{1,0:T(8,128)(2,1)S(1)} %get-tuple-element.98.refs_0_, bf16[128,8]{1,0:T(8,128)(2,1)S(1)} %get-tuple-element.99.refs_1_, bf16[2,2048,512]{2,1,0:T(8,128)(2,1)S(1)} %get-tuple-element.69.wkq_ref.refs_6_.refs_2_, ...), custom_call_target="tpu_custom_call" | custom-call | tf_op jit(solution)/shard_map/own_chunk/pallas_call | solution.py:463
  64.4 4.4 %collective-permute-done.12 = f32[128,512]{1,0:T(8,128)S(1)} collective-permute-done((f32[128,512]{1,0:T(8,128)S(1)}, f32[128,512]{1,0:T(8,128)S(1)}, u32[]{:S(2)}, u32[]{:S(2)}) %collective-permute-start.12) | collective-permute-done | bytes 262176 | tf_op jit(solution)/shard_map/ppermute | solution.py:538
  (20 shorter events, 6.2 us)
Async XLA Ops:
  8.4 7.1 %collective-permute-start = (f32[4,3,128,128]{3,2,1,0:T(8,128)S(1)}, f32[4,3,128,128]{3,2,1,0:T(8,128)S(1)}, u32[]{:S(2)}, u32[]{:S(2)}) collective-permute-start(f32[4,3,128,128]{3,2,1,0:T(8,128)S(1)} %get-tuple-element.71), channel_id=1, source_target_pairs={{0,4},{4,0},{8,12},{12,8},{16,20},{20,16},{24,28},{28,24},{32,36},... | collective-permute-start | bytes 2359304 | tf_op jit(solution)/shard_map/ppermute | solution.py:484
  16.1 7.8 %collective-permute-start.1 = (f32[3,128,128]{2,1,0:T(8,128)S(1)}, f32[3,128,128]{2,1,0:T(8,128)S(1)}, u32[]{:S(2)}, u32[]{:S(2)}) collective-permute-start(f32[3,128,128]{2,1,0:T(8,128)S(1)} %get-tuple-element.79), channel_id=1, source_target_pairs={{0,8},{4,12},{8,16},{12,20},{16,24},{20,28},{24,0},{28,4},{32,40},... | collective-permute-start | bytes 589832 | tf_op jit(solution)/shard_map/ppermute | solution.py:503
  17.5 11.7 %collective-permute-start.2 = (f32[3,128,128]{2,1,0:T(8,128)S(1)}, f32[3,128,128]{2,1,0:T(8,128)S(1)}, u32[]{:S(2)}, u32[]{:S(2)}) collective-permute-start(f32[3,128,128]{2,1,0:T(8,128)S(1)} %get-tuple-element.80), channel_id=1, source_target_pairs={{0,16},{4,20},{8,24},{12,28},{16,0},{20,4},{24,8},{28,12},{32,48},... | collective-permute-start | bytes 589832 | tf_op jit(solution)/shard_map/ppermute | solution.py:503
  19.9 9.3 %collective-permute-start.3 = (f32[3,128,128]{2,1,0:T(8,128)S(1)}, f32[3,128,128]{2,1,0:T(8,128)S(1)}, u32[]{:S(2)}, u32[]{:S(2)}) collective-permute-start(f32[3,128,128]{2,1,0:T(8,128)S(1)} %get-tuple-element.81), channel_id=1, source_target_pairs={{0,24},{4,28},{8,0},{12,4},{16,8},{20,12},{24,16},{28,20},{32,56},... | collective-permute-start | bytes 589832 | tf_op jit(solution)/shard_map/ppermute | solution.py:503
  21.8 25.8 %copy-start = (bf16[2048,8]{0,1:T(8,128)(2,1)S(1)}, bf16[2048,8]{0,1:T(8,128)(2,1)}, u32[]{:S(2)}) copy-start(bf16[2048,8]{0,1:T(8,128)(2,1)} %param.14) | copy-start | bytes 98308
  29.8 5.5 %collective-permute-start.4 = (f32[128,128]{1,0:T(8,128)S(1)}, f32[128,128]{1,0:T(8,128)S(1)}, u32[]{:S(2)}, u32[]{:S(2)}) collective-permute-start(f32[128,128]{1,0:T(8,128)S(1)} %get-tuple-element.89), channel_id=1, source_target_pairs={{0,32},{4,36},{8,40},{12,44},{16,48},{20,52},{24,56},{28,60},{32,6... | collective-permute-start | bytes 196616 | tf_op jit(solution)/shard_map/ppermute | solution.py:519
  31.5 3.8 %collective-permute-start.5 = (f32[128,128]{1,0:T(8,128)S(1)}, f32[128,128]{1,0:T(8,128)S(1)}, u32[]{:S(2)}, u32[]{:S(2)}) collective-permute-start(f32[128,128]{1,0:T(8,128)S(1)} %get-tuple-element.90), channel_id=1, source_target_pairs={{32,0},{36,4},{40,8},{44,12},{48,16},{52,20},{56,24},{60,28},{64,3... | collective-permute-start | bytes 196616 | tf_op jit(solution)/shard_map/ppermute | solution.py:520
  35.8 5.1 %collective-permute-start.6 = (f32[2,128,128]{2,1,0:T(8,128)S(1)}, f32[2,128,128]{2,1,0:T(8,128)S(1)}, u32[]{:S(2)}, u32[]{:S(2)}) collective-permute-start(f32[2,128,128]{2,1,0:T(8,128)S(1)} %get-tuple-element.92), channel_id=1, source_target_pairs={{0,8},{4,12},{8,16},{12,20},{16,24},{20,28},{24,0},{28,4},{32,40},... | collective-permute-start | bytes 393224 | tf_op jit(solution)/shard_map/ppermute | solution.py:503
  36.6 8.2 %collective-permute-start.7 = (f32[2,128,128]{2,1,0:T(8,128)S(1)}, f32[2,128,128]{2,1,0:T(8,128)S(1)}, u32[]{:S(2)}, u32[]{:S(2)}) collective-permute-start(f32[2,128,128]{2,1,0:T(8,128)S(1)} %get-tuple-element.93), channel_id=1, source_target_pairs={{0,16},{4,20},{8,24},{12,28},{16,0},{20,4},{24,8},{28,12},{32,48},... | collective-permute-start | bytes 393224 | tf_op jit(solution)/shard_map/ppermute | solution.py:503
  39.8 5.0 %collective-permute-start.8 = (f32[2,128,128]{2,1,0:T(8,128)S(1)}, f32[2,128,128]{2,1,0:T(8,128)S(1)}, u32[]{:S(2)}, u32[]{:S(2)}) collective-permute-start(f32[2,128,128]{2,1,0:T(8,128)S(1)} %get-tuple-element.94), channel_id=1, source_target_pairs={{0,24},{4,28},{8,0},{12,4},{16,8},{20,12},{24,16},{28,20},{32,56},... | collective-permute-start | bytes 393224 | tf_op jit(solution)/shard_map/ppermute | solution.py:503
  45.2 5.3 %collective-permute-start.9 = (f32[4,2,128,128]{3,2,1,0:T(8,128)S(1)}, f32[4,2,128,128]{3,2,1,0:T(8,128)S(1)}, u32[]{:S(2)}, u32[]{:S(2)}) collective-permute-start(f32[4,2,128,128]{3,2,1,0:T(8,128)S(1)} %get-tuple-element.100), channel_id=1, source_target_pairs={{0,4},{4,0},{8,12},{12,8},{16,20},{20,16},{24,28},{28,24},{32,36},... | collective-permute-start | bytes 1572872 | tf_op jit(solution)/shard_map/ppermute | solution.py:527
  53.9 6.5 %collective-permute-start.10 = (f32[64,512]{1,0:T(8,128)S(1)}, f32[64,512]{1,0:T(8,128)S(1)}, u32[]{:S(2)}, u32[]{:S(2)}) collective-permute-start(f32[64,512]{1,0:T(8,128)S(1)} %get-tuple-element.110), channel_id=1, source_target_pairs={{0,1},{1,2},{2,3},{3,0},{4,5},{5,6},{6,7},{7,4},{8,9},{9,10},{10,1... | collective-permute-start | bytes 393224 | tf_op jit(solution)/shard_map/ppermute | solution.py:534
  55.2 5.2 %collective-permute-start.11 = (f32[64,512]{1,0:T(8,128)S(1)}, f32[64,512]{1,0:T(8,128)S(1)}, u32[]{:S(2)}, u32[]{:S(2)}) collective-permute-start(f32[64,512]{1,0:T(8,128)S(1)} %get-tuple-element.111), channel_id=1, source_target_pairs={{1,0},{2,1},{3,2},{0,3},{5,4},{6,5},{7,6},{4,7},{9,8},{10,9},{11,1... | collective-permute-start | bytes 393224 | tf_op jit(solution)/shard_map/ppermute | solution.py:534
  60.5 8.4 %collective-permute-start.12 = (f32[128,512]{1,0:T(8,128)S(1)}, f32[128,512]{1,0:T(8,128)S(1)}, u32[]{:S(2)}, u32[]{:S(2)}) collective-permute-start(f32[128,512]{1,0:T(8,128)S(1)} %get-tuple-element.119), channel_id=1, source_target_pairs={{0,1},{1,2},{2,3},{3,0},{4,5},{5,6},{6,7},{7,4},{8,9},{9,10},{10,1... | collective-permute-start | bytes 786440 | tf_op jit(solution)/shard_map/ppermute | solution.py:538
  61.4 7.4 %collective-permute-start.13 = (f32[128,512]{1,0:T(8,128)S(1)}, f32[128,512]{1,0:T(8,128)S(1)}, u32[]{:S(2)}, u32[]{:S(2)}) collective-permute-start(f32[128,512]{1,0:T(8,128)S(1)} %get-tuple-element.120), channel_id=1, source_target_pairs={{1,0},{2,1},{3,2},{0,3},{5,4},{6,5},{7,6},{4,7},{9,8},{10,9},{11,1... | collective-permute-start | bytes 786440 | tf_op jit(solution)/shard_map/ppermute | solution.py:538

commit v12 on v11

--- a/solution.py
+++ b/solution.py
@@ -317,17 +317,16 @@
     place_ref, side_ref, back_ref, kept_ref, early_ref, wb_ref, wkq_ref, wv_ref = refs[:8]
     refs = refs[8:]
     if chained:
-        before_ref, gd_before_ref, up_ref, down_ref, gd_ref, grads_ref, db_ref = refs
+        before_ref, up_ref, down_ref, grads_ref, db_ref, pairs_ref, terms_ref = refs
         wide = up_ref.shape[-1]
     else:
-        total_ref, gd_ref, grads_ref, db_ref = refs
+        total_ref, grads_ref, db_ref, pairs_ref, terms_ref = refs
         wide = total_ref.shape[-1]
     keep0 = (place_ref[0] & 1) * GROUP
     head0 = GROUP - keep0 if chained else keep0
     side = side_ref[0]
     ti, si = iotas((W, W))
     strict = ti > si
-    upper = jnp.where(si >= ti, 1.0, 0.0)
     t8, h8 = iotas((W, 8))
     none = jnp.zeros((W, 8), F32)
     heads = range(GROUP)
@@ -342,17 +341,13 @@
     dp = [early_ref[i, 2] - mm3(ds[i][:W], kw[i], NT) for i in heads]
     dkk = [jnp.where(strict, weight[i], 0.0) * da[i] * beta[i] for i in heads]
     dqk = [weight[i] * dp[i] for i in heads]
-    pairs = [halves(dp[i] * pmat[i] + da[i] * wkk[i] * beta[i]) for i in heads]
-    ub = upper.astype(BF16)
     front = [mm3(jnp.concatenate([dqk[i], dkk[i]], axis=0), k[i]) for i in heads]
     under = [mm3(jnp.concatenate([dkk[i], dqk[i]], axis=0), jnp.concatenate([k[i], q[i]], axis=0), TN) for i in heads]
-    across = [dot(ub, high) + dot(ub, low) for high, low in pairs]
     dq_state = [carried[i] * ds[i][:W] for i in heads]
     dr_s = [carried[i] * ds[i][W:] for i in heads]
     total = lambda a: jnp.sum(a, axis=1, keepdims=True)
     known = [total(dr_s[i] * k[i]) for i in heads]
     dbeta = [total(dr[i] * v[i] + da[i] * wkk[i]) - known[i] for i in heads]
-    evec = [total(jnp.where(strict, across[i], 0.0)) for i in heads]
     fvec = [total(ug[i] * k[i]) for i in heads]
     cvec = [total(dq_state[i] * q[i]) - beta[i] * known[i] for i in heads]
     ends = [carried[i][W - 1:W, :] * jnp.sum(total(g1[i] * s0[i]), axis=0, keepdims=True) for i in heads]
@@ -364,12 +359,12 @@
     gks = [(inv_k[i] * (dk[i] - k[i] * along_k[i])).astype(BF16) for i in heads]
     gqs = [((inv_q[i] * (W ** -0.5)) * (dq[i] - (q[i] * float(W)) * along_q[i])).astype(BF16) for i in heads]
     gvs = [(beta[i] * dr[i]).astype(BF16) for i in heads]
-    cterm, fterm, eterm, dball = none, none, none, none
+    cterm, fterm, dball = none, none, none
     for i in heads:
         here = h8 == head0 + i
         cterm = jnp.where(here, cvec[i], cterm)
         fterm = jnp.where(here, fvec[i], fterm)
-        eterm = jnp.where(here, evec[i], eterm)
+        pairs_ref[i] = dp[i] * pmat[i] + da[i] * wkk[i] * beta[i]
         dball = jnp.where(here, dbeta[i] * beta[i] * (1.0 - beta[i]), dball)
     grads = jnp.concatenate(gqs + gks + gvs, axis=1)
     db = dball.astype(BF16)
@@ -382,13 +377,28 @@
         down_ref[...] = far[HALF:]
     else:
         total_ref[...] = project(2)
-    eye = jnp.where(ti == si, 1.0, 0.0)
-    terms = jnp.concatenate([cterm, fterm, eterm], axis=0)
+    terms_ref[:W] = cterm
+    terms_ref[W:] = fterm
+
+
+def decay_kernel(place_ref, keep_pairs_ref, keep_terms_ref, give_pairs_ref, give_terms_ref, out_ref):
+    keep0 = (place_ref[0] & 1) * GROUP
+    ti, si = iotas((W, W))
+    upper = jnp.where(si >= ti, 1.0, 0.0).astype(BF16)
+    h8 = iotas((W, 8))[1]
+    eterm = jnp.zeros((W, 8), F32)
+    for head0, ref in ((keep0, keep_pairs_ref), (GROUP - keep0, give_pairs_ref)):
+        pairs = [halves(ref[i]) for i in range(GROUP)]
+        across = [dot(upper, high) + dot(upper, low) for high, low in pairs]
+        for i in range(GROUP):
+            evec = jnp.sum(jnp.where(ti > si, across[i], 0.0), axis=1, keepdims=True)
+            eterm = jnp.where(h8 == head0 + i, evec, eterm)
+    terms = jnp.concatenate([keep_terms_ref[...] + give_terms_ref[...], eterm], axis=0)
     top = terms.astype(BF16)
     middle, bottom = halves(terms - top.astype(F32))
-    sums = dot(jnp.concatenate([top, middle, bottom], axis=1), jnp.concatenate([jnp.where(ti >= si, 1.0, 0.0), jnp.where(si > ti, 1.0, 0.0), eye], axis=0).astype(BF16), TN)
-    decays = sums[:8] + sums[8:16] + sums[16:]
-    gd_ref[...] = gd_before_ref[...] + decays if chained else decays
+    reach = [jnp.where(ti >= si, 1.0, 0.0), jnp.where(si > ti, 1.0, 0.0), jnp.where(ti == si, 1.0, 0.0)]
+    sums = dot(jnp.concatenate([top, middle, bottom], axis=1), jnp.concatenate(reach, axis=0).astype(BF16), TN)
+    out_ref[...] = sums[:8] + sums[8:16] + sums[16:]
 
 
 SMEM = pl.BlockSpec(memory_space=pltpu.SMEM)
@@ -447,7 +457,8 @@
     heads, width = beta_t.shape
     wide = width // SIDES
     out_shape = [shape(HALF, wide)] * 2 if before else [shape(W, wide)]
-    out_shape += [shape(heads, W), jax.ShapeDtypeStruct((W, 3 * GROUP * W), BF16), jax.ShapeDtypeStruct((W, heads), BF16)]
+    out_shape += [jax.ShapeDtypeStruct((W, 3 * GROUP * W), BF16), jax.ShapeDtypeStruct((W, heads), BF16)]
+    out_shape += [shape(GROUP, W, W), shape(2 * W, heads)]
     return pl.pallas_call(
         partial(second_kernel, bool(before)),
         in_specs=[SMEM] * 2 + [VMEM] * 6 + [VMEM] * len(before),
@@ -525,15 +536,19 @@
         part_kernel, "chip_part", (place,), (own, other, *along_x(spread)), [shape(GROUP, 2, W, W)] * 2
     )
     other_back = lax.ppermute(give_back, "ctx", pair)
-    *before, keep_grads, keep_db = run_backward(place, side, own_back, own_kept, own_early, beta_t, keep_w, keep_v, ())
-    up, down, grad_d, grads, db = run_backward(place, side, other_back, give_kept, give_early, beta_t, *give_w, before)
+    before, keep_grads, keep_db, *keep_sums = run_backward(place, side, own_back, own_kept, own_early, beta_t, keep_w, keep_v, ())
+    up, down, grads, db, *give_sums = run_backward(
+        place, side, other_back, give_kept, give_early, beta_t, *give_w, (before,)
+    )
     after = [(j, (j + 1) % SIDES) for j in range(SIDES)]
     ahead = [((j + 1) % SIDES, j) for j in range(SIDES)]
     kept_part = (keep_grads, keep_db, keep_w, keep_v)
     near = run_chunk((1, 3), side, beta_t, kept_part, (grads, db, *give_w))
     halfway = (*near, lax.ppermute(up, "head", after), lax.ppermute(down, "head", ahead))
     near = call(relay_kernel, "relay", (), lax.optimization_barrier(halfway), [shape(*near[0].shape)] * 2)
-    *near, grads = lax.optimization_barrier((*near, grads))
+    *near, grads, keep_pairs = lax.optimization_barrier((*near, grads, keep_sums[0]))
+    sums = (keep_pairs, keep_sums[1], *give_sums)
+    (grad_d,) = call(decay_kernel, "decay_sums", (place,), sums, [shape(2 * GROUP, W)])
     (total,) = run_chunk((0,), side, beta_t, kept_part, (grads, db, *give_w))
     total = total + lax.ppermute(near[0], "head", after) + lax.ppermute(near[1], "head", ahead)
     return (total.astype(BF16), grad_d.T)

time: 69.9 us -> 68.9 us (0.986)
  waiting for transfers between devices: 18.9 us -> 17.6 us
    ppermute x1, waiting for transfers between devices: 4.42 us -> 3.18 us  [per_device(): lax.ppermute(near[0], 'head', after)]
    pallas_call x5 -> x6, Pallas kernels: 2.15 us -> 3.39 us  [call(): pl.pallas_call(kernel, in_specs=[SMEM] * len(scalars) + [VMEM] * len(arra...]
    pallas_call x2, Pallas kernels: 6.38 us -> 5.29 us  [run_backward(): pl.pallas_call(partial(second_kernel, bool(before)), in_specs=[SMEM] * 2...]
  transfers between devices with their start and end apart: 14 -> 14, of which waited for: 7 -> 7; matrix products, arithmetic and copies ran while one was open for 0% -> 0% of each run, Pallas kernels for 19% -> 21%
where the time goes in v12:
time: 68.9 us; the launch traced here: 68.5 us
  Pallas kernels  26.9 us (39%)
  starting transfers between devices  22.6 us (33%)
  waiting for transfers between devices  17.6 us (26%)
  between operations  0.75 us (1%)
  other arithmetic  0.72 us (1%)
    ppermute x6, waiting for transfers between devices, along_x(): got[d] = lax.ppermute(parts[d], 'ctx', moves)  11.4 us
    ppermute x6, starting transfers between devices, along_x(): got[d] = lax.ppermute(parts[d], 'ctx', moves)  9.17 us
    pallas_call x1, Pallas kernels, run_give(): pl.pallas_call(give_kernel, in_specs=[SMEM] * 2 + [HBM] * 9, out_specs=[V...  7.78 us
    pallas_call x1, Pallas kernels, run_keep(): pl.pallas_call(keep_kernel, in_specs=[SMEM] + [VMEM] * 8 + [HBM] * 2, out...  5.61 us
    pallas_call x2, Pallas kernels, run_backward(): pl.pallas_call(partial(second_kernel, bool(before)), in_specs=[SMEM] * 2...  5.29 us
    pallas_call x2, Pallas kernels, run_chunk(): pl.pallas_call(partial(chunk_kernel, distances), in_specs=[SMEM] + [VMEM]...  3.47 us
    pallas_call x6, Pallas kernels, call(): pl.pallas_call(kernel, in_specs=[SMEM] * len(scalars) + [VMEM] * len(arra...  3.39 us
    ppermute x1, waiting for transfers between devices, per_device(): lax.ppermute(near[0], 'head', after)  3.18 us
  transfers between devices with their start and end apart: 14, of which 7 were waited for; matrix products, arithmetic and copies ran while one was open for 0% of the time, Pallas kernels for 21%

profile of v12, /device:TPU:1, one launch (start us, length us, event | category | flops | bytes accessed | tf_op | source)
XLA Modules:
  0.0 68.5 jit_solution(131228296557638363)
XLA Ops:
  0.6 7.8 %block_forward_give.1 = (f32[4,3,128,128]{3,2,1,0:T(8,128)S(1)}, f32[4,11,128,128]{3,2,1,0:T(8,128)S(1)}, bf16[128,2048]{1,0:T(8,128)(2,1)S(1)}, bf16[128,2048]{...) custom-call(s32[1]{0:T(128)} %bitcast.2.place_ref.refs_0_, ...), custom_call_target="tpu_custom_call" | custom-call | tf_op jit(solution)/shard_map/block_forward_give/pallas_call | solution.py:427
  8.4 1.5 %collective-permute-start = (f32[4,3,128,128]{3,2,1,0:T(8,128)S(1)}, f32[4,3,128,128]{3,2,1,0:T(8,128)S(1)}, u32[]{:S(2)}, u32[]{:S(2)}) collective-permute-start(f32[4,3,128,128]{3,2,1,0:T(8,128)S(1)} %get-tuple-element.74), channel_id=1, source_target_pairs={{0,4},{4,0},{8,12},{12,8},{16,20},{20,16},{24,28},{28,24},{32,36},... | collective-permute-start | bytes 2359304 | tf_op jit(solution)/shard_map/ppermute | solution.py:495
  9.9 5.6 %block_forward_keep.1 = (f32[4,3,128,128]{3,2,1,0:T(8,128)S(1)}, f32[4,11,128,128]{3,2,1,0:T(8,128)S(1)}, bf16[2048,512]{1,0:T(8,128)(2,1)S(1)}) custom-call(s32[1]{0:T(128)} %bitcast.2.place_ref.refs_0_, bf16[128,2048]{1,0:T(8,128)(2,1)S(1)} %get-tuple-element.65.x_ref, bf16[128,2048]{1,0:T(8,128)(2,1)S(1)} %get-tuple-element.66.go_ref, ...), custom_call_target="tpu_custom_call" | custom-call | tf_op jit(solution)/shard_map/block_forward_keep/pallas_call | solution.py:444
  16.1 1.4 %collective-permute-start.1 = (f32[3,128,128]{2,1,0:T(8,128)S(1)}, f32[3,128,128]{2,1,0:T(8,128)S(1)}, u32[]{:S(2)}, u32[]{:S(2)}) collective-permute-start(f32[3,128,128]{2,1,0:T(8,128)S(1)} %get-tuple-element.82), channel_id=1, source_target_pairs={{0,8},{4,12},{8,16},{12,20},{16,24},{20,28},{24,0},{28,4},{32,40},... | collective-permute-start | bytes 589832 | tf_op jit(solution)/shard_map/ppermute | solution.py:514
  17.4 2.4 %collective-permute-start.2 = (f32[3,128,128]{2,1,0:T(8,128)S(1)}, f32[3,128,128]{2,1,0:T(8,128)S(1)}, u32[]{:S(2)}, u32[]{:S(2)}) collective-permute-start(f32[3,128,128]{2,1,0:T(8,128)S(1)} %get-tuple-element.83), channel_id=1, source_target_pairs={{0,16},{4,20},{8,24},{12,28},{16,0},{20,4},{24,8},{28,12},{32,48},... | collective-permute-start | bytes 589832 | tf_op jit(solution)/shard_map/ppermute | solution.py:514
  19.9 1.2 %collective-permute-start.3 = (f32[3,128,128]{2,1,0:T(8,128)S(1)}, f32[3,128,128]{2,1,0:T(8,128)S(1)}, u32[]{:S(2)}, u32[]{:S(2)}) collective-permute-start(f32[3,128,128]{2,1,0:T(8,128)S(1)} %get-tuple-element.84), channel_id=1, source_target_pairs={{0,24},{4,28},{8,0},{12,4},{16,8},{20,12},{24,16},{28,20},{32,56},... | collective-permute-start | bytes 589832 | tf_op jit(solution)/shard_map/ppermute | solution.py:514
  22.5 1.4 %collective-permute-done.1.refs_1_ = f32[3,128,128]{2,1,0:T(8,128)S(1)} collective-permute-done((f32[3,128,128]{2,1,0:T(8,128)S(1)}, f32[3,128,128]{2,1,0:T(8,128)S(1)}, u32[]{:S(2)}, u32[]{:S(2)}) %collective-permute-start.1) | collective-permute-done | bytes 196640 | tf_op jit(solution)/shard_map/ppermute | solution.py:514
  23.9 5.3 %collective-permute-done.2.refs_2_ = f32[3,128,128]{2,1,0:T(8,128)S(1)} collective-permute-done((f32[3,128,128]{2,1,0:T(8,128)S(1)}, f32[3,128,128]{2,1,0:T(8,128)S(1)}, u32[]{:S(2)}, u32[]{:S(2)}) %collective-permute-start.2) | collective-permute-done | bytes 196640 | tf_op jit(solution)/shard_map/ppermute | solution.py:514
  29.8 1.7 %collective-permute-start.4 = (f32[128,128]{1,0:T(8,128)S(1)}, f32[128,128]{1,0:T(8,128)S(1)}, u32[]{:S(2)}, u32[]{:S(2)}) collective-permute-start(f32[128,128]{1,0:T(8,128)S(1)} %get-tuple-element.92), channel_id=1, source_target_pairs={{0,32},{4,36},{8,40},{12,44},{16,48},{20,52},{24,56},{28,60},{32,6... | collective-permute-start | bytes 196616 | tf_op jit(solution)/shard_map/ppermute | solution.py:530
  31.5 2.2 %collective-permute-start.5 = (f32[128,128]{1,0:T(8,128)S(1)}, f32[128,128]{1,0:T(8,128)S(1)}, u32[]{:S(2)}, u32[]{:S(2)}) collective-permute-start(f32[128,128]{1,0:T(8,128)S(1)} %get-tuple-element.93), channel_id=1, source_target_pairs={{32,0},{36,4},{40,8},{44,12},{48,16},{52,20},{56,24},{60,28},{64,3... | collective-permute-start | bytes 196616 | tf_op jit(solution)/shard_map/ppermute | solution.py:531
  33.7 1.6 %collective-permute-done.4.s_ref = f32[128,128]{1,0:T(8,128)S(1)} collective-permute-done((f32[128,128]{1,0:T(8,128)S(1)}, f32[128,128]{1,0:T(8,128)S(1)}, u32[]{:S(2)}, u32[]{:S(2)}) %collective-permute-start.4) | collective-permute-done | bytes 65568 | tf_op jit(solution)/shard_map/ppermute | solution.py:530
  36.6 3.2 %collective-permute-start.7 = (f32[2,128,128]{2,1,0:T(8,128)S(1)}, f32[2,128,128]{2,1,0:T(8,128)S(1)}, u32[]{:S(2)}, u32[]{:S(2)}) collective-permute-start(f32[2,128,128]{2,1,0:T(8,128)S(1)} %get-tuple-element.96), channel_id=1, source_target_pairs={{0,16},{4,20},{8,24},{12,28},{16,0},{20,4},{24,8},{28,12},{32,48},... | collective-permute-start | bytes 393224 | tf_op jit(solution)/shard_map/ppermute | solution.py:514
  40.9 3.8 %collective-permute-done.7.refs_2_ = f32[2,128,128]{2,1,0:T(8,128)S(1)} collective-permute-done((f32[2,128,128]{2,1,0:T(8,128)S(1)}, f32[2,128,128]{2,1,0:T(8,128)S(1)}, u32[]{:S(2)}, u32[]{:S(2)}) %collective-permute-start.7) | collective-permute-done | bytes 131104 | tf_op jit(solution)/shard_map/ppermute | solution.py:514
  45.2 2.4 %collective-permute-start.9 = (f32[4,2,128,128]{3,2,1,0:T(8,128)S(1)}, f32[4,2,128,128]{3,2,1,0:T(8,128)S(1)}, u32[]{:S(2)}, u32[]{:S(2)}) collective-permute-start(f32[4,2,128,128]{3,2,1,0:T(8,128)S(1)} %get-tuple-element.103), channel_id=1, source_target_pairs={{0,4},{4,0},{8,12},{12,8},{16,20},{20,16},{24,28},{28,24},{32,36},... | collective-permute-start | bytes 1572872 | tf_op jit(solution)/shard_map/ppermute | solution.py:538
  47.6 2.7 %block_backward.2 = (f32[128,512]{1,0:T(8,128)S(1)}, bf16[128,1536]{1,0:T(8,128)(2,1)S(1)}, bf16[128,8]{1,0:T(8,128)(2,1)S(1)}, f32[4,128,128]{2,1,0:T(8,128)S(1)}, f32[256,8]{1,0:T(8,128)S(1)}) custom-call(s32[1]{0:T(128)} %bitcast.2.place_ref.refs_0_, s32[1]{0:T(128)} %bitcast.side_ref.refs_1_, f32[4,2,128,128]{3,2,1,0:T(8,128)S(1)} %get-tuple-element.98.refs_2_, ...), custom_call_target="tpu_custom_call" | custom-call | tf_op jit(solution)/shard_map/block_backward/pallas_call | solution.py:462
  50.2 2.6 %block_backward.3 = (f32[64,512]{1,0:T(8,128)S(1)}, f32[64,512]{1,0:T(8,128)S(1)}, bf16[128,1536]{1,0:T(8,128)(2,1)S(1)}, bf16[128,8]{1,0:T(8,128)(2,1)S(1)}, f3...) custom-call(s32[1]{0:T(128)} %bitcast.2.place_ref.refs_0_, s32[1]{0:T(128)} %bitcast.side_ref.refs_1_, ...), custom_call_target="tpu_custom_call" | custom-call | tf_op jit(solution)/shard_map/block_backward/pallas_call | solution.py:462
  52.9 1.4 %collective-permute-start.10 = (f32[64,512]{1,0:T(8,128)S(1)}, f32[64,512]{1,0:T(8,128)S(1)}, u32[]{:S(2)}, u32[]{:S(2)}) collective-permute-start(f32[64,512]{1,0:T(8,128)S(1)} %get-tuple-element.112), channel_id=1, source_target_pairs={{0,1},{1,2},{2,3},{3,0},{4,5},{5,6},{6,7},{7,4},{8,9},{9,10},{10,1... | collective-permute-start | bytes 393224 | tf_op jit(solution)/shard_map/ppermute | solution.py:547
  54.2 1.5 %collective-permute-start.11 = (f32[64,512]{1,0:T(8,128)S(1)}, f32[64,512]{1,0:T(8,128)S(1)}, u32[]{:S(2)}, u32[]{:S(2)}) collective-permute-start(f32[64,512]{1,0:T(8,128)S(1)} %get-tuple-element.113), channel_id=1, source_target_pairs={{1,0},{2,1},{3,2},{0,3},{5,4},{6,5},{7,6},{4,7},{9,8},{10,9},{11,1... | collective-permute-start | bytes 393224 | tf_op jit(solution)/shard_map/ppermute | solution.py:547
  55.8 2.3 %near_chunks.1 = (f32[128,512]{1,0:T(8,128)S(1)}, f32[128,512]{1,0:T(8,128)S(1)}) custom-call(s32[1]{0:T(128)} %bitcast.side_ref.refs_1_, bf16[8,2048]{1,0:T(8,128)(2,1)S(1)} %bitcast.8, bf16[128,1536]{1,0:T(8,128)(2,1)S(1)} %get-tuple-element.101.refs_0_, bf16[128,8]{1,0:T(8,128)(2,1)S(1)} %get-tuple-element.102.refs_1_, ...), custom_call_target="tpu_custom_call" | custom-call | tf_op jit(solution)/shard_map/near_chunks/pallas_call | solution.py:474
  58.0 1.4 %collective-permute-done.10.up_ref = f32[64,512]{1,0:T(8,128)S(1)} collective-permute-done((f32[64,512]{1,0:T(8,128)S(1)}, f32[64,512]{1,0:T(8,128)S(1)}, u32[]{:S(2)}, u32[]{:S(2)}) %collective-permute-start.10) | collective-permute-done | bytes 131104 | tf_op jit(solution)/shard_map/ppermute | solution.py:547
  60.4 1.8 %collective-permute-start.13 = (f32[128,512]{1,0:T(8,128)S(1)}, f32[128,512]{1,0:T(8,128)S(1)}, u32[]{:S(2)}, u32[]{:S(2)}) collective-permute-start(f32[128,512]{1,0:T(8,128)S(1)} %get-tuple-element.123), channel_id=1, source_target_pairs={{1,0},{2,1},{3,2},{0,3},{5,4},{6,5},{7,6},{4,7},{9,8},{10,9},{11,1... | collective-permute-start | bytes 786440 | tf_op jit(solution)/shard_map/ppermute | solution.py:553
  62.2 1.2 %own_chunk.1 = f32[128,512]{1,0:T(8,128)S(1)} custom-call(s32[1]{0:T(128)} %bitcast.side_ref.refs_1_, bf16[8,2048]{1,0:T(8,128)(2,1)S(1)} %bitcast.9, bf16[128,1536]{1,0:T(8,128)(2,1)S(1)} %get-tuple-element.101.refs_0_, bf16[128,8]{1,0:T(8,128)(2,1)S(1)} %get-tuple-element.102.refs_1_, bf16[2,2048,512]{2,1,0:T(8,128)(2,1)S(1)} %get-tuple-element.72.wkq_ref.refs_6_.refs_2_, ...), custom_call_target="tpu_custom_call" | custom-call | tf_op jit(solution)/shard_map/own_chunk/pallas_call | solution.py:474
  63.4 1.2 %decay_sums.1 = f32[8,128]{1,0:T(8,128)} custom-call(s32[1]{0:T(128)} %bitcast.2.place_ref.refs_0_, f32[4,128,128]{2,1,0:T(8,128)S(1)} %get-tuple-element.124.keep_pairs_ref, f32[256,8]{1,0:T(8,128)S(1)} %get-tuple-element.125.keep_terms_ref, f32[4,128,128]{2,1,0:T(8,128)S(1)} %get-tuple-element.126.give_pairs_ref, ...), custom_call_target="tpu_custom_call" | custom-call | tf_op jit(solution)/shard_map/decay_sums/pallas_call | solution.py:500
  64.6 3.2 %collective-permute-done.12 = f32[128,512]{1,0:T(8,128)S(1)} collective-permute-done((f32[128,512]{1,0:T(8,128)S(1)}, f32[128,512]{1,0:T(8,128)S(1)}, u32[]{:S(2)}, u32[]{:S(2)}) %collective-permute-start.12) | collective-permute-done | bytes 262176 | tf_op jit(solution)/shard_map/ppermute | solution.py:553
  (21 shorter events, 7.2 us)
Async XLA Ops:
  8.4 7.1 %collective-permute-start = (f32[4,3,128,128]{3,2,1,0:T(8,128)S(1)}, f32[4,3,128,128]{3,2,1,0:T(8,128)S(1)}, u32[]{:S(2)}, u32[]{:S(2)}) collective-permute-start(f32[4,3,128,128]{3,2,1,0:T(8,128)S(1)} %get-tuple-element.74), channel_id=1, source_target_pairs={{0,4},{4,0},{8,12},{12,8},{16,20},{20,16},{24,28},{28,24},{32,36},... | collective-permute-start | bytes 2359304 | tf_op jit(solution)/shard_map/ppermute | solution.py:495
  16.1 7.8 %collective-permute-start.1 = (f32[3,128,128]{2,1,0:T(8,128)S(1)}, f32[3,128,128]{2,1,0:T(8,128)S(1)}, u32[]{:S(2)}, u32[]{:S(2)}) collective-permute-start(f32[3,128,128]{2,1,0:T(8,128)S(1)} %get-tuple-element.82), channel_id=1, source_target_pairs={{0,8},{4,12},{8,16},{12,20},{16,24},{20,28},{24,0},{28,4},{32,40},... | collective-permute-start | bytes 589832 | tf_op jit(solution)/shard_map/ppermute | solution.py:514
  17.4 11.7 %collective-permute-start.2 = (f32[3,128,128]{2,1,0:T(8,128)S(1)}, f32[3,128,128]{2,1,0:T(8,128)S(1)}, u32[]{:S(2)}, u32[]{:S(2)}) collective-permute-start(f32[3,128,128]{2,1,0:T(8,128)S(1)} %get-tuple-element.83), channel_id=1, source_target_pairs={{0,16},{4,20},{8,24},{12,28},{16,0},{20,4},{24,8},{28,12},{32,48},... | collective-permute-start | bytes 589832 | tf_op jit(solution)/shard_map/ppermute | solution.py:514
  19.9 9.3 %collective-permute-start.3 = (f32[3,128,128]{2,1,0:T(8,128)S(1)}, f32[3,128,128]{2,1,0:T(8,128)S(1)}, u32[]{:S(2)}, u32[]{:S(2)}) collective-permute-start(f32[3,128,128]{2,1,0:T(8,128)S(1)} %get-tuple-element.84), channel_id=1, source_target_pairs={{0,24},{4,28},{8,0},{12,4},{16,8},{20,12},{24,16},{28,20},{32,56},... | collective-permute-start | bytes 589832 | tf_op jit(solution)/shard_map/ppermute | solution.py:514
  21.8 25.8 %copy-start = (bf16[2048,8]{0,1:T(8,128)(2,1)S(1)}, bf16[2048,8]{0,1:T(8,128)(2,1)}, u32[]{:S(2)}) copy-start(bf16[2048,8]{0,1:T(8,128)(2,1)} %param.14) | copy-start | bytes 98308
  29.8 5.5 %collective-permute-start.4 = (f32[128,128]{1,0:T(8,128)S(1)}, f32[128,128]{1,0:T(8,128)S(1)}, u32[]{:S(2)}, u32[]{:S(2)}) collective-permute-start(f32[128,128]{1,0:T(8,128)S(1)} %get-tuple-element.92), channel_id=1, source_target_pairs={{0,32},{4,36},{8,40},{12,44},{16,48},{20,52},{24,56},{28,60},{32,6... | collective-permute-start | bytes 196616 | tf_op jit(solution)/shard_map/ppermute | solution.py:530
  31.5 3.8 %collective-permute-start.5 = (f32[128,128]{1,0:T(8,128)S(1)}, f32[128,128]{1,0:T(8,128)S(1)}, u32[]{:S(2)}, u32[]{:S(2)}) collective-permute-start(f32[128,128]{1,0:T(8,128)S(1)} %get-tuple-element.93), channel_id=1, source_target_pairs={{32,0},{36,4},{40,8},{44,12},{48,16},{52,20},{56,24},{60,28},{64,3... | collective-permute-start | bytes 196616 | tf_op jit(solution)/shard_map/ppermute | solution.py:531
  35.8 5.1 %collective-permute-start.6 = (f32[2,128,128]{2,1,0:T(8,128)S(1)}, f32[2,128,128]{2,1,0:T(8,128)S(1)}, u32[]{:S(2)}, u32[]{:S(2)}) collective-permute-start(f32[2,128,128]{2,1,0:T(8,128)S(1)} %get-tuple-element.95), channel_id=1, source_target_pairs={{0,8},{4,12},{8,16},{12,20},{16,24},{20,28},{24,0},{28,4},{32,40},... | collective-permute-start | bytes 393224 | tf_op jit(solution)/shard_map/ppermute | solution.py:514
  36.6 8.2 %collective-permute-start.7 = (f32[2,128,128]{2,1,0:T(8,128)S(1)}, f32[2,128,128]{2,1,0:T(8,128)S(1)}, u32[]{:S(2)}, u32[]{:S(2)}) collective-permute-start(f32[2,128,128]{2,1,0:T(8,128)S(1)} %get-tuple-element.96), channel_id=1, source_target_pairs={{0,16},{4,20},{8,24},{12,28},{16,0},{20,4},{24,8},{28,12},{32,48},... | collective-permute-start | bytes 393224 | tf_op jit(solution)/shard_map/ppermute | solution.py:514
  39.7 5.0 %collective-permute-start.8 = (f32[2,128,128]{2,1,0:T(8,128)S(1)}, f32[2,128,128]{2,1,0:T(8,128)S(1)}, u32[]{:S(2)}, u32[]{:S(2)}) collective-permute-start(f32[2,128,128]{2,1,0:T(8,128)S(1)} %get-tuple-element.97), channel_id=1, source_target_pairs={{0,24},{4,28},{8,0},{12,4},{16,8},{20,12},{24,16},{28,20},{32,56},... | collective-permute-start | bytes 393224 | tf_op jit(solution)/shard_map/ppermute | solution.py:514
  45.2 5.0 %collective-permute-start.9 = (f32[4,2,128,128]{3,2,1,0:T(8,128)S(1)}, f32[4,2,128,128]{3,2,1,0:T(8,128)S(1)}, u32[]{:S(2)}, u32[]{:S(2)}) collective-permute-start(f32[4,2,128,128]{3,2,1,0:T(8,128)S(1)} %get-tuple-element.103), channel_id=1, source_target_pairs={{0,4},{4,0},{8,12},{12,8},{16,20},{20,16},{24,28},{28,24},{32,36},... | collective-permute-start | bytes 1572872 | tf_op jit(solution)/shard_map/ppermute | solution.py:538
  52.9 6.5 %collective-permute-start.10 = (f32[64,512]{1,0:T(8,128)S(1)}, f32[64,512]{1,0:T(8,128)S(1)}, u32[]{:S(2)}, u32[]{:S(2)}) collective-permute-start(f32[64,512]{1,0:T(8,128)S(1)} %get-tuple-element.112), channel_id=1, source_target_pairs={{0,1},{1,2},{2,3},{3,0},{4,5},{5,6},{6,7},{7,4},{8,9},{9,10},{10,1... | collective-permute-start | bytes 393224 | tf_op jit(solution)/shard_map/ppermute | solution.py:547
  54.2 5.2 %collective-permute-start.11 = (f32[64,512]{1,0:T(8,128)S(1)}, f32[64,512]{1,0:T(8,128)S(1)}, u32[]{:S(2)}, u32[]{:S(2)}) collective-permute-start(f32[64,512]{1,0:T(8,128)S(1)} %get-tuple-element.113), channel_id=1, source_target_pairs={{1,0},{2,1},{3,2},{0,3},{5,4},{6,5},{7,6},{4,7},{9,8},{10,9},{11,1... | collective-permute-start | bytes 393224 | tf_op jit(solution)/shard_map/ppermute | solution.py:547
  59.4 8.4 %collective-permute-start.12 = (f32[128,512]{1,0:T(8,128)S(1)}, f32[128,512]{1,0:T(8,128)S(1)}, u32[]{:S(2)}, u32[]{:S(2)}) collective-permute-start(f32[128,512]{1,0:T(8,128)S(1)} %get-tuple-element.122), channel_id=1, source_target_pairs={{0,1},{1,2},{2,3},{3,0},{4,5},{5,6},{6,7},{7,4},{8,9},{9,10},{10,1... | collective-permute-start | bytes 786440 | tf_op jit(solution)/shard_map/ppermute | solution.py:553
  60.4 7.4 %collective-permute-start.13 = (f32[128,512]{1,0:T(8,128)S(1)}, f32[128,512]{1,0:T(8,128)S(1)}, u32[]{:S(2)}, u32[]{:S(2)}) collective-permute-start(f32[128,512]{1,0:T(8,128)S(1)} %get-tuple-element.123), channel_id=1, source_target_pairs={{1,0},{2,1},{3,2},{0,3},{5,4},{6,5},{7,6},{4,7},{9,8},{10,9},{11,1... | collective-permute-start | bytes 786440 | tf_op jit(solution)/shard_map/ppermute | solution.py:553

commit v13 on v12

--- a/solution.py
+++ b/solution.py
@@ -509,7 +509,7 @@
 
     def along_x(parts):
         got = {0: parts[0]}
-        for d in (2, 1, 3):
+        for d in (1, 3, 2):
             moves = [(j, j - j % row + (j + 2 * d) % row) for j in range(size)]
             got[d] = lax.ppermute(parts[d], "ctx", moves)
         return [got[d] for d in range(GROUP)]

time: 68.9 us -> 68.9 us (level)
  no operation moved by 1% of the time
where the time goes in v13:
time: 68.9 us; the launch traced here: 68.5 us
  Pallas kernels  26.9 us (39%)
  starting transfers between devices  22.6 us (33%)
  waiting for transfers between devices  17.6 us (26%)
  between operations  0.75 us (1%)
  other arithmetic  0.72 us (1%)
    ppermute x6, waiting for transfers between devices, along_x(): got[d] = lax.ppermute(parts[d], 'ctx', moves)  11.4 us
    ppermute x6, starting transfers between devices, along_x(): got[d] = lax.ppermute(parts[d], 'ctx', moves)  9.17 us
    pallas_call x1, Pallas kernels, run_give(): pl.pallas_call(give_kernel, in_specs=[SMEM] * 2 + [HBM] * 9, out_specs=[V...  7.78 us
    pallas_call x1, Pallas kernels, run_keep(): pl.pallas_call(keep_kernel, in_specs=[SMEM] + [VMEM] * 8 + [HBM] * 2, out...  5.61 us
    pallas_call x2, Pallas kernels, run_backward(): pl.pallas_call(partial(second_kernel, bool(before)), in_specs=[SMEM] * 2...  5.29 us
    pallas_call x2, Pallas kernels, run_chunk(): pl.pallas_call(partial(chunk_kernel, distances), in_specs=[SMEM] + [VMEM]...  3.47 us
    pallas_call x6, Pallas kernels, call(): pl.pallas_call(kernel, in_specs=[SMEM] * len(scalars) + [VMEM] * len(arra...  3.39 us
    ppermute x1, waiting for transfers between devices, per_device(): lax.ppermute(near[0], 'head', after)  3.18 us
  transfers between devices with their start and end apart: 14, of which 7 were waited for; matrix products, arithmetic and copies ran while one was open for 0% of the time, Pallas kernels for 21%

profile of v13, /device:TPU:1, one launch (start us, length us, event | category | flops | bytes accessed | tf_op | source)
XLA Modules:
  0.0 68.5 jit_solution(131228296557638363)
XLA Ops:
  0.6 7.8 %block_forward_give.1 = (f32[4,3,128,128]{3,2,1,0:T(8,128)S(1)}, f32[4,11,128,128]{3,2,1,0:T(8,128)S(1)}, bf16[128,2048]{1,0:T(8,128)(2,1)S(1)}, bf16[128,2048]{...) custom-call(s32[1]{0:T(128)} %bitcast.2.place_ref.refs_0_, ...), custom_call_target="tpu_custom_call" | custom-call | tf_op jit(solution)/shard_map/block_forward_give/pallas_call | solution.py:427
  8.4 1.5 %collective-permute-start = (f32[4,3,128,128]{3,2,1,0:T(8,128)S(1)}, f32[4,3,128,128]{3,2,1,0:T(8,128)S(1)}, u32[]{:S(2)}, u32[]{:S(2)}) collective-permute-start(f32[4,3,128,128]{3,2,1,0:T(8,128)S(1)} %get-tuple-element.74), channel_id=1, source_target_pairs={{0,4},{4,0},{8,12},{12,8},{16,20},{20,16},{24,28},{28,24},{32,36},... | collective-permute-start | bytes 2359304 | tf_op jit(solution)/shard_map/ppermute | solution.py:495
  9.9 5.6 %block_forward_keep.1 = (f32[4,3,128,128]{3,2,1,0:T(8,128)S(1)}, f32[4,11,128,128]{3,2,1,0:T(8,128)S(1)}, bf16[2048,512]{1,0:T(8,128)(2,1)S(1)}) custom-call(s32[1]{0:T(128)} %bitcast.2.place_ref.refs_0_, bf16[128,2048]{1,0:T(8,128)(2,1)S(1)} %get-tuple-element.65.x_ref, bf16[128,2048]{1,0:T(8,128)(2,1)S(1)} %get-tuple-element.66.go_ref, ...), custom_call_target="tpu_custom_call" | custom-call | tf_op jit(solution)/shard_map/block_forward_keep/pallas_call | solution.py:444
  16.1 1.4 %collective-permute-start.1 = (f32[3,128,128]{2,1,0:T(8,128)S(1)}, f32[3,128,128]{2,1,0:T(8,128)S(1)}, u32[]{:S(2)}, u32[]{:S(2)}) collective-permute-start(f32[3,128,128]{2,1,0:T(8,128)S(1)} %get-tuple-element.82), channel_id=1, source_target_pairs={{0,8},{4,12},{8,16},{12,20},{16,24},{20,28},{24,0},{28,4},{32,40},... | collective-permute-start | bytes 589832 | tf_op jit(solution)/shard_map/ppermute | solution.py:514
  17.4 2.4 %collective-permute-start.2 = (f32[3,128,128]{2,1,0:T(8,128)S(1)}, f32[3,128,128]{2,1,0:T(8,128)S(1)}, u32[]{:S(2)}, u32[]{:S(2)}) collective-permute-start(f32[3,128,128]{2,1,0:T(8,128)S(1)} %get-tuple-element.83), channel_id=1, source_target_pairs={{0,16},{4,20},{8,24},{12,28},{16,0},{20,4},{24,8},{28,12},{32,48},... | collective-permute-start | bytes 589832 | tf_op jit(solution)/shard_map/ppermute | solution.py:514
  19.9 1.2 %collective-permute-start.3 = (f32[3,128,128]{2,1,0:T(8,128)S(1)}, f32[3,128,128]{2,1,0:T(8,128)S(1)}, u32[]{:S(2)}, u32[]{:S(2)}) collective-permute-start(f32[3,128,128]{2,1,0:T(8,128)S(1)} %get-tuple-element.84), channel_id=1, source_target_pairs={{0,24},{4,28},{8,0},{12,4},{16,8},{20,12},{24,16},{28,20},{32,56},... | collective-permute-start | bytes 589832 | tf_op jit(solution)/shard_map/ppermute | solution.py:514
  22.5 1.4 %collective-permute-done.1.refs_1_ = f32[3,128,128]{2,1,0:T(8,128)S(1)} collective-permute-done((f32[3,128,128]{2,1,0:T(8,128)S(1)}, f32[3,128,128]{2,1,0:T(8,128)S(1)}, u32[]{:S(2)}, u32[]{:S(2)}) %collective-permute-start.1) | collective-permute-done | bytes 196640 | tf_op jit(solution)/shard_map/ppermute | solution.py:514
  23.9 5.3 %collective-permute-done.2.refs_2_ = f32[3,128,128]{2,1,0:T(8,128)S(1)} collective-permute-done((f32[3,128,128]{2,1,0:T(8,128)S(1)}, f32[3,128,128]{2,1,0:T(8,128)S(1)}, u32[]{:S(2)}, u32[]{:S(2)}) %collective-permute-start.2) | collective-permute-done | bytes 196640 | tf_op jit(solution)/shard_map/ppermute | solution.py:514
  29.8 1.7 %collective-permute-start.4 = (f32[128,128]{1,0:T(8,128)S(1)}, f32[128,128]{1,0:T(8,128)S(1)}, u32[]{:S(2)}, u32[]{:S(2)}) collective-permute-start(f32[128,128]{1,0:T(8,128)S(1)} %get-tuple-element.92), channel_id=1, source_target_pairs={{0,32},{4,36},{8,40},{12,44},{16,48},{20,52},{24,56},{28,60},{32,6... | collective-permute-start | bytes 196616 | tf_op jit(solution)/shard_map/ppermute | solution.py:530
  31.5 2.2 %collective-permute-start.5 = (f32[128,128]{1,0:T(8,128)S(1)}, f32[128,128]{1,0:T(8,128)S(1)}, u32[]{:S(2)}, u32[]{:S(2)}) collective-permute-start(f32[128,128]{1,0:T(8,128)S(1)} %get-tuple-element.93), channel_id=1, source_target_pairs={{32,0},{36,4},{40,8},{44,12},{48,16},{52,20},{56,24},{60,28},{64,3... | collective-permute-start | bytes 196616 | tf_op jit(solution)/shard_map/ppermute | solution.py:531
  33.7 1.6 %collective-permute-done.4.s_ref = f32[128,128]{1,0:T(8,128)S(1)} collective-permute-done((f32[128,128]{1,0:T(8,128)S(1)}, f32[128,128]{1,0:T(8,128)S(1)}, u32[]{:S(2)}, u32[]{:S(2)}) %collective-permute-start.4) | collective-permute-done | bytes 65568 | tf_op jit(solution)/shard_map/ppermute | solution.py:530
  36.6 3.2 %collective-permute-start.7 = (f32[2,128,128]{2,1,0:T(8,128)S(1)}, f32[2,128,128]{2,1,0:T(8,128)S(1)}, u32[]{:S(2)}, u32[]{:S(2)}) collective-permute-start(f32[2,128,128]{2,1,0:T(8,128)S(1)} %get-tuple-element.96), channel_id=1, source_target_pairs={{0,16},{4,20},{8,24},{12,28},{16,0},{20,4},{24,8},{28,12},{32,48},... | collective-permute-start | bytes 393224 | tf_op jit(solution)/shard_map/ppermute | solution.py:514
  40.9 3.8 %collective-permute-done.7.refs_2_ = f32[2,128,128]{2,1,0:T(8,128)S(1)} collective-permute-done((f32[2,128,128]{2,1,0:T(8,128)S(1)}, f32[2,128,128]{2,1,0:T(8,128)S(1)}, u32[]{:S(2)}, u32[]{:S(2)}) %collective-permute-start.7) | collective-permute-done | bytes 131104 | tf_op jit(solution)/shard_map/ppermute | solution.py:514
  45.2 2.4 %collective-permute-start.9 = (f32[4,2,128,128]{3,2,1,0:T(8,128)S(1)}, f32[4,2,128,128]{3,2,1,0:T(8,128)S(1)}, u32[]{:S(2)}, u32[]{:S(2)}) collective-permute-start(f32[4,2,128,128]{3,2,1,0:T(8,128)S(1)} %get-tuple-element.103), channel_id=1, source_target_pairs={{0,4},{4,0},{8,12},{12,8},{16,20},{20,16},{24,28},{28,24},{32,36},... | collective-permute-start | bytes 1572872 | tf_op jit(solution)/shard_map/ppermute | solution.py:538
  47.6 2.7 %block_backward.2 = (f32[128,512]{1,0:T(8,128)S(1)}, bf16[128,1536]{1,0:T(8,128)(2,1)S(1)}, bf16[128,8]{1,0:T(8,128)(2,1)S(1)}, f32[4,128,128]{2,1,0:T(8,128)S(1)}, f32[256,8]{1,0:T(8,128)S(1)}) custom-call(s32[1]{0:T(128)} %bitcast.2.place_ref.refs_0_, s32[1]{0:T(128)} %bitcast.side_ref.refs_1_, f32[4,2,128,128]{3,2,1,0:T(8,128)S(1)} %get-tuple-element.98.refs_2_, ...), custom_call_target="tpu_custom_call" | custom-call | tf_op jit(solution)/shard_map/block_backward/pallas_call | solution.py:462
  50.2 2.6 %block_backward.3 = (f32[64,512]{1,0:T(8,128)S(1)}, f32[64,512]{1,0:T(8,128)S(1)}, bf16[128,1536]{1,0:T(8,128)(2,1)S(1)}, bf16[128,8]{1,0:T(8,128)(2,1)S(1)}, f3...) custom-call(s32[1]{0:T(128)} %bitcast.2.place_ref.refs_0_, s32[1]{0:T(128)} %bitcast.side_ref.refs_1_, ...), custom_call_target="tpu_custom_call" | custom-call | tf_op jit(solution)/shard_map/block_backward/pallas_call | solution.py:462
  52.9 1.4 %collective-permute-start.10 = (f32[64,512]{1,0:T(8,128)S(1)}, f32[64,512]{1,0:T(8,128)S(1)}, u32[]{:S(2)}, u32[]{:S(2)}) collective-permute-start(f32[64,512]{1,0:T(8,128)S(1)} %get-tuple-element.112), channel_id=1, source_target_pairs={{0,1},{1,2},{2,3},{3,0},{4,5},{5,6},{6,7},{7,4},{8,9},{9,10},{10,1... | collective-permute-start | bytes 393224 | tf_op jit(solution)/shard_map/ppermute | solution.py:547
  54.2 1.5 %collective-permute-start.11 = (f32[64,512]{1,0:T(8,128)S(1)}, f32[64,512]{1,0:T(8,128)S(1)}, u32[]{:S(2)}, u32[]{:S(2)}) collective-permute-start(f32[64,512]{1,0:T(8,128)S(1)} %get-tuple-element.113), channel_id=1, source_target_pairs={{1,0},{2,1},{3,2},{0,3},{5,4},{6,5},{7,6},{4,7},{9,8},{10,9},{11,1... | collective-permute-start | bytes 393224 | tf_op jit(solution)/shard_map/ppermute | solution.py:547
  55.8 2.3 %near_chunks.1 = (f32[128,512]{1,0:T(8,128)S(1)}, f32[128,512]{1,0:T(8,128)S(1)}) custom-call(s32[1]{0:T(128)} %bitcast.side_ref.refs_1_, bf16[8,2048]{1,0:T(8,128)(2,1)S(1)} %bitcast.8, bf16[128,1536]{1,0:T(8,128)(2,1)S(1)} %get-tuple-element.101.refs_0_, bf16[128,8]{1,0:T(8,128)(2,1)S(1)} %get-tuple-element.102.refs_1_, ...), custom_call_target="tpu_custom_call" | custom-call | tf_op jit(solution)/shard_map/near_chunks/pallas_call | solution.py:474
  58.0 1.4 %collective-permute-done.10.up_ref = f32[64,512]{1,0:T(8,128)S(1)} collective-permute-done((f32[64,512]{1,0:T(8,128)S(1)}, f32[64,512]{1,0:T(8,128)S(1)}, u32[]{:S(2)}, u32[]{:S(2)}) %collective-permute-start.10) | collective-permute-done | bytes 131104 | tf_op jit(solution)/shard_map/ppermute | solution.py:547
  60.4 1.8 %collective-permute-start.13 = (f32[128,512]{1,0:T(8,128)S(1)}, f32[128,512]{1,0:T(8,128)S(1)}, u32[]{:S(2)}, u32[]{:S(2)}) collective-permute-start(f32[128,512]{1,0:T(8,128)S(1)} %get-tuple-element.123), channel_id=1, source_target_pairs={{1,0},{2,1},{3,2},{0,3},{5,4},{6,5},{7,6},{4,7},{9,8},{10,9},{11,1... | collective-permute-start | bytes 786440 | tf_op jit(solution)/shard_map/ppermute | solution.py:553
  62.2 1.2 %own_chunk.1 = f32[128,512]{1,0:T(8,128)S(1)} custom-call(s32[1]{0:T(128)} %bitcast.side_ref.refs_1_, bf16[8,2048]{1,0:T(8,128)(2,1)S(1)} %bitcast.9, bf16[128,1536]{1,0:T(8,128)(2,1)S(1)} %get-tuple-element.101.refs_0_, bf16[128,8]{1,0:T(8,128)(2,1)S(1)} %get-tuple-element.102.refs_1_, bf16[2,2048,512]{2,1,0:T(8,128)(2,1)S(1)} %get-tuple-element.72.wkq_ref.refs_6_.refs_2_, ...), custom_call_target="tpu_custom_call" | custom-call | tf_op jit(solution)/shard_map/own_chunk/pallas_call | solution.py:474
  63.4 1.2 %decay_sums.1 = f32[8,128]{1,0:T(8,128)} custom-call(s32[1]{0:T(128)} %bitcast.2.place_ref.refs_0_, f32[4,128,128]{2,1,0:T(8,128)S(1)} %get-tuple-element.124.keep_pairs_ref, f32[256,8]{1,0:T(8,128)S(1)} %get-tuple-element.125.keep_terms_ref, f32[4,128,128]{2,1,0:T(8,128)S(1)} %get-tuple-element.126.give_pairs_ref, ...), custom_call_target="tpu_custom_call" | custom-call | tf_op jit(solution)/shard_map/decay_sums/pallas_call | solution.py:500
  64.6 3.2 %collective-permute-done.12 = f32[128,512]{1,0:T(8,128)S(1)} collective-permute-done((f32[128,512]{1,0:T(8,128)S(1)}, f32[128,512]{1,0:T(8,128)S(1)}, u32[]{:S(2)}, u32[]{:S(2)}) %collective-permute-start.12) | collective-permute-done | bytes 262176 | tf_op jit(solution)/shard_map/ppermute | solution.py:553
  (21 shorter events, 7.2 us)
Async XLA Ops:
  8.4 7.1 %collective-permute-start = (f32[4,3,128,128]{3,2,1,0:T(8,128)S(1)}, f32[4,3,128,128]{3,2,1,0:T(8,128)S(1)}, u32[]{:S(2)}, u32[]{:S(2)}) collective-permute-start(f32[4,3,128,128]{3,2,1,0:T(8,128)S(1)} %get-tuple-element.74), channel_id=1, source_target_pairs={{0,4},{4,0},{8,12},{12,8},{16,20},{20,16},{24,28},{28,24},{32,36},... | collective-permute-start | bytes 2359304 | tf_op jit(solution)/shard_map/ppermute | solution.py:495
  16.1 7.8 %collective-permute-start.1 = (f32[3,128,128]{2,1,0:T(8,128)S(1)}, f32[3,128,128]{2,1,0:T(8,128)S(1)}, u32[]{:S(2)}, u32[]{:S(2)}) collective-permute-start(f32[3,128,128]{2,1,0:T(8,128)S(1)} %get-tuple-element.82), channel_id=1, source_target_pairs={{0,8},{4,12},{8,16},{12,20},{16,24},{20,28},{24,0},{28,4},{32,40},... | collective-permute-start | bytes 589832 | tf_op jit(solution)/shard_map/ppermute | solution.py:514
  17.4 11.7 %collective-permute-start.2 = (f32[3,128,128]{2,1,0:T(8,128)S(1)}, f32[3,128,128]{2,1,0:T(8,128)S(1)}, u32[]{:S(2)}, u32[]{:S(2)}) collective-permute-start(f32[3,128,128]{2,1,0:T(8,128)S(1)} %get-tuple-element.83), channel_id=1, source_target_pairs={{0,16},{4,20},{8,24},{12,28},{16,0},{20,4},{24,8},{28,12},{32,48},... | collective-permute-start | bytes 589832 | tf_op jit(solution)/shard_map/ppermute | solution.py:514
  19.9 9.3 %collective-permute-start.3 = (f32[3,128,128]{2,1,0:T(8,128)S(1)}, f32[3,128,128]{2,1,0:T(8,128)S(1)}, u32[]{:S(2)}, u32[]{:S(2)}) collective-permute-start(f32[3,128,128]{2,1,0:T(8,128)S(1)} %get-tuple-element.84), channel_id=1, source_target_pairs={{0,24},{4,28},{8,0},{12,4},{16,8},{20,12},{24,16},{28,20},{32,56},... | collective-permute-start | bytes 589832 | tf_op jit(solution)/shard_map/ppermute | solution.py:514
  21.8 25.8 %copy-start = (bf16[2048,8]{0,1:T(8,128)(2,1)S(1)}, bf16[2048,8]{0,1:T(8,128)(2,1)}, u32[]{:S(2)}) copy-start(bf16[2048,8]{0,1:T(8,128)(2,1)} %param.14) | copy-start | bytes 98308
  29.8 5.5 %collective-permute-start.4 = (f32[128,128]{1,0:T(8,128)S(1)}, f32[128,128]{1,0:T(8,128)S(1)}, u32[]{:S(2)}, u32[]{:S(2)}) collective-permute-start(f32[128,128]{1,0:T(8,128)S(1)} %get-tuple-element.92), channel_id=1, source_target_pairs={{0,32},{4,36},{8,40},{12,44},{16,48},{20,52},{24,56},{28,60},{32,6... | collective-permute-start | bytes 196616 | tf_op jit(solution)/shard_map/ppermute | solution.py:530
  31.5 3.8 %collective-permute-start.5 = (f32[128,128]{1,0:T(8,128)S(1)}, f32[128,128]{1,0:T(8,128)S(1)}, u32[]{:S(2)}, u32[]{:S(2)}) collective-permute-start(f32[128,128]{1,0:T(8,128)S(1)} %get-tuple-element.93), channel_id=1, source_target_pairs={{32,0},{36,4},{40,8},{44,12},{48,16},{52,20},{56,24},{60,28},{64,3... | collective-permute-start | bytes 196616 | tf_op jit(solution)/shard_map/ppermute | solution.py:531
  35.8 5.1 %collective-permute-start.6 = (f32[2,128,128]{2,1,0:T(8,128)S(1)}, f32[2,128,128]{2,1,0:T(8,128)S(1)}, u32[]{:S(2)}, u32[]{:S(2)}) collective-permute-start(f32[2,128,128]{2,1,0:T(8,128)S(1)} %get-tuple-element.95), channel_id=1, source_target_pairs={{0,8},{4,12},{8,16},{12,20},{16,24},{20,28},{24,0},{28,4},{32,40},... | collective-permute-start | bytes 393224 | tf_op jit(solution)/shard_map/ppermute | solution.py:514
  36.6 8.2 %collective-permute-start.7 = (f32[2,128,128]{2,1,0:T(8,128)S(1)}, f32[2,128,128]{2,1,0:T(8,128)S(1)}, u32[]{:S(2)}, u32[]{:S(2)}) collective-permute-start(f32[2,128,128]{2,1,0:T(8,128)S(1)} %get-tuple-element.96), channel_id=1, source_target_pairs={{0,16},{4,20},{8,24},{12,28},{16,0},{20,4},{24,8},{28,12},{32,48},... | collective-permute-start | bytes 393224 | tf_op jit(solution)/shard_map/ppermute | solution.py:514
  39.7 5.0 %collective-permute-start.8 = (f32[2,128,128]{2,1,0:T(8,128)S(1)}, f32[2,128,128]{2,1,0:T(8,128)S(1)}, u32[]{:S(2)}, u32[]{:S(2)}) collective-permute-start(f32[2,128,128]{2,1,0:T(8,128)S(1)} %get-tuple-element.97), channel_id=1, source_target_pairs={{0,24},{4,28},{8,0},{12,4},{16,8},{20,12},{24,16},{28,20},{32,56},... | collective-permute-start | bytes 393224 | tf_op jit(solution)/shard_map/ppermute | solution.py:514
  45.2 5.0 %collective-permute-start.9 = (f32[4,2,128,128]{3,2,1,0:T(8,128)S(1)}, f32[4,2,128,128]{3,2,1,0:T(8,128)S(1)}, u32[]{:S(2)}, u32[]{:S(2)}) collective-permute-start(f32[4,2,128,128]{3,2,1,0:T(8,128)S(1)} %get-tuple-element.103), channel_id=1, source_target_pairs={{0,4},{4,0},{8,12},{12,8},{16,20},{20,16},{24,28},{28,24},{32,36},... | collective-permute-start | bytes 1572872 | tf_op jit(solution)/shard_map/ppermute | solution.py:538
  52.9 6.5 %collective-permute-start.10 = (f32[64,512]{1,0:T(8,128)S(1)}, f32[64,512]{1,0:T(8,128)S(1)}, u32[]{:S(2)}, u32[]{:S(2)}) collective-permute-start(f32[64,512]{1,0:T(8,128)S(1)} %get-tuple-element.112), channel_id=1, source_target_pairs={{0,1},{1,2},{2,3},{3,0},{4,5},{5,6},{6,7},{7,4},{8,9},{9,10},{10,1... | collective-permute-start | bytes 393224 | tf_op jit(solution)/shard_map/ppermute | solution.py:547
  54.2 5.2 %collective-permute-start.11 = (f32[64,512]{1,0:T(8,128)S(1)}, f32[64,512]{1,0:T(8,128)S(1)}, u32[]{:S(2)}, u32[]{:S(2)}) collective-permute-start(f32[64,512]{1,0:T(8,128)S(1)} %get-tuple-element.113), channel_id=1, source_target_pairs={{1,0},{2,1},{3,2},{0,3},{5,4},{6,5},{7,6},{4,7},{9,8},{10,9},{11,1... | collective-permute-start | bytes 393224 | tf_op jit(solution)/shard_map/ppermute | solution.py:547
  59.4 8.4 %collective-permute-start.12 = (f32[128,512]{1,0:T(8,128)S(1)}, f32[128,512]{1,0:T(8,128)S(1)}, u32[]{:S(2)}, u32[]{:S(2)}) collective-permute-start(f32[128,512]{1,0:T(8,128)S(1)} %get-tuple-element.122), channel_id=1, source_target_pairs={{0,1},{1,2},{2,3},{3,0},{4,5},{5,6},{6,7},{7,4},{8,9},{9,10},{10,1... | collective-permute-start | bytes 786440 | tf_op jit(solution)/shard_map/ppermute | solution.py:553
  60.4 7.4 %collective-permute-start.13 = (f32[128,512]{1,0:T(8,128)S(1)}, f32[128,512]{1,0:T(8,128)S(1)}, u32[]{:S(2)}, u32[]{:S(2)}) collective-permute-start(f32[128,512]{1,0:T(8,128)S(1)} %get-tuple-element.123), channel_id=1, source_target_pairs={{1,0},{2,1},{3,2},{0,3},{5,4},{6,5},{7,6},{4,7},{9,8},{10,9},{11,1... | collective-permute-start | bytes 786440 | tf_op jit(solution)/shard_map/ppermute | solution.py:553
